TPU v7x, 32 devices: a whole 2x2x4 slice. The times are simulated.
32 devices in a mesh: rep: 2 (over core), shard: 16 (over z, y, x).
Axes of the slice: x: 2, y: 2, z: 4, core: 2. Of those that a mesh axis runs over, the one named last changes fastest.
Arguments:
- tokens: bfloat16 [12288, 1536], P(('rep', 'shard')), may hold values from -6 to 6
- prompt_ids: int32 [32, 4], P(('rep', 'shard')), may hold values from 0 to 1
- seq_offsets: int32 [32, 4], P(('rep', 'shard')), may hold values from 32 to 64, as said below
- attn_gain: bfloat16 [1536], P('shard'), may hold values from 0.5 to 1.5
- w_query: bfloat16 [1536, 1536], P('shard'), may hold values from -0.15625 to 0.15625
- w_key: bfloat16 [1536, 1536], P('shard'), may hold values from -0.15625 to 0.15625
- w_value: bfloat16 [1536, 1536], P('shard'), may hold values from -0.15625 to 0.15625
- w_outgate: bfloat16 [1536, 1536], P('shard'), may hold values from -0.15625 to 0.15625
- w_forget: bfloat16 [1536, 24], P('shard'), may hold values from -0.15625 to 0.15625
- forget_bias: bfloat16 [24], replicated, may hold values from 1 to 8
- w_output: bfloat16 [1536, 1536], P('shard'), may hold values from -0.625 to 0.625
- ffn_gain: bfloat16 [1536], P('shard'), may hold values from 0.5 to 1.5
- w_gate: bfloat16 [1536, 4096], P('shard'), may hold values from -0.15625 to 0.15625
- w_up: bfloat16 [1536, 4096], P('shard'), may hold values from -0.15625 to 0.15625
- w_down: bfloat16 [4096, 1536], P('shard'), may hold values from -0.09375 to 0.09375
- cotangent: bfloat16 [12288, 1536], P(('rep', 'shard')), may hold values from -6 to 6
Outputs:
- layer_out: bfloat16 [12288, 1536], P(('rep', 'shard'))
- tokens_grad: float32 [12288, 1536], P(('rep', 'shard'))
- attn_gain_grad: float32 [1536], P('shard')
- query_grad: float32 [1536, 1536], P('shard')
- key_grad: float32 [1536, 1536], P('shard')
- value_grad: float32 [1536, 1536], P('shard')
- outgate_grad: float32 [1536, 1536], P('shard')
- forget_grad: float32 [1536, 24], P('shard')
- forget_bias_grad: float32 [24], replicated
- output_grad: float32 [1536, 1536], P('shard')
- ffn_gain_grad: float32 [1536], P('shard')
- gate_grad: float32 [1536, 4096], P('shard')
- up_grad: float32 [1536, 4096], P('shard')
- down_grad: float32 [4096, 1536], P('shard')
Inputs may be any that keep to these rules, and one draw needn't show every extreme that they name: `prompt_ids`: each continuation follows one of the 2 prompts of its own block. `seq_offsets`: in every block at least one continuation follows its whole prompt.
All inputs are finite; a program needn't handle non-finite values.
Results may differ from a plain program's by a relative error of at most 0.023.
Values may be sent and summed in bfloat16 or wider, within the bound.
No kernel may reach another device: no remote copies, remote signals or barrier semaphores. Data moves between devices by JAX's collectives and lax.ppermute only.
A program may use at most 320 MiB of HBM per device.

v0:
```python
import jax
import jax.numpy as jnp
from jax import lax
from jax.sharding import PartitionSpec as P

PLEN = 64
CLEN = 64
NP = 2
NC = 4


EPS = 1e-06
NEGATIVE = -1e30


def chain_mask(prompt_ids, offsets):
    positions = jnp.arange(NP * PLEN + NC * CLEN, dtype=jnp.int32)
    in_prompt = positions < NP * PLEN
    after_prompts = positions - NP * PLEN
    sequence = jnp.where(in_prompt, positions // PLEN, NP + after_prompts // CLEN)
    within = jnp.where(in_prompt, positions % PLEN, after_prompts % CLEN)
    cont_index = sequence - NP
    selector = (cont_index[:, None] == jnp.arange(NC, dtype=jnp.int32)[None, :]).astype(jnp.int32)
    owner_id = jnp.where(in_prompt, -1, jnp.sum(selector * prompt_ids[None, :], axis=1))
    reach_end = jnp.sum(selector * offsets[None, :], axis=1)
    same_seq = (sequence[:, None] == sequence[None, :]) & (within[None, :] <= within[:, None])
    from_prompt = (owner_id[:, None] == sequence[None, :]) & (within[None, :] < reach_end[:, None])
    return same_seq | from_prompt


def normalize(values):
    inverse = lax.rsqrt(jnp.mean(values * values, axis=1, keepdims=True) + EPS)
    return (values * inverse, inverse)


def norm_back(grad_scaled, scaled, inverse):
    return inverse * (grad_scaled - scaled * jnp.mean(grad_scaled * scaled, axis=1, keepdims=True))


def matmul(left_side, right_side):
    return jnp.dot(left_side, right_side, preferred_element_type=jnp.float32)


def matmul_tn(left_side, right_side):
    return lax.dot_general(
        left_side, right_side, (((0,), (0,)), ((), ())), preferred_element_type=jnp.float32
    )


def matmul_nt(left_side, right_side):
    return lax.dot_general(
        left_side, right_side, (((1,), (1,)), ((), ())), preferred_element_type=jnp.float32
    )


def decayed_scores(query_low, key_low, decay_sum, chain_ok, score_scale):
    logits = jnp.einsum("qhd,khd->hqk", query_low, key_low, preferred_element_type=jnp.float32)
    decay_t = decay_sum.T
    logits = logits * score_scale + decay_t[:, :, None] - decay_t[:, None, :]
    return jnp.where(chain_ok[None, :, :], logits, NEGATIVE)


def local(
    tokens,
    prompt_ids,
    seq_offsets,
    attn_gain,
    w_query,
    w_key,
    w_value,
    w_outgate,
    w_forget,
    forget_bias,
    w_output,
    ffn_gain,
    w_gate,
    w_up,
    w_down,
    cotangent,
):
    row_count = tokens.shape[0]
    model_width = tokens.shape[1]
    head_count = w_forget.shape[1]
    head_dim = model_width // head_count
    score_scale = head_dim ** (-0.5)
    chain_ok = chain_mask(prompt_ids[0], seq_offsets[0])
    chain_float = chain_ok.astype(jnp.float32)
    inputs = tokens.astype(jnp.float32)
    scaled1, inverse1 = normalize(inputs)
    gain_part = lax.all_gather(attn_gain, "shard", axis=0, tiled=True)
    query_part = lax.all_gather(w_query, "shard", axis=0, tiled=True)
    key_part = lax.all_gather(w_key, "shard", axis=0, tiled=True)
    value_part = lax.all_gather(w_value, "shard", axis=0, tiled=True)
    outgate_part = lax.all_gather(w_outgate, "shard", axis=0, tiled=True)
    forget_part = lax.all_gather(w_forget, "shard", axis=0, tiled=True)
    normed_part = (scaled1 * gain_part.astype(jnp.float32)).astype(jnp.bfloat16)
    gain_one = gain_part
    normed1 = normed_part
    query_proj = matmul(normed_part, query_part)
    key_proj = matmul(normed_part, key_part)
    value_proj = matmul(normed_part, value_part)
    outgate_pre = matmul(normed_part, outgate_part)
    forget_pre = matmul(normed_part, forget_part)
    query_low = query_proj.astype(jnp.bfloat16).reshape(row_count, head_count, head_dim)
    key_low = key_proj.astype(jnp.bfloat16).reshape(row_count, head_count, head_dim)
    value_low = value_proj.astype(jnp.bfloat16).reshape(row_count, head_count, head_dim)
    forget_in = forget_pre + forget_bias.astype(jnp.float32)[None, :]
    decay_sum = jnp.dot(chain_float, jax.nn.log_sigmoid(forget_in), precision=lax.Precision.HIGHEST)
    logits = decayed_scores(query_low, key_low, decay_sum, chain_ok, score_scale)
    top_score = jnp.max(logits, axis=2, keepdims=True)
    exp_scores = jnp.exp(logits - top_score)
    denominator = jnp.sum(exp_scores, axis=2, keepdims=True)
    log_total = top_score + jnp.log(denominator)
    probs_low = (exp_scores / denominator).astype(jnp.bfloat16)
    attended = jnp.einsum(
        "hqk,khd->qhd", probs_low, value_low, preferred_element_type=jnp.float32
    ).reshape(row_count, model_width)
    gate_open = jax.nn.sigmoid(outgate_pre)
    gated_low = (attended * gate_open).astype(jnp.bfloat16)
    branch_attn = matmul(gated_low, lax.all_gather(w_output, "shard", axis=0, tiled=True))
    residual = inputs + branch_attn
    scaled2, inverse2 = normalize(residual)
    gain_part = lax.all_gather(ffn_gain, "shard", axis=0, tiled=True)
    gate_part = lax.all_gather(w_gate, "shard", axis=0, tiled=True)
    up_part = lax.all_gather(w_up, "shard", axis=0, tiled=True)
    normed_part = (scaled2 * gain_part.astype(jnp.float32)).astype(jnp.bfloat16)
    gate_pre = matmul(normed_part, gate_part)
    up_pre = matmul(normed_part, up_part)
    sig_gate = jax.nn.sigmoid(gate_pre)
    silu_gate = gate_pre * sig_gate
    act_low = (silu_gate * up_pre).astype(jnp.bfloat16)
    branch_ffn = matmul(act_low, lax.all_gather(w_down, "shard", axis=0, tiled=True))
    layer_out = (residual + branch_ffn).astype(jnp.bfloat16)
    grad_out = cotangent.astype(jnp.float32)
    grad_act = matmul_nt(cotangent, lax.all_gather(w_down, "shard", axis=0, tiled=True))
    grad_gate = (grad_act * up_pre * sig_gate * (1.0 + gate_pre * (1.0 - sig_gate))).astype(
        jnp.bfloat16
    )
    grad_up = (grad_act * silu_gate).astype(jnp.bfloat16)
    gate_part = lax.all_gather(w_gate, "shard", axis=0, tiled=True)
    up_part = lax.all_gather(w_up, "shard", axis=0, tiled=True)
    contribution = matmul_nt(grad_gate, gate_part) + matmul_nt(grad_up, up_part)
    grad_normed2 = contribution
    grad_down = matmul_tn(act_low, cotangent)
    grad_gate_w = matmul_tn(normed_part, grad_gate)
    grad_up_w = matmul_tn(normed_part, grad_up)
    grad_gain2 = jnp.sum(grad_normed2 * scaled2, axis=0)
    ffn_parts = (
        lax.psum_scatter(
            grad_gain2.astype(jnp.bfloat16), "shard", scatter_dimension=0, tiled=True
        ).astype(jnp.float32),
        lax.psum_scatter(
            grad_gate_w.astype(jnp.bfloat16), "shard", scatter_dimension=0, tiled=True
        ).astype(jnp.float32),
        lax.psum_scatter(
            grad_up_w.astype(jnp.bfloat16), "shard", scatter_dimension=0, tiled=True
        ).astype(jnp.float32),
        lax.psum_scatter(
            grad_down.astype(jnp.bfloat16), "shard", scatter_dimension=0, tiled=True
        ).astype(jnp.float32),
    )
    grad_resid = grad_out + norm_back(
        grad_normed2 * gain_part.astype(jnp.float32), scaled2, inverse2
    )
    grad_attn = grad_resid.astype(jnp.bfloat16)
    grad_gated = matmul_nt(grad_attn, lax.all_gather(w_output, "shard", axis=0, tiled=True))
    grad_output_w = matmul_tn(gated_low, grad_attn)
    grad_attended = (
        (grad_gated * gate_open).astype(jnp.bfloat16).reshape(row_count, head_count, head_dim)
    )
    grad_outgate = (grad_gated * attended * gate_open * (1.0 - gate_open)).astype(jnp.bfloat16)
    logits = decayed_scores(query_low, key_low, decay_sum, chain_ok, score_scale)
    prob_full = jnp.exp(logits - log_total)
    prob_again = prob_full.astype(jnp.bfloat16)
    grad_probs = jnp.einsum(
        "qhd,khd->hqk", grad_attended, value_low, preferred_element_type=jnp.float32
    )
    grad_value = jnp.einsum(
        "hqk,qhd->khd", prob_again, grad_attended, preferred_element_type=jnp.float32
    )
    grad_logits = prob_full * (grad_probs - jnp.sum(prob_full * grad_probs, axis=2, keepdims=True))
    grad_qk = (grad_logits * score_scale).astype(jnp.bfloat16)
    grad_query = jnp.einsum("hqk,khd->qhd", grad_qk, key_low, preferred_element_type=jnp.float32)
    grad_key = jnp.einsum("hqk,qhd->khd", grad_qk, query_low, preferred_element_type=jnp.float32)
    grad_decay = (jnp.sum(grad_logits, axis=2) - jnp.sum(grad_logits, axis=1)).T
    grad_log_forget = lax.dot_general(
        chain_float, grad_decay, (((0,), (0,)), ((), ())), precision=lax.Precision.HIGHEST
    )
    grad_forget_in = grad_log_forget * jax.nn.sigmoid(-forget_in)
    grad_bias = lax.psum(jnp.sum(grad_forget_in, axis=0), ("rep", "shard"))
    grad_query_low = grad_query.reshape(row_count, model_width).astype(jnp.bfloat16)
    grad_key_low = grad_key.reshape(row_count, model_width).astype(jnp.bfloat16)
    grad_value_low = grad_value.reshape(row_count, model_width).astype(jnp.bfloat16)
    grad_forget_low = grad_forget_in.astype(jnp.bfloat16)
    query_part = lax.all_gather(w_query, "shard", axis=0, tiled=True)
    key_part = lax.all_gather(w_key, "shard", axis=0, tiled=True)
    value_part = lax.all_gather(w_value, "shard", axis=0, tiled=True)
    outgate_part = lax.all_gather(w_outgate, "shard", axis=0, tiled=True)
    forget_part = lax.all_gather(w_forget, "shard", axis=0, tiled=True)
    contribution = (
        matmul_nt(grad_query_low, query_part)
        + matmul_nt(grad_key_low, key_part)
        + matmul_nt(grad_value_low, value_part)
        + matmul_nt(grad_outgate, outgate_part)
        + matmul_nt(grad_forget_low, forget_part)
    )
    grad_query_w = matmul_tn(normed1, grad_query_low)
    grad_key_w = matmul_tn(normed1, grad_key_low)
    grad_value_w = matmul_tn(normed1, grad_value_low)
    grad_outgate_w = matmul_tn(normed1, grad_outgate)
    grad_forget_w = matmul_tn(normed1, grad_forget_low)
    grad_gain1 = jnp.sum(contribution * scaled1, axis=0)
    grad_inputs = grad_resid + norm_back(
        contribution * gain_one.astype(jnp.float32), scaled1, inverse1
    )
    attn_parts = (
        lax.psum_scatter(
            grad_gain1.astype(jnp.bfloat16), "shard", scatter_dimension=0, tiled=True
        ).astype(jnp.float32),
        lax.psum_scatter(
            grad_query_w.astype(jnp.bfloat16), "shard", scatter_dimension=0, tiled=True
        ).astype(jnp.float32),
        lax.psum_scatter(
            grad_key_w.astype(jnp.bfloat16), "shard", scatter_dimension=0, tiled=True
        ).astype(jnp.float32),
        lax.psum_scatter(
            grad_value_w.astype(jnp.bfloat16), "shard", scatter_dimension=0, tiled=True
        ).astype(jnp.float32),
        lax.psum_scatter(
            grad_outgate_w.astype(jnp.bfloat16), "shard", scatter_dimension=0, tiled=True
        ).astype(jnp.float32),
        lax.psum_scatter(
            grad_forget_w.astype(jnp.bfloat16), "shard", scatter_dimension=0, tiled=True
        ).astype(jnp.float32),
        lax.psum_scatter(
            grad_output_w.astype(jnp.bfloat16), "shard", scatter_dimension=0, tiled=True
        ).astype(jnp.float32),
    )
    summed = (
        lax.psum(attn_parts[0].astype(jnp.bfloat16), "rep").astype(jnp.float32),
        lax.psum(attn_parts[1].astype(jnp.bfloat16), "rep").astype(jnp.float32),
        lax.psum(attn_parts[2].astype(jnp.bfloat16), "rep").astype(jnp.float32),
        lax.psum(attn_parts[3].astype(jnp.bfloat16), "rep").astype(jnp.float32),
        lax.psum(attn_parts[4].astype(jnp.bfloat16), "rep").astype(jnp.float32),
        lax.psum(attn_parts[5].astype(jnp.bfloat16), "rep").astype(jnp.float32),
        lax.psum(attn_parts[6].astype(jnp.bfloat16), "rep").astype(jnp.float32),
        lax.psum(ffn_parts[0].astype(jnp.bfloat16), "rep").astype(jnp.float32),
        lax.psum(ffn_parts[1].astype(jnp.bfloat16), "rep").astype(jnp.float32),
        lax.psum(ffn_parts[2].astype(jnp.bfloat16), "rep").astype(jnp.float32),
        lax.psum(ffn_parts[3].astype(jnp.bfloat16), "rep").astype(jnp.float32),
    )
    return (
        layer_out,
        grad_inputs,
        summed[0],
        summed[1],
        summed[2],
        summed[3],
        summed[4],
        summed[5],
        grad_bias,
        summed[6],
        summed[7],
        summed[8],
        summed[9],
        summed[10],
    )


def solution(mesh):
    in_specs = (
        P(("rep", "shard"), None),
        P(("rep", "shard"), None),
        P(("rep", "shard"), None),
        P("shard"),
        P("shard", None),
        P("shard", None),
        P("shard", None),
        P("shard", None),
        P("shard", None),
        P(),
        P("shard", None),
        P("shard"),
        P("shard", None),
        P("shard", None),
        P("shard", None),
        P(("rep", "shard"), None),
    )
    out_specs = (
        P(("rep", "shard"), None),
        P(("rep", "shard"), None),
        P("shard"),
        P("shard", None),
        P("shard", None),
        P("shard", None),
        P("shard", None),
        P("shard", None),
        P(),
        P("shard", None),
        P("shard"),
        P("shard", None),
        P("shard", None),
        P("shard", None),
    )
    return jax.shard_map(local, mesh=mesh, in_specs=in_specs, out_specs=out_specs, check_vma=False)
```

profile of v0, /device:TPU:0, one launch (start us, length us, event | category | flops | bytes accessed | tf_op | source)
XLA Modules:
  0.0 2422.7 jit_solution(16868182657455146212)
XLA Ops:
  14.6 45.2 %all-reduce.5 = (bf16[1536]{0:T(1024)(128)(2,1)S(1)}, bf16[1536]{0:T(1024)(128)(2,1)S(1)}) all-reduce(bf16[1536]{0:T(1024)(128)(2,1)S(1)} %dynamic-update-slice, bf16[1536]{0:T(1024)(128)(2,1)S(1)} %dynamic-update-slice.1), channel_id=1, replica_groups=mesh['rep'=2,'shard'=16] {'shard'}, use_global_device_ids=true, to_apply=%add | all-reduce | flops 3072 | bytes 12288
  59.8 37.5 %all-gather = bf16[16,96,24]{1,2,0:T(8,128)(2,1)S(1)} all-gather(bf16[1,96,24]{1,2,0:T(8,128)(2,1)S(1)} %bitcast.93), channel_id=1, replica_groups=mesh['rep'=2,'shard'=16] {'shard'}, dimensions={0}, use_global_device_ids=true | all-gather | bytes 78336 | tf_op jit(solution)/shard_map/all_gather | solution.py:95
  105.3 71.1 %all-gather.14.cloned.1.call-done = bf16[1536,1536]{1,0:T(8,128)(2,1)} async-done(((bf16[96,1536]{1,0:T(8,128)(2,1)}), bf16[1536,1536]{1,0:T(8,128)(2,1)}) %all-gather.14.cloned.1.call-update) | async-done | bytes 4718608 | tf_op jit(solution)/shard_map/all_gather | solution.py:92
  183.5 74.1 %all-gather.10.cloned.1.call-done = bf16[1536,1536]{1,0:T(8,128)(2,1)} async-done(((bf16[96,1536]{1,0:T(8,128)(2,1)}), bf16[1536,1536]{1,0:T(8,128)(2,1)}) %all-gather.10.cloned.1.call-update) | async-done | bytes 4718608 | tf_op jit(solution)/shard_map/all_gather | solution.py:93
  280.6 9.0 fusion.10
  292.0 46.6 %all-gather.16.cloned.1.call-done = bf16[1536,1536]{1,0:T(8,128)(2,1)} async-done(((bf16[96,1536]{1,0:T(8,128)(2,1)}), bf16[1536,1536]{1,0:T(8,128)(2,1)}) %all-gather.16.cloned.1.call-update) | async-done | bytes 4718608 | tf_op jit(solution)/shard_map/all_gather | solution.py:94
  345.1 74.6 %all-gather.18.cloned.1.call-done = bf16[1536,1536]{1,0:T(8,128)(2,1)} async-done(((bf16[96,1536]{1,0:T(8,128)(2,1)}), bf16[1536,1536]{1,0:T(8,128)(2,1)}) %all-gather.18.cloned.1.call-update) | async-done | bytes 4718608 | tf_op jit(solution)/shard_map/all_gather | solution.py:120
  426.4 146.0 %all-gather.22.cloned.1.call-done = bf16[1536,4096]{1,0:T(8,128)(2,1)} async-done(((bf16[96,4096]{1,0:T(8,128)(2,1)}), bf16[1536,4096]{1,0:T(8,128)(2,1)}) %all-gather.22.cloned.1.call-update) | async-done | bytes 12582928 | tf_op jit(solution)/shard_map/all_gather | solution.py:125
  572.4 9.9 fusion.88
  582.3 142.5 %all-gather.20.cloned.1.call-done = bf16[1536,4096]{1,0:T(8,128)(2,1)} async-done(((bf16[96,4096]{1,0:T(8,128)(2,1)}), bf16[1536,4096]{1,0:T(8,128)(2,1)}) %all-gather.20.cloned.1.call-update) | async-done | bytes 12582928 | tf_op jit(solution)/shard_map/all_gather | solution.py:124
  724.8 9.9 fusion.87
  734.7 142.5 %all-gather.24.cloned.1.call-done = bf16[4096,1536]{1,0:T(8,128)(2,1)} async-done(((bf16[256,1536]{1,0:T(8,128)(2,1)}), bf16[4096,1536]{1,0:T(8,128)(2,1)}) %all-gather.24.cloned.1.call-update) | async-done | bytes 12582928 | tf_op jit(solution)/shard_map/all_gather | solution.py:132
  877.2 15.0 multiply_convert_fusion.1
  892.2 9.7 fusion.89
  902.0 9.3 multiply_reduce_fusion.1
  948.4 22.3 fusion.83
  970.7 8.2 fusion.30
  997.1 11.3 convolution_convert_fusion
  1008.5 11.3 convolution_convert_fusion.1
  1020.0 11.4 convolution_convert_fusion.2
  1048.1 38.9 %psum.90 = f32[24]{0:T(128)} all-reduce(f32[24]{0:T(128)S(1)} %get-tuple-element.53), channel_id=1, replica_groups=mesh['rep'=2,'shard'=16] {'rep','shard'}, use_global_device_ids=true, to_apply=%region_25.26 | all-reduce | flops 24 | bytes 192 | tf_op jit(solution)/shard_map/psum | solution.py:190
  1086.9 110.5 %reduce-scatter.18.cloned.1.call-done = bf16[96,1536]{1,0:T(8,128)(2,1)} async-done(((bf16[1536,1536]{1,0:T(8,128)(2,1)}), bf16[96,1536]{1,0:T(8,128)(2,1)}) %reduce-scatter.18.cloned.1.call-update) | async-done | bytes 294928 | tf_op jit(solution)/shard_map/reduce_scatter | solution.py:229
  1197.4 143.3 %reduce-scatter.16.cloned.1.call-done = bf16[96,1536]{1,0:T(8,128)(2,1)} async-done(((bf16[1536,1536]{1,0:T(8,128)(2,1)}), bf16[96,1536]{1,0:T(8,128)(2,1)}) %reduce-scatter.16.cloned.1.call-update) | async-done | bytes 294928 | tf_op jit(solution)/shard_map/reduce_scatter | solution.py:226
  1340.7 142.9 %reduce-scatter.14.cloned.1.call-done = bf16[96,1536]{1,0:T(8,128)(2,1)} async-done(((bf16[1536,1536]{1,0:T(8,128)(2,1)}), bf16[96,1536]{1,0:T(8,128)(2,1)}) %reduce-scatter.14.cloned.1.call-update) | async-done | bytes 294928 | tf_op jit(solution)/shard_map/reduce_scatter | solution.py:223
  1483.7 143.1 %reduce-scatter.12.cloned.1.call-done = bf16[96,1536]{1,0:T(8,128)(2,1)} async-done(((bf16[1536,1536]{1,0:T(8,128)(2,1)}), bf16[96,1536]{1,0:T(8,128)(2,1)}) %reduce-scatter.12.cloned.1.call-update) | async-done | bytes 294928 | tf_op jit(solution)/shard_map/reduce_scatter | solution.py:220
  1626.7 207.2 %reduce-scatter.26.cloned.1.call-done = bf16[256,1536]{1,0:T(8,128)(2,1)} async-done(((bf16[4096,1536]{1,0:T(8,128)(2,1)}), bf16[256,1536]{1,0:T(8,128)(2,1)}) %reduce-scatter.26.cloned.1.call-update) | async-done | bytes 786448 | tf_op jit(solution)/shard_map/reduce_scatter | solution.py:158
  1834.0 207.7 %reduce-scatter.24.cloned.1.call-done = bf16[96,4096]{1,0:T(8,128)(2,1)} async-done(((bf16[1536,4096]{1,0:T(8,128)(2,1)}), bf16[96,4096]{1,0:T(8,128)(2,1)}) %reduce-scatter.24.cloned.1.call-update) | async-done | bytes 786448 | tf_op jit(solution)/shard_map/reduce_scatter | solution.py:155
  2041.7 207.7 %reduce-scatter.22.cloned.1.call-done = bf16[96,4096]{1,0:T(8,128)(2,1)} async-done(((bf16[1536,4096]{1,0:T(8,128)(2,1)}), bf16[96,4096]{1,0:T(8,128)(2,1)}) %reduce-scatter.22.cloned.1.call-update) | async-done | bytes 786448 | tf_op jit(solution)/shard_map/reduce_scatter | solution.py:152
  2262.4 41.8 %all-reduce.4 = (bf16[1536]{0:T(1024)(128)(2,1)}, bf16[1536]{0:T(1024)(128)(2,1)}) all-reduce(bf16[1536]{0:T(1024)(128)(2,1)S(1)} %get-tuple-element.18, bf16[1536]{0:T(1024)(128)(2,1)} %get-tuple-element.16), channel_id=2, replica_groups=mesh['rep'=2,'shard'=16] {'shard'}, use_global_device_ids=true, to_apply=%region_12.13.clone | all-reduce | flops 3072 | bytes 12288
  2310.8 9.3 fusion.19
  2320.1 56.9 %reduce-scatter.28.cloned.1.call-done = bf16[96,24]{1,0:T(8,128)(2,1)} async-done(((bf16[1536,24]{1,0:T(8,128)(2,1)}), bf16[96,24]{1,0:T(8,128)(2,1)}) %reduce-scatter.28.cloned.1.call-update) | async-done | bytes 4624
  2382.0 22.1 all-reduce.10.cloned.1.call-done
  (191 shorter events, 166.9 us)
Async XLA Ops:
  7.2 52.6 %copy-start.30 = (bf16[96,24]{0,1:T(8,128)(2,1)S(1)}, bf16[96,24]{0,1:T(8,128)(2,1)}, u32[]{:S(2)}) copy-start(bf16[96,24]{0,1:T(8,128)(2,1)} %param.24) | copy-start | bytes 13828
  7.2 90.3 %copy-start.33 = (s32[1,4]{1,0:T(1,128)S(1)}, s32[1,4]{1,0:T(1,128)}, u32[]{:S(2)}) copy-start(s32[1,4]{1,0:T(1,128)} %param.18) | copy-start | bytes 52
  7.2 90.3 %copy-start.32 = (s32[1,4]{1,0:T(1,128)S(1)}, s32[1,4]{1,0:T(1,128)}, u32[]{:S(2)}) copy-start(s32[1,4]{1,0:T(1,128)} %param.17) | copy-start | bytes 52
  7.3 90.4 %copy-start = (bf16[384,1536]{1,0:T(8,128)(2,1)S(1)}, bf16[384,1536]{1,0:T(8,128)(2,1)}, u32[]{:S(2)}) copy-start(bf16[384,1536]{1,0:T(8,128)(2,1)} %param.16) | copy-start | bytes 3538948
  7.3 92.6 %all-gather.12.cloned.1.call-start = ((), (), s32[]{:S(2)}) async-start(), calls=%async_computation.10 | async-start | bytes 5013504 | tf_op jit(solution)/shard_map/all_gather | solution.py:91
  8.0 168.4 %all-gather.14.cloned.1.call-start = ((), (), s32[]{:S(2)}) async-start(), calls=%async_computation.11 | async-start | bytes 5013504 | tf_op jit(solution)/shard_map/all_gather | solution.py:92
  8.7 248.8 %all-gather.10.cloned.1.call-start = ((), (), s32[]{:S(2)}) async-start(), calls=%async_computation.9 | async-start | bytes 5013504 | tf_op jit(solution)/shard_map/all_gather | solution.py:93
  9.5 329.1 %all-gather.16.cloned.1.call-start = ((), (), s32[]{:S(2)}) async-start(), calls=%async_computation.12 | async-start | bytes 5013504 | tf_op jit(solution)/shard_map/all_gather | solution.py:94
  10.1 409.6 %all-gather.18.cloned.1.call-start = ((), (), s32[]{:S(2)}) async-start(), calls=%async_computation.13 | async-start | bytes 5013504 | tf_op jit(solution)/shard_map/all_gather | solution.py:120
  10.6 561.7 %all-gather.22.cloned.1.call-start = ((), (), s32[]{:S(2)}) async-start(), calls=%async_computation.15 | async-start | bytes 13369344 | tf_op jit(solution)/shard_map/all_gather | solution.py:125
  11.2 713.6 %all-gather.20.cloned.1.call-start = ((), (), s32[]{:S(2)}) async-start(), calls=%async_computation.14 | async-start | bytes 13369344 | tf_op jit(solution)/shard_map/all_gather | solution.py:124
  12.0 865.2 %all-gather.24.cloned.1.call-start = ((), (), s32[]{:S(2)}) async-start(), calls=%async_computation.16 | async-start | bytes 13369344 | tf_op jit(solution)/shard_map/all_gather | solution.py:132
  12.7 1074.2 %reduce-scatter.20.cloned.1.call-start = ((), (), s32[]{:S(2)}) async-start(), calls=%async_computation.21 | async-start | bytes 5013504 | tf_op jit(solution)/shard_map/reduce_scatter | solution.py:235
  105.2 160.1 %copy-start.5 = (bf16[384,1536]{0,1:T(8,128)(2,1)}, bf16[384,1536]{0,1:T(8,128)(2,1)S(1)}, u32[]{:S(2)}) copy-start(bf16[384,1536]{0,1:T(8,128)(2,1)S(1)} %copy.67) | copy-start | bytes 3538948
  183.5 81.9 %copy-start.4 = (bf16[384,1536]{0,1:T(8,128)(2,1)}, bf16[384,1536]{0,1:T(8,128)(2,1)S(1)}, u32[]{:S(2)}) copy-start(bf16[384,1536]{0,1:T(8,128)(2,1)S(1)} %copy.68) | copy-start | bytes 3538948
  280.6 9.1 copy-start.22
  292.0 53.1 %copy-start.1 = (f32[384,1536]{1,0:T(8,128)}, f32[384,1536]{1,0:T(8,128)S(1)}, u32[]{:S(2)}) copy-start(f32[384,1536]{1,0:T(8,128)S(1)} %copy.71) | copy-start | bytes 7077892
  424.4 477.5 %copy-start.2 = (f32[384,1536]{1,0:T(8,128)}, f32[384,1536]{1,0:T(8,128)S(1)}, u32[]{:S(2)}) copy-start(f32[384,1536]{1,0:T(8,128)S(1)} %get-tuple-element.49) | copy-start | bytes 7077892
  892.2 9.8 copy-start.29
  892.2 9.8 copy-start.40
  902.0 9.3 copy-start.6
  918.1 279.3 %reduce-scatter.18.cloned.1.call-start = ((), (), s32[]{:S(2)}) async-start(), calls=%async_computation.20 | async-start | bytes 5013504 | tf_op jit(solution)/shard_map/reduce_scatter | solution.py:229
  918.2 7.9 copy-start.27
  930.6 410.2 %reduce-scatter.16.cloned.1.call-start = ((), (), s32[]{:S(2)}) async-start(), calls=%async_computation.19 | async-start | bytes 5013504 | tf_op jit(solution)/shard_map/reduce_scatter | solution.py:226
  948.4 535.3 %reduce-scatter.14.cloned.1.call-start = ((), (), s32[]{:S(2)}) async-start(), calls=%async_computation.18 | async-start | bytes 5013504 | tf_op jit(solution)/shard_map/reduce_scatter | solution.py:223
  984.5 642.2 %reduce-scatter.12.cloned.1.call-start = ((), (), s32[]{:S(2)}) async-start(), calls=%async_computation.17 | async-start | bytes 5013504 | tf_op jit(solution)/shard_map/reduce_scatter | solution.py:220
  997.1 836.9 %reduce-scatter.26.cloned.1.call-start = ((), (), s32[]{:S(2)}) async-start(), calls=%async_computation.24 | async-start | bytes 13369344 | tf_op jit(solution)/shard_map/reduce_scatter | solution.py:158
  1008.5 1033.2 %reduce-scatter.24.cloned.1.call-start = ((), (), s32[]{:S(2)}) async-start(), calls=%async_computation.23 | async-start | bytes 13369344 | tf_op jit(solution)/shard_map/reduce_scatter | solution.py:155
  1019.9 1229.5 %reduce-scatter.22.cloned.1.call-start = ((), (), s32[]{:S(2)}) async-start(), calls=%async_computation.22 | async-start | bytes 13369344 | tf_op jit(solution)/shard_map/reduce_scatter | solution.py:152
  1031.4 1345.7 %reduce-scatter.28.cloned.1.call-start = ((), (), s32[]{:S(2)}) async-start(), calls=%async_computation.25 | async-start | bytes 417792
  1037.0 1367.0 %all-reduce.10.cloned.1.call-start = ((), (), s32[]{:S(2)}) async-start(), calls=%async_computation.26 | async-start | bytes 7667712 | tf_op jit(solution)/shard_map/psum | solution.py:241
  2310.7 67.1 %copy-start.34 = (bf16[96]{0:T(256)(128)(2,1)S(1)}, bf16[96]{0:T(256)(128)(2,1)}, u32[]{:S(2)}) copy-start(bf16[96]{0:T(256)(128)(2,1)} %dynamic-slice.5) | copy-start | bytes 580
  (28 other events, 108.1 us)
Sparse Core Ops, SparseCore 0:
  10.9 83.8 all-gather.11
  97.6 78.7 all-gather.13
  179.2 78.3 all-gather.9
  260.2 78.3 all-gather.15
  341.3 78.3 all-gather.17
  422.3 150.0 all-gather.21
  575.2 149.5 all-gather.19
  727.6 149.5 all-gather.23
  918.3 136.5 reduce-scatter.19
  1059.9 137.4 reduce-scatter.17
  1202.6 138.0 reduce-scatter.15
  1345.8 137.8 reduce-scatter.13
  1488.8 137.8 reduce-scatter.11
  1632.2 201.6 reduce-scatter.25
  1839.5 202.1 reduce-scatter.23
  2047.2 202.1 reduce-scatter.21
  2254.5 122.4 reduce-scatter.27
  2379.7 24.2 all-reduce.9
where the time goes:
time: 2430 us; the launch traced here: 2420 us
  waiting for transfers between devices  1940 us (80%)
  matrix products  243 us (10%)
  blocking collectives  166 us (7%)
  other arithmetic  30.7 us (1%)
    reduce_scatter x1, waiting for transfers between devices, local(): lax.psum_scatter(grad_up_w.astype(jnp.bfloat16), 'shard', scatter_dimensi...  208 us
    reduce_scatter x1, waiting for transfers between devices, local(): lax.psum_scatter(grad_gate_w.astype(jnp.bfloat16), 'shard', scatter_dimen...  208 us
    reduce_scatter x1, waiting for transfers between devices, local(): lax.psum_scatter(grad_down.astype(jnp.bfloat16), 'shard', scatter_dimensi...  207 us
    all_gather x1, waiting for transfers between devices, local(): up_part = lax.all_gather(w_up, 'shard', axis=0, tiled=True)  146 us
    reduce_scatter x1, waiting for transfers between devices, local(): lax.psum_scatter(grad_value_w.astype(jnp.bfloat16), 'shard', scatter_dime...  143 us
    reduce_scatter x1, waiting for transfers between devices, local(): lax.psum_scatter(grad_query_w.astype(jnp.bfloat16), 'shard', scatter_dime...  143 us
    reduce_scatter x1, waiting for transfers between devices, local(): lax.psum_scatter(grad_key_w.astype(jnp.bfloat16), 'shard', scatter_dimens...  143 us
    all_gather x1, waiting for transfers between devices, local(): gate_part = lax.all_gather(w_gate, 'shard', axis=0, tiled=True)  142 us
  transfers between devices with their start and end apart: 18, of which 16 were waited for; matrix products, arithmetic and copies ran while one was open for 10% of the time, Pallas kernels for 0%

commit v1 on v0

v1 whole, which is shorter than its diff:
```python
import jax
import jax.numpy as jnp
from jax import lax
from jax.sharding import PartitionSpec as P

PLEN = 64
CLEN = 64
NP = 2
NC = 4


EPS = 1e-06
NEGATIVE = -1e30


def chain_mask(prompt_ids, offsets):
    positions = jnp.arange(NP * PLEN + NC * CLEN, dtype=jnp.int32)
    in_prompt = positions < NP * PLEN
    after_prompts = positions - NP * PLEN
    sequence = jnp.where(in_prompt, positions // PLEN, NP + after_prompts // CLEN)
    within = jnp.where(in_prompt, positions % PLEN, after_prompts % CLEN)
    cont_index = sequence - NP
    selector = (cont_index[:, None] == jnp.arange(NC, dtype=jnp.int32)[None, :]).astype(jnp.int32)
    owner_id = jnp.where(in_prompt, -1, jnp.sum(selector * prompt_ids[None, :], axis=1))
    reach_end = jnp.sum(selector * offsets[None, :], axis=1)
    same_seq = (sequence[:, None] == sequence[None, :]) & (within[None, :] <= within[:, None])
    from_prompt = (owner_id[:, None] == sequence[None, :]) & (within[None, :] < reach_end[:, None])
    return same_seq | from_prompt


def normalize(values):
    inverse = lax.rsqrt(jnp.mean(values * values, axis=1, keepdims=True) + EPS)
    return (values * inverse, inverse)


def norm_back(grad_scaled, scaled, inverse):
    return inverse * (grad_scaled - scaled * jnp.mean(grad_scaled * scaled, axis=1, keepdims=True))


def matmul(left_side, right_side):
    return jnp.dot(left_side, right_side, preferred_element_type=jnp.float32)


def matmul_tn(left_side, right_side):
    return lax.dot_general(
        left_side, right_side, (((0,), (0,)), ((), ())), preferred_element_type=jnp.float32
    )


def matmul_nt(left_side, right_side):
    return lax.dot_general(
        left_side, right_side, (((1,), (1,)), ((), ())), preferred_element_type=jnp.float32
    )


def grid_of(count):
    grid = ((4, count // 4), (2, count // 8))
    return grid if count == 16 else grid + ((2, count // 16),)


def coord_of(index, dim):
    return (index // dim[1]) % dim[0]


def moves(count, dim, steps):
    pairs = []
    for source in range(count):
        at = coord_of(source, dim)
        if at in steps:
            pairs.append((source, source + (steps[at] - at) * dim[1]))
    return pairs


SWAP2 = {0: 1, 1: 0}
PAIRS = {0: 1, 1: 0, 2: 3, 3: 2}
MIDDLE = {1: 2, 2: 1}
OUTWARD = {1: 0, 2: 3}
INWARD = {0: 1, 3: 2}
FARTHER = {0: 2, 2: 0, 1: 3, 3: 1}


def both(low_first, mine, other):
    return jnp.stack([jnp.where(low_first, mine, other), jnp.where(low_first, other, mine)])


def gather_dim(held, count, index, dim):
    at = coord_of(index, dim)
    if dim[0] == 2:
        other = lax.ppermute(held, "shard", moves(count, dim, SWAP2))
        return both(at == 0, held, other)
    other = lax.ppermute(held, "shard", moves(count, dim, PAIRS))
    half = both(at % 2 == 0, held, other)
    middle = lax.ppermute(half, "shard", moves(count, dim, MIDDLE))
    outer = lax.ppermute(middle, "shard", moves(count, dim, OUTWARD))
    far = jnp.where((at == 1) | (at == 2), middle, outer)
    return both(at < 2, half, far).reshape((4,) + held.shape)


def gather_rows(block, count, index):
    grid = grid_of(count)
    held = block
    for dim in grid:
        held = gather_dim(held, count, index, dim)
    turn = tuple(range(len(grid) - 1, -1, -1))
    held = jnp.transpose(held, turn + (len(grid), len(grid) + 1))
    return held.reshape(-1, block.shape[-1])


def add_low(left_side, right_side):
    return (left_side.astype(jnp.float32) + right_side.astype(jnp.float32)).astype(jnp.bfloat16)


def pick(values, at, axis):
    return lax.dynamic_index_in_dim(values, at, axis, keepdims=False)


def scatter_dim(values, axis, count, index, dim):
    at = coord_of(index, dim)
    if dim[0] == 2:
        other = lax.ppermute(pick(values, 1 - at, axis), "shard", moves(count, dim, SWAP2))
        return add_low(pick(values, at, axis), other)
    shape = values.shape
    halves = values.reshape(shape[:axis] + (2, 2) + shape[axis + 1 :])
    far = pick(halves, 1 - at // 2, axis)
    near = pick(halves, at // 2, axis)
    arrived = lax.ppermute(far, "shard", moves(count, dim, INWARD))
    arrived = lax.ppermute(add_low(far, arrived), "shard", moves(count, dim, MIDDLE))
    near = add_low(near, arrived)
    other = lax.ppermute(pick(near, 1 - at % 2, axis), "shard", moves(count, dim, PAIRS))
    return add_low(pick(near, at % 2, axis), other)


def scatter_rows(values, count, index):
    grid = grid_of(count)
    rows = values.shape[0] // (count // 2)
    held = values.reshape(tuple(dim[0] for dim in grid) + (rows, values.shape[1]))
    for axis in range(len(grid) - 1, -1, -1):
        held = scatter_dim(held, axis, count, index, grid[axis])
    return held


def sum_all(values, count, reps):
    total = values
    for dim in grid_of(count) + ((2, 1),):
        if dim[0] == 2:
            total = total + lax.ppermute(total, "shard", moves(count, dim, SWAP2))
        else:
            total = total + lax.ppermute(total, "shard", moves(count, dim, PAIRS))
            total = total + lax.ppermute(total, "shard", moves(count, dim, FARTHER))
    step = 1
    while step < reps:
        total = total + lax.ppermute(total, "rep", [(r, r ^ step) for r in range(reps)])
        step *= 2
    return total


def local(
    tokens,
    prompt_ids,
    seq_offsets,
    attn_gain,
    w_query,
    w_key,
    w_value,
    w_outgate,
    w_forget,
    forget_bias,
    w_output,
    ffn_gain,
    w_gate,
    w_up,
    w_down,
    cotangent,
    *,
    reps,
    count,
):
    own_rows = tokens.shape[0]
    model_width = tokens.shape[1]
    head_count = w_forget.shape[1]
    head_dim = model_width // head_count
    score_scale = head_dim ** (-0.5)
    team = 4
    core = lax.axis_index("rep") % 2
    index = lax.axis_index("shard")
    side = index % 2
    rank = 2 * side + core
    quarter = model_width // team
    heads = head_count // team
    shard_rows = w_query.shape[0]
    shard_ff = w_down.shape[0]
    unit = shard_ff // 2
    quarter_ff = w_gate.shape[1] // team
    core_pairs = [(r, r ^ 1) for r in range(reps)]
    side_pairs = [(s, s ^ 1) for s in range(count)]

    def swap_core(values):
        return lax.ppermute(values, "rep", core_pairs)

    def swap_side(values):
        return lax.ppermute(values, "shard", side_pairs)

    def team_rows(values):
        pair = jnp.concatenate([values, swap_side(values)], axis=0)
        return jnp.concatenate([pair, swap_core(pair)], axis=0)

    def team_sum(partial):
        half = 2 * own_rows
        pair = partial[:half] + swap_core(partial[half:].astype(jnp.bfloat16)).astype(jnp.float32)
        return pair[:own_rows] + swap_side(pair[own_rows:].astype(jnp.bfloat16)).astype(jnp.float32)

    def gather(block):
        return gather_rows(block, count, index)

    def scatter(values):
        return scatter_rows(values, count, index)

    def cols_of(values, who):
        return lax.dynamic_slice_in_dim(values, who * quarter, quarter, axis=1)

    def units_of(values, which_side):
        cut = values.reshape(values.shape[0], count // 2, 2, 2, unit)
        return pick(pick(cut, core, 3), which_side, 2).reshape(values.shape[0], quarter_ff)

    def pair_rows(mine, sent):
        return both(side == 0, mine, swap_side(sent)).reshape(-1, mine.shape[1])

    small = jnp.concatenate(
        [
            w_forget,
            attn_gain[:, None],
            ffn_gain[:, None],
            jnp.zeros((shard_rows, 128 - head_count - 2), jnp.bfloat16),
        ],
        axis=1,
    )
    far_rank = rank ^ 2

    def columns(who, *weights):
        return [cols_of(w, who) for w in weights]

    first = gather(
        pair_rows(
            jnp.concatenate(columns(rank, w_query, w_key, w_value) + [small], axis=1),
            jnp.concatenate(columns(far_rank, w_query, w_key, w_value) + [small], axis=1),
        )
    )
    second = gather(
        pair_rows(
            jnp.concatenate(columns(rank, w_outgate, w_output), axis=1),
            jnp.concatenate(columns(far_rank, w_outgate, w_output), axis=1),
        )
    )
    gate_w = gather(pair_rows(units_of(w_gate, side), units_of(w_gate, 1 - side)))
    up_w = gather(pair_rows(units_of(w_up, side), units_of(w_up, 1 - side)))
    down_w = gather(lax.dynamic_slice_in_dim(w_down, core * unit, unit, axis=0))

    query_w = first[:, :quarter]
    key_w = first[:, quarter : 2 * quarter]
    value_w = first[:, 2 * quarter : 3 * quarter]
    forget_w = lax.dynamic_slice_in_dim(
        first[:, 3 * quarter : 3 * quarter + head_count], rank * heads, heads, axis=1
    )
    gain_one = first[:, 3 * quarter + head_count].astype(jnp.float32)
    gain_two = first[:, 3 * quarter + head_count + 1].astype(jnp.float32)
    outgate_w = second[:, :quarter]
    output_cols = second[:, quarter:]

    def turn_rows(values):
        cut = values.reshape(2, 2, quarter, quarter)
        mine = pick(cut, side, 0)
        pair = both(side == 0, mine, swap_side(pick(cut, 1 - side, 0)))
        kept = pick(pair, core, 1)
        quad = both(core == 0, kept, swap_core(pick(pair, 1 - core, 1)))
        return jnp.transpose(quad, (2, 1, 0, 3)).reshape(quarter, model_width)

    def turn_cols(values):
        cut = values.reshape(quarter, 2, 2, quarter)
        mine = pick(cut, core, 2)
        pair = both(core == 0, mine, swap_core(pick(cut, 1 - core, 2)))
        kept = pick(pair, side, 2)
        quad = both(side == 0, kept, swap_side(pick(pair, 1 - side, 2)))
        return quad.reshape(model_width, quarter)

    output_w = turn_rows(output_cols)

    tokens_all = team_rows(tokens)
    cotangent_all = team_rows(cotangent)
    facts_all = team_rows(jnp.concatenate([prompt_ids[0], seq_offsets[0]])[None, :])
    chain_ok = jnp.stack([chain_mask(facts_all[b, :NC], facts_all[b, NC:]) for b in range(team)])
    chain_float = chain_ok.astype(jnp.float32)

    inputs_all = tokens_all.astype(jnp.float32)
    scaled_all, inverse_all = normalize(inputs_all)
    scaled1 = scaled_all[:own_rows]
    inverse1 = inverse_all[:own_rows]
    inputs = inputs_all[:own_rows]
    normed1 = (scaled_all * gain_one).astype(jnp.bfloat16)
    row_count = normed1.shape[0]

    def split_heads(values):
        return values.reshape(team, own_rows, heads, head_dim)

    query_low = split_heads(matmul(normed1, query_w).astype(jnp.bfloat16))
    key_low = split_heads(matmul(normed1, key_w).astype(jnp.bfloat16))
    value_low = split_heads(matmul(normed1, value_w).astype(jnp.bfloat16))
    outgate_pre = matmul(normed1, outgate_w)
    bias_mine = lax.dynamic_slice_in_dim(
        forget_bias.astype(jnp.float32), rank * heads, heads, axis=0
    )
    forget_in = matmul(normed1, forget_w) + bias_mine[None, :]
    log_forget = jax.nn.log_sigmoid(forget_in).reshape(team, own_rows, heads)
    decay_sum = jnp.einsum(
        "bij,bjh->bhi", chain_float, log_forget, precision=lax.Precision.HIGHEST
    )

    def decayed_scores():
        logits = jnp.einsum(
            "bqhd,bkhd->bhqk", query_low, key_low, preferred_element_type=jnp.float32
        )
        logits = logits * score_scale + decay_sum[:, :, :, None] - decay_sum[:, :, None, :]
        return jnp.where(chain_ok[:, None, :, :], logits, NEGATIVE)

    logits = decayed_scores()
    top_score = jnp.max(logits, axis=3, keepdims=True)
    exp_scores = jnp.exp(logits - top_score)
    denominator = jnp.sum(exp_scores, axis=3, keepdims=True)
    log_total = top_score + jnp.log(denominator)
    probs_low = (exp_scores / denominator).astype(jnp.bfloat16)
    attended = jnp.einsum(
        "bhqk,bkhd->bqhd", probs_low, value_low, preferred_element_type=jnp.float32
    ).reshape(row_count, quarter)
    gate_open = jax.nn.sigmoid(outgate_pre)
    gated_low = (attended * gate_open).astype(jnp.bfloat16)

    residual = inputs + team_sum(matmul(gated_low, output_w))
    scaled2, inverse2 = normalize(residual)
    normed2 = team_rows((scaled2 * gain_two).astype(jnp.bfloat16))
    gate_pre = matmul(normed2, gate_w)
    up_pre = matmul(normed2, up_w)
    sig_gate = jax.nn.sigmoid(gate_pre)
    silu_gate = gate_pre * sig_gate
    act_low = (silu_gate * up_pre).astype(jnp.bfloat16)
    layer_out = (residual + team_sum(matmul(act_low, down_w))).astype(jnp.bfloat16)

    grad_act = matmul_nt(cotangent_all, down_w)
    grad_gate = (grad_act * up_pre * sig_gate * (1.0 + gate_pre * (1.0 - sig_gate))).astype(
        jnp.bfloat16
    )
    grad_up = (grad_act * silu_gate).astype(jnp.bfloat16)
    grad_down = scatter(matmul_tn(act_low, cotangent_all).astype(jnp.bfloat16))
    grad_gate_w = scatter(matmul_tn(normed2, grad_gate).astype(jnp.bfloat16))
    grad_up_w = scatter(matmul_tn(normed2, grad_up).astype(jnp.bfloat16))
    grad_normed2 = team_sum(matmul_nt(grad_gate, gate_w) + matmul_nt(grad_up, up_w))
    grad_gain2 = jnp.sum(grad_normed2 * scaled2, axis=0)
    grad_resid = cotangent.astype(jnp.float32) + norm_back(
        grad_normed2 * gain_two, scaled2, inverse2
    )
    grad_attn = team_rows(grad_resid.astype(jnp.bfloat16))
    grad_gated = matmul_nt(grad_attn, output_w)
    grad_output_cols = turn_cols(matmul_tn(gated_low, grad_attn).astype(jnp.bfloat16))
    grad_attended = split_heads((grad_gated * gate_open).astype(jnp.bfloat16))
    grad_outgate = (grad_gated * attended * gate_open * (1.0 - gate_open)).astype(jnp.bfloat16)
    grad_outgate_w = matmul_tn(normed1, grad_outgate).astype(jnp.bfloat16)
    sum_second = scatter(jnp.concatenate([grad_outgate_w, grad_output_cols], axis=1))
    logits = decayed_scores()
    prob_full = jnp.exp(logits - log_total)
    prob_again = prob_full.astype(jnp.bfloat16)
    grad_probs = jnp.einsum(
        "bqhd,bkhd->bhqk", grad_attended, value_low, preferred_element_type=jnp.float32
    )
    grad_value = jnp.einsum(
        "bhqk,bqhd->bkhd", prob_again, grad_attended, preferred_element_type=jnp.float32
    )
    grad_logits = prob_full * (grad_probs - jnp.sum(prob_full * grad_probs, axis=3, keepdims=True))
    grad_qk = (grad_logits * score_scale).astype(jnp.bfloat16)
    grad_query = jnp.einsum("bhqk,bkhd->bqhd", grad_qk, key_low, preferred_element_type=jnp.float32)
    grad_key = jnp.einsum("bhqk,bqhd->bkhd", grad_qk, query_low, preferred_element_type=jnp.float32)
    grad_decay = jnp.sum(grad_logits, axis=3) - jnp.sum(grad_logits, axis=2)
    grad_log_forget = jnp.einsum(
        "bij,bhi->bjh", chain_float, grad_decay, precision=lax.Precision.HIGHEST
    ).reshape(row_count, heads)
    grad_forget_in = grad_log_forget * jax.nn.sigmoid(-forget_in)
    bias_sum = lax.dynamic_update_slice_in_dim(
        jnp.zeros((head_count,), jnp.float32),
        jnp.sum(grad_forget_in, axis=0),
        rank * heads,
        axis=0,
    )
    grad_bias = sum_all(bias_sum[None, :], count, reps)[0]
    grad_query_low = grad_query.reshape(row_count, quarter).astype(jnp.bfloat16)
    grad_key_low = grad_key.reshape(row_count, quarter).astype(jnp.bfloat16)
    grad_value_low = grad_value.reshape(row_count, quarter).astype(jnp.bfloat16)
    grad_forget_low = grad_forget_in.astype(jnp.bfloat16)

    grad_normed1 = team_sum(
        matmul_nt(grad_query_low, query_w)
        + matmul_nt(grad_key_low, key_w)
        + matmul_nt(grad_value_low, value_w)
        + matmul_nt(grad_outgate, outgate_w)
        + matmul_nt(grad_forget_low, forget_w)
    )
    grad_query_w = matmul_tn(normed1, grad_query_low).astype(jnp.bfloat16)
    grad_key_w = matmul_tn(normed1, grad_key_low).astype(jnp.bfloat16)
    grad_value_w = matmul_tn(normed1, grad_value_low).astype(jnp.bfloat16)
    grad_forget_w = lax.dynamic_update_slice_in_dim(
        jnp.zeros((model_width, head_count), jnp.float32),
        matmul_tn(normed1, grad_forget_low),
        rank * heads,
        axis=1,
    )
    grad_gain1 = jnp.sum(grad_normed1 * scaled1, axis=0)
    tokens_grad = grad_resid + norm_back(grad_normed1 * gain_one, scaled1, inverse1)
    grad_small = jnp.concatenate(
        [
            grad_forget_w,
            grad_gain1[:, None],
            grad_gain2[:, None],
            jnp.zeros((model_width, 128 - head_count - 2), jnp.float32),
        ],
        axis=1,
    ).astype(jnp.bfloat16)
    sum_first = scatter(jnp.concatenate([grad_query_w, grad_key_w, grad_value_w], axis=1))
    sum_small = scatter(grad_small)

    def replicas(values):
        total = values
        step = 2
        while step < reps:
            other = lax.ppermute(total, "rep", [(r, r ^ step) for r in range(reps)])
            total = add_low(total, other)
            step *= 2
        return total

    def own_of(values):
        pair = replicas(values).reshape(2, shard_rows, values.shape[1])
        sides = both(side == 0, pick(pair, side, 0), swap_side(pick(pair, 1 - side, 0)))
        cores = both(core == 0, sides, swap_core(sides))
        return jnp.transpose(cores.astype(jnp.float32), (1, 0, 2, 3))

    def whole_cols(values):
        parts = values.shape[1] // quarter
        quad = own_of(values).reshape(2, 2, shard_rows, parts, quarter)
        quad = jnp.transpose(quad, (3, 2, 0, 1, 4)).reshape(parts, shard_rows, model_width)
        return [quad[p] for p in range(parts)]

    def whole_units(values):
        quad = own_of(values).reshape(2, 2, shard_rows, count // 2, unit)
        return jnp.transpose(quad, (2, 3, 0, 1, 4)).reshape(shard_rows, team * quarter_ff)

    small_pair = replicas(sum_small).reshape(2, shard_rows, sum_small.shape[1])
    small_own = add_low(pick(small_pair, side, 0), swap_side(pick(small_pair, 1 - side, 0)))
    small_own = small_own.astype(jnp.float32) + swap_core(small_own).astype(jnp.float32)
    down_mine = replicas(grad_down)
    down_own = both(core == 0, down_mine, swap_core(down_mine)).astype(jnp.float32)
    query_g, key_g, value_g = whole_cols(sum_first)
    outgate_g, output_g = whole_cols(sum_second)
    return (
        layer_out,
        tokens_grad,
        small_own[:, head_count],
        query_g,
        key_g,
        value_g,
        outgate_g,
        small_own[:, :head_count],
        grad_bias,
        output_g,
        small_own[:, head_count + 1],
        whole_units(grad_gate_w),
        whole_units(grad_up_w),
        down_own.reshape(shard_ff, model_width),
    )


def solution(mesh):
    in_specs = (
        P(("rep", "shard"), None),
        P(("rep", "shard"), None),
        P(("rep", "shard"), None),
        P("shard"),
        P("shard", None),
        P("shard", None),
        P("shard", None),
        P("shard", None),
        P("shard", None),
        P(),
        P("shard", None),
        P("shard"),
        P("shard", None),
        P("shard", None),
        P("shard", None),
        P(("rep", "shard"), None),
    )
    out_specs = (
        P(("rep", "shard"), None),
        P(("rep", "shard"), None),
        P("shard"),
        P("shard", None),
        P("shard", None),
        P("shard", None),
        P("shard", None),
        P("shard", None),
        P(),
        P("shard", None),
        P("shard"),
        P("shard", None),
        P("shard", None),
        P("shard", None),
    )

    def program(*arrays):
        return local(*arrays, reps=mesh.shape["rep"], count=mesh.shape["shard"])

    return jax.shard_map(program, mesh=mesh, in_specs=in_specs, out_specs=out_specs, check_vma=False)
```

time: 2430 us -> 956 us (0.39)
  waiting for transfers between devices: 1940 us -> 279 us
  starting transfers between devices: 0.97 us -> 226 us
  blocking collectives: 166 us -> 0 us
  local copies, waits for them, and re-layouts: 21.3 us -> 127 us
  other arithmetic: 30.7 us -> 115 us
  matrix products: 243 us -> 197 us
    reduce_scatter x8 -> x0, waiting for transfers between devices: 1160 us -> none  [the longest x1 208 us: local(): lax.psum_scatter(grad_up_w.astype(jnp.bfloat16), 'shard', scatter_dimensi...]
    all_gather x8 -> x0, waiting for transfers between devices: 697 us -> none  [the longest x1 146 us: local(): up_part = lax.all_gather(w_up, 'shard', axis=0, tiled=True)]
    ppermute x0 -> x86, waiting for transfers between devices: none -> 279 us  [the longest x20 74.7 us: swap_side(): return lax.ppermute(values, 'shard', side_pairs)]
    ppermute x0 -> x86, starting transfers between devices: none -> 226 us  [the longest x6 84.6 us: scatter_dim(): arrived = lax.ppermute(far, 'shard', moves(count, dim, INWARD))]
    unnamed x2 -> x0, blocking collectives: 87 us -> none
    unnamed x19 -> x0, waiting for transfers between devices: 62.1 us -> none
    psum x2 -> x0, blocking collectives: 41.4 us -> none  [the longest x1 38.9 us: local(): grad_bias = lax.psum(jnp.sum(grad_forget_in, axis=0), ('rep', 'shard'))]
    all_gather x1 -> x0, blocking collectives: 37.5 us -> none  [local(): forget_part = lax.all_gather(w_forget, 'shard', axis=0, tiled=True)]
  transfers between devices with their start and end apart: 18 -> 86, of which waited for: 16 -> 30; matrix products, arithmetic and copies ran while one was open for 10% -> 33% of each run, Pallas kernels for 0% -> 0%
where the time goes in v1:
time: 956 us; the launch traced here: 946 us
  waiting for transfers between devices  279 us (29%)
  starting transfers between devices  226 us (24%)
  matrix products  197 us (21%)
  local copies, waits for them, and re-layouts  127 us (13%)
  other arithmetic  115 us (12%)
    ppermute x6, starting transfers between devices, scatter_dim(): arrived = lax.ppermute(far, 'shard', moves(count, dim, INWARD))  84.6 us
    ppermute x20, waiting for transfers between devices, swap_side(): return lax.ppermute(values, 'shard', side_pairs)  74.7 us
    ppermute x5, waiting for transfers between devices, gather_dim(): other = lax.ppermute(held, 'shard', moves(count, dim, SWAP2))  69.4 us
    ppermute x6, starting transfers between devices, scatter_dim(): lax.ppermute(pick(near, 1 - at % 2, axis), 'shard', moves(count, dim, PAI...  64.6 us
    dot_general x9, matrix products, matmul_nt(): lax.dot_general(left_side, right_side, (((1,), (1,)), ((), ())), preferre...  62.2 us
    ppermute x5, waiting for transfers between devices, gather_dim(): outer = lax.ppermute(middle, 'shard', moves(count, dim, OUTWARD))  57.5 us
    dot_general x9, matrix products, matmul(): return jnp.dot(left_side, right_side, preferred_element_type=jnp.float32)  49.5 us
    dot_general x9, matrix products, matmul_tn(): lax.dot_general(left_side, right_side, (((0,), (0,)), ((), ())), preferre...  33.7 us
  transfers between devices with their start and end apart: 86, of which 30 were waited for; matrix products, arithmetic and copies ran while one was open for 33% of the time, Pallas kernels for 0%

profile of v1, /device:TPU:0, one launch (start us, length us, event | category | flops | bytes accessed | tf_op | source)
XLA Modules:
  0.0 946.0 jit_solution(7676814455442185831)
XLA Ops:
  32.5 8.0 collective-permute-done.3
  48.6 11.8 %collective-permute-done.12 = bf16[2,192,768]{2,1,0:T(8,128)(2,1)S(1)} collective-permute-done((bf16[2,192,768]{2,1,0:T(8,128)(2,1)S(1)}, bf16[2,192,768]{2,1,0:T(8,128)(2,1)S(1)}, u32[]{:S(2)}, u32[]{:S(2)}) %collective-permute-start.12) | collective-permute-done | bytes 589856 | tf_op jit(solution)/shard_map/ppermute | solution.py:94
  61.1 9.0 collective-permute-done
  73.2 16.4 %collective-permute-done.5 = bf16[2,192,1280]{2,1,0:T(8,128)(2,1)S(1)} collective-permute-done((bf16[2,192,1280]{2,1,0:T(8,128)(2,1)S(1)}, bf16[2,192,1280]{2,1,0:T(8,128)(2,1)S(1)}, u32[]{:S(2)}, u32[]{:S(2)}) %collective-permute-start.5) | collective-permute-done | bytes 983072 | tf_op jit(solution)/shard_map/ppermute | solution.py:94
  100.7 11.3 %collective-permute-done.14 = bf16[2,384,384]{2,1,0:T(8,128)(2,1)S(1)} collective-permute-done((bf16[2,384,384]{2,1,0:T(8,128)(2,1)S(1)}, bf16[2,384,384]{2,1,0:T(8,128)(2,1)S(1)}, u32[]{:S(2)}, u32[]{:S(2)}) %collective-permute-start.14) | collective-permute-done | bytes 589856 | tf_op jit(solution)/shard_map/ppermute | solution.py:201
  127.5 9.2 collective-permute-done.6
  140.4 9.6 %broadcast_multiply_fusion = (f32[1536,1536]{1,0:T(8,128)}, bf16[1536,1536]{1,0:T(8,128)(2,1)S(1)}) fusion(f32[1536]{0:T(1024)S(1)} %add_rsqrt_fusion, bf16[768,1536]{1,0:T(8,128)(2,1)S(1)} %collective-permute-done.1, bf16[384,1536]{1,0:T(8,128)(2,1)S(1)} %copy-done.8, bf16[384,1536]{1,0:T(8,128)(2,1)S(1)} %copy-done.6, f32[1536]{0:T(1024)S(1)} %get-tuple-element.63), kind=kLoop, calls=%fused_computation.38 | loop fusion | flops 21233664 | bytes 18886656 | tf_op jit(solution)/shard_map/mul | solution.py:33
  211.5 7.7 multiply_convert_fusion.10
  258.1 15.3 %collective-permute-done.32 = bf16[2,128,1536]{2,1,0:T(8,128)(2,1)S(1)} collective-permute-done((bf16[2,128,1536]{2,1,0:T(8,128)(2,1)}, bf16[2,128,1536]{2,1,0:T(8,128)(2,1)S(1)}, u32[]{:S(2)}, u32[]{:S(2)}) %collective-permute-start.32) | collective-permute-done | bytes 786464 | tf_op jit(solution)/shard_map/ppermute | solution.py:94
  276.7 9.4 collective-permute-done.17
  292.9 14.0 %collective-permute-done.28 = bf16[2,192,1024]{2,1,0:T(8,128)(2,1)} collective-permute-done((bf16[2,192,1024]{2,1,0:T(8,128)(2,1)}, bf16[2,192,1024]{2,1,0:T(8,128)(2,1)}, u32[]{:S(2)}, u32[]{:S(2)}) %collective-permute-start.28) | collective-permute-done | bytes 786464 | tf_op jit(solution)/shard_map/ppermute | solution.py:94
  318.8 27.3 %collective-permute-done.29 = bf16[4,192,1024]{2,1,0:T(8,128)(2,1)S(1)} collective-permute-done((bf16[4,192,1024]{2,1,0:T(8,128)(2,1)S(1)}, bf16[4,192,1024]{2,1,0:T(8,128)(2,1)S(1)}, u32[]{:S(2)}, u32[]{:S(2)}) %collective-permute-start.29) | collective-permute-done | bytes 1572896 | tf_op jit(solution)/shard_map/ppermute | solution.py:89
  347.0 30.6 %collective-permute-done.24 = bf16[4,192,1024]{2,1,0:T(8,128)(2,1)S(1)} collective-permute-done((bf16[4,192,1024]{2,1,0:T(8,128)(2,1)S(1)}, bf16[4,192,1024]{2,1,0:T(8,128)(2,1)S(1)}, u32[]{:S(2)}, u32[]{:S(2)}) %collective-permute-start.24) | collective-permute-done | bytes 1572896 | tf_op jit(solution)/shard_map/ppermute | solution.py:89
  379.4 9.3 fusion.140
  388.7 9.0 fusion.141
  397.7 14.4 %multiply_convert_fusion.2 = (bf16[1536,1024]{1,0:T(8,128)(2,1)}, bf16[1536,1024]{1,0:T(8,128)(2,1)}, bf16[1536,1024]{1,0:T(8,128)(2,1)}) fusion(f32[1536,1024]{1,0:T(8,128)} %fusion.141, f32[1536,1024]{1,0:T(8,128)} %fusion.140, bf16[1536,1536]{1,0:T(8,128)(2,1)} %copy-done.73, bf16[1024,1536]{1,0:T(8,128)(2,1)S(1)} %bitcast.620), kind=kOutput, calls=%fused_computation.22 | convolution fusion | flops 4855431168 | bytes 29884416 | tf_op jit(solution)/shard_map/dot_general | solution.py:51
  412.2 7.7 convolution_convert_fusion
  451.0 11.0 %convolution_add_fusion.4 = f32[1536,1536]{1,0:T(8,128)} fusion(f32[1536,1536]{1,0:T(8,128)} %fusion.160, bf16[1536,1024]{1,0:T(8,128)(2,1)} %get-tuple-element.84, bf16[1536,1024]{1,0:T(8,128)(2,1)S(1)} %bitcast.615), kind=kOutput, calls=%fused_computation.17 | convolution fusion | flops 4834197504 | bytes 25165824 | tf_op jit(solution)/shard_map/dot_general | solution.py:51
  468.0 25.7 %collective-permute-start.82 = (bf16[2,128,1536]{2,1,0:T(8,128)(2,1)}, bf16[2,128,1536]{2,1,0:T(8,128)(2,1)}, u32[]{:S(2)}, u32[]{:S(2)}) collective-permute-start(bf16[2,128,1536]{2,1,0:T(8,128)(2,1)} %dynamic-slice_bitcast_fusion.5), channel_id=1, source_target_pairs={{0,4},{1,5},{2,6},{3,7},{12,8},{13,9},{14,10},{15,11},{16,20},{17,... | collective-permute-start | bytes 2359304 | tf_op jit(solution)/shard_map/ppermute | solution.py:126
  499.3 25.8 %collective-permute-start.76 = (bf16[2,192,1024]{2,1,0:T(8,128)(2,1)}, bf16[2,192,1024]{2,1,0:T(8,128)(2,1)}, u32[]{:S(2)}, u32[]{:S(2)}) collective-permute-start(bf16[2,192,1024]{2,1,0:T(8,128)(2,1)} %dynamic-slice_bitcast_fusion.6), channel_id=1, source_target_pairs={{0,4},{1,5},{2,6},{3,7},{12,8},{13,9},{14,10},{15,11},{16,20},{17,... | collective-permute-start | bytes 2359304 | tf_op jit(solution)/shard_map/ppermute | solution.py:126
  529.9 25.9 %collective-permute-start.70 = (bf16[2,192,1024]{2,1,0:T(8,128)(2,1)}, bf16[2,192,1024]{2,1,0:T(8,128)(2,1)}, u32[]{:S(2)}, u32[]{:S(2)}) collective-permute-start(bf16[2,192,1024]{2,1,0:T(8,128)(2,1)} %dynamic-slice_bitcast_fusion.7), channel_id=1, source_target_pairs={{0,4},{1,5},{2,6},{3,7},{12,8},{13,9},{14,10},{15,11},{16,20},{17,... | collective-permute-start | bytes 2359304 | tf_op jit(solution)/shard_map/ppermute | solution.py:126
  573.0 9.3 collective-permute-start.84
  583.4 15.8 %collective-permute-start.78 = (bf16[192,1024]{1,0:T(8,128)(2,1)}, bf16[192,1024]{1,0:T(8,128)(2,1)}, u32[]{:S(2)}, u32[]{:S(2)}) collective-permute-start(bf16[192,1024]{1,0:T(8,128)(2,1)} %dynamic-slice_bitcast_fusion.12), channel_id=1, source_target_pairs={{0,4},{1,5},{2,6},{3,7},{4,0},{5,1},{6,2},{7,3},{8,12},{9,13},{10,... | collective-permute-start | bytes 1179656 | tf_op jit(solution)/shard_map/ppermute | solution.py:129
  600.3 12.0 %collective-permute-start.72 = (bf16[192,1024]{1,0:T(8,128)(2,1)}, bf16[192,1024]{1,0:T(8,128)(2,1)}, u32[]{:S(2)}, u32[]{:S(2)}) collective-permute-start(bf16[192,1024]{1,0:T(8,128)(2,1)} %dynamic-slice_bitcast_fusion.13), channel_id=1, source_target_pairs={{0,4},{1,5},{2,6},{3,7},{4,0},{5,1},{6,2},{7,3},{8,12},{9,13},{10,... | collective-permute-start | bytes 1179656 | tf_op jit(solution)/shard_map/ppermute | solution.py:129
  625.2 22.5 %collective-permute-done.79 = bf16[96,1024]{1,0:T(8,128)(2,1)S(1)} collective-permute-done((bf16[96,1024]{1,0:T(8,128)(2,1)S(1)}, bf16[96,1024]{1,0:T(8,128)(2,1)S(1)}, u32[]{:S(2)}, u32[]{:S(2)}) %collective-permute-start.79) | collective-permute-done | bytes 196640 | tf_op jit(solution)/shard_map/ppermute | solution.py:201
  661.2 8.2 multiply_convert_fusion.7
  671.3 20.8 %fusion.142 = (f32[4,6,384]{2,1,0:T(8,128)}, f32[4,6,384]{2,1,0:T(8,128)}, f32[4,6,384,384]{2,3,1,0:T(8,128)}) fusion(f32[4,6,384,384]{2,3,1,0:T(8,128)} %get-tuple-element.190, f32[4,6,384]{2,1,0:T(8,128)S(1)} %copy-done.75, bf16[4,384,6,64]{1,0,3,2:T(4,128)(2,1)S(1)} %reshape.1205, bf16[4,384,6,64]{1,0,3,2:T(4,128)(2,1)} %reshape.1181), kind=kOutput, calls=%fused_computation.434 | convolution fusion | flops 930733440 | bytes 30781440 | tf_op jit(solution)/shard_map/sub | solution.py:375
  692.1 8.8 fusion.38
  770.5 8.1 collective-permute-done.57
  790.4 23.9 %collective-permute-done.66 = f32[1,24]{1,0:T(1,128)S(1)} collective-permute-done((f32[1,24]{1,0:T(1,128)S(1)}, f32[1,24]{1,0:T(1,128)S(1)}, u32[]{:S(2)}, u32[]{:S(2)}) %collective-permute-start.66) | collective-permute-done | bytes 128 | tf_op jit(solution)/shard_map/ppermute | solution.py:146
  832.0 23.8 %collective-permute-done.59 = bf16[2,192,768]{2,1,0:T(8,128)(2,1)S(1)} collective-permute-done((bf16[2,192,768]{2,1,0:T(8,128)(2,1)S(1)}, bf16[2,192,768]{2,1,0:T(8,128)(2,1)S(1)}, u32[]{:S(2)}, u32[]{:S(2)}) %collective-permute-start.59) | collective-permute-done | bytes 589856 | tf_op jit(solution)/shard_map/ppermute | solution.py:126
  860.9 16.6 %collective-permute-start.61 = (bf16[192,768]{1,0:T(8,128)(2,1)}, bf16[192,768]{1,0:T(8,128)(2,1)}, u32[]{:S(2)}, u32[]{:S(2)}) collective-permute-start(bf16[192,768]{1,0:T(8,128)(2,1)} %dynamic-slice_bitcast_fusion.14), channel_id=1, source_target_pairs={{0,4},{1,5},{2,6},{3,7},{4,0},{5,1},{6,2},{7,3},{8,12},{9,13},{10,... | collective-permute-start | bytes 884744 | tf_op jit(solution)/shard_map/ppermute | solution.py:129
  (656 shorter events, 464.4 us)
Async XLA Ops:
  2.6 227.6 %collective-permute-start.30 = (bf16[128,1536]{1,0:T(8,128)(2,1)}, bf16[128,1536]{1,0:T(8,128)(2,1)}, u32[]{:S(2)}, u32[]{:S(2)}) collective-permute-start(bf16[128,1536]{1,0:T(8,128)(2,1)} %constant_dynamic-slice_fusion.3), channel_id=1, source_target_pairs={{0,4},{1,5},{2,6},{3,7},{4,0},{5,1},{6,2},{7,3},{8,12},{9,13},{10,... | collective-permute-start | bytes 1179656 | tf_op jit(solution)/shard_map/ppermute | solution.py:91
  12.0 83.8 %collective-permute-start.20 = (bf16[96,1024]{1,0:T(8,128)(2,1)}, bf16[96,1024]{1,0:T(8,128)(2,1)}, u32[]{:S(2)}, u32[]{:S(2)}) collective-permute-start(bf16[96,1024]{1,0:T(8,128)(2,1)} %bitcast.549), channel_id=1, source_target_pairs={{0,1},{1,0},{2,3},{3,2},{4,5},{5,4},{6,7},{7,6},{8,9},{9,8},{10,11... | collective-permute-start | bytes 589832 | tf_op jit(solution)/shard_map/ppermute | solution.py:201
  44.6 45.0 %collective-permute-start.5 = (bf16[2,192,1280]{2,1,0:T(8,128)(2,1)S(1)}, bf16[2,192,1280]{2,1,0:T(8,128)(2,1)S(1)}, u32[]{:S(2)}, u32[]{:S(2)}) collective-permute-start(bf16[2,192,1280]{2,1,0:T(8,128)(2,1)S(1)} %collective-permute-done.4), channel_id=1, source_target_pairs={{4,0},{5,1},{6,2},{7,3},{8,12},{9,13},{10,14},{11,15},{20,16},{21,... | collective-permute-start | bytes 2949128 | tf_op jit(solution)/shard_map/ppermute | solution.py:94
  60.3 38.7 %collective-permute-start.25 = (bf16[96,1024]{1,0:T(8,128)(2,1)}, bf16[96,1024]{1,0:T(8,128)(2,1)S(1)}, u32[]{:S(2)}, u32[]{:S(2)}) collective-permute-start(bf16[96,1024]{1,0:T(8,128)(2,1)} %bitcast.548), channel_id=1, source_target_pairs={{0,1},{1,0},{2,3},{3,2},{4,5},{5,4},{6,7},{7,6},{8,9},{9,8},{10,11... | collective-permute-start | bytes 589832 | tf_op jit(solution)/shard_map/ppermute | solution.py:201
  93.5 43.2 %collective-permute-start.6 = (bf16[4,192,1280]{2,1,0:T(8,128)(2,1)}, bf16[4,192,1280]{2,1,0:T(8,128)(2,1)}, u32[]{:S(2)}, u32[]{:S(2)}) collective-permute-start(bf16[4,192,1280]{2,1,0:T(8,128)(2,1)} %bitcast.9), channel_id=1, source_target_pairs={{0,2},{1,3},{2,0},{3,1},{4,6},{5,7},{6,4},{7,5},{8,10},{9,11},{10,... | collective-permute-start | bytes 5898248 | tf_op jit(solution)/shard_map/ppermute | solution.py:89
  99.1 147.2 %collective-permute-start.36 = (bf16[384,1536]{1,0:T(8,128)(2,1)}, bf16[384,1536]{1,0:T(8,128)(2,1)}, u32[]{:S(2)}, u32[]{:S(2)}) collective-permute-start(bf16[384,1536]{1,0:T(8,128)(2,1)} %param.31), channel_id=1, source_target_pairs={{0,1},{1,0},{2,3},{3,2},{4,5},{5,4},{6,7},{7,6},{8,9},{9,8},{10,11... | collective-permute-start | bytes 3538952 | tf_op jit(solution)/shard_map/ppermute | solution.py:201
  112.0 121.9 %collective-permute-start.21 = (bf16[192,1024]{1,0:T(8,128)(2,1)}, bf16[192,1024]{1,0:T(8,128)(2,1)}, u32[]{:S(2)}, u32[]{:S(2)}) collective-permute-start(bf16[192,1024]{1,0:T(8,128)(2,1)} %bitcast.57), channel_id=1, source_target_pairs={{0,4},{1,5},{2,6},{3,7},{4,0},{5,1},{6,2},{7,3},{8,12},{9,13},{10,... | collective-permute-start | bytes 1179656 | tf_op jit(solution)/shard_map/ppermute | solution.py:91
  249.4 61.6 %collective-permute-start.37 = (bf16[768,1536]{1,0:T(8,128)(2,1)}, bf16[768,1536]{1,0:T(8,128)(2,1)}, u32[]{:S(2)}, u32[]{:S(2)}) collective-permute-start(bf16[768,1536]{1,0:T(8,128)(2,1)} %pad_maximum_fusion.9), channel_id=1, source_target_pairs={{0,16},{16,0},{1,17},{17,1},{2,18},{18,2},{3,19},{19,3},{4,20},{20... | collective-permute-start | bytes 7077896 | tf_op jit(solution)/shard_map/ppermute | solution.py:198
  250.7 41.2 %collective-permute-start.23 = (bf16[2,192,1024]{2,1,0:T(8,128)(2,1)}, bf16[2,192,1024]{2,1,0:T(8,128)(2,1)S(1)}, u32[]{:S(2)}, u32[]{:S(2)}) collective-permute-start(bf16[2,192,1024]{2,1,0:T(8,128)(2,1)} %collective-permute-done.22), channel_id=1, source_target_pairs={{4,0},{5,1},{6,2},{7,3},{8,12},{9,13},{10,14},{11,15},{20,16},{21,... | collective-permute-start | bytes 2359304 | tf_op jit(solution)/shard_map/ppermute | solution.py:94
  252.1 54.8 %collective-permute-start.28 = (bf16[2,192,1024]{2,1,0:T(8,128)(2,1)}, bf16[2,192,1024]{2,1,0:T(8,128)(2,1)}, u32[]{:S(2)}, u32[]{:S(2)}) collective-permute-start(bf16[2,192,1024]{2,1,0:T(8,128)(2,1)} %collective-permute-done.27), channel_id=1, source_target_pairs={{4,0},{5,1},{6,2},{7,3},{8,12},{9,13},{10,14},{11,15},{20,16},{21,... | collective-permute-start | bytes 2359304 | tf_op jit(solution)/shard_map/ppermute | solution.py:94
  273.8 43.1 %collective-permute-start.33 = (bf16[4,128,1536]{2,1,0:T(8,128)(2,1)S(1)}, bf16[4,128,1536]{2,1,0:T(8,128)(2,1)}, u32[]{:S(2)}, u32[]{:S(2)}) collective-permute-start(bf16[4,128,1536]{2,1,0:T(8,128)(2,1)S(1)} %bitcast.598), channel_id=1, source_target_pairs={{0,2},{1,3},{2,0},{3,1},{4,6},{5,7},{6,4},{7,5},{8,10},{9,11},{10,... | collective-permute-start | bytes 4718600 | tf_op jit(solution)/shard_map/ppermute | solution.py:89
  308.8 37.3 %collective-permute-start.29 = (bf16[4,192,1024]{2,1,0:T(8,128)(2,1)S(1)}, bf16[4,192,1024]{2,1,0:T(8,128)(2,1)S(1)}, u32[]{:S(2)}, u32[]{:S(2)}) collective-permute-start(bf16[4,192,1024]{2,1,0:T(8,128)(2,1)S(1)} %bitcast.600), channel_id=1, source_target_pairs={{0,2},{1,3},{2,0},{3,1},{4,6},{5,7},{6,4},{7,5},{8,10},{9,11},{10,... | collective-permute-start | bytes 4718600 | tf_op jit(solution)/shard_map/ppermute | solution.py:89
  310.5 67.1 %collective-permute-start.24 = (bf16[4,192,1024]{2,1,0:T(8,128)(2,1)S(1)}, bf16[4,192,1024]{2,1,0:T(8,128)(2,1)S(1)}, u32[]{:S(2)}, u32[]{:S(2)}) collective-permute-start(bf16[4,192,1024]{2,1,0:T(8,128)(2,1)S(1)} %bitcast.599), channel_id=1, source_target_pairs={{0,2},{1,3},{2,0},{3,1},{4,6},{5,7},{6,4},{7,5},{8,10},{9,11},{10,... | collective-permute-start | bytes 4718600 | tf_op jit(solution)/shard_map/ppermute | solution.py:89
  316.8 62.6 %collective-permute-start.19 = (bf16[768,1536]{1,0:T(8,128)(2,1)S(1)}, bf16[768,1536]{1,0:T(8,128)(2,1)S(1)}, u32[]{:S(2)}, u32[]{:S(2)}) collective-permute-start(bf16[768,1536]{1,0:T(8,128)(2,1)S(1)} %pad_maximum_fusion.8), channel_id=1, source_target_pairs={{0,16},{16,0},{1,17},{17,1},{2,18},{18,2},{3,19},{19,3},{4,20},{20... | collective-permute-start | bytes 7077896 | tf_op jit(solution)/shard_map/ppermute | solution.py:198
  425.2 40.1 %collective-permute-start.81 = (bf16[4,128,1536]{2,1,0:T(8,128)(2,1)S(1)}, bf16[4,128,1536]{2,1,0:T(8,128)(2,1)}, u32[]{:S(2)}, u32[]{:S(2)}) collective-permute-start(bf16[4,128,1536]{2,1,0:T(8,128)(2,1)S(1)} %dynamic-slice_bitcast_fusion.1), channel_id=1, source_target_pairs={{0,2},{1,3},{2,0},{3,1},{4,6},{5,7},{6,4},{7,5},{8,10},{9,11},{10,... | collective-permute-start | bytes 4718600 | tf_op jit(solution)/shard_map/ppermute | solution.py:120
  433.4 62.9 %collective-permute-start.75 = (bf16[4,192,1024]{2,1,0:T(8,128)(2,1)}, bf16[4,192,1024]{2,1,0:T(8,128)(2,1)}, u32[]{:S(2)}, u32[]{:S(2)}) collective-permute-start(bf16[4,192,1024]{2,1,0:T(8,128)(2,1)} %dynamic-slice_bitcast_fusion.2), channel_id=1, source_target_pairs={{0,2},{1,3},{2,0},{3,1},{4,6},{5,7},{6,4},{7,5},{8,10},{9,11},{10,... | collective-permute-start | bytes 4718600 | tf_op jit(solution)/shard_map/ppermute | solution.py:120
  449.5 77.4 %collective-permute-start.69 = (bf16[4,192,1024]{2,1,0:T(8,128)(2,1)}, bf16[4,192,1024]{2,1,0:T(8,128)(2,1)}, u32[]{:S(2)}, u32[]{:S(2)}) collective-permute-start(bf16[4,192,1024]{2,1,0:T(8,128)(2,1)} %dynamic-slice_bitcast_fusion.3), channel_id=1, source_target_pairs={{0,2},{1,3},{2,0},{3,1},{4,6},{5,7},{6,4},{7,5},{8,10},{9,11},{10,... | collective-permute-start | bytes 4718600 | tf_op jit(solution)/shard_map/ppermute | solution.py:120
  450.9 104.9 %collective-permute-start.34 = (bf16[768,1536]{1,0:T(8,128)(2,1)S(1)}, bf16[768,1536]{1,0:T(8,128)(2,1)}, u32[]{:S(2)}, u32[]{:S(2)}) collective-permute-start(bf16[768,1536]{1,0:T(8,128)(2,1)S(1)} %slice.289), channel_id=1, source_target_pairs={{0,16},{16,0},{1,17},{17,1},{2,18},{18,2},{3,19},{19,3},{4,20},{20... | collective-permute-start | bytes 7077896 | tf_op jit(solution)/shard_map/ppermute | solution.py:198
  464.7 96.5 %collective-permute-start.38 = (bf16[768,1536]{1,0:T(8,128)(2,1)S(1)}, bf16[768,1536]{1,0:T(8,128)(2,1)}, u32[]{:S(2)}, u32[]{:S(2)}) collective-permute-start(bf16[768,1536]{1,0:T(8,128)(2,1)S(1)} %slice.288), channel_id=1, source_target_pairs={{0,16},{16,0},{1,17},{17,1},{2,18},{18,2},{3,19},{19,3},{4,20},{20... | collective-permute-start | bytes 7077896 | tf_op jit(solution)/shard_map/ppermute | solution.py:198
  468.0 91.1 %collective-permute-start.82 = (bf16[2,128,1536]{2,1,0:T(8,128)(2,1)}, bf16[2,128,1536]{2,1,0:T(8,128)(2,1)}, u32[]{:S(2)}, u32[]{:S(2)}) collective-permute-start(bf16[2,128,1536]{2,1,0:T(8,128)(2,1)} %dynamic-slice_bitcast_fusion.5), channel_id=1, source_target_pairs={{0,4},{1,5},{2,6},{3,7},{12,8},{13,9},{14,10},{15,11},{16,20},{17,... | collective-permute-start | bytes 2359304 | tf_op jit(solution)/shard_map/ppermute | solution.py:126
  499.3 67.2 %collective-permute-start.76 = (bf16[2,192,1024]{2,1,0:T(8,128)(2,1)}, bf16[2,192,1024]{2,1,0:T(8,128)(2,1)}, u32[]{:S(2)}, u32[]{:S(2)}) collective-permute-start(bf16[2,192,1024]{2,1,0:T(8,128)(2,1)} %dynamic-slice_bitcast_fusion.6), channel_id=1, source_target_pairs={{0,4},{1,5},{2,6},{3,7},{12,8},{13,9},{14,10},{15,11},{16,20},{17,... | collective-permute-start | bytes 2359304 | tf_op jit(solution)/shard_map/ppermute | solution.py:126
  529.9 39.5 %collective-permute-start.70 = (bf16[2,192,1024]{2,1,0:T(8,128)(2,1)}, bf16[2,192,1024]{2,1,0:T(8,128)(2,1)}, u32[]{:S(2)}, u32[]{:S(2)}) collective-permute-start(bf16[2,192,1024]{2,1,0:T(8,128)(2,1)} %dynamic-slice_bitcast_fusion.7), channel_id=1, source_target_pairs={{0,4},{1,5},{2,6},{3,7},{12,8},{13,9},{14,10},{15,11},{16,20},{17,... | collective-permute-start | bytes 2359304 | tf_op jit(solution)/shard_map/ppermute | solution.py:126
  558.3 54.9 %collective-permute-start.35 = (bf16[384,1536]{1,0:T(8,128)(2,1)S(1)}, bf16[384,1536]{1,0:T(8,128)(2,1)S(1)}, u32[]{:S(2)}, u32[]{:S(2)}) collective-permute-start(bf16[384,1536]{1,0:T(8,128)(2,1)S(1)} %slice.293), channel_id=1, source_target_pairs={{0,1},{1,0},{2,3},{3,2},{4,5},{5,4},{6,7},{7,6},{8,9},{9,8},{10,11... | collective-permute-start | bytes 3538952 | tf_op jit(solution)/shard_map/ppermute | solution.py:201
  565.2 47.2 %collective-permute-start.39 = (bf16[384,1536]{1,0:T(8,128)(2,1)S(1)}, bf16[384,1536]{1,0:T(8,128)(2,1)S(1)}, u32[]{:S(2)}, u32[]{:S(2)}) collective-permute-start(bf16[384,1536]{1,0:T(8,128)(2,1)S(1)} %slice.292), channel_id=1, source_target_pairs={{0,1},{1,0},{2,3},{3,2},{4,5},{5,4},{6,7},{7,6},{8,9},{9,8},{10,11... | collective-permute-start | bytes 3538952 | tf_op jit(solution)/shard_map/ppermute | solution.py:201
  573.0 46.6 %collective-permute-start.84 = (bf16[128,1536]{1,0:T(8,128)(2,1)}, bf16[128,1536]{1,0:T(8,128)(2,1)}, u32[]{:S(2)}, u32[]{:S(2)}) collective-permute-start(bf16[128,1536]{1,0:T(8,128)(2,1)} %dynamic-slice_bitcast_fusion.11), channel_id=1, source_target_pairs={{0,4},{1,5},{2,6},{3,7},{4,0},{5,1},{6,2},{7,3},{8,12},{9,13},{10,... | collective-permute-start | bytes 1179656 | tf_op jit(solution)/shard_map/ppermute | solution.py:129
  583.4 37.3 %collective-permute-start.78 = (bf16[192,1024]{1,0:T(8,128)(2,1)}, bf16[192,1024]{1,0:T(8,128)(2,1)}, u32[]{:S(2)}, u32[]{:S(2)}) collective-permute-start(bf16[192,1024]{1,0:T(8,128)(2,1)} %dynamic-slice_bitcast_fusion.12), channel_id=1, source_target_pairs={{0,4},{1,5},{2,6},{3,7},{4,0},{5,1},{6,2},{7,3},{8,12},{9,13},{10,... | collective-permute-start | bytes 1179656 | tf_op jit(solution)/shard_map/ppermute | solution.py:129
  719.7 62.3 %collective-permute-start.64 = (f32[1,24]{1,0:T(1,128)S(1)}, f32[1,24]{1,0:T(1,128)S(1)}, u32[]{:S(2)}, u32[]{:S(2)}) collective-permute-start(f32[1,24]{1,0:T(1,128)S(1)} %dynamic_update_slice.10), channel_id=1, source_target_pairs={{0,4},{1,5},{2,6},{3,7},{4,0},{5,1},{6,2},{7,3},{8,12},{9,13},{10,... | collective-permute-start | bytes 296 | tf_op jit(solution)/shard_map/ppermute | solution.py:148
  747.9 70.0 %collective-permute-start.50 = (bf16[4,192,1152]{2,1,0:T(8,128)(2,1)}, bf16[4,192,1152]{2,1,0:T(8,128)(2,1)}, u32[]{:S(2)}, u32[]{:S(2)}) collective-permute-start(bf16[4,192,1152]{2,1,0:T(8,128)(2,1)} %dynamic-slice_bitcast_fusion), channel_id=1, source_target_pairs={{0,2},{1,3},{2,0},{3,1},{4,6},{5,7},{6,4},{7,5},{8,10},{9,11},{10,... | collective-permute-start | bytes 5308424 | tf_op jit(solution)/shard_map/ppermute | solution.py:120
  767.8 59.2 %collective-permute-start.42 = (bf16[768,1536]{1,0:T(8,128)(2,1)}, bf16[768,1536]{1,0:T(8,128)(2,1)}, u32[]{:S(2)}, u32[]{:S(2)}) collective-permute-start(bf16[768,1536]{1,0:T(8,128)(2,1)} %slice.287), channel_id=1, source_target_pairs={{0,16},{16,0},{1,17},{17,1},{2,18},{18,2},{3,19},{19,3},{4,20},{20... | collective-permute-start | bytes 7077896 | tf_op jit(solution)/shard_map/ppermute | solution.py:198
  780.0 44.0 %collective-permute-start.58 = (bf16[4,192,768]{2,1,0:T(8,128)(2,1)}, bf16[4,192,768]{2,1,0:T(8,128)(2,1)}, u32[]{:S(2)}, u32[]{:S(2)}) collective-permute-start(bf16[4,192,768]{2,1,0:T(8,128)(2,1)} %fusion.44), channel_id=1, source_target_pairs={{0,2},{1,3},{2,0},{3,1},{4,6},{5,7},{6,4},{7,5},{8,10},{9,11},{10,... | collective-permute-start | bytes 3538952 | tf_op jit(solution)/shard_map/ppermute | solution.py:120
  817.8 38.8 %collective-permute-start.68 = (f32[1,24]{1,0:T(1,128)S(1)}, f32[1,24]{1,0:T(1,128)S(1)}, u32[]{:S(2)}, u32[]{:S(2)}) collective-permute-start(f32[1,24]{1,0:T(1,128)S(1)} %add.661), channel_id=1, source_target_pairs={{0,16},{16,0},{1,17},{17,1},{2,18},{18,2},{3,19},{19,3},{4,20},{20... | collective-permute-start | bytes 296 | tf_op jit(solution)/shard_map/ppermute | solution.py:152
  830.9 46.5 %collective-permute-start.43 = (bf16[384,1536]{1,0:T(8,128)(2,1)S(1)}, bf16[384,1536]{1,0:T(8,128)(2,1)S(1)}, u32[]{:S(2)}, u32[]{:S(2)}) collective-permute-start(bf16[384,1536]{1,0:T(8,128)(2,1)S(1)} %slice.291), channel_id=1, source_target_pairs={{0,1},{1,0},{2,3},{3,2},{4,5},{5,4},{6,7},{7,6},{8,9},{9,8},{10,11... | collective-permute-start | bytes 3538952 | tf_op jit(solution)/shard_map/ppermute | solution.py:201
  (168 other events, 2109.9 us)

commit v2 on v1

v2 whole, which is shorter than its diff:
```python
import jax
import jax.numpy as jnp
from jax import lax
from jax.experimental import pallas as pl
from jax.experimental.pallas import tpu as pltpu
from jax.sharding import PartitionSpec as P

PLEN = 64
CLEN = 64
NP = 2
NC = 4


EPS = 1e-06
NEGATIVE = -1e30


def chain_mask(prompt_ids, offsets):
    positions = jnp.arange(NP * PLEN + NC * CLEN, dtype=jnp.int32)
    in_prompt = positions < NP * PLEN
    after_prompts = positions - NP * PLEN
    sequence = jnp.where(in_prompt, positions // PLEN, NP + after_prompts // CLEN)
    within = jnp.where(in_prompt, positions % PLEN, after_prompts % CLEN)
    cont_index = sequence - NP
    selector = (cont_index[:, None] == jnp.arange(NC, dtype=jnp.int32)[None, :]).astype(jnp.int32)
    owner_id = jnp.where(in_prompt, -1, jnp.sum(selector * prompt_ids[None, :], axis=1))
    reach_end = jnp.sum(selector * offsets[None, :], axis=1)
    same_seq = (sequence[:, None] == sequence[None, :]) & (within[None, :] <= within[:, None])
    from_prompt = (owner_id[:, None] == sequence[None, :]) & (within[None, :] < reach_end[:, None])
    return same_seq | from_prompt


def normalize(values):
    inverse = lax.rsqrt(jnp.mean(values * values, axis=1, keepdims=True) + EPS)
    return (values * inverse, inverse)


def norm_back(grad_scaled, scaled, inverse):
    return inverse * (grad_scaled - scaled * jnp.mean(grad_scaled * scaled, axis=1, keepdims=True))


PROMPTS = NP * PLEN


def dot_nn(left_side, right_side):
    return jnp.dot(left_side, right_side, preferred_element_type=jnp.float32)


def dot_nt(left_side, right_side):
    return lax.dot_general(
        left_side, right_side, (((1,), (1,)), ((), ())), preferred_element_type=jnp.float32
    )


def dot_tn(left_side, right_side):
    return lax.dot_general(
        left_side, right_side, (((0,), (0,)), ((), ())), preferred_element_type=jnp.float32
    )


def key_mask(facts, block, rows):
    row = lax.broadcasted_iota(jnp.int32, (PROMPTS, PROMPTS), 0)
    col = lax.broadcasted_iota(jnp.int32, (PROMPTS, PROMPTS), 1)
    parts = [(row // PLEN == col // PLEN) & (col <= row)]
    within = lax.broadcasted_iota(jnp.int32, (CLEN, PLEN + CLEN), 0)
    key = lax.broadcasted_iota(jnp.int32, (CLEN, PLEN + CLEN), 1)
    for c in range(NC):
        reach = facts[block, NC + c]
        parts.append(((key < PLEN) & (key < reach)) | ((key >= PLEN) & (key - PLEN <= within)))
    return parts


def probs_of(query, keys, decay_col, decay_row, facts, block, masks, scale):
    logits = []
    for part, mask in enumerate(masks):
        if part == 0:
            rows = slice(0, PROMPTS)
            row_decay = decay_row[:, :PROMPTS]
        else:
            start = PROMPTS + (part - 1) * CLEN
            rows = slice(start, start + CLEN)
            first = facts[block, part - 1] == 0
            prompt_decay = jnp.where(first, decay_row[:, :PLEN], decay_row[:, PLEN:PROMPTS])
            row_decay = jnp.concatenate([prompt_decay, decay_row[:, start : start + CLEN]], axis=1)
        product = dot_nt(query[rows], keys[part]) * scale
        logits.append(jnp.where(mask, product + decay_col[rows] - row_decay, NEGATIVE))
    logits = jnp.concatenate(logits, axis=0)
    shifted = jnp.exp(logits - jnp.max(logits, axis=1, keepdims=True))
    return shifted / jnp.sum(shifted, axis=1, keepdims=True)


def part_rows(part):
    if part == 0:
        return slice(0, PROMPTS)
    start = PROMPTS + (part - 1) * CLEN
    return slice(start, start + CLEN)


def part_keys(ref, lanes, facts, block):
    parts = [ref[:PROMPTS, lanes]]
    for c in range(NC):
        start = pl.multiple_of(facts[block, c] * PLEN, PLEN)
        own = part_rows(c + 1)
        parts.append(jnp.concatenate([ref[pl.ds(start, PLEN), lanes], ref[own, lanes]], axis=0))
    return parts


def attend(qkv, decay_cols, decay_rows, facts, heads, head_dim, team, rows):
    width = heads * head_dim
    scale = head_dim ** (-0.5)

    def body(facts_ref, qkv_ref, col_ref, row_ref, out_ref):
        block = pl.program_id(0)
        masks = key_mask(facts_ref, block, rows)
        for h in range(heads):
            lanes = slice(h * head_dim, (h + 1) * head_dim)
            key_lanes = slice(width + h * head_dim, width + (h + 1) * head_dim)
            value_lanes = slice(2 * width + h * head_dim, 2 * width + (h + 1) * head_dim)
            keys = part_keys(qkv_ref, key_lanes, facts_ref, block)
            values = part_keys(qkv_ref, value_lanes, facts_ref, block)
            probs = probs_of(
                qkv_ref[:, lanes], keys, col_ref[0, :, h : h + 1], row_ref[0, h : h + 1, :],
                facts_ref, block, masks, scale,
            ).astype(jnp.bfloat16)
            for part in range(NC + 1):
                at = part_rows(part)
                out_ref[at, lanes] = dot_nn(probs[at], values[part])

    return pl.pallas_call(
        body,
        grid_spec=pltpu.PrefetchScalarGridSpec(
            num_scalar_prefetch=1,
            grid=(team,),
            in_specs=[
                pl.BlockSpec((rows, qkv.shape[1]), lambda b, f: (b, 0)),
                pl.BlockSpec((1, rows, heads), lambda b, f: (b, 0, 0)),
                pl.BlockSpec((1, heads, rows), lambda b, f: (b, 0, 0)),
            ],
            out_specs=pl.BlockSpec((rows, width), lambda b, f: (b, 0)),
        ),
        out_shape=jax.ShapeDtypeStruct((team * rows, width), jnp.float32),
        cost_estimate=pl.CostEstimate(
            flops=4 * team * rows * PROMPTS * width,
            bytes_accessed=8 * team * rows * width * 2,
            transcendentals=team * rows * PROMPTS * heads,
        ),
        name="attend",
    )(facts, qkv, decay_cols, decay_rows)


def attend_back(qkv, grad_attended, decay_cols, decay_rows, facts, heads, head_dim, team, rows):
    width = heads * head_dim
    scale = head_dim ** (-0.5)

    def body(facts_ref, qkv_ref, grad_ref, col_ref, row_ref, out_ref, sum_ref, low_ref, key_acc, value_acc):
        block = pl.program_id(0)
        masks = key_mask(facts_ref, block, rows)
        for h in range(heads):
            lanes = slice(h * head_dim, (h + 1) * head_dim)
            key_lanes = slice(width + h * head_dim, width + (h + 1) * head_dim)
            value_lanes = slice(2 * width + h * head_dim, 2 * width + (h + 1) * head_dim)
            keys = part_keys(qkv_ref, key_lanes, facts_ref, block)
            values = part_keys(qkv_ref, value_lanes, facts_ref, block)
            query = qkv_ref[:, lanes]
            grad = grad_ref[:, lanes]
            probs = probs_of(
                query, keys, col_ref[0, :, h : h + 1], row_ref[0, h : h + 1, :],
                facts_ref, block, masks, scale,
            )
            grad_probs = jnp.concatenate(
                [dot_nt(grad[part_rows(p)], values[p]) for p in range(NC + 1)], axis=0
            )
            mean = jnp.sum(probs * grad_probs, axis=1, keepdims=True)
            grad_logits = probs * (grad_probs - mean)
            sum_ref[0, :, h : h + 1] = jnp.sum(grad_logits, axis=1, keepdims=True)
            probs_low = probs.astype(jnp.bfloat16)
            grad_qk = (grad_logits * scale).astype(jnp.bfloat16)
            prompt_sum = jnp.sum(grad_logits[:PROMPTS], axis=0, keepdims=True)
            for part in range(NC + 1):
                at = part_rows(part)
                out_ref[at, lanes] = dot_nn(grad_qk[at], keys[part]).astype(jnp.bfloat16)
                grad_keys = dot_tn(grad_qk[at], query[at])
                grad_values = dot_tn(probs_low[at], grad[at])
                if part == 0:
                    key_acc[...] = grad_keys
                    value_acc[...] = grad_values
                    continue
                start = pl.multiple_of(facts_ref[block, part - 1] * PLEN, PLEN)
                key_acc[pl.ds(start, PLEN), :] += grad_keys[:PLEN]
                value_acc[pl.ds(start, PLEN), :] += grad_values[:PLEN]
                out_ref[at, key_lanes] = grad_keys[PLEN:].astype(jnp.bfloat16)
                out_ref[at, value_lanes] = grad_values[PLEN:].astype(jnp.bfloat16)
                column = jnp.sum(grad_logits[at], axis=0, keepdims=True)
                first = facts_ref[block, part - 1] == 0
                nothing = jnp.zeros((1, PLEN), jnp.float32)
                prompt_sum += jnp.concatenate(
                    [
                        jnp.where(first, column[:, :PLEN], nothing),
                        jnp.where(first, nothing, column[:, :PLEN]),
                    ],
                    axis=1,
                )
                low_ref[0, h : h + 1, at] = column[:, PLEN:]
            low_ref[0, h : h + 1, :PROMPTS] = prompt_sum
            out_ref[:PROMPTS, key_lanes] = key_acc[...].astype(jnp.bfloat16)
            out_ref[:PROMPTS, value_lanes] = value_acc[...].astype(jnp.bfloat16)

    return pl.pallas_call(
        body,
        grid_spec=pltpu.PrefetchScalarGridSpec(
            num_scalar_prefetch=1,
            grid=(team,),
            in_specs=[
                pl.BlockSpec((rows, qkv.shape[1]), lambda b, f: (b, 0)),
                pl.BlockSpec((rows, width), lambda b, f: (b, 0)),
                pl.BlockSpec((1, rows, heads), lambda b, f: (b, 0, 0)),
                pl.BlockSpec((1, heads, rows), lambda b, f: (b, 0, 0)),
            ],
            out_specs=[
                pl.BlockSpec((rows, 3 * width), lambda b, f: (b, 0)),
                pl.BlockSpec((1, rows, heads), lambda b, f: (b, 0, 0)),
                pl.BlockSpec((1, heads, rows), lambda b, f: (b, 0, 0)),
            ],
            scratch_shapes=[
                pltpu.VMEM((PROMPTS, head_dim), jnp.float32),
                pltpu.VMEM((PROMPTS, head_dim), jnp.float32),
            ],
        ),
        out_shape=[
            jax.ShapeDtypeStruct((team * rows, 3 * width), jnp.bfloat16),
            jax.ShapeDtypeStruct((team, rows, heads), jnp.float32),
            jax.ShapeDtypeStruct((team, heads, rows), jnp.float32),
        ],
        cost_estimate=pl.CostEstimate(
            flops=10 * team * rows * PROMPTS * width,
            bytes_accessed=7 * team * rows * width * 2,
            transcendentals=team * rows * PROMPTS * heads,
        ),
        name="attend_back",
    )(facts, qkv, grad_attended, decay_cols, decay_rows)


def matmul(left_side, right_side):
    return jnp.dot(left_side, right_side, preferred_element_type=jnp.float32)


def matmul_tn(left_side, right_side):
    return lax.dot_general(
        left_side, right_side, (((0,), (0,)), ((), ())), preferred_element_type=jnp.float32
    )


def matmul_nt(left_side, right_side):
    return lax.dot_general(
        left_side, right_side, (((1,), (1,)), ((), ())), preferred_element_type=jnp.float32
    )


def line_groups(count):
    step = count // 4
    return [[first + step * k for k in range(4)] for first in range(step)]


def middle_strides(count):
    strides = []
    step = count // 8
    while step > 1:
        strides.append(step)
        step //= 2
    return strides


def swap_pairs(count, step):
    return [(s, s ^ step) for s in range(count)]


def both(low_first, mine, other, axis=0):
    return jnp.stack(
        [jnp.where(low_first, mine, other), jnp.where(low_first, other, mine)], axis=axis
    )


def pick(values, at, axis):
    return lax.dynamic_index_in_dim(values, at, axis, keepdims=False)


def add_low(left_side, right_side):
    return (left_side.astype(jnp.float32) + right_side.astype(jnp.float32)).astype(jnp.bfloat16)


def after(values, *others):
    return lax.optimization_barrier((values,) + others)[0]


def gather_line(block, count):
    return lax.all_gather(block, "shard", axis=0, tiled=True, axis_index_groups=line_groups(count))


def gather_rest(line, count, index):
    width = line.shape[1]
    held = line.reshape(4, -1, width)
    for step in reversed(middle_strides(count)):
        other = lax.ppermute(held, "shard", swap_pairs(count, step))
        held = both((index // step) % 2 == 0, held, other, axis=1).reshape(4, -1, width)
    return held.reshape(-1, width), other


def scatter_rest(values, count, index):
    width = values.shape[1]
    held = values.reshape(4, -1, width)
    strides = middle_strides(count)
    parts = []
    for step in strides:
        if parts:
            held = add_low(*parts)
        at = (index // step) % 2
        halves = held.reshape(4, 2, -1, width)
        other = lax.ppermute(pick(halves, 1 - at, 1), "shard", swap_pairs(count, step))
        parts = [pick(halves, at, 1), other]

    def finish(*others):
        return add_low(parts[0], after(parts[1], *others)).reshape(-1, width)

    return finish


def scatter_line(values, count):
    return lax.psum_scatter(
        values, "shard", scatter_dimension=0, tiled=True, axis_index_groups=line_groups(count)
    )


def sum_all(values, count, reps):
    total = values
    step = 1
    while step < count:
        total = total + lax.ppermute(total, "shard", swap_pairs(count, step))
        step *= 2
    step = 1
    while step < reps:
        total = total + lax.ppermute(total, "rep", [(r, r ^ step) for r in range(reps)])
        step *= 2
    return total


def local(
    tokens,
    prompt_ids,
    seq_offsets,
    attn_gain,
    w_query,
    w_key,
    w_value,
    w_outgate,
    w_forget,
    forget_bias,
    w_output,
    ffn_gain,
    w_gate,
    w_up,
    w_down,
    cotangent,
    *,
    reps,
    count,
):
    own_rows = tokens.shape[0]
    model_width = tokens.shape[1]
    head_count = w_forget.shape[1]
    head_dim = model_width // head_count
    score_scale = head_dim ** (-0.5)
    team = 4
    core = lax.axis_index("rep") % 2
    index = lax.axis_index("shard")
    side = index % 2
    rank = 2 * side + core
    quarter = model_width // team
    heads = head_count // team
    shard_rows = w_query.shape[0]
    shard_ff = w_down.shape[0]
    unit = shard_ff // 2
    quarter_ff = w_gate.shape[1] // team
    core_pairs = [(r, r ^ 1) for r in range(reps)]
    side_pairs = [(s, s ^ 1) for s in range(count)]

    def swap_core(values):
        return lax.ppermute(values, "rep", core_pairs)

    def swap_side(values):
        return lax.ppermute(values, "shard", side_pairs)

    def team_rows(values):
        pair = jnp.concatenate([values, swap_side(values)], axis=0)
        return jnp.concatenate([pair, swap_core(pair)], axis=0)

    def core_sum(partial):
        half = 2 * own_rows
        return partial[:half] + swap_core(partial[half:].astype(jnp.bfloat16)).astype(jnp.float32)

    def side_sum(pair):
        return pair[:own_rows] + swap_side(pair[own_rows:].astype(jnp.bfloat16)).astype(jnp.float32)

    def team_sum(partial):
        return side_sum(core_sum(partial))

    def cols_of(values, who):
        return lax.dynamic_slice_in_dim(values, who * quarter, quarter, axis=1)

    def units_of(values, which_side):
        cut = values.reshape(values.shape[0], count // 2, 2, 2, unit)
        return pick(pick(cut, core, 3), which_side, 2).reshape(values.shape[0], quarter_ff)

    def pair_rows(mine, sent):
        return both(side == 0, mine, swap_side(sent)).reshape(-1, mine.shape[1])

    small = jnp.concatenate(
        [
            w_forget,
            attn_gain[:, None],
            ffn_gain[:, None],
            jnp.zeros((shard_rows, 128 - head_count - 2), jnp.bfloat16),
        ],
        axis=1,
    )
    far_rank = rank ^ 2

    def columns(who, *weights):
        return [cols_of(w, who) for w in weights]

    first_block = pair_rows(
        jnp.concatenate(columns(rank, w_query, w_key, w_value) + [small], axis=1),
        jnp.concatenate(columns(far_rank, w_query, w_key, w_value) + [small], axis=1),
    )
    rest_block = pair_rows(
        jnp.concatenate(
            columns(rank, w_outgate, w_output) + [units_of(w_gate, side), units_of(w_up, side)],
            axis=1,
        ),
        after(
            jnp.concatenate(
                columns(far_rank, w_outgate, w_output)
                + [units_of(w_gate, 1 - side), units_of(w_up, 1 - side)],
                axis=1,
            ),
            first_block,
        ),
    )
    first_line = gather_line(first_block, count)
    second_line = gather_line(after(rest_block[:, : 2 * quarter], first_line), count)
    gate_line = gather_line(
        after(rest_block[:, 2 * quarter : 2 * quarter + quarter_ff], second_line), count
    )
    up_line = gather_line(after(rest_block[:, 2 * quarter + quarter_ff :], gate_line), count)
    down_line = gather_line(
        after(lax.dynamic_slice_in_dim(w_down, core * unit, unit, axis=0), up_line), count
    )
    first, first_last = gather_rest(first_line, count, index)
    second, second_last = gather_rest(second_line, count, index)
    gate_w, gate_last = gather_rest(gate_line, count, index)
    up_w, up_last = gather_rest(up_line, count, index)
    down_w, down_last = gather_rest(down_line, count, index)

    forget_w = lax.dynamic_slice_in_dim(
        first[:, 3 * quarter : 3 * quarter + head_count], rank * heads, heads, axis=1
    )
    gain_one = first[:, 3 * quarter + head_count].astype(jnp.float32)
    gain_two = first[:, 3 * quarter + head_count + 1].astype(jnp.float32)
    outgate_w = second[:, :quarter]
    output_cols = second[:, quarter:]

    def turn_rows(values):
        cut = values.reshape(2, 2, quarter, quarter)
        mine = pick(cut, side, 0)
        pair = both(side == 0, mine, swap_side(pick(cut, 1 - side, 0)))
        kept = pick(pair, core, 1)
        quad = both(core == 0, kept, swap_core(pick(pair, 1 - core, 1)))
        return jnp.transpose(quad, (2, 1, 0, 3)).reshape(quarter, model_width)

    def turn_cols(values):
        cut = values.reshape(quarter, 2, 2, quarter)
        mine = pick(cut, core, 2)
        pair = both(core == 0, mine, swap_core(pick(cut, 1 - core, 2)))
        kept = pick(pair, side, 2)
        quad = both(side == 0, kept, swap_side(pick(pair, 1 - side, 2)))
        return quad.reshape(model_width, quarter)

    output_w = turn_rows(output_cols)

    tokens_all = team_rows(after(tokens, rest_block))
    cotangent_all = team_rows(after(cotangent, tokens_all))
    facts_all = team_rows(jnp.concatenate([prompt_ids[0], seq_offsets[0]])[None, :])
    chain_ok = jnp.stack([chain_mask(facts_all[b, :NC], facts_all[b, NC:]) for b in range(team)])
    chain_float = chain_ok.astype(jnp.float32)

    inputs_all = tokens_all.astype(jnp.float32)
    scaled_all, inverse_all = normalize(inputs_all)
    scaled1 = scaled_all[:own_rows]
    inverse1 = inverse_all[:own_rows]
    inputs = inputs_all[:own_rows]
    normed1 = after(
        (scaled_all * gain_one).astype(jnp.bfloat16), gate_line, cotangent_all
    )
    row_count = normed1.shape[0]

    qkv_low = matmul(normed1, first[:, : 3 * quarter]).astype(jnp.bfloat16)
    outgate_pre = matmul(normed1, outgate_w)
    bias_mine = lax.dynamic_slice_in_dim(
        forget_bias.astype(jnp.float32), rank * heads, heads, axis=0
    )
    forget_in = matmul(normed1, forget_w) + bias_mine[None, :]
    log_forget = jax.nn.log_sigmoid(forget_in).reshape(team, own_rows, heads)
    decay_sum = jnp.einsum(
        "bij,bjh->bhi", chain_float, log_forget, precision=lax.Precision.HIGHEST
    )

    decay_cols = jnp.transpose(decay_sum, (0, 2, 1))
    attended = attend(
        after(qkv_low, gate_last),
        decay_cols,
        decay_sum,
        facts_all,
        heads,
        head_dim,
        team,
        own_rows,
    )
    gate_open = jax.nn.sigmoid(outgate_pre)
    gated_low = after((attended * gate_open).astype(jnp.bfloat16), up_line)

    residual = inputs + after(team_sum(matmul(gated_low, output_w)), up_last)
    scaled2, inverse2 = normalize(residual)
    normed2 = after(team_rows((scaled2 * gain_two).astype(jnp.bfloat16)), down_line)
    gate_pre = matmul(normed2, gate_w)
    up_pre = matmul(normed2, up_w)
    sig_gate = jax.nn.sigmoid(gate_pre)
    silu_gate = gate_pre * sig_gate
    act_low = (silu_gate * up_pre).astype(jnp.bfloat16)
    grad_act = matmul_nt(cotangent_all, down_w)
    grad_gate = (grad_act * up_pre * sig_gate * (1.0 + gate_pre * (1.0 - sig_gate))).astype(
        jnp.bfloat16
    )
    grad_up = (grad_act * silu_gate).astype(jnp.bfloat16)
    down_sum = scatter_rest(matmul_tn(act_low, cotangent_all).astype(jnp.bfloat16), count, index)
    pair_normed2 = core_sum(matmul_nt(grad_gate, gate_w) + matmul_nt(grad_up, up_w))
    normed2_gate = after(normed2, pair_normed2)
    part_gate_w = matmul_tn(normed2_gate, grad_gate).astype(jnp.bfloat16)
    gate_sum = scatter_rest(part_gate_w, count, index)
    down_held = down_sum(pair_normed2)
    grad_down = scatter_line(down_held, count)
    normed2_up = after(normed2_gate, down_held)
    part_up_w = matmul_tn(normed2_up, grad_up).astype(jnp.bfloat16)
    up_sum = scatter_rest(part_up_w, count, index)
    grad_normed2 = after(side_sum(pair_normed2), down_held, part_gate_w, part_up_w)
    grad_gain2 = jnp.sum(grad_normed2 * scaled2, axis=0)
    grad_resid = cotangent.astype(jnp.float32) + norm_back(
        grad_normed2 * gain_two, scaled2, inverse2
    )
    grad_attn_own = grad_resid.astype(jnp.bfloat16)
    pair_out = core_sum(matmul(after(act_low, grad_attn_own), down_w))
    gate_held = gate_sum(pair_out)
    grad_gate_w = scatter_line(gate_held, count)
    grad_attn = after(team_rows(grad_attn_own), gate_held)
    layer_out = (residual + side_sum(after(pair_out, grad_attn))).astype(jnp.bfloat16)
    grad_gated = matmul_nt(grad_attn, output_w)
    grad_output_cols = turn_cols(matmul_tn(gated_low, grad_attn).astype(jnp.bfloat16))
    grad_attended = (grad_gated * gate_open).astype(jnp.bfloat16)
    grad_outgate = (grad_gated * attended * gate_open * (1.0 - gate_open)).astype(jnp.bfloat16)
    grad_outgate_w = matmul_tn(normed1, grad_outgate).astype(jnp.bfloat16)
    second_sum = scatter_rest(
        jnp.concatenate([grad_outgate_w, grad_output_cols], axis=1), count, index
    )
    grad_qkv, grad_logit_rows, grad_logit_cols = attend_back(
        qkv_low, grad_attended, decay_cols, decay_sum, facts_all, heads, head_dim, team, own_rows
    )
    up_held = up_sum(grad_qkv)
    grad_up_w = scatter_line(up_held, count)
    grad_decay = jnp.transpose(grad_logit_rows, (0, 2, 1)) - grad_logit_cols
    grad_log_forget = jnp.einsum(
        "bij,bhi->bjh", chain_float, grad_decay, precision=lax.Precision.HIGHEST
    ).reshape(row_count, heads)
    grad_forget_in = grad_log_forget * jax.nn.sigmoid(-forget_in)
    bias_sum = lax.dynamic_update_slice_in_dim(
        jnp.zeros((head_count,), jnp.float32),
        jnp.sum(grad_forget_in, axis=0),
        rank * heads,
        axis=0,
    )
    grad_bias = sum_all(bias_sum[None, :], count, reps)[0]
    grad_forget_low = lax.dynamic_update_slice_in_dim(
        jnp.zeros((row_count, small.shape[1]), jnp.bfloat16),
        grad_forget_in.astype(jnp.bfloat16),
        rank * heads,
        axis=1,
    )
    grad_first = jnp.concatenate([grad_qkv, grad_forget_low], axis=1)
    part_normed1 = matmul_nt(grad_first, first) + matmul_nt(grad_outgate, outgate_w)
    grad_gain1 = jnp.sum(part_normed1 * scaled_all, axis=0)
    grad_normed1 = team_sum(part_normed1)
    tokens_grad = grad_resid + norm_back(grad_normed1 * gain_one, scaled1, inverse1)
    column = jnp.arange(first.shape[1], dtype=jnp.int32)[None, :] - 3 * quarter - head_count
    grad_first_w = (
        matmul_tn(normed1, grad_first)
        + jnp.where(column == 0, grad_gain1[:, None], 0.0)
        + jnp.where(column == 1, grad_gain2[:, None], 0.0)
    )
    first_sum = scatter_rest(after(grad_first_w.astype(jnp.bfloat16), up_held), count, index)
    second_held = second_sum(grad_first_w)
    sum_second = scatter_line(second_held, count)
    first_held = first_sum(second_held)
    sum_first = scatter_line(first_held, count)
    grad_down = after(grad_down, grad_first_w)
    grad_gate_w = after(grad_gate_w, grad_first_w)
    grad_up_w = after(grad_up_w, second_held)
    sum_second = after(sum_second, first_held)
    sum_small = sum_first[:, 3 * quarter :]
    sum_first = sum_first[:, : 3 * quarter]

    def replicas(values):
        total = values
        step = 2
        while step < reps:
            other = lax.ppermute(total, "rep", [(r, r ^ step) for r in range(reps)])
            total = add_low(total, other)
            step *= 2
        return total

    def own_of(values):
        pair = replicas(values).reshape(2, shard_rows, values.shape[1])
        sides = both(side == 0, pick(pair, side, 0), swap_side(pick(pair, 1 - side, 0)))
        cores = both(core == 0, sides, swap_core(sides))
        return jnp.transpose(cores.astype(jnp.float32), (1, 0, 2, 3))

    def whole_cols(values):
        parts = values.shape[1] // quarter
        quad = own_of(values).reshape(2, 2, shard_rows, parts, quarter)
        quad = jnp.transpose(quad, (3, 2, 0, 1, 4)).reshape(parts, shard_rows, model_width)
        return [quad[p] for p in range(parts)]

    def whole_units(values):
        quad = own_of(values).reshape(2, 2, shard_rows, count // 2, unit)
        return jnp.transpose(quad, (2, 3, 0, 1, 4)).reshape(shard_rows, team * quarter_ff)

    small_pair = replicas(sum_small).reshape(2, shard_rows, sum_small.shape[1])
    small_own = add_low(pick(small_pair, side, 0), swap_side(pick(small_pair, 1 - side, 0)))
    small_own = small_own.astype(jnp.float32) + swap_core(small_own).astype(jnp.float32)
    down_mine = replicas(grad_down)
    down_own = both(core == 0, down_mine, swap_core(down_mine)).astype(jnp.float32)
    query_g, key_g, value_g = whole_cols(sum_first)
    outgate_g, output_g = whole_cols(sum_second)
    return (
        layer_out,
        tokens_grad,
        small_own[:, head_count],
        query_g,
        key_g,
        value_g,
        outgate_g,
        small_own[:, :head_count],
        grad_bias,
        output_g,
        small_own[:, head_count + 1],
        whole_units(grad_gate_w),
        whole_units(grad_up_w),
        down_own.reshape(shard_ff, model_width),
    )


def solution(mesh):
    in_specs = (
        P(("rep", "shard"), None),
        P(("rep", "shard"), None),
        P(("rep", "shard"), None),
        P("shard"),
        P("shard", None),
        P("shard", None),
        P("shard", None),
        P("shard", None),
        P("shard", None),
        P(),
        P("shard", None),
        P("shard"),
        P("shard", None),
        P("shard", None),
        P("shard", None),
        P(("rep", "shard"), None),
    )
    out_specs = (
        P(("rep", "shard"), None),
        P(("rep", "shard"), None),
        P("shard"),
        P("shard", None),
        P("shard", None),
        P("shard", None),
        P("shard", None),
        P("shard", None),
        P(),
        P("shard", None),
        P("shard"),
        P("shard", None),
        P("shard", None),
        P("shard", None),
    )

    def program(*arrays):
        return local(*arrays, reps=mesh.shape["rep"], count=mesh.shape["shard"])

    return jax.shard_map(program, mesh=mesh, in_specs=in_specs, out_specs=out_specs, check_vma=False)
```

time: 956 us -> 863 us (0.903)
  starting transfers between devices: 226 us -> 43.6 us
  waiting for transfers between devices: 279 us -> 384 us
  matrix products: 197 us -> 149 us
  Pallas kernels: 0 us -> 42.9 us
  local copies, waits for them, and re-layouts: 127 us -> 107 us
  between operations: 3.57 us -> 16.4 us
    ppermute x48 -> x14, starting transfers between devices: 204 us -> 19.8 us  [the longest x5 7.57 us: gather_rest(): other = lax.ppermute(held, 'shard', swap_pairs(count, step))]
    ppermute x20 -> x18, waiting for transfers between devices: 74.7 us -> 169 us  [swap_side(): return lax.ppermute(values, 'shard', side_pairs)]
    pallas_call x0 -> x2, Pallas kernels: none -> 42.9 us  [the longest x1 24 us: attend_back(): pl.pallas_call(body, grid_spec=pltpu.PrefetchScalarGridSpec(num_scalar_pr...]
    dot_general x5 -> x0, matrix products: 28.5 us -> none  [the longest x1 8.83 us: local(): jnp.einsum('bhqk,bqhd->bkhd', prob_again, grad_attended, preferred_elemen...]
    all_gather x0 -> x5, waiting for transfers between devices: none -> 25.5 us  [gather_line(): lax.all_gather(block, 'shard', axis=0, tiled=True, axis_index_groups=line...]
    ppermute x48 -> x14, waiting for transfers between devices: 204 us -> 181 us  [the longest x5 67.6 us: gather_rest(): other = lax.ppermute(held, 'shard', swap_pairs(count, step))]
    sub x1 -> x0, matrix products: 20.8 us -> none  [local(): grad_probs - jnp.sum(prob_full * grad_probs, axis=3, keepdims=True)]
    reshape x5 -> x0, local copies, waits for them, and re-layouts: 13.1 us -> none  [the longest x4 10.1 us: split_heads(): return values.reshape(team, own_rows, heads, head_dim)]
  transfers between devices with their start and end apart: 86 -> 60, of which waited for: 30 -> 27; matrix products, arithmetic and copies ran while one was open for 33% -> 30% of each run, Pallas kernels for 0% -> 5%
where the time goes in v2:
time: 863 us; the launch traced here: 854 us
  waiting for transfers between devices  384 us (44%)
  matrix products  149 us (17%)
  other arithmetic  111 us (13%)
  local copies, waits for them, and re-layouts  107 us (12%)
  starting transfers between devices  43.6 us (5%)
  Pallas kernels  42.9 us (5%)
  between operations  16.4 us (2%)
    ppermute x18, waiting for transfers between devices, swap_side(): return lax.ppermute(values, 'shard', side_pairs)  169 us
    ppermute x5, waiting for transfers between devices, gather_rest(): other = lax.ppermute(held, 'shard', swap_pairs(count, step))  67.6 us
    ppermute x4, waiting for transfers between devices, sum_all(): total = total + lax.ppermute(total, 'shard', swap_pairs(count, step))  56.8 us
    dot_general x6, matrix products, matmul_nt(): lax.dot_general(left_side, right_side, (((1,), (1,)), ((), ())), preferre...  56.6 us
    ppermute x5, waiting for transfers between devices, scatter_rest(): lax.ppermute(pick(halves, 1 - at, 1), 'shard', swap_pairs(count, step))  56.5 us
    dot_general x6, matrix products, matmul_tn(): lax.dot_general(left_side, right_side, (((0,), (0,)), ((), ())), preferre...  45.8 us
    dot_general x7, matrix products, matmul(): return jnp.dot(left_side, right_side, preferred_element_type=jnp.float32)  44.1 us
    unnamed x203, local copies, waits for them, and re-layouts  29.3 us
  transfers between devices with their start and end apart: 60, of which 27 were waited for; matrix products, arithmetic and copies ran while one was open for 30% of the time, Pallas kernels for 5%

profile of v2, /device:TPU:0, one launch (start us, length us, event | category | flops | bytes accessed | tf_op | source)
XLA Modules:
  0.0 853.9 jit_solution(9267317109742596608)
XLA Ops:
  25.7 12.4 %collective-permute-done.1 = bf16[96,2816]{1,0:T(8,128)(2,1)} collective-permute-done((bf16[96,2816]{1,0:T(8,128)(2,1)S(1)}, bf16[96,2816]{1,0:T(8,128)(2,1)}, u32[]{:S(2)}, u32[]{:S(2)}) %collective-permute-start.1) | collective-permute-done | bytes 540704 | tf_op jit(solution)/shard_map/ppermute | solution.py:390
  42.6 24.4 %collective-permute-done.2 = bf16[384,1536]{1,0:T(8,128)(2,1)S(1)} collective-permute-done((bf16[384,1536]{1,0:T(8,128)(2,1)S(1)}, bf16[384,1536]{1,0:T(8,128)(2,1)S(1)}, u32[]{:S(2)}, u32[]{:S(2)}) %collective-permute-start.2) | collective-permute-done | bytes 1179680 | tf_op jit(solution)/shard_map/ppermute | solution.py:390
  87.0 19.7 %all-gather.8.cloned.1.call-done = bf16[768,768]{1,0:T(8,128)(2,1)} async-done(((bf16[192,768]{1,0:T(8,128)(2,1)}), bf16[768,768]{1,0:T(8,128)(2,1)}) %all-gather.8.cloned.1.call-update) | async-done | bytes 1179664 | tf_op jit(solution)/shard_map/all_gather | solution.py:296
  109.5 14.4 %collective-permute-done.6 = bf16[4,192,1280]{2,1,0:T(8,128)(2,1)} collective-permute-done((bf16[4,192,1280]{2,1,0:T(8,128)(2,1)}, bf16[4,192,1280]{2,1,0:T(8,128)(2,1)}, u32[]{:S(2)}, u32[]{:S(2)}) %collective-permute-start.6) | collective-permute-done | bytes 1966112 | tf_op jit(solution)/shard_map/ppermute | solution.py:303
  126.3 22.0 %collective-permute-done.10 = bf16[4,192,768]{2,1,0:T(8,128)(2,1)} collective-permute-done((bf16[4,192,768]{2,1,0:T(8,128)(2,1)}, bf16[4,192,768]{2,1,0:T(8,128)(2,1)}, u32[]{:S(2)}, u32[]{:S(2)}) %collective-permute-start.10) | collective-permute-done | bytes 1179680 | tf_op jit(solution)/shard_map/ppermute | solution.py:303
  155.1 11.2 %collective-permute-done.11 = bf16[2,384,384]{2,1,0:T(8,128)(2,1)S(1)} collective-permute-done((bf16[2,384,384]{2,1,0:T(8,128)(2,1)S(1)}, bf16[2,384,384]{2,1,0:T(8,128)(2,1)S(1)}, u32[]{:S(2)}, u32[]{:S(2)}) %collective-permute-start.11) | collective-permute-done | bytes 589856 | tf_op jit(solution)/shard_map/ppermute | solution.py:390
  189.7 10.6 %convolution_convert_fusion.qkv_ref = bf16[1536,1152]{1,0:T(8,128)(2,1)} fusion(bf16[1536,1536]{1,0:T(8,128)(2,1)} %multiply_convert_fusion, bf16[1536,1280]{1,0:T(8,128)(2,1)} %bitcast.362), kind=kOutput, calls=%fused_computation.7 | convolution fusion | flops 5437587456 | bytes 11796480 | tf_op jit(solution)/shard_map/dot_general | solution.py:244
  200.3 15.3 %collective-permute-done.9 = bf16[4,192,1024]{2,1,0:T(8,128)(2,1)S(1)} collective-permute-done((bf16[4,192,1024]{2,1,0:T(8,128)(2,1)}, bf16[4,192,1024]{2,1,0:T(8,128)(2,1)S(1)}, u32[]{:S(2)}, u32[]{:S(2)}) %collective-permute-start.9) | collective-permute-done | bytes 1572896 | tf_op jit(solution)/shard_map/ppermute | solution.py:303
  216.8 18.8 %attend.1 = f32[1536,384]{1,0:T(8,128)} custom-call(s32[4,8]{1,0:T(4,128)} %pad_add_fusion.1.facts_ref, bf16[1536,1152]{1,0:T(8,128)(2,1)} %convolution_convert_fusion.qkv_ref, f32[4,384,6]{2,1,0:T(8,128)} %bitcast.358, f32[4,6,384]{2,1,0:T(8,128)} %copy-done.46), custom_call_target="tpu_custom_call" | custom-call | flops 301989888 | bytes 9437184 | tf_op jit(solution)/shard_map/attend/pallas_call | solution.py:129
  235.7 7.7 multiply_convert_fusion.7
  259.1 7.4 convert_element_type.209
  266.5 17.2 %collective-permute-done.14 = bf16[384,1536]{1,0:T(8,128)(2,1)} collective-permute-done((bf16[384,1536]{1,0:T(8,128)(2,1)S(1)}, bf16[384,1536]{1,0:T(8,128)(2,1)}, u32[]{:S(2)}, u32[]{:S(2)}) %collective-permute-start.14) | collective-permute-done | bytes 1179680 | tf_op jit(solution)/shard_map/ppermute | solution.py:390
  304.8 19.7 %collective-permute-done.16 = bf16[384,1536]{1,0:T(8,128)(2,1)} collective-permute-done((bf16[384,1536]{1,0:T(8,128)(2,1)}, bf16[384,1536]{1,0:T(8,128)(2,1)}, u32[]{:S(2)}, u32[]{:S(2)}) %collective-permute-start.16) | collective-permute-done | bytes 1179680 | tf_op jit(solution)/shard_map/ppermute | solution.py:390
  330.2 8.5 %collective-permute-done.18 = bf16[4,128,1536]{2,1,0:T(8,128)(2,1)S(1)} collective-permute-done((bf16[4,128,1536]{2,1,0:T(8,128)(2,1)}, bf16[4,128,1536]{2,1,0:T(8,128)(2,1)S(1)}, u32[]{:S(2)}, u32[]{:S(2)}) %collective-permute-start.18) | collective-permute-done | bytes 1572896 | tf_op jit(solution)/shard_map/ppermute | solution.py:303
  356.1 12.8 %multiply_convert_fusion.1 = (bf16[1536,1024]{1,0:T(8,128)(2,1)}, bf16[1536,1024]{1,0:T(8,128)(2,1)}, bf16[1536,1024]{1,0:T(8,128)(2,1)}) fusion(f32[1536,1024]{1,0:T(8,128)} %fusion.76, f32[1536,1024]{1,0:T(8,128)} %fusion.77, bf16[1536,1536]{1,0:T(8,128)(2,1)S(1)} %bitcast.424, bf16[1024,1536]{1,0:T(8,128)(2,1)S(1)} %bitcast.387), kind=kOutput, calls=%fused_computation.8 | convolution fusion | flops 4855431168 | bytes 29884416 | tf_op jit(solution)/shard_map/dot_general | solution.py:254
  368.9 9.6 %fusion.78 = f32[1536,1536]{1,0:T(8,128)} fusion(bf16[1536,1024]{1,0:T(8,128)(2,1)} %get-tuple-element.153, bf16[1536,1024]{1,0:T(8,128)(2,1)S(1)} %bitcast.392), kind=kOutput, calls=%fused_computation.302 | convolution fusion | flops 4831838208 | bytes 15728640 | tf_op jit(solution)/shard_map/dot_general | solution.py:254
  378.5 7.9 convolution_add_fusion.2
  391.8 8.3 convolution_convert_fusion.3
  409.7 30.4 %collective-permute-done.21 = bf16[4,128,1536]{2,1,0:T(8,128)(2,1)} collective-permute-done((bf16[4,128,1536]{2,1,0:T(8,128)(2,1)}, bf16[4,128,1536]{2,1,0:T(8,128)(2,1)}, u32[]{:S(2)}, u32[]{:S(2)}) %collective-permute-start.21) | collective-permute-done | bytes 1572896 | tf_op jit(solution)/shard_map/ppermute | solution.py:318
  440.1 8.9 %convolution_convert_fusion.2 = bf16[1536,1024]{1,0:T(8,128)(2,1)} fusion(bf16[1536,1536]{1,0:T(8,128)(2,1)} %copy-done.20, bf16[1536,1024]{1,0:T(8,128)(2,1)S(1)} %copy-done.88), kind=kOutput, calls=%fused_computation.29 | convolution fusion | flops 4833411072 | bytes 11010048 | tf_op jit(solution)/shard_map/dot_general | solution.py:248
  453.4 9.7 %convolution_convert_fusion.1 = bf16[1536,1024]{1,0:T(8,128)(2,1)} fusion(bf16[1536,1536]{1,0:T(8,128)(2,1)} %copy-done.20, bf16[1536,1024]{1,0:T(8,128)(2,1)} %get-tuple-element.152), kind=kOutput, calls=%fused_computation.28 | convolution fusion | flops 4833411072 | bytes 11010048 | tf_op jit(solution)/shard_map/dot_general | solution.py:248
  463.1 13.7 %collective-permute-done.20 = bf16[384,1536]{1,0:T(8,128)(2,1)} collective-permute-done((bf16[384,1536]{1,0:T(8,128)(2,1)}, bf16[384,1536]{1,0:T(8,128)(2,1)}, u32[]{:S(2)}, u32[]{:S(2)}) %collective-permute-start.20) | collective-permute-done | bytes 1179680 | tf_op jit(solution)/shard_map/ppermute | solution.py:390
  494.4 14.7 %collective-permute-done.23 = bf16[384,1536]{1,0:T(8,128)(2,1)S(1)} collective-permute-done((bf16[384,1536]{1,0:T(8,128)(2,1)}, bf16[384,1536]{1,0:T(8,128)(2,1)S(1)}, u32[]{:S(2)}, u32[]{:S(2)}) %collective-permute-start.23) | collective-permute-done | bytes 1179680 | tf_op jit(solution)/shard_map/ppermute | solution.py:390
  524.7 26.0 %collective-permute-done.25 = bf16[4,192,1024]{2,1,0:T(8,128)(2,1)} collective-permute-done((bf16[4,192,1024]{2,1,0:T(8,128)(2,1)}, bf16[4,192,1024]{2,1,0:T(8,128)(2,1)}, u32[]{:S(2)}, u32[]{:S(2)}) %collective-permute-start.25) | collective-permute-done | bytes 1572896 | tf_op jit(solution)/shard_map/ppermute | solution.py:318
  561.7 24.0 %attend_back.1 = (bf16[1536,1152]{1,0:T(8,128)(2,1)}, f32[4,384,6]{2,1,0:T(8,128)}, f32[4,6,384]{2,1,0:T(8,128)}) custom-call(s32[4,8]{1,0:T(4,128)} %pad_add_fusion.1.facts_ref, bf16[1536,1152]{1,0:T(8,128)(2,1)} %convolution_convert_fusion.qkv_ref, bf16[1536,384]{1,0:T(8,128)(2,1)} %get-tuple-element.158.grad_ref, f32[4,384,6]{2,1,0:T(8,128)} %bitcast.359, ...), custom_call_target="tpu_custom_call" | custom-call | flops 754974720 | bytes 8257536 | tf_op jit(solution)/shard_map/attend_back/pallas_call | solution.py:208
  599.0 11.6 %fusion.10 = f32[1536,1536]{1,0:T(8,128)} fusion(bf16[1536,1280]{1,0:T(8,128)(2,1)} %bitcast.363, bf16[1536,128]{1,0:T(8,128)(2,1)S(1)} %dynamic_update_slice.9, bf16[1536,1152]{1,0:T(8,128)(2,1)} %get-tuple-element.65), kind=kOutput, calls=%fused_computation.51 | convolution fusion | flops 6047662080 | bytes 17301504 | tf_op jit(solution)/shard_map/dot_general | solution.py:254
  610.6 10.8 %multiply_reduce_fusion = (f32[1536]{0:T(1024)S(1)}, f32[1536,1536]{1,0:T(8,128)}, f32[1536,1536]{1,0:T(8,128)S(1)}) fusion(f32[1536]{0:T(1024)S(1)} %copy-done.71, bf16[1536,1536]{1,0:T(8,128)(2,1)S(1)} %bitcast.350, f32[1536,1536]{1,0:T(8,128)} %fusion.10, bf16[1536,384]{1,0:T(8,128)(2,1)} %get-tuple-element.157, bf16[1536,768]{1,0:T(8,128)(2,1)} %bitcast.354), kind=kOutput, calls=%fused_computation.1 | convolution fusion | flops 1823734272 | bytes 35401728 | tf_op jit(solution)/shard_map/dot_general | solution.py:254
  644.1 9.3 %fusion = bf16[1536,1280]{1,0:T(8,128)(2,1)S(1)} fusion(bf16[1536,1536]{1,0:T(8,128)(2,1)} %multiply_convert_fusion, f32[1536]{0:T(1024)S(1)} %get-tuple-element.132, f32[1536]{0:T(1024)S(1)} %get-tuple-element.155, pred[1280]{0:T(1024)(128)(4,1)S(1)} %copy-done.78, pred[1280]{0:T(1024)(128)(4,1)S(1)} %copy-done.79, ...), kind=kOutput, calls=%fused_computation.5 | convolution fusion | flops 6057492480 | bytes 12597760 | tf_op jit(solution)/shard_map/dot_general | solution.py:248
  662.7 50.4 %collective-permute-done.41 = f32[1,24]{1,0:T(1,128)S(1)} collective-permute-done((f32[1,24]{1,0:T(1,128)S(1)}, f32[1,24]{1,0:T(1,128)S(1)}, u32[]{:S(2)}, u32[]{:S(2)}) %collective-permute-start.41) | collective-permute-done | bytes 128 | tf_op jit(solution)/shard_map/ppermute | solution.py:337
  730.4 26.4 %collective-permute-done.45 = bf16[96,1024]{1,0:T(8,128)(2,1)S(1)} collective-permute-done((bf16[96,1024]{1,0:T(8,128)(2,1)S(1)}, bf16[96,1024]{1,0:T(8,128)(2,1)S(1)}, u32[]{:S(2)}, u32[]{:S(2)}) %collective-permute-start.45) | collective-permute-done | bytes 196640 | tf_op jit(solution)/shard_map/ppermute | solution.py:390
  775.7 20.2 %collective-permute-done.47 = bf16[96,1024]{1,0:T(8,128)(2,1)} collective-permute-done((bf16[96,1024]{1,0:T(8,128)(2,1)}, bf16[96,1024]{1,0:T(8,128)(2,1)}, u32[]{:S(2)}, u32[]{:S(2)}) %collective-permute-start.47) | collective-permute-done | bytes 196640 | tf_op jit(solution)/shard_map/ppermute | solution.py:390
  803.7 7.5 multiply_add_fusion
  (494 shorter events, 325.7 us)
Async XLA Ops:
  7.2 68.7 %all-gather.6.cloned.1.call-start = ((), (), s32[]{:S(2)}) async-start(), calls=%async_computation.5 | async-start | bytes 2457600 | tf_op jit(solution)/shard_map/all_gather | solution.py:296
  25.6 81.1 %all-gather.8.cloned.1.call-start = ((), (), s32[]{:S(2)}) async-start(), calls=%async_computation.6 | async-start | bytes 1474560 | tf_op jit(solution)/shard_map/all_gather | solution.py:296
  41.2 27.5 %collective-permute-start.4 = (s32[1,8]{1,0:T(1,128)S(1)}, s32[1,8]{1,0:T(1,128)S(1)}, u32[]{:S(2)}, u32[]{:S(2)}) collective-permute-start(s32[1,8]{1,0:T(1,128)S(1)} %add_bitcast_fusion), channel_id=1, source_target_pairs={{0,1},{1,0},{2,3},{3,2},{4,5},{5,4},{6,7},{7,6},{8,9},{9,8},{10,11... | collective-permute-start | bytes 104 | tf_op jit(solution)/shard_map/ppermute | solution.py:390
  76.0 102.5 %all-gather.10.cloned.1.call-start = ((), (), s32[]{:S(2)}) async-start(), calls=%async_computation.7 | async-start | bytes 1966080 | tf_op jit(solution)/shard_map/all_gather | solution.py:296
  77.9 46.0 %collective-permute-start.6 = (bf16[4,192,1280]{2,1,0:T(8,128)(2,1)}, bf16[4,192,1280]{2,1,0:T(8,128)(2,1)}, u32[]{:S(2)}, u32[]{:S(2)}) collective-permute-start(bf16[4,192,1280]{2,1,0:T(8,128)(2,1)} %bitcast.398), channel_id=1, source_target_pairs={{0,2},{1,3},{2,0},{3,1},{4,6},{5,7},{6,4},{7,5},{8,10},{9,11},{10,... | collective-permute-start | bytes 5898248 | tf_op jit(solution)/shard_map/ppermute | solution.py:303
  83.7 69.3 %collective-permute-start.7 = (bf16[384,1536]{1,0:T(8,128)(2,1)S(1)}, bf16[384,1536]{1,0:T(8,128)(2,1)S(1)}, u32[]{:S(2)}, u32[]{:S(2)}) collective-permute-start(bf16[384,1536]{1,0:T(8,128)(2,1)S(1)} %copy-done.8), channel_id=1, source_target_pairs={{0,1},{1,0},{2,3},{3,2},{4,5},{5,4},{6,7},{7,6},{8,9},{9,8},{10,11... | collective-permute-start | bytes 3538952 | tf_op jit(solution)/shard_map/ppermute | solution.py:390
  106.7 41.7 %collective-permute-start.10 = (bf16[4,192,768]{2,1,0:T(8,128)(2,1)}, bf16[4,192,768]{2,1,0:T(8,128)(2,1)}, u32[]{:S(2)}, u32[]{:S(2)}) collective-permute-start(bf16[4,192,768]{2,1,0:T(8,128)(2,1)} %bitcast.408), channel_id=1, source_target_pairs={{0,2},{1,3},{2,0},{3,1},{4,6},{5,7},{6,4},{7,5},{8,10},{9,11},{10,... | collective-permute-start | bytes 3538952 | tf_op jit(solution)/shard_map/ppermute | solution.py:303
  109.3 134.1 %all-gather.12.cloned.1.call-start = ((), (), s32[]{:S(2)}) async-start(), calls=%async_computation.8 | async-start | bytes 1966080 | tf_op jit(solution)/shard_map/all_gather | solution.py:296
  155.1 27.5 %collective-permute-start.8 = (bf16[768,1536]{1,0:T(8,128)(2,1)}, bf16[768,1536]{1,0:T(8,128)(2,1)}, u32[]{:S(2)}, u32[]{:S(2)}) collective-permute-start(bf16[768,1536]{1,0:T(8,128)(2,1)} %pad_maximum_fusion.10), channel_id=1, source_target_pairs={{0,16},{16,0},{1,17},{17,1},{2,18},{18,2},{3,19},{19,3},{4,20},{20... | collective-permute-start | bytes 7077896 | tf_op jit(solution)/shard_map/ppermute | solution.py:387
  178.5 124.8 %all-gather.14.cloned.1.call-start = ((), (), s32[]{:S(2)}) async-start(), calls=%async_computation.9 | async-start | bytes 1966080 | tf_op jit(solution)/shard_map/all_gather | solution.py:296
  178.6 37.1 %collective-permute-start.9 = (bf16[4,192,1024]{2,1,0:T(8,128)(2,1)}, bf16[4,192,1024]{2,1,0:T(8,128)(2,1)S(1)}, u32[]{:S(2)}, u32[]{:S(2)}) collective-permute-start(bf16[4,192,1024]{2,1,0:T(8,128)(2,1)} %bitcast.402), channel_id=1, source_target_pairs={{0,2},{1,3},{2,0},{3,1},{4,6},{5,7},{6,4},{7,5},{8,10},{9,11},{10,... | collective-permute-start | bytes 4718600 | tf_op jit(solution)/shard_map/ppermute | solution.py:303
  255.5 28.2 %collective-permute-start.14 = (bf16[384,1536]{1,0:T(8,128)(2,1)S(1)}, bf16[384,1536]{1,0:T(8,128)(2,1)}, u32[]{:S(2)}, u32[]{:S(2)}) collective-permute-start(bf16[384,1536]{1,0:T(8,128)(2,1)S(1)} %slice.285), channel_id=1, source_target_pairs={{0,1},{1,0},{2,3},{3,2},{4,5},{5,4},{6,7},{7,6},{8,9},{9,8},{10,11... | collective-permute-start | bytes 3538952 | tf_op jit(solution)/shard_map/ppermute | solution.py:390
  256.8 36.5 %collective-permute-start.15 = (bf16[4,192,1024]{2,1,0:T(8,128)(2,1)S(1)}, bf16[4,192,1024]{2,1,0:T(8,128)(2,1)}, u32[]{:S(2)}, u32[]{:S(2)}) collective-permute-start(bf16[4,192,1024]{2,1,0:T(8,128)(2,1)S(1)} %bitcast.404), channel_id=1, source_target_pairs={{0,2},{1,3},{2,0},{3,1},{4,6},{5,7},{6,4},{7,5},{8,10},{9,11},{10,... | collective-permute-start | bytes 4718600 | tf_op jit(solution)/shard_map/ppermute | solution.py:303
  266.5 393.4 %reduce-scatter.14.cloned.1.call-start = ((), (), s32[]{:S(2)}) async-start(), calls=%async_computation.14 | async-start | bytes 1966080 | tf_op jit(solution)/shard_map/reduce_scatter | solution.py:328
  297.0 27.4 %collective-permute-start.16 = (bf16[384,1536]{1,0:T(8,128)(2,1)}, bf16[384,1536]{1,0:T(8,128)(2,1)}, u32[]{:S(2)}, u32[]{:S(2)}) collective-permute-start(bf16[384,1536]{1,0:T(8,128)(2,1)} %multiply_convert_fusion.6), channel_id=1, source_target_pairs={{0,1},{1,0},{2,3},{3,2},{4,5},{5,4},{6,7},{7,6},{8,9},{9,8},{10,11... | collective-permute-start | bytes 3538952 | tf_op jit(solution)/shard_map/ppermute | solution.py:390
  303.3 35.5 %collective-permute-start.18 = (bf16[4,128,1536]{2,1,0:T(8,128)(2,1)}, bf16[4,128,1536]{2,1,0:T(8,128)(2,1)S(1)}, u32[]{:S(2)}, u32[]{:S(2)}) collective-permute-start(bf16[4,128,1536]{2,1,0:T(8,128)(2,1)} %bitcast.406), channel_id=1, source_target_pairs={{0,2},{1,3},{2,0},{3,1},{4,6},{5,7},{6,4},{7,5},{8,10},{9,11},{10,... | collective-permute-start | bytes 4718600 | tf_op jit(solution)/shard_map/ppermute | solution.py:303
  403.0 37.1 %collective-permute-start.21 = (bf16[4,128,1536]{2,1,0:T(8,128)(2,1)}, bf16[4,128,1536]{2,1,0:T(8,128)(2,1)}, u32[]{:S(2)}, u32[]{:S(2)}) collective-permute-start(bf16[4,128,1536]{2,1,0:T(8,128)(2,1)} %dynamic-slice_bitcast_fusion.3), channel_id=1, source_target_pairs={{0,2},{1,3},{2,0},{3,1},{4,6},{5,7},{6,4},{7,5},{8,10},{9,11},{10,... | collective-permute-start | bytes 4718600 | tf_op jit(solution)/shard_map/ppermute | solution.py:318
  449.0 27.8 %collective-permute-start.20 = (bf16[384,1536]{1,0:T(8,128)(2,1)}, bf16[384,1536]{1,0:T(8,128)(2,1)}, u32[]{:S(2)}, u32[]{:S(2)}) collective-permute-start(bf16[384,1536]{1,0:T(8,128)(2,1)} %slice.284), channel_id=1, source_target_pairs={{0,1},{1,0},{2,3},{3,2},{4,5},{5,4},{6,7},{7,6},{8,9},{9,8},{10,11... | collective-permute-start | bytes 3538952 | tf_op jit(solution)/shard_map/ppermute | solution.py:390
  494.3 234.1 %reduce-scatter.10.cloned.1.call-start = ((), (), s32[]{:S(2)}) async-start(), calls=%async_computation.12 | async-start | bytes 1966080 | tf_op jit(solution)/shard_map/reduce_scatter | solution.py:328
  511.9 42.2 %collective-permute-start.24 = (bf16[768,1536]{1,0:T(8,128)(2,1)}, bf16[768,1536]{1,0:T(8,128)(2,1)}, u32[]{:S(2)}, u32[]{:S(2)}) collective-permute-start(bf16[768,1536]{1,0:T(8,128)(2,1)} %pad_maximum_fusion.13), channel_id=1, source_target_pairs={{0,16},{16,0},{1,17},{17,1},{2,18},{18,2},{3,19},{19,3},{4,20},{20... | collective-permute-start | bytes 7077896 | tf_op jit(solution)/shard_map/ppermute | solution.py:387
  513.2 37.6 %collective-permute-start.25 = (bf16[4,192,1024]{2,1,0:T(8,128)(2,1)}, bf16[4,192,1024]{2,1,0:T(8,128)(2,1)}, u32[]{:S(2)}, u32[]{:S(2)}) collective-permute-start(bf16[4,192,1024]{2,1,0:T(8,128)(2,1)} %dynamic-slice_bitcast_fusion.2), channel_id=1, source_target_pairs={{0,2},{1,3},{2,0},{3,1},{4,6},{5,7},{6,4},{7,5},{8,10},{9,11},{10,... | collective-permute-start | bytes 4718600 | tf_op jit(solution)/shard_map/ppermute | solution.py:318
  517.9 79.4 %collective-permute-start.29 = (bf16[4,192,1024]{2,1,0:T(8,128)(2,1)}, bf16[4,192,1024]{2,1,0:T(8,128)(2,1)}, u32[]{:S(2)}, u32[]{:S(2)}) collective-permute-start(bf16[4,192,1024]{2,1,0:T(8,128)(2,1)} %dynamic-slice_bitcast_fusion.1), channel_id=1, source_target_pairs={{0,2},{1,3},{2,0},{3,1},{4,6},{5,7},{6,4},{7,5},{8,10},{9,11},{10,... | collective-permute-start | bytes 4718600 | tf_op jit(solution)/shard_map/ppermute | solution.py:318
  554.0 215.0 %reduce-scatter.12.cloned.1.call-start = ((), (), s32[]{:S(2)}) async-start(), calls=%async_computation.13 | async-start | bytes 1966080 | tf_op jit(solution)/shard_map/reduce_scatter | solution.py:328
  631.8 126.1 %collective-permute-start.27 = (bf16[768,1536]{1,0:T(8,128)(2,1)}, bf16[768,1536]{1,0:T(8,128)(2,1)}, u32[]{:S(2)}, u32[]{:S(2)}) collective-permute-start(bf16[768,1536]{1,0:T(8,128)(2,1)} %slice.278), channel_id=1, source_target_pairs={{0,16},{16,0},{1,17},{17,1},{2,18},{18,2},{3,19},{19,3},{4,20},{20... | collective-permute-start | bytes 7077896 | tf_op jit(solution)/shard_map/ppermute | solution.py:387
  633.0 168.5 %reduce-scatter.8.cloned.1.call-start = ((), (), s32[]{:S(2)}) async-start(), calls=%async_computation.11 | async-start | bytes 1474560 | tf_op jit(solution)/shard_map/reduce_scatter | solution.py:328
  642.7 83.0 %collective-permute-start.33 = (bf16[4,192,768]{2,1,0:T(8,128)(2,1)}, bf16[4,192,768]{2,1,0:T(8,128)(2,1)}, u32[]{:S(2)}, u32[]{:S(2)}) collective-permute-start(bf16[4,192,768]{2,1,0:T(8,128)(2,1)} %fusion.14), channel_id=1, source_target_pairs={{0,2},{1,3},{2,0},{3,1},{4,6},{5,7},{6,4},{7,5},{8,10},{9,11},{10,... | collective-permute-start | bytes 3538952 | tf_op jit(solution)/shard_map/ppermute | solution.py:318
  656.8 101.1 %collective-permute-start.30 = (bf16[4,192,1280]{2,1,0:T(8,128)(2,1)}, bf16[4,192,1280]{2,1,0:T(8,128)(2,1)}, u32[]{:S(2)}, u32[]{:S(2)}) collective-permute-start(bf16[4,192,1280]{2,1,0:T(8,128)(2,1)} %dynamic-slice_bitcast_fusion), channel_id=1, source_target_pairs={{0,2},{1,3},{2,0},{3,1},{4,6},{5,7},{6,4},{7,5},{8,10},{9,11},{10,... | collective-permute-start | bytes 5898248 | tf_op jit(solution)/shard_map/ppermute | solution.py:318
  661.9 51.2 %collective-permute-start.41 = (f32[1,24]{1,0:T(1,128)S(1)}, f32[1,24]{1,0:T(1,128)S(1)}, u32[]{:S(2)}, u32[]{:S(2)}) collective-permute-start(f32[1,24]{1,0:T(1,128)S(1)} %add.507), channel_id=1, source_target_pairs={{0,2},{1,3},{2,0},{3,1},{4,6},{5,7},{6,4},{7,5},{8,10},{9,11},{10,... | collective-permute-start | bytes 296 | tf_op jit(solution)/shard_map/ppermute | solution.py:337
  724.0 79.7 %collective-permute-start.26 = (bf16[384,1536]{1,0:T(8,128)(2,1)}, bf16[384,1536]{1,0:T(8,128)(2,1)}, u32[]{:S(2)}, u32[]{:S(2)}) collective-permute-start(bf16[384,1536]{1,0:T(8,128)(2,1)} %slice.283), channel_id=1, source_target_pairs={{0,1},{1,0},{2,3},{3,2},{4,5},{5,4},{6,7},{7,6},{8,9},{9,8},{10,11... | collective-permute-start | bytes 3538952 | tf_op jit(solution)/shard_map/ppermute | solution.py:390
  728.3 89.3 %reduce-scatter.6.cloned.1.call-start = ((), (), s32[]{:S(2)}) async-start(), calls=%async_computation.10 | async-start | bytes 2457600 | tf_op jit(solution)/shard_map/reduce_scatter | solution.py:328
  729.4 27.4 %collective-permute-start.45 = (bf16[96,1024]{1,0:T(8,128)(2,1)S(1)}, bf16[96,1024]{1,0:T(8,128)(2,1)S(1)}, u32[]{:S(2)}, u32[]{:S(2)}) collective-permute-start(bf16[96,1024]{1,0:T(8,128)(2,1)S(1)} %dynamic-slice_bitcast_fusion.7), channel_id=1, source_target_pairs={{0,1},{1,0},{2,3},{3,2},{4,5},{5,4},{6,7},{7,6},{8,9},{9,8},{10,11... | collective-permute-start | bytes 589832 | tf_op jit(solution)/shard_map/ppermute | solution.py:390
  763.1 34.0 %collective-permute-start.28 = (bf16[384,1536]{1,0:T(8,128)(2,1)}, bf16[384,1536]{1,0:T(8,128)(2,1)S(1)}, u32[]{:S(2)}, u32[]{:S(2)}) collective-permute-start(bf16[384,1536]{1,0:T(8,128)(2,1)} %slice.282), channel_id=1, source_target_pairs={{0,1},{1,0},{2,3},{3,2},{4,5},{5,4},{6,7},{7,6},{8,9},{9,8},{10,11... | collective-permute-start | bytes 3538952 | tf_op jit(solution)/shard_map/ppermute | solution.py:390
  (124 other events, 1848.8 us)
Sparse Core Ops, SparseCore 0:
  25.8 44.0 all-gather.5
  76.1 30.5 all-gather.7
  109.4 35.6 all-gather.9
  178.6 37.4 all-gather.11
  266.6 36.6 all-gather.13
  494.4 35.4 reduce-scatter.13
  554.2 35.2 reduce-scatter.9
  633.1 35.3 reduce-scatter.11
  728.4 28.5 reduce-scatter.7
  767.8 40.8 reduce-scatter.5

commit v3 on v2

--- a/solution.py
+++ b/solution.py
@@ -140,7 +140,7 @@
         ),
         out_shape=jax.ShapeDtypeStruct((team * rows, width), jnp.float32),
         cost_estimate=pl.CostEstimate(
-            flops=4 * team * rows * PROMPTS * width,
+            flops=64 * team * rows * rows * width,
             bytes_accessed=8 * team * rows * width * 2,
             transcendentals=team * rows * PROMPTS * heads,
         ),
@@ -232,7 +232,7 @@
             jax.ShapeDtypeStruct((team, heads, rows), jnp.float32),
         ],
         cost_estimate=pl.CostEstimate(
-            flops=10 * team * rows * PROMPTS * width,
+            flops=80 * team * rows * rows * width,
             bytes_accessed=7 * team * rows * width * 2,
             transcendentals=team * rows * PROMPTS * heads,
         ),
@@ -332,15 +332,16 @@
 
 def sum_all(values, count, reps):
     total = values
-    step = 1
-    while step < count:
+    for step in middle_strides(count):
         total = total + lax.ppermute(total, "shard", swap_pairs(count, step))
-        step *= 2
+    near = total
+    for step in (count // 2, count // 4, 1):
+        total = total + lax.ppermute(total, "shard", swap_pairs(count, step))
     step = 1
     while step < reps:
         total = total + lax.ppermute(total, "rep", [(r, r ^ step) for r in range(reps)])
         step *= 2
-    return total
+    return near, total[0]
 
 
 def local(
@@ -484,8 +485,6 @@
         quad = both(side == 0, kept, swap_side(pick(pair, 1 - side, 2)))
         return quad.reshape(model_width, quarter)
 
-    output_w = turn_rows(output_cols)
-
     tokens_all = team_rows(after(tokens, rest_block))
     cotangent_all = team_rows(after(cotangent, tokens_all))
     facts_all = team_rows(jnp.concatenate([prompt_ids[0], seq_offsets[0]])[None, :])
@@ -498,11 +497,12 @@
     inverse1 = inverse_all[:own_rows]
     inputs = inputs_all[:own_rows]
     normed1 = after(
-        (scaled_all * gain_one).astype(jnp.bfloat16), gate_line, cotangent_all
+        (scaled_all * gain_one).astype(jnp.bfloat16), second_line, cotangent_all
     )
     row_count = normed1.shape[0]
 
     qkv_low = matmul(normed1, first[:, : 3 * quarter]).astype(jnp.bfloat16)
+    output_w = turn_rows(after(output_cols, qkv_low))
     outgate_pre = matmul(normed1, outgate_w)
     bias_mine = lax.dynamic_slice_in_dim(
         forget_bias.astype(jnp.float32), rank * heads, heads, axis=0
@@ -515,7 +515,7 @@
 
     decay_cols = jnp.transpose(decay_sum, (0, 2, 1))
     attended = attend(
-        after(qkv_low, gate_last),
+        after(qkv_low, gate_line),
         decay_cols,
         decay_sum,
         facts_all,
@@ -525,7 +525,7 @@
         own_rows,
     )
     gate_open = jax.nn.sigmoid(outgate_pre)
-    gated_low = after((attended * gate_open).astype(jnp.bfloat16), up_line)
+    gated_low = (after(attended, up_line, gate_last) * gate_open).astype(jnp.bfloat16)
 
     residual = inputs + after(team_sum(matmul(gated_low, output_w)), up_last)
     scaled2, inverse2 = normalize(residual)
@@ -542,16 +542,14 @@
     grad_up = (grad_act * silu_gate).astype(jnp.bfloat16)
     down_sum = scatter_rest(matmul_tn(act_low, cotangent_all).astype(jnp.bfloat16), count, index)
     pair_normed2 = core_sum(matmul_nt(grad_gate, gate_w) + matmul_nt(grad_up, up_w))
-    normed2_gate = after(normed2, pair_normed2)
-    part_gate_w = matmul_tn(normed2_gate, grad_gate).astype(jnp.bfloat16)
-    gate_sum = scatter_rest(part_gate_w, count, index)
-    down_held = down_sum(pair_normed2)
+    normed2_late = after(normed2, pair_normed2)
+    part_gate_w = matmul_tn(normed2_late, grad_gate).astype(jnp.bfloat16)
+    part_up_w = matmul_tn(normed2_late, grad_up).astype(jnp.bfloat16)
+    grad_normed2 = after(side_sum(pair_normed2), part_gate_w, part_up_w)
+    down_held = down_sum(grad_normed2)
     grad_down = scatter_line(down_held, count)
-    normed2_up = after(normed2_gate, down_held)
-    part_up_w = matmul_tn(normed2_up, grad_up).astype(jnp.bfloat16)
+    gate_sum = scatter_rest(after(part_gate_w, part_up_w), count, index)
     up_sum = scatter_rest(part_up_w, count, index)
-    grad_normed2 = after(side_sum(pair_normed2), down_held, part_gate_w, part_up_w)
-    grad_gain2 = jnp.sum(grad_normed2 * scaled2, axis=0)
     grad_resid = cotangent.astype(jnp.float32) + norm_back(
         grad_normed2 * gain_two, scaled2, inverse2
     )
@@ -559,21 +557,31 @@
     pair_out = core_sum(matmul(after(act_low, grad_attn_own), down_w))
     gate_held = gate_sum(pair_out)
     grad_gate_w = scatter_line(gate_held, count)
-    grad_attn = after(team_rows(grad_attn_own), gate_held)
-    layer_out = (residual + side_sum(after(pair_out, grad_attn))).astype(jnp.bfloat16)
+    grad_attn = after(team_rows(grad_attn_own), gate_held, grad_down)
     grad_gated = matmul_nt(grad_attn, output_w)
     grad_output_cols = turn_cols(matmul_tn(gated_low, grad_attn).astype(jnp.bfloat16))
     grad_attended = (grad_gated * gate_open).astype(jnp.bfloat16)
     grad_outgate = (grad_gated * attended * gate_open * (1.0 - gate_open)).astype(jnp.bfloat16)
     grad_outgate_w = matmul_tn(normed1, grad_outgate).astype(jnp.bfloat16)
-    second_sum = scatter_rest(
-        jnp.concatenate([grad_outgate_w, grad_output_cols], axis=1), count, index
-    )
+    part_second_w = jnp.concatenate([grad_outgate_w, grad_output_cols], axis=1)
+    second_sum = scatter_rest(part_second_w, count, index)
+    up_held = up_sum(part_second_w)
+    grad_up_w = scatter_line(up_held, count)
     grad_qkv, grad_logit_rows, grad_logit_cols = attend_back(
-        qkv_low, grad_attended, decay_cols, decay_sum, facts_all, heads, head_dim, team, own_rows
-    )
-    up_held = up_sum(grad_qkv)
-    grad_up_w = scatter_line(up_held, count)
+        qkv_low,
+        after(grad_attended, up_held, part_second_w),
+        decay_cols,
+        decay_sum,
+        facts_all,
+        heads,
+        head_dim,
+        team,
+        own_rows,
+    )
+    second_held = second_sum(grad_qkv)
+    grad_qkv = after(grad_qkv, grad_gate_w, second_held)
+    sum_second = scatter_line(second_held, count)
+    layer_out = (residual + side_sum(after(pair_out, grad_qkv))).astype(jnp.bfloat16)
     grad_decay = jnp.transpose(grad_logit_rows, (0, 2, 1)) - grad_logit_cols
     grad_log_forget = jnp.einsum(
         "bij,bhi->bjh", chain_float, grad_decay, precision=lax.Precision.HIGHEST
@@ -585,7 +593,7 @@
         rank * heads,
         axis=0,
     )
-    grad_bias = sum_all(bias_sum[None, :], count, reps)[0]
+    bias_near, grad_bias = sum_all(bias_sum[None, :], count, reps)
     grad_forget_low = lax.dynamic_update_slice_in_dim(
         jnp.zeros((row_count, small.shape[1]), jnp.bfloat16),
         grad_forget_in.astype(jnp.bfloat16),
@@ -593,24 +601,18 @@
         axis=1,
     )
     grad_first = jnp.concatenate([grad_qkv, grad_forget_low], axis=1)
-    part_normed1 = matmul_nt(grad_first, first) + matmul_nt(grad_outgate, outgate_w)
-    grad_gain1 = jnp.sum(part_normed1 * scaled_all, axis=0)
-    grad_normed1 = team_sum(part_normed1)
+    part_first_w = matmul_tn(normed1, grad_first).astype(jnp.bfloat16)
+    first_sum = scatter_rest(after(part_first_w, bias_near), count, index)
+    part_normed1 = matmul_nt(after(grad_first, part_first_w), first) + matmul_nt(
+        grad_outgate, outgate_w
+    )
+    first_held = first_sum()
+    grad_normed1 = team_sum(after(part_normed1, first_held))
     tokens_grad = grad_resid + norm_back(grad_normed1 * gain_one, scaled1, inverse1)
-    column = jnp.arange(first.shape[1], dtype=jnp.int32)[None, :] - 3 * quarter - head_count
-    grad_first_w = (
-        matmul_tn(normed1, grad_first)
-        + jnp.where(column == 0, grad_gain1[:, None], 0.0)
-        + jnp.where(column == 1, grad_gain2[:, None], 0.0)
-    )
-    first_sum = scatter_rest(after(grad_first_w.astype(jnp.bfloat16), up_held), count, index)
-    second_held = second_sum(grad_first_w)
-    sum_second = scatter_line(second_held, count)
-    first_held = first_sum(second_held)
     sum_first = scatter_line(first_held, count)
-    grad_down = after(grad_down, grad_first_w)
-    grad_gate_w = after(grad_gate_w, grad_first_w)
-    grad_up_w = after(grad_up_w, second_held)
+    grad_down = after(grad_down, part_first_w)
+    grad_gate_w = after(grad_gate_w, part_first_w)
+    grad_up_w = after(grad_up_w, part_first_w)
     sum_second = after(sum_second, first_held)
     sum_small = sum_first[:, 3 * quarter :]
     sum_first = sum_first[:, : 3 * quarter]
@@ -647,20 +649,37 @@
     down_own = both(core == 0, down_mine, swap_core(down_mine)).astype(jnp.float32)
     query_g, key_g, value_g = whole_cols(sum_first)
     outgate_g, output_g = whole_cols(sum_second)
+    gate_g = whole_units(grad_gate_w)
+    up_g = whole_units(grad_up_w)
+    forget_g = small_own[:, :head_count]
+
+    def gain_grad(gain, *pairs):
+        total = sum(jnp.sum(w.astype(jnp.float32) * grad, axis=1) for w, grad in pairs)
+        return total / gain.astype(jnp.float32)
+
+    gain_one_g = gain_grad(
+        attn_gain,
+        (w_query, query_g),
+        (w_key, key_g),
+        (w_value, value_g),
+        (w_outgate, outgate_g),
+        (w_forget, forget_g),
+    )
+    gain_two_g = gain_grad(ffn_gain, (w_gate, gate_g), (w_up, up_g))
     return (
         layer_out,
         tokens_grad,
-        small_own[:, head_count],
+        gain_one_g,
         query_g,
         key_g,
         value_g,
         outgate_g,
-        small_own[:, :head_count],
+        forget_g,
         grad_bias,
         output_g,
-        small_own[:, head_count + 1],
-        whole_units(grad_gate_w),
-        whole_units(grad_up_w),
+        gain_two_g,
+        gate_g,
+        up_g,
         down_own.reshape(shard_ff, model_width),
     )
 

time: 863 us -> 769 us (0.89)
  waiting for transfers between devices: 384 us -> 278 us
  matrix products: 149 us -> 136 us
  local copies, waits for them, and re-layouts: 107 us -> 120 us
  other arithmetic: 111 us -> 123 us
    ppermute x4, waiting for transfers between devices: 56.8 us -> 9.92 us  [sum_all(): total = total + lax.ppermute(total, 'shard', swap_pairs(count, step))]
    ppermute x18, waiting for transfers between devices: 169 us -> 126 us  [swap_side(): return lax.ppermute(values, 'shard', side_pairs)]
    ppermute x5, waiting for transfers between devices: 67.6 us -> 35.6 us  [gather_rest(): other = lax.ppermute(held, 'shard', swap_pairs(count, step))]
    ppermute x5, waiting for transfers between devices: 56.5 us -> 65.1 us  [scatter_rest(): lax.ppermute(pick(halves, 1 - at, 1), 'shard', swap_pairs(count, step))]
    unnamed x203 -> x215, local copies, waits for them, and re-layouts: 29.3 us -> 23.1 us
  transfers between devices with their start and end apart: 60 -> 60, of which waited for: 27 -> 28; matrix products, arithmetic and copies ran while one was open for 30% -> 35% of each run, Pallas kernels for 5% -> 6%
where the time goes in v3:
time: 769 us; the launch traced here: 759 us
  waiting for transfers between devices  278 us (36%)
  matrix products  136 us (18%)
  other arithmetic  123 us (16%)
  local copies, waits for them, and re-layouts  120 us (16%)
  Pallas kernels  43.4 us (6%)
  starting transfers between devices  42.7 us (6%)
  between operations  16.2 us (2%)
    ppermute x18, waiting for transfers between devices, swap_side(): return lax.ppermute(values, 'shard', side_pairs)  126 us
    ppermute x5, waiting for transfers between devices, scatter_rest(): lax.ppermute(pick(halves, 1 - at, 1), 'shard', swap_pairs(count, step))  65.1 us
    dot_general x6, matrix products, matmul_nt(): lax.dot_general(left_side, right_side, (((1,), (1,)), ((), ())), preferre...  53 us
    dot_general x7, matrix products, matmul(): return jnp.dot(left_side, right_side, preferred_element_type=jnp.float32)  40.2 us
    dot_general x6, matrix products, matmul_tn(): lax.dot_general(left_side, right_side, (((0,), (0,)), ((), ())), preferre...  39.8 us
    ppermute x5, waiting for transfers between devices, gather_rest(): other = lax.ppermute(held, 'shard', swap_pairs(count, step))  35.6 us
    all_gather x5, waiting for transfers between devices, gather_line(): lax.all_gather(block, 'shard', axis=0, tiled=True, axis_index_groups=line...  33.3 us
    another operation x35, other arithmetic, both(): jnp.stack([jnp.where(low_first, mine, other), jnp.where(low_first, other,...  26.7 us
  transfers between devices with their start and end apart: 60, of which 28 were waited for; matrix products, arithmetic and copies ran while one was open for 35% of the time, Pallas kernels for 6%

profile of v3, /device:TPU:0, one launch (start us, length us, event | category | flops | bytes accessed | tf_op | source)
XLA Modules:
  0.0 759.1 jit_solution(7234687616635619514)
XLA Ops:
  26.9 13.6 %collective-permute-done.1 = bf16[96,2816]{1,0:T(8,128)(2,1)S(1)} collective-permute-done((bf16[96,2816]{1,0:T(8,128)(2,1)S(1)}, bf16[96,2816]{1,0:T(8,128)(2,1)S(1)}, u32[]{:S(2)}, u32[]{:S(2)}) %collective-permute-start.1) | collective-permute-done | bytes 540704 | tf_op jit(solution)/shard_map/ppermute | solution.py:391
  44.0 24.3 %collective-permute-done.2 = bf16[384,1536]{1,0:T(8,128)(2,1)S(1)} collective-permute-done((bf16[384,1536]{1,0:T(8,128)(2,1)S(1)}, bf16[384,1536]{1,0:T(8,128)(2,1)S(1)}, u32[]{:S(2)}, u32[]{:S(2)}) %collective-permute-start.2) | collective-permute-done | bytes 1179680 | tf_op jit(solution)/shard_map/ppermute | solution.py:391
  79.1 8.1 %all-gather.6.cloned.1.call-done = bf16[768,1280]{1,0:T(8,128)(2,1)} async-done(((bf16[192,1280]{1,0:T(8,128)(2,1)}), bf16[768,1280]{1,0:T(8,128)(2,1)}) %all-gather.6.cloned.1.call-update) | async-done | bytes 1966096 | tf_op jit(solution)/shard_map/all_gather | solution.py:296
  96.6 21.8 %all-gather.8.cloned.1.call-done = bf16[768,768]{1,0:T(8,128)(2,1)} async-done(((bf16[192,768]{1,0:T(8,128)(2,1)}), bf16[768,768]{1,0:T(8,128)(2,1)}) %all-gather.8.cloned.1.call-update) | async-done | bytes 1179664 | tf_op jit(solution)/shard_map/all_gather | solution.py:296
  120.3 13.1 %collective-permute-done.6 = bf16[4,192,1280]{2,1,0:T(8,128)(2,1)} collective-permute-done((bf16[4,192,1280]{2,1,0:T(8,128)(2,1)}, bf16[4,192,1280]{2,1,0:T(8,128)(2,1)}, u32[]{:S(2)}, u32[]{:S(2)}) %collective-permute-start.6) | collective-permute-done | bytes 1966112 | tf_op jit(solution)/shard_map/ppermute | solution.py:303
  146.5 10.6 %collective-permute-done.10 = bf16[4,192,768]{2,1,0:T(8,128)(2,1)S(1)} collective-permute-done((bf16[4,192,768]{2,1,0:T(8,128)(2,1)}, bf16[4,192,768]{2,1,0:T(8,128)(2,1)S(1)}, u32[]{:S(2)}, u32[]{:S(2)}) %collective-permute-start.10) | collective-permute-done | bytes 1179680 | tf_op jit(solution)/shard_map/ppermute | solution.py:303
  163.8 9.6 %convolution_convert_fusion.1.qkv_ref = bf16[1536,1152]{1,0:T(8,128)(2,1)} fusion(bf16[1536,1536]{1,0:T(8,128)(2,1)} %get-tuple-element.53, bf16[1536,1280]{1,0:T(8,128)(2,1)S(1)} %bitcast.361), kind=kOutput, calls=%fused_computation.5 | convolution fusion | flops 5437587456 | bytes 11796480 | tf_op jit(solution)/shard_map/dot_general | solution.py:244
  181.0 19.1 %attend.1 = f32[1536,384]{1,0:T(8,128)} custom-call(s32[4,8]{1,0:T(4,128)} %pad_add_fusion.1.facts_ref, bf16[1536,1152]{1,0:T(8,128)(2,1)} %convolution_convert_fusion.1.qkv_ref, f32[4,384,6]{2,1,0:T(8,128)} %bitcast.420, f32[4,6,384]{2,1,0:T(8,128)} %copy-done.74), custom_call_target="tpu_custom_call" | custom-call | flops 14495514624 | bytes 9437184 | tf_op jit(solution)/shard_map/attend/pallas_call | solution.py:129
  204.7 6.6 fusion.8
  231.4 7.3 convert_element_type.236
  238.8 18.4 %collective-permute-done.14 = bf16[384,1536]{1,0:T(8,128)(2,1)} collective-permute-done((bf16[384,1536]{1,0:T(8,128)(2,1)S(1)}, bf16[384,1536]{1,0:T(8,128)(2,1)}, u32[]{:S(2)}, u32[]{:S(2)}) %collective-permute-start.14) | collective-permute-done | bytes 1179680 | tf_op jit(solution)/shard_map/ppermute | solution.py:391
  259.5 7.3 collective-permute-done.15
  275.7 22.3 %collective-permute-done.16 = bf16[384,1536]{1,0:T(8,128)(2,1)} collective-permute-done((bf16[384,1536]{1,0:T(8,128)(2,1)}, bf16[384,1536]{1,0:T(8,128)(2,1)}, u32[]{:S(2)}, u32[]{:S(2)}) %collective-permute-start.16) | collective-permute-done | bytes 1179680 | tf_op jit(solution)/shard_map/ppermute | solution.py:391
  313.1 6.9 fusion.71
  320.0 6.8 fusion.70
  326.8 12.9 %multiply_convert_fusion.1 = (bf16[1536,1024]{1,0:T(8,128)(2,1)}, bf16[1536,1024]{1,0:T(8,128)(2,1)}, bf16[1536,1024]{1,0:T(8,128)(2,1)}) fusion(f32[1536,1024]{1,0:T(8,128)} %fusion.70, f32[1536,1024]{1,0:T(8,128)} %fusion.71, bf16[1536,1536]{1,0:T(8,128)(2,1)S(1)} %bitcast.431, bf16[1024,1536]{1,0:T(8,128)(2,1)S(1)} %bitcast.391), kind=kOutput, calls=%fused_computation.6 | convolution fusion | flops 4855431168 | bytes 29884416 | tf_op jit(solution)/shard_map/dot_general | solution.py:254
  339.7 9.6 %fusion.72 = f32[1536,1536]{1,0:T(8,128)} fusion(bf16[1536,1024]{1,0:T(8,128)(2,1)} %get-tuple-element.145, bf16[1536,1024]{1,0:T(8,128)(2,1)S(1)} %bitcast.398), kind=kOutput, calls=%fused_computation.302 | convolution fusion | flops 4831838208 | bytes 15728640 | tf_op jit(solution)/shard_map/dot_general | solution.py:254
  349.3 7.9 %convolution_add_fusion.1 = f32[1536,1536]{1,0:T(8,128)S(1)} fusion(f32[1536,1536]{1,0:T(8,128)} %fusion.72, bf16[1536,1024]{1,0:T(8,128)(2,1)S(1)} %copy-done.85, bf16[1536,1024]{1,0:T(8,128)(2,1)S(1)} %bitcast.400), kind=kOutput, calls=%fused_computation.3 | convolution fusion | flops 4834197504 | bytes 25165824 | tf_op jit(solution)/shard_map/dot_general | solution.py:254
  362.6 8.5 %convolution_convert_fusion.2 = bf16[1024,1536]{1,0:T(8,128)(2,1)S(1)} fusion(bf16[1536,1024]{1,0:T(8,128)(2,1)} %get-tuple-element.64, bf16[1536,1536]{1,0:T(8,128)(2,1)} %constant_dynamic-update-slice_fusion.3), kind=kOutput, calls=%fused_computation.26 | convolution fusion | flops 4833411072 | bytes 11010048 | tf_op jit(solution)/shard_map/dot_general | solution.py:248
  379.6 6.7 convolution_convert_fusion.3
  386.3 6.9 convolution_convert_fusion.4
  393.3 13.3 %collective-permute-done.20 = bf16[384,1536]{1,0:T(8,128)(2,1)S(1)} collective-permute-done((bf16[384,1536]{1,0:T(8,128)(2,1)S(1)}, bf16[384,1536]{1,0:T(8,128)(2,1)S(1)}, u32[]{:S(2)}, u32[]{:S(2)}) %collective-permute-start.20) | collective-permute-done | bytes 1179680 | tf_op jit(solution)/shard_map/ppermute | solution.py:391
  426.2 12.4 %collective-permute-done.22 = bf16[384,1536]{1,0:T(8,128)(2,1)} collective-permute-done((bf16[384,1536]{1,0:T(8,128)(2,1)}, bf16[384,1536]{1,0:T(8,128)(2,1)}, u32[]{:S(2)}, u32[]{:S(2)}) %collective-permute-start.22) | collective-permute-done | bytes 1179680 | tf_op jit(solution)/shard_map/ppermute | solution.py:391
  447.2 30.2 %collective-permute-done.24 = bf16[4,192,1024]{2,1,0:T(8,128)(2,1)S(1)} collective-permute-done((bf16[4,192,1024]{2,1,0:T(8,128)(2,1)S(1)}, bf16[4,192,1024]{2,1,0:T(8,128)(2,1)S(1)}, u32[]{:S(2)}, u32[]{:S(2)}) %collective-permute-start.24) | collective-permute-done | bytes 1572896 | tf_op jit(solution)/shard_map/ppermute | solution.py:318
  503.4 7.2 multiply_convert_fusion.4
  521.1 15.6 %collective-permute-done.26 = bf16[4,192,1024]{2,1,0:T(8,128)(2,1)} collective-permute-done((bf16[4,192,1024]{2,1,0:T(8,128)(2,1)}, bf16[4,192,1024]{2,1,0:T(8,128)(2,1)}, u32[]{:S(2)}, u32[]{:S(2)}) %collective-permute-start.26) | collective-permute-done | bytes 1572896 | tf_op jit(solution)/shard_map/ppermute | solution.py:318
  540.0 24.3 %attend_back.1 = (bf16[1536,1152]{1,0:T(8,128)(2,1)}, f32[4,384,6]{2,1,0:T(8,128)}, f32[4,6,384]{2,1,0:T(8,128)}) custom-call(s32[4,8]{1,0:T(4,128)} %pad_add_fusion.1.facts_ref, bf16[1536,1152]{1,0:T(8,128)(2,1)} %convolution_convert_fusion.1.qkv_ref, bf16[1536,384]{1,0:T(8,128)(2,1)} %get-tuple-element.70.grad_ref, f32[4,384,6]{2,1,0:T(8,128)} %bitcast.421, ...), custom_call_target="tpu_custom_call" | custom-call | flops 18119393280 | bytes 8257536 | tf_op jit(solution)/shard_map/attend_back/pallas_call | solution.py:208
  589.0 9.4 %convolution_convert_fusion = bf16[1536,1280]{1,0:T(8,128)(2,1)S(1)} fusion(bf16[1536,1536]{1,0:T(8,128)(2,1)} %get-tuple-element.53, bf16[1536,128]{1,0:T(8,128)(2,1)S(1)} %dynamic_update_slice.9, bf16[1536,1152]{1,0:T(8,128)(2,1)} %get-tuple-element.73), kind=kOutput, calls=%fused_computation.4 | convolution fusion | flops 6049628160 | bytes 12582912 | tf_op jit(solution)/shard_map/dot_general | solution.py:248
  610.6 10.0 %fusion.74 = f32[1536,1536]{1,0:T(8,128)S(1)} fusion(bf16[1536,1280]{1,0:T(8,128)(2,1)} %pad_maximum_fusion.3, bf16[1536,1280]{1,0:T(8,128)(2,1)} %bitcast.360), kind=kOutput, calls=%fused_computation.304 | convolution fusion | flops 6039797760 | bytes 17301504 | tf_op jit(solution)/shard_map/dot_general | solution.py:254
  629.3 19.3 %collective-permute-done.32 = bf16[4,192,1280]{2,1,0:T(8,128)(2,1)} collective-permute-done((bf16[4,192,1280]{2,1,0:T(8,128)(2,1)}, bf16[4,192,1280]{2,1,0:T(8,128)(2,1)}, u32[]{:S(2)}, u32[]{:S(2)}) %collective-permute-start.32) | collective-permute-done | bytes 1966112 | tf_op jit(solution)/shard_map/ppermute | solution.py:318
  709.7 9.1 %collective-permute-done.34 = bf16[384,1536]{1,0:T(8,128)(2,1)} collective-permute-done((bf16[384,1536]{1,0:T(8,128)(2,1)}, bf16[384,1536]{1,0:T(8,128)(2,1)}, u32[]{:S(2)}, u32[]{:S(2)}) %collective-permute-start.34) | collective-permute-done | bytes 1179680 | tf_op jit(solution)/shard_map/ppermute | solution.py:391
  732.8 7.2 multiply_add_fusion
  (518 shorter events, 336.8 us)
Async XLA Ops:
  7.2 80.0 %all-gather.6.cloned.1.call-start = ((), (), s32[]{:S(2)}) async-start(), calls=%async_computation.5 | async-start | bytes 2457600 | tf_op jit(solution)/shard_map/all_gather | solution.py:296
  42.0 76.4 %all-gather.8.cloned.1.call-start = ((), (), s32[]{:S(2)}) async-start(), calls=%async_computation.6 | async-start | bytes 1474560 | tf_op jit(solution)/shard_map/all_gather | solution.py:296
  42.2 28.3 %collective-permute-start.4 = (s32[1,8]{1,0:T(1,128)S(1)}, s32[1,8]{1,0:T(1,128)S(1)}, u32[]{:S(2)}, u32[]{:S(2)}) collective-permute-start(s32[1,8]{1,0:T(1,128)S(1)} %add_bitcast_fusion), channel_id=1, source_target_pairs={{0,1},{1,0},{2,3},{3,2},{4,5},{5,4},{6,7},{7,6},{8,9},{9,8},{10,11... | collective-permute-start | bytes 104 | tf_op jit(solution)/shard_map/ppermute | solution.py:391
  87.2 71.6 %all-gather.10.cloned.1.call-start = ((), (), s32[]{:S(2)}) async-start(), calls=%async_computation.7 | async-start | bytes 1966080 | tf_op jit(solution)/shard_map/all_gather | solution.py:296
  87.3 46.1 %collective-permute-start.6 = (bf16[4,192,1280]{2,1,0:T(8,128)(2,1)}, bf16[4,192,1280]{2,1,0:T(8,128)(2,1)}, u32[]{:S(2)}, u32[]{:S(2)}) collective-permute-start(bf16[4,192,1280]{2,1,0:T(8,128)(2,1)} %bitcast.402), channel_id=1, source_target_pairs={{0,2},{1,3},{2,0},{3,1},{4,6},{5,7},{6,4},{7,5},{8,10},{9,11},{10,... | collective-permute-start | bytes 5898248 | tf_op jit(solution)/shard_map/ppermute | solution.py:303
  93.0 43.9 %collective-permute-start.7 = (bf16[384,1536]{1,0:T(8,128)(2,1)S(1)}, bf16[384,1536]{1,0:T(8,128)(2,1)S(1)}, u32[]{:S(2)}, u32[]{:S(2)}) collective-permute-start(bf16[384,1536]{1,0:T(8,128)(2,1)S(1)} %copy-done.5), channel_id=1, source_target_pairs={{0,1},{1,0},{2,3},{3,2},{4,5},{5,4},{6,7},{7,6},{8,9},{9,8},{10,11... | collective-permute-start | bytes 3538952 | tf_op jit(solution)/shard_map/ppermute | solution.py:391
  118.5 95.6 %all-gather.12.cloned.1.call-start = ((), (), s32[]{:S(2)}) async-start(), calls=%async_computation.8 | async-start | bytes 1966080 | tf_op jit(solution)/shard_map/all_gather | solution.py:296
  118.7 38.4 %collective-permute-start.10 = (bf16[4,192,768]{2,1,0:T(8,128)(2,1)}, bf16[4,192,768]{2,1,0:T(8,128)(2,1)S(1)}, u32[]{:S(2)}, u32[]{:S(2)}) collective-permute-start(bf16[4,192,768]{2,1,0:T(8,128)(2,1)} %bitcast.412), channel_id=1, source_target_pairs={{0,2},{1,3},{2,0},{3,1},{4,6},{5,7},{6,4},{7,5},{8,10},{9,11},{10,... | collective-permute-start | bytes 3538952 | tf_op jit(solution)/shard_map/ppermute | solution.py:303
  158.8 115.4 %all-gather.14.cloned.1.call-start = ((), (), s32[]{:S(2)}) async-start(), calls=%async_computation.9 | async-start | bytes 1966080 | tf_op jit(solution)/shard_map/all_gather | solution.py:296
  158.9 55.1 %collective-permute-start.9 = (bf16[4,192,1024]{2,1,0:T(8,128)(2,1)}, bf16[4,192,1024]{2,1,0:T(8,128)(2,1)}, u32[]{:S(2)}, u32[]{:S(2)}) collective-permute-start(bf16[4,192,1024]{2,1,0:T(8,128)(2,1)} %bitcast.406), channel_id=1, source_target_pairs={{0,2},{1,3},{2,0},{3,1},{4,6},{5,7},{6,4},{7,5},{8,10},{9,11},{10,... | collective-permute-start | bytes 4718600 | tf_op jit(solution)/shard_map/ppermute | solution.py:303
  228.7 28.4 %collective-permute-start.14 = (bf16[384,1536]{1,0:T(8,128)(2,1)S(1)}, bf16[384,1536]{1,0:T(8,128)(2,1)}, u32[]{:S(2)}, u32[]{:S(2)}) collective-permute-start(bf16[384,1536]{1,0:T(8,128)(2,1)S(1)} %slice.275), channel_id=1, source_target_pairs={{0,1},{1,0},{2,3},{3,2},{4,5},{5,4},{6,7},{7,6},{8,9},{9,8},{10,11... | collective-permute-start | bytes 3538952 | tf_op jit(solution)/shard_map/ppermute | solution.py:391
  230.0 36.8 %collective-permute-start.15 = (bf16[4,192,1024]{2,1,0:T(8,128)(2,1)S(1)}, bf16[4,192,1024]{2,1,0:T(8,128)(2,1)}, u32[]{:S(2)}, u32[]{:S(2)}) collective-permute-start(bf16[4,192,1024]{2,1,0:T(8,128)(2,1)S(1)} %bitcast.408), channel_id=1, source_target_pairs={{0,2},{1,3},{2,0},{3,1},{4,6},{5,7},{6,4},{7,5},{8,10},{9,11},{10,... | collective-permute-start | bytes 4718600 | tf_op jit(solution)/shard_map/ppermute | solution.py:303
  238.7 244.3 %reduce-scatter.6.cloned.1.call-start = ((), (), s32[]{:S(2)}) async-start(), calls=%async_computation.10 | async-start | bytes 1966080 | tf_op jit(solution)/shard_map/reduce_scatter | solution.py:328
  270.2 27.7 %collective-permute-start.16 = (bf16[384,1536]{1,0:T(8,128)(2,1)}, bf16[384,1536]{1,0:T(8,128)(2,1)}, u32[]{:S(2)}, u32[]{:S(2)}) collective-permute-start(bf16[384,1536]{1,0:T(8,128)(2,1)} %multiply_convert_fusion.6), channel_id=1, source_target_pairs={{0,1},{1,0},{2,3},{3,2},{4,5},{5,4},{6,7},{7,6},{8,9},{9,8},{10,11... | collective-permute-start | bytes 3538952 | tf_op jit(solution)/shard_map/ppermute | solution.py:391
  274.2 35.5 %collective-permute-start.18 = (bf16[4,128,1536]{2,1,0:T(8,128)(2,1)}, bf16[4,128,1536]{2,1,0:T(8,128)(2,1)S(1)}, u32[]{:S(2)}, u32[]{:S(2)}) collective-permute-start(bf16[4,128,1536]{2,1,0:T(8,128)(2,1)} %bitcast.410), channel_id=1, source_target_pairs={{0,2},{1,3},{2,0},{3,1},{4,6},{5,7},{6,4},{7,5},{8,10},{9,11},{10,... | collective-permute-start | bytes 4718600 | tf_op jit(solution)/shard_map/ppermute | solution.py:303
  373.9 48.7 %collective-permute-start.25 = (bf16[4,128,1536]{2,1,0:T(8,128)(2,1)}, bf16[4,128,1536]{2,1,0:T(8,128)(2,1)}, u32[]{:S(2)}, u32[]{:S(2)}) collective-permute-start(bf16[4,128,1536]{2,1,0:T(8,128)(2,1)} %dynamic-slice_bitcast_fusion.2), channel_id=1, source_target_pairs={{0,2},{1,3},{2,0},{3,1},{4,6},{5,7},{6,4},{7,5},{8,10},{9,11},{10,... | collective-permute-start | bytes 4718600 | tf_op jit(solution)/shard_map/ppermute | solution.py:318
  378.1 28.4 %collective-permute-start.20 = (bf16[384,1536]{1,0:T(8,128)(2,1)S(1)}, bf16[384,1536]{1,0:T(8,128)(2,1)S(1)}, u32[]{:S(2)}, u32[]{:S(2)}) collective-permute-start(bf16[384,1536]{1,0:T(8,128)(2,1)S(1)} %slice.274), channel_id=1, source_target_pairs={{0,1},{1,0},{2,3},{3,2},{4,5},{5,4},{6,7},{7,6},{8,9},{9,8},{10,11... | collective-permute-start | bytes 3538952 | tf_op jit(solution)/shard_map/ppermute | solution.py:391
  410.7 27.9 %collective-permute-start.22 = (bf16[384,1536]{1,0:T(8,128)(2,1)}, bf16[384,1536]{1,0:T(8,128)(2,1)}, u32[]{:S(2)}, u32[]{:S(2)}) collective-permute-start(bf16[384,1536]{1,0:T(8,128)(2,1)} %fusion.64), channel_id=1, source_target_pairs={{0,1},{1,0},{2,3},{3,2},{4,5},{5,4},{6,7},{7,6},{8,9},{9,8},{10,11... | collective-permute-start | bytes 3538952 | tf_op jit(solution)/shard_map/ppermute | solution.py:391
  426.1 162.9 %reduce-scatter.8.cloned.1.call-start = ((), (), s32[]{:S(2)}) async-start(), calls=%async_computation.11 | async-start | bytes 1966080 | tf_op jit(solution)/shard_map/reduce_scatter | solution.py:328
  440.4 38.9 %collective-permute-start.23 = (bf16[768,1536]{1,0:T(8,128)(2,1)S(1)}, bf16[768,1536]{1,0:T(8,128)(2,1)S(1)}, u32[]{:S(2)}, u32[]{:S(2)}) collective-permute-start(bf16[768,1536]{1,0:T(8,128)(2,1)S(1)} %pad_maximum_fusion.11), channel_id=1, source_target_pairs={{0,16},{16,0},{1,17},{17,1},{2,18},{18,2},{3,19},{19,3},{4,20},{20... | collective-permute-start | bytes 7077896 | tf_op jit(solution)/shard_map/ppermute | solution.py:388
  440.6 36.8 %collective-permute-start.24 = (bf16[4,192,1024]{2,1,0:T(8,128)(2,1)S(1)}, bf16[4,192,1024]{2,1,0:T(8,128)(2,1)S(1)}, u32[]{:S(2)}, u32[]{:S(2)}) collective-permute-start(bf16[4,192,1024]{2,1,0:T(8,128)(2,1)S(1)} %dynamic-slice_bitcast_fusion.3), channel_id=1, source_target_pairs={{0,2},{1,3},{2,0},{3,1},{4,6},{5,7},{6,4},{7,5},{8,10},{9,11},{10,... | collective-permute-start | bytes 4718600 | tf_op jit(solution)/shard_map/ppermute | solution.py:318
  499.1 37.6 %collective-permute-start.26 = (bf16[4,192,1024]{2,1,0:T(8,128)(2,1)}, bf16[4,192,1024]{2,1,0:T(8,128)(2,1)}, u32[]{:S(2)}, u32[]{:S(2)}) collective-permute-start(bf16[4,192,1024]{2,1,0:T(8,128)(2,1)} %dynamic-slice_bitcast_fusion.1), channel_id=1, source_target_pairs={{0,2},{1,3},{2,0},{3,1},{4,6},{5,7},{6,4},{7,5},{8,10},{9,11},{10,... | collective-permute-start | bytes 4718600 | tf_op jit(solution)/shard_map/ppermute | solution.py:318
  499.7 157.6 %reduce-scatter.14.cloned.1.call-start = ((), (), s32[]{:S(2)}) async-start(), calls=%async_computation.14 | async-start | bytes 1966080 | tf_op jit(solution)/shard_map/reduce_scatter | solution.py:328
  519.8 66.3 %collective-permute-start.29 = (bf16[4,192,768]{2,1,0:T(8,128)(2,1)}, bf16[4,192,768]{2,1,0:T(8,128)(2,1)}, u32[]{:S(2)}, u32[]{:S(2)}) collective-permute-start(bf16[4,192,768]{2,1,0:T(8,128)(2,1)} %fusion.12), channel_id=1, source_target_pairs={{0,2},{1,3},{2,0},{3,1},{4,6},{5,7},{6,4},{7,5},{8,10},{9,11},{10,... | collective-permute-start | bytes 3538952 | tf_op jit(solution)/shard_map/ppermute | solution.py:318
  581.7 88.3 %reduce-scatter.12.cloned.1.call-start = ((), (), s32[]{:S(2)}) async-start(), calls=%async_computation.13 | async-start | bytes 1474560 | tf_op jit(solution)/shard_map/reduce_scatter | solution.py:328
  598.4 29.6 %collective-permute-start.49 = (bf16[128,1536]{1,0:T(8,128)(2,1)}, bf16[128,1536]{1,0:T(8,128)(2,1)}, u32[]{:S(2)}, u32[]{:S(2)}) collective-permute-start(bf16[128,1536]{1,0:T(8,128)(2,1)} %reduce-scatter.6.cloned.1.call-done), channel_id=1, source_target_pairs={{0,16},{16,0},{1,17},{17,1},{2,18},{18,2},{3,19},{19,3},{4,20},{20... | collective-permute-start | bytes 1179656 | tf_op jit(solution)/shard_map/ppermute | solution.py:388
  603.3 45.3 %collective-permute-start.32 = (bf16[4,192,1280]{2,1,0:T(8,128)(2,1)}, bf16[4,192,1280]{2,1,0:T(8,128)(2,1)}, u32[]{:S(2)}, u32[]{:S(2)}) collective-permute-start(bf16[4,192,1280]{2,1,0:T(8,128)(2,1)} %dynamic-slice_bitcast_fusion), channel_id=1, source_target_pairs={{0,2},{1,3},{2,0},{3,1},{4,6},{5,7},{6,4},{7,5},{8,10},{9,11},{10,... | collective-permute-start | bytes 5898248 | tf_op jit(solution)/shard_map/ppermute | solution.py:318
  606.1 115.9 %reduce-scatter.10.cloned.1.call-start = ((), (), s32[]{:S(2)}) async-start(), calls=%async_computation.12 | async-start | bytes 2457600 | tf_op jit(solution)/shard_map/reduce_scatter | solution.py:328
  609.1 123.8 %collective-permute-start.30 = (bf16[384,1536]{1,0:T(8,128)(2,1)}, bf16[384,1536]{1,0:T(8,128)(2,1)}, u32[]{:S(2)}, u32[]{:S(2)}) collective-permute-start(bf16[384,1536]{1,0:T(8,128)(2,1)} %slice.273), channel_id=1, source_target_pairs={{0,1},{1,0},{2,3},{3,2},{4,5},{5,4},{6,7},{7,6},{8,9},{9,8},{10,11... | collective-permute-start | bytes 3538952 | tf_op jit(solution)/shard_map/ppermute | solution.py:391
  627.8 32.8 %collective-permute-start.46 = (bf16[2,96,1024]{2,1,0:T(8,128)(2,1)}, bf16[2,96,1024]{2,1,0:T(8,128)(2,1)}, u32[]{:S(2)}, u32[]{:S(2)}) collective-permute-start(bf16[2,96,1024]{2,1,0:T(8,128)(2,1)} %pad_maximum_fusion.21), channel_id=1, source_target_pairs={{0,16},{16,0},{1,17},{17,1},{2,18},{18,2},{3,19},{19,3},{4,20},{20... | collective-permute-start | bytes 1179656 | tf_op jit(solution)/shard_map/ppermute | solution.py:388
  656.0 29.2 %collective-permute-start.33 = (bf16[768,1536]{1,0:T(8,128)(2,1)}, bf16[768,1536]{1,0:T(8,128)(2,1)}, u32[]{:S(2)}, u32[]{:S(2)}) collective-permute-start(bf16[768,1536]{1,0:T(8,128)(2,1)} %slice.268), channel_id=1, source_target_pairs={{0,16},{16,0},{1,17},{17,1},{2,18},{18,2},{3,19},{19,3},{4,20},{20... | collective-permute-start | bytes 7077896 | tf_op jit(solution)/shard_map/ppermute | solution.py:388
  690.1 28.7 %collective-permute-start.34 = (bf16[384,1536]{1,0:T(8,128)(2,1)}, bf16[384,1536]{1,0:T(8,128)(2,1)}, u32[]{:S(2)}, u32[]{:S(2)}) collective-permute-start(bf16[384,1536]{1,0:T(8,128)(2,1)} %slice.272), channel_id=1, source_target_pairs={{0,1},{1,0},{2,3},{3,2},{4,5},{5,4},{6,7},{7,6},{8,9},{9,8},{10,11... | collective-permute-start | bytes 3538952 | tf_op jit(solution)/shard_map/ppermute | solution.py:391
  (130 other events, 1354.2 us)
Sparse Core Ops, SparseCore 0:
  42.2 44.9 all-gather.5
  89.3 29.0 all-gather.7
  120.6 36.2 all-gather.9
  158.9 36.1 all-gather.11
  238.8 35.2 all-gather.13
  426.2 34.8 reduce-scatter.5
  499.8 35.2 reduce-scatter.7
  581.8 33.4 reduce-scatter.13
  618.2 28.1 reduce-scatter.11
  667.9 39.6 reduce-scatter.9

commit v4 on v3

--- a/solution.py
+++ b/solution.py
@@ -296,11 +296,13 @@
     return lax.all_gather(block, "shard", axis=0, tiled=True, axis_index_groups=line_groups(count))
 
 
-def gather_rest(line, count, index):
+def gather_rest(line, count, index, *others):
     width = line.shape[1]
     held = line.reshape(4, -1, width)
     for step in reversed(middle_strides(count)):
         other = lax.ppermute(held, "shard", swap_pairs(count, step))
+        if others:
+            other = after(other, *others)
         held = both((index // step) % 2 == 0, held, other, axis=1).reshape(4, -1, width)
     return held.reshape(-1, width), other
 
@@ -390,8 +392,10 @@
     def swap_side(values):
         return lax.ppermute(values, "shard", side_pairs)
 
-    def team_rows(values):
+    def team_rows(values, *others):
         pair = jnp.concatenate([values, swap_side(values)], axis=0)
+        if others:
+            pair = after(pair, *others)
         return jnp.concatenate([pair, swap_core(pair)], axis=0)
 
     def core_sum(partial):
@@ -455,20 +459,16 @@
     down_line = gather_line(
         after(lax.dynamic_slice_in_dim(w_down, core * unit, unit, axis=0), up_line), count
     )
-    first, first_last = gather_rest(first_line, count, index)
-    second, second_last = gather_rest(second_line, count, index)
+    first, _ = gather_rest(first_line, count, index)
     gate_w, gate_last = gather_rest(gate_line, count, index)
     up_w, up_last = gather_rest(up_line, count, index)
-    down_w, down_last = gather_rest(down_line, count, index)
+    down_w, _ = gather_rest(down_line, count, index)
 
     forget_w = lax.dynamic_slice_in_dim(
         first[:, 3 * quarter : 3 * quarter + head_count], rank * heads, heads, axis=1
     )
     gain_one = first[:, 3 * quarter + head_count].astype(jnp.float32)
     gain_two = first[:, 3 * quarter + head_count + 1].astype(jnp.float32)
-    outgate_w = second[:, :quarter]
-    output_cols = second[:, quarter:]
-
     def turn_rows(values):
         cut = values.reshape(2, 2, quarter, quarter)
         mine = pick(cut, side, 0)
@@ -485,7 +485,7 @@
         quad = both(side == 0, kept, swap_side(pick(pair, 1 - side, 2)))
         return quad.reshape(model_width, quarter)
 
-    tokens_all = team_rows(after(tokens, rest_block))
+    tokens_all = team_rows(after(tokens, rest_block), first_line)
     cotangent_all = team_rows(after(cotangent, tokens_all))
     facts_all = team_rows(jnp.concatenate([prompt_ids[0], seq_offsets[0]])[None, :])
     chain_ok = jnp.stack([chain_mask(facts_all[b, :NC], facts_all[b, NC:]) for b in range(team)])
@@ -502,7 +502,9 @@
     row_count = normed1.shape[0]
 
     qkv_low = matmul(normed1, first[:, : 3 * quarter]).astype(jnp.bfloat16)
-    output_w = turn_rows(after(output_cols, qkv_low))
+    second = gather_rest(second_line, count, index, qkv_low)[0]
+    outgate_w = second[:, :quarter]
+    output_w = turn_rows(second[:, quarter:])
     outgate_pre = matmul(normed1, outgate_w)
     bias_mine = lax.dynamic_slice_in_dim(
         forget_bias.astype(jnp.float32), rank * heads, heads, axis=0
@@ -554,18 +556,18 @@
         grad_normed2 * gain_two, scaled2, inverse2
     )
     grad_attn_own = grad_resid.astype(jnp.bfloat16)
-    pair_out = core_sum(matmul(after(act_low, grad_attn_own), down_w))
-    gate_held = gate_sum(pair_out)
+    pair_out = core_sum(matmul(after(act_low, grad_attn_own, down_held), down_w))
+    gate_held = gate_sum()
     grad_gate_w = scatter_line(gate_held, count)
-    grad_attn = after(team_rows(grad_attn_own), gate_held, grad_down)
+    grad_attn = after(team_rows(grad_attn_own, gate_held), grad_down)
     grad_gated = matmul_nt(grad_attn, output_w)
     grad_output_cols = turn_cols(matmul_tn(gated_low, grad_attn).astype(jnp.bfloat16))
     grad_attended = (grad_gated * gate_open).astype(jnp.bfloat16)
     grad_outgate = (grad_gated * attended * gate_open * (1.0 - gate_open)).astype(jnp.bfloat16)
-    grad_outgate_w = matmul_tn(normed1, grad_outgate).astype(jnp.bfloat16)
+    up_held = up_sum(grad_outgate)
+    grad_outgate_w = matmul_tn(after(normed1, up_held), grad_outgate).astype(jnp.bfloat16)
     part_second_w = jnp.concatenate([grad_outgate_w, grad_output_cols], axis=1)
     second_sum = scatter_rest(part_second_w, count, index)
-    up_held = up_sum(part_second_w)
     grad_up_w = scatter_line(up_held, count)
     grad_qkv, grad_logit_rows, grad_logit_cols = attend_back(
         qkv_low,
@@ -612,10 +614,8 @@
     sum_first = scatter_line(first_held, count)
     grad_down = after(grad_down, part_first_w)
     grad_gate_w = after(grad_gate_w, part_first_w)
-    grad_up_w = after(grad_up_w, part_first_w)
-    sum_second = after(sum_second, first_held)
-    sum_small = sum_first[:, 3 * quarter :]
-    sum_first = sum_first[:, : 3 * quarter]
+    grad_up_w = after(grad_up_w, grad_normed1)
+    sum_second = after(sum_second, grad_normed1)
 
     def replicas(values):
         total = values
@@ -632,9 +632,9 @@
         cores = both(core == 0, sides, swap_core(sides))
         return jnp.transpose(cores.astype(jnp.float32), (1, 0, 2, 3))
 
-    def whole_cols(values):
-        parts = values.shape[1] // quarter
-        quad = own_of(values).reshape(2, 2, shard_rows, parts, quarter)
+    def whole_cols(own):
+        parts = own.shape[3] // quarter
+        quad = own.reshape(2, 2, shard_rows, parts, quarter)
         quad = jnp.transpose(quad, (3, 2, 0, 1, 4)).reshape(parts, shard_rows, model_width)
         return [quad[p] for p in range(parts)]
 
@@ -642,16 +642,14 @@
         quad = own_of(values).reshape(2, 2, shard_rows, count // 2, unit)
         return jnp.transpose(quad, (2, 3, 0, 1, 4)).reshape(shard_rows, team * quarter_ff)
 
-    small_pair = replicas(sum_small).reshape(2, shard_rows, sum_small.shape[1])
-    small_own = add_low(pick(small_pair, side, 0), swap_side(pick(small_pair, 1 - side, 0)))
-    small_own = small_own.astype(jnp.float32) + swap_core(small_own).astype(jnp.float32)
     down_mine = replicas(grad_down)
     down_own = both(core == 0, down_mine, swap_core(down_mine)).astype(jnp.float32)
-    query_g, key_g, value_g = whole_cols(sum_first)
-    outgate_g, output_g = whole_cols(sum_second)
+    first_own = own_of(sum_first)
+    query_g, key_g, value_g = whole_cols(first_own[..., : 3 * quarter])
+    forget_g = jnp.sum(first_own[..., 3 * quarter : 3 * quarter + head_count], axis=(0, 1))
+    outgate_g, output_g = whole_cols(own_of(sum_second))
     gate_g = whole_units(grad_gate_w)
     up_g = whole_units(grad_up_w)
-    forget_g = small_own[:, :head_count]
 
     def gain_grad(gain, *pairs):
         total = sum(jnp.sum(w.astype(jnp.float32) * grad, axis=1) for w, grad in pairs)

time: 769 us -> 731 us (0.951)
  waiting for transfers between devices: 278 us -> 259 us
  local copies, waits for them, and re-layouts: 120 us -> 111 us
    ppermute x18 -> x17, waiting for transfers between devices: 126 us -> 147 us  [swap_side(): return lax.ppermute(values, 'shard', side_pairs)]
    ppermute x5, waiting for transfers between devices: 65.1 us -> 48 us  [scatter_rest(): lax.ppermute(pick(halves, 1 - at, 1), 'shard', swap_pairs(count, step))]
    ppermute x5, waiting for transfers between devices: 35.6 us -> 23.7 us  [gather_rest(): other = lax.ppermute(held, 'shard', swap_pairs(count, step))]
    unnamed x215 -> x211, local copies, waits for them, and re-layouts: 23.1 us -> 29.6 us
    ppermute x18 -> x17, starting transfers between devices: 21.7 us -> 18.9 us  [swap_side(): return lax.ppermute(values, 'shard', side_pairs)]
    convert_element_type x6 -> x5, other arithmetic: 14.8 us -> 16.9 us  [add_low(): (left_side.astype(jnp.float32) + right_side.astype(jnp.float32)).astype(j...]
  transfers between devices with their start and end apart: 60 -> 58, of which waited for: 28 -> 23; matrix products, arithmetic and copies ran while one was open for 35% -> 37% of each run, Pallas kernels for 6% -> 6%
where the time goes in v4:
time: 731 us; the launch traced here: 723 us
  waiting for transfers between devices  259 us (35%)
  matrix products  135 us (18%)
  other arithmetic  117 us (16%)
  local copies, waits for them, and re-layouts  111 us (15%)
  Pallas kernels  43.5 us (6%)
  starting transfers between devices  40.9 us (6%)
  between operations  16.5 us (2%)
    ppermute x17, waiting for transfers between devices, swap_side(): return lax.ppermute(values, 'shard', side_pairs)  147 us
    dot_general x6, matrix products, matmul_nt(): lax.dot_general(left_side, right_side, (((1,), (1,)), ((), ())), preferre...  49.7 us
    ppermute x5, waiting for transfers between devices, scatter_rest(): lax.ppermute(pick(halves, 1 - at, 1), 'shard', swap_pairs(count, step))  48 us
    dot_general x7, matrix products, matmul(): return jnp.dot(left_side, right_side, preferred_element_type=jnp.float32)  42 us
    dot_general x6, matrix products, matmul_tn(): lax.dot_general(left_side, right_side, (((0,), (0,)), ((), ())), preferre...  41.3 us
    unnamed x211, local copies, waits for them, and re-layouts  29.6 us
    all_gather x5, waiting for transfers between devices, gather_line(): lax.all_gather(block, 'shard', axis=0, tiled=True, axis_index_groups=line...  29.1 us
    pallas_call x1, Pallas kernels, attend_back(): pl.pallas_call(body, grid_spec=pltpu.PrefetchScalarGridSpec(num_scalar_pr...  24.3 us
  transfers between devices with their start and end apart: 58, of which 23 were waited for; matrix products, arithmetic and copies ran while one was open for 37% of the time, Pallas kernels for 6%

profile of v4, /device:TPU:0, one launch (start us, length us, event | category | flops | bytes accessed | tf_op | source)
XLA Modules:
  0.0 723.0 jit_solution(11957816510176433107)
XLA Ops:
  27.0 13.5 %collective-permute-done.1 = bf16[96,2816]{1,0:T(8,128)(2,1)S(1)} collective-permute-done((bf16[96,2816]{1,0:T(8,128)(2,1)S(1)}, bf16[96,2816]{1,0:T(8,128)(2,1)S(1)}, u32[]{:S(2)}, u32[]{:S(2)}) %collective-permute-start.1) | collective-permute-done | bytes 540704 | tf_op jit(solution)/shard_map/ppermute | solution.py:393
  43.9 24.4 %collective-permute-done.2 = bf16[384,1536]{1,0:T(8,128)(2,1)S(1)} collective-permute-done((bf16[384,1536]{1,0:T(8,128)(2,1)S(1)}, bf16[384,1536]{1,0:T(8,128)(2,1)S(1)}, u32[]{:S(2)}, u32[]{:S(2)}) %collective-permute-start.2) | collective-permute-done | bytes 1179680 | tf_op jit(solution)/shard_map/ppermute | solution.py:393
  83.2 20.8 %all-gather.8.cloned.1.call-done = bf16[768,768]{1,0:T(8,128)(2,1)} async-done(((bf16[192,768]{1,0:T(8,128)(2,1)}), bf16[768,768]{1,0:T(8,128)(2,1)}) %all-gather.8.cloned.1.call-update) | async-done | bytes 1179664 | tf_op jit(solution)/shard_map/all_gather | solution.py:296
  110.6 10.3 %collective-permute-done.6 = bf16[4,192,1280]{2,1,0:T(8,128)(2,1)} collective-permute-done((bf16[4,192,1280]{2,1,0:T(8,128)(2,1)}, bf16[4,192,1280]{2,1,0:T(8,128)(2,1)}, u32[]{:S(2)}, u32[]{:S(2)}) %collective-permute-start.6) | collective-permute-done | bytes 1966112 | tf_op jit(solution)/shard_map/ppermute | solution.py:303
  127.6 8.3 %collective-permute-done.7 = bf16[384,1536]{1,0:T(8,128)(2,1)S(1)} collective-permute-done((bf16[384,1536]{1,0:T(8,128)(2,1)S(1)}, bf16[384,1536]{1,0:T(8,128)(2,1)S(1)}, u32[]{:S(2)}, u32[]{:S(2)}) %collective-permute-start.7) | collective-permute-done | bytes 1179680 | tf_op jit(solution)/shard_map/ppermute | solution.py:393
  138.6 6.2 broadcast_multiply_fusion
  148.5 9.5 %convolution_convert_fusion.1.qkv_ref = bf16[1536,1152]{1,0:T(8,128)(2,1)} fusion(bf16[1536,1536]{1,0:T(8,128)(2,1)} %get-tuple-element.75, bf16[1536,1280]{1,0:T(8,128)(2,1)S(1)} %bitcast.353), kind=kOutput, calls=%fused_computation.5 | convolution fusion | flops 5437587456 | bytes 11796480 | tf_op jit(solution)/shard_map/dot_general | solution.py:244
  168.7 19.1 %attend.1 = f32[1536,384]{1,0:T(8,128)} custom-call(s32[4,8]{1,0:T(4,128)} %pad_add_fusion.1.facts_ref, bf16[1536,1152]{1,0:T(8,128)(2,1)} %convolution_convert_fusion.1.qkv_ref, f32[4,384,6]{2,1,0:T(8,128)} %bitcast.408, f32[4,6,384]{2,1,0:T(8,128)} %copy-done.76), custom_call_target="tpu_custom_call" | custom-call | flops 14495514624 | bytes 9437184 | tf_op jit(solution)/shard_map/attend/pallas_call | solution.py:129
  187.8 6.7 fusion.8
  214.3 7.3 %convert_element_type.218 = f32[1536,1536]{1,0:T(8,128)} convert(bf16[1536,1536]{1,0:T(8,128)(2,1)} %constant_dynamic-update-slice_fusion) | non-fusion elementwise | flops 2359296 | bytes 14155776 | tf_op jit(solution)/shard_map/convert_element_type | solution.py:494
  221.7 18.2 %collective-permute-done.14 = bf16[384,1536]{1,0:T(8,128)(2,1)} collective-permute-done((bf16[384,1536]{1,0:T(8,128)(2,1)S(1)}, bf16[384,1536]{1,0:T(8,128)(2,1)}, u32[]{:S(2)}, u32[]{:S(2)}) %collective-permute-start.14) | collective-permute-done | bytes 1179680 | tf_op jit(solution)/shard_map/ppermute | solution.py:393
  242.2 7.3 %collective-permute-done.15 = bf16[4,192,1024]{2,1,0:T(8,128)(2,1)} collective-permute-done((bf16[4,192,1024]{2,1,0:T(8,128)(2,1)S(1)}, bf16[4,192,1024]{2,1,0:T(8,128)(2,1)}, u32[]{:S(2)}, u32[]{:S(2)}) %collective-permute-start.15) | collective-permute-done | bytes 1572896 | tf_op jit(solution)/shard_map/ppermute | solution.py:303
  259.6 20.8 %collective-permute-done.16 = bf16[384,1536]{1,0:T(8,128)(2,1)} collective-permute-done((bf16[384,1536]{1,0:T(8,128)(2,1)}, bf16[384,1536]{1,0:T(8,128)(2,1)}, u32[]{:S(2)}, u32[]{:S(2)}) %collective-permute-start.16) | collective-permute-done | bytes 1179680 | tf_op jit(solution)/shard_map/ppermute | solution.py:393
  287.6 6.0 collective-permute-done.18
  297.1 6.9 fusion.69
  304.0 6.9 fusion.68
  310.8 13.2 %multiply_convert_fusion.1 = (bf16[1536,1024]{1,0:T(8,128)(2,1)S(1)}, bf16[1536,1024]{1,0:T(8,128)(2,1)S(1)}, bf16[1536,1024]{1,0:T(8,128)(2,1)}) fusion(f32[1536,1024]{1,0:T(8,128)} %fusion.68, f32[1536,1024]{1,0:T(8,128)} %fusion.69, bf16[1536,1536]{1,0:T(8,128)(2,1)} %constant_dynamic-update-slice_fusion.2, bf16[1024,1536]{1,0:T(8,128)(2,1)S(1)} %bitcast.381), kind=kOutput, calls=%fused_computation.6 | convolution fusion | flops 4855431168 | bytes 29884416 | tf_op jit(solution)/shard_map/dot_general | solution.py:254
  324.1 7.7 %fusion.70 = f32[1536,1536]{1,0:T(8,128)} fusion(bf16[1536,1024]{1,0:T(8,128)(2,1)S(1)} %get-tuple-element.149, bf16[1536,1024]{1,0:T(8,128)(2,1)S(1)} %bitcast.388), kind=kOutput, calls=%fused_computation.295 | convolution fusion | flops 4831838208 | bytes 15728640 | tf_op jit(solution)/shard_map/dot_general | solution.py:254
  331.7 7.9 %convolution_add_fusion.1 = f32[1536,1536]{1,0:T(8,128)S(1)} fusion(f32[1536,1536]{1,0:T(8,128)} %fusion.70, bf16[1536,1024]{1,0:T(8,128)(2,1)S(1)} %get-tuple-element.148, bf16[1536,1024]{1,0:T(8,128)(2,1)S(1)} %bitcast.390), kind=kOutput, calls=%fused_computation.3 | convolution fusion | flops 4834197504 | bytes 25165824 | tf_op jit(solution)/shard_map/dot_general | solution.py:254
  344.9 8.7 %convolution_convert_fusion.2 = bf16[1024,1536]{1,0:T(8,128)(2,1)S(1)} fusion(bf16[1536,1024]{1,0:T(8,128)(2,1)} %get-tuple-element.68, bf16[1536,1536]{1,0:T(8,128)(2,1)} %constant_dynamic-update-slice_fusion.2), kind=kOutput, calls=%fused_computation.26 | convolution fusion | flops 4833411072 | bytes 11010048 | tf_op jit(solution)/shard_map/dot_general | solution.py:248
  360.8 6.6 convolution_convert_fusion.3
  376.9 18.9 %collective-permute-done.20 = bf16[384,1536]{1,0:T(8,128)(2,1)S(1)} collective-permute-done((bf16[384,1536]{1,0:T(8,128)(2,1)S(1)}, bf16[384,1536]{1,0:T(8,128)(2,1)S(1)}, u32[]{:S(2)}, u32[]{:S(2)}) %collective-permute-start.20) | collective-permute-done | bytes 1179680 | tf_op jit(solution)/shard_map/ppermute | solution.py:393
  404.8 22.6 %collective-permute-done.24 = bf16[4,192,1024]{2,1,0:T(8,128)(2,1)} collective-permute-done((bf16[4,192,1024]{2,1,0:T(8,128)(2,1)}, bf16[4,192,1024]{2,1,0:T(8,128)(2,1)}, u32[]{:S(2)}, u32[]{:S(2)}) %collective-permute-start.24) | collective-permute-done | bytes 1572896 | tf_op jit(solution)/shard_map/ppermute | solution.py:320
  438.7 7.0 fusion.71
  456.3 5.8 convolution_convert_fusion.5
  488.0 5.6 collective-permute-done.28
  498.0 24.3 %attend_back.1 = (bf16[1536,1152]{1,0:T(8,128)(2,1)}, f32[4,384,6]{2,1,0:T(8,128)}, f32[4,6,384]{2,1,0:T(8,128)}) custom-call(s32[4,8]{1,0:T(4,128)} %pad_add_fusion.1.facts_ref, bf16[1536,1152]{1,0:T(8,128)(2,1)} %convolution_convert_fusion.1.qkv_ref, bf16[1536,384]{1,0:T(8,128)(2,1)} %get-tuple-element.73.grad_ref, f32[4,384,6]{2,1,0:T(8,128)} %bitcast.409, ...), custom_call_target="tpu_custom_call" | custom-call | flops 18119393280 | bytes 8257536 | tf_op jit(solution)/shard_map/attend_back/pallas_call | solution.py:208
  532.4 9.3 %convolution_convert_fusion = bf16[1536,1280]{1,0:T(8,128)(2,1)S(1)} fusion(bf16[1536,1536]{1,0:T(8,128)(2,1)} %get-tuple-element.75, bf16[1536,128]{1,0:T(8,128)(2,1)S(1)} %dynamic_update_slice.9, bf16[1536,1152]{1,0:T(8,128)(2,1)} %get-tuple-element.77), kind=kOutput, calls=%fused_computation.4 | convolution fusion | flops 6049628160 | bytes 12582912 | tf_op jit(solution)/shard_map/dot_general | solution.py:248
  549.0 10.1 %fusion.72 = f32[1536,1536]{1,0:T(8,128)S(1)} fusion(bf16[1536,1280]{1,0:T(8,128)(2,1)} %pad_maximum_fusion.3, bf16[1536,1280]{1,0:T(8,128)(2,1)} %bitcast.352), kind=kOutput, calls=%fused_computation.297 | convolution fusion | flops 6039797760 | bytes 17301504 | tf_op jit(solution)/shard_map/dot_general | solution.py:254
  564.4 25.4 %collective-permute-done.32 = bf16[4,192,1280]{2,1,0:T(8,128)(2,1)} collective-permute-done((bf16[4,192,1280]{2,1,0:T(8,128)(2,1)}, bf16[4,192,1280]{2,1,0:T(8,128)(2,1)}, u32[]{:S(2)}, u32[]{:S(2)}) %collective-permute-start.32) | collective-permute-done | bytes 1966112 | tf_op jit(solution)/shard_map/ppermute | solution.py:320
  637.2 31.6 %collective-permute-done.34 = bf16[384,1536]{1,0:T(8,128)(2,1)} collective-permute-done((bf16[384,1536]{1,0:T(8,128)(2,1)}, bf16[384,1536]{1,0:T(8,128)(2,1)}, u32[]{:S(2)}, u32[]{:S(2)}) %collective-permute-start.34) | collective-permute-done | bytes 1179680 | tf_op jit(solution)/shard_map/ppermute | solution.py:393
  677.4 6.8 multiply_add_fusion
  (507 shorter events, 303.0 us)
Async XLA Ops:
  7.2 65.0 %all-gather.6.cloned.1.call-start = ((), (), s32[]{:S(2)}) async-start(), calls=%async_computation.5 | async-start | bytes 2457600 | tf_op jit(solution)/shard_map/all_gather | solution.py:296
  26.8 77.1 %all-gather.8.cloned.1.call-start = ((), (), s32[]{:S(2)}) async-start(), calls=%async_computation.6 | async-start | bytes 1474560 | tf_op jit(solution)/shard_map/all_gather | solution.py:296
  41.7 26.6 %collective-permute-start.2 = (bf16[384,1536]{1,0:T(8,128)(2,1)S(1)}, bf16[384,1536]{1,0:T(8,128)(2,1)S(1)}, u32[]{:S(2)}, u32[]{:S(2)}) collective-permute-start(bf16[384,1536]{1,0:T(8,128)(2,1)S(1)} %copy-done.52), channel_id=1, source_target_pairs={{0,1},{1,0},{2,3},{3,2},{4,5},{5,4},{6,7},{7,6},{8,9},{9,8},{10,11... | collective-permute-start | bytes 3538952 | tf_op jit(solution)/shard_map/ppermute | solution.py:393
  42.1 30.3 %collective-permute-start.4 = (s32[1,8]{1,0:T(1,128)S(1)}, s32[1,8]{1,0:T(1,128)S(1)}, u32[]{:S(2)}, u32[]{:S(2)}) collective-permute-start(s32[1,8]{1,0:T(1,128)S(1)} %add_bitcast_fusion), channel_id=1, source_target_pairs={{0,1},{1,0},{2,3},{3,2},{4,5},{5,4},{6,7},{7,6},{8,9},{9,8},{10,11... | collective-permute-start | bytes 104 | tf_op jit(solution)/shard_map/ppermute | solution.py:393
  72.2 33.6 %collective-permute-start.3 = (bf16[768,1536]{1,0:T(8,128)(2,1)S(1)}, bf16[768,1536]{1,0:T(8,128)(2,1)}, u32[]{:S(2)}, u32[]{:S(2)}) collective-permute-start(bf16[768,1536]{1,0:T(8,128)(2,1)S(1)} %pad_maximum_fusion.7), channel_id=1, source_target_pairs={{0,16},{16,0},{1,17},{17,1},{2,18},{18,2},{3,19},{19,3},{4,20},{20... | collective-permute-start | bytes 7077896 | tf_op jit(solution)/shard_map/ppermute | solution.py:390
  74.7 71.1 %all-gather.10.cloned.1.call-start = ((), (), s32[]{:S(2)}) async-start(), calls=%async_computation.7 | async-start | bytes 1966080 | tf_op jit(solution)/shard_map/all_gather | solution.py:296
  74.8 46.0 %collective-permute-start.6 = (bf16[4,192,1280]{2,1,0:T(8,128)(2,1)}, bf16[4,192,1280]{2,1,0:T(8,128)(2,1)}, u32[]{:S(2)}, u32[]{:S(2)}) collective-permute-start(bf16[4,192,1280]{2,1,0:T(8,128)(2,1)} %bitcast.392), channel_id=1, source_target_pairs={{0,2},{1,3},{2,0},{3,1},{4,6},{5,7},{6,4},{7,5},{8,10},{9,11},{10,... | collective-permute-start | bytes 5898248 | tf_op jit(solution)/shard_map/ppermute | solution.py:303
  104.0 93.2 %all-gather.12.cloned.1.call-start = ((), (), s32[]{:S(2)}) async-start(), calls=%async_computation.8 | async-start | bytes 1966080 | tf_op jit(solution)/shard_map/all_gather | solution.py:296
  104.3 53.7 %collective-permute-start.10 = (bf16[4,192,768]{2,1,0:T(8,128)(2,1)}, bf16[4,192,768]{2,1,0:T(8,128)(2,1)}, u32[]{:S(2)}, u32[]{:S(2)}) collective-permute-start(bf16[4,192,768]{2,1,0:T(8,128)(2,1)} %bitcast.400), channel_id=1, source_target_pairs={{0,2},{1,3},{2,0},{3,1},{4,6},{5,7},{6,4},{7,5},{8,10},{9,11},{10,... | collective-permute-start | bytes 3538952 | tf_op jit(solution)/shard_map/ppermute | solution.py:303
  109.1 26.8 %collective-permute-start.7 = (bf16[384,1536]{1,0:T(8,128)(2,1)S(1)}, bf16[384,1536]{1,0:T(8,128)(2,1)S(1)}, u32[]{:S(2)}, u32[]{:S(2)}) collective-permute-start(bf16[384,1536]{1,0:T(8,128)(2,1)S(1)} %copy-done.3), channel_id=1, source_target_pairs={{0,1},{1,0},{2,3},{3,2},{4,5},{5,4},{6,7},{7,6},{8,9},{9,8},{10,11... | collective-permute-start | bytes 3538952 | tf_op jit(solution)/shard_map/ppermute | solution.py:393
  145.9 112.3 %all-gather.14.cloned.1.call-start = ((), (), s32[]{:S(2)}) async-start(), calls=%async_computation.9 | async-start | bytes 1966080 | tf_op jit(solution)/shard_map/all_gather | solution.py:296
  145.9 51.2 %collective-permute-start.9 = (bf16[4,192,1024]{2,1,0:T(8,128)(2,1)}, bf16[4,192,1024]{2,1,0:T(8,128)(2,1)}, u32[]{:S(2)}, u32[]{:S(2)}) collective-permute-start(bf16[4,192,1024]{2,1,0:T(8,128)(2,1)} %bitcast.394), channel_id=1, source_target_pairs={{0,2},{1,3},{2,0},{3,1},{4,6},{5,7},{6,4},{7,5},{8,10},{9,11},{10,... | collective-permute-start | bytes 4718600 | tf_op jit(solution)/shard_map/ppermute | solution.py:303
  162.1 32.4 %collective-permute-start.11 = (bf16[2,384,384]{2,1,0:T(8,128)(2,1)}, bf16[2,384,384]{2,1,0:T(8,128)(2,1)}, u32[]{:S(2)}, u32[]{:S(2)}) collective-permute-start(bf16[2,384,384]{2,1,0:T(8,128)(2,1)} %dynamic-slice_bitcast_fusion.4), channel_id=1, source_target_pairs={{0,1},{1,0},{2,3},{3,2},{4,5},{5,4},{6,7},{7,6},{8,9},{9,8},{10,11... | collective-permute-start | bytes 1769480 | tf_op jit(solution)/shard_map/ppermute | solution.py:393
  211.7 28.2 %collective-permute-start.14 = (bf16[384,1536]{1,0:T(8,128)(2,1)S(1)}, bf16[384,1536]{1,0:T(8,128)(2,1)}, u32[]{:S(2)}, u32[]{:S(2)}) collective-permute-start(bf16[384,1536]{1,0:T(8,128)(2,1)S(1)} %slice.262), channel_id=1, source_target_pairs={{0,1},{1,0},{2,3},{3,2},{4,5},{5,4},{6,7},{7,6},{8,9},{9,8},{10,11... | collective-permute-start | bytes 3538952 | tf_op jit(solution)/shard_map/ppermute | solution.py:393
  213.0 36.5 %collective-permute-start.15 = (bf16[4,192,1024]{2,1,0:T(8,128)(2,1)S(1)}, bf16[4,192,1024]{2,1,0:T(8,128)(2,1)}, u32[]{:S(2)}, u32[]{:S(2)}) collective-permute-start(bf16[4,192,1024]{2,1,0:T(8,128)(2,1)S(1)} %bitcast.396), channel_id=1, source_target_pairs={{0,2},{1,3},{2,0},{3,1},{4,6},{5,7},{6,4},{7,5},{8,10},{9,11},{10,... | collective-permute-start | bytes 4718600 | tf_op jit(solution)/shard_map/ppermute | solution.py:303
  221.7 234.6 %reduce-scatter.6.cloned.1.call-start = ((), (), s32[]{:S(2)}) async-start(), calls=%async_computation.10 | async-start | bytes 1966080 | tf_op jit(solution)/shard_map/reduce_scatter | solution.py:330
  253.0 27.5 %collective-permute-start.16 = (bf16[384,1536]{1,0:T(8,128)(2,1)}, bf16[384,1536]{1,0:T(8,128)(2,1)}, u32[]{:S(2)}, u32[]{:S(2)}) collective-permute-start(bf16[384,1536]{1,0:T(8,128)(2,1)} %multiply_convert_fusion.6), channel_id=1, source_target_pairs={{0,1},{1,0},{2,3},{3,2},{4,5},{5,4},{6,7},{7,6},{8,9},{9,8},{10,11... | collective-permute-start | bytes 3538952 | tf_op jit(solution)/shard_map/ppermute | solution.py:393
  258.2 35.5 %collective-permute-start.18 = (bf16[4,128,1536]{2,1,0:T(8,128)(2,1)}, bf16[4,128,1536]{2,1,0:T(8,128)(2,1)S(1)}, u32[]{:S(2)}, u32[]{:S(2)}) collective-permute-start(bf16[4,128,1536]{2,1,0:T(8,128)(2,1)} %bitcast.398), channel_id=1, source_target_pairs={{0,2},{1,3},{2,0},{3,1},{4,6},{5,7},{6,4},{7,5},{8,10},{9,11},{10,... | collective-permute-start | bytes 4718600 | tf_op jit(solution)/shard_map/ppermute | solution.py:303
  356.6 44.7 %collective-permute-start.21 = (bf16[4,128,1536]{2,1,0:T(8,128)(2,1)}, bf16[4,128,1536]{2,1,0:T(8,128)(2,1)}, u32[]{:S(2)}, u32[]{:S(2)}) collective-permute-start(bf16[4,128,1536]{2,1,0:T(8,128)(2,1)} %dynamic-slice_bitcast_fusion.3), channel_id=1, source_target_pairs={{0,2},{1,3},{2,0},{3,1},{4,6},{5,7},{6,4},{7,5},{8,10},{9,11},{10,... | collective-permute-start | bytes 4718600 | tf_op jit(solution)/shard_map/ppermute | solution.py:320
  367.4 28.4 %collective-permute-start.20 = (bf16[384,1536]{1,0:T(8,128)(2,1)S(1)}, bf16[384,1536]{1,0:T(8,128)(2,1)S(1)}, u32[]{:S(2)}, u32[]{:S(2)}) collective-permute-start(bf16[384,1536]{1,0:T(8,128)(2,1)S(1)} %slice.261), channel_id=1, source_target_pairs={{0,1},{1,0},{2,3},{3,2},{4,5},{5,4},{6,7},{7,6},{8,9},{9,8},{10,11... | collective-permute-start | bytes 3538952 | tf_op jit(solution)/shard_map/ppermute | solution.py:393
  375.7 51.8 %collective-permute-start.24 = (bf16[4,192,1024]{2,1,0:T(8,128)(2,1)}, bf16[4,192,1024]{2,1,0:T(8,128)(2,1)}, u32[]{:S(2)}, u32[]{:S(2)}) collective-permute-start(bf16[4,192,1024]{2,1,0:T(8,128)(2,1)} %dynamic-slice_bitcast_fusion.2), channel_id=1, source_target_pairs={{0,2},{1,3},{2,0},{3,1},{4,6},{5,7},{6,4},{7,5},{8,10},{9,11},{10,... | collective-permute-start | bytes 4718600 | tf_op jit(solution)/shard_map/ppermute | solution.py:320
  399.9 31.3 %collective-permute-start.23 = (bf16[384,1536]{1,0:T(8,128)(2,1)}, bf16[384,1536]{1,0:T(8,128)(2,1)}, u32[]{:S(2)}, u32[]{:S(2)}) collective-permute-start(bf16[384,1536]{1,0:T(8,128)(2,1)} %fusion.62), channel_id=1, source_target_pairs={{0,1},{1,0},{2,3},{3,2},{4,5},{5,4},{6,7},{7,6},{8,9},{9,8},{10,11... | collective-permute-start | bytes 3538952 | tf_op jit(solution)/shard_map/ppermute | solution.py:393
  404.8 127.6 %reduce-scatter.8.cloned.1.call-start = ((), (), s32[]{:S(2)}) async-start(), calls=%async_computation.11 | async-start | bytes 1966080 | tf_op jit(solution)/shard_map/reduce_scatter | solution.py:330
  437.2 38.7 %collective-permute-start.26 = (bf16[4,192,1024]{2,1,0:T(8,128)(2,1)}, bf16[4,192,1024]{2,1,0:T(8,128)(2,1)}, u32[]{:S(2)}, u32[]{:S(2)}) collective-permute-start(bf16[4,192,1024]{2,1,0:T(8,128)(2,1)} %dynamic-slice_bitcast_fusion.1), channel_id=1, source_target_pairs={{0,2},{1,3},{2,0},{3,1},{4,6},{5,7},{6,4},{7,5},{8,10},{9,11},{10,... | collective-permute-start | bytes 4718600 | tf_op jit(solution)/shard_map/ppermute | solution.py:320
  450.9 155.8 %collective-permute-start.22 = (bf16[768,1536]{1,0:T(8,128)(2,1)}, bf16[768,1536]{1,0:T(8,128)(2,1)}, u32[]{:S(2)}, u32[]{:S(2)}) collective-permute-start(bf16[768,1536]{1,0:T(8,128)(2,1)} %slice.256), channel_id=1, source_target_pairs={{0,16},{16,0},{1,17},{17,1},{2,18},{18,2},{3,19},{19,3},{4,20},{20... | collective-permute-start | bytes 7077896 | tf_op jit(solution)/shard_map/ppermute | solution.py:390
  451.2 222.1 %reduce-scatter.14.cloned.1.call-start = ((), (), s32[]{:S(2)}) async-start(), calls=%async_computation.14 | async-start | bytes 1966080 | tf_op jit(solution)/shard_map/reduce_scatter | solution.py:330
  497.2 32.2 %collective-permute-start.29 = (bf16[4,192,768]{2,1,0:T(8,128)(2,1)}, bf16[4,192,768]{2,1,0:T(8,128)(2,1)}, u32[]{:S(2)}, u32[]{:S(2)}) collective-permute-start(bf16[4,192,768]{2,1,0:T(8,128)(2,1)} %fusion.11), channel_id=1, source_target_pairs={{0,2},{1,3},{2,0},{3,1},{4,6},{5,7},{6,4},{7,5},{8,10},{9,11},{10,... | collective-permute-start | bytes 3538952 | tf_op jit(solution)/shard_map/ppermute | solution.py:320
  523.9 151.1 %reduce-scatter.12.cloned.1.call-start = ((), (), s32[]{:S(2)}) async-start(), calls=%async_computation.13 | async-start | bytes 1474560 | tf_op jit(solution)/shard_map/reduce_scatter | solution.py:330
  545.1 44.6 %collective-permute-start.32 = (bf16[4,192,1280]{2,1,0:T(8,128)(2,1)}, bf16[4,192,1280]{2,1,0:T(8,128)(2,1)}, u32[]{:S(2)}, u32[]{:S(2)}) collective-permute-start(bf16[4,192,1280]{2,1,0:T(8,128)(2,1)} %dynamic-slice_bitcast_fusion), channel_id=1, source_target_pairs={{0,2},{1,3},{2,0},{3,1},{4,6},{5,7},{6,4},{7,5},{8,10},{9,11},{10,... | collective-permute-start | bytes 5898248 | tf_op jit(solution)/shard_map/ppermute | solution.py:320
  548.7 137.0 %reduce-scatter.10.cloned.1.call-start = ((), (), s32[]{:S(2)}) async-start(), calls=%async_computation.12 | async-start | bytes 2457600 | tf_op jit(solution)/shard_map/reduce_scatter | solution.py:330
  613.8 63.5 %collective-permute-start.30 = (bf16[384,1536]{1,0:T(8,128)(2,1)}, bf16[384,1536]{1,0:T(8,128)(2,1)}, u32[]{:S(2)}, u32[]{:S(2)}) collective-permute-start(bf16[384,1536]{1,0:T(8,128)(2,1)} %slice.260), channel_id=1, source_target_pairs={{0,1},{1,0},{2,3},{3,2},{4,5},{5,4},{6,7},{7,6},{8,9},{9,8},{10,11... | collective-permute-start | bytes 3538952 | tf_op jit(solution)/shard_map/ppermute | solution.py:393
  625.7 43.1 %collective-permute-start.34 = (bf16[384,1536]{1,0:T(8,128)(2,1)}, bf16[384,1536]{1,0:T(8,128)(2,1)}, u32[]{:S(2)}, u32[]{:S(2)}) collective-permute-start(bf16[384,1536]{1,0:T(8,128)(2,1)} %slice.259), channel_id=1, source_target_pairs={{0,1},{1,0},{2,3},{3,2},{4,5},{5,4},{6,7},{7,6},{8,9},{9,8},{10,11... | collective-permute-start | bytes 3538952 | tf_op jit(solution)/shard_map/ppermute | solution.py:393
  (127 other events, 1062.1 us)
Sparse Core Ops, SparseCore 0:
  26.9 45.1 all-gather.5
  74.8 29.0 all-gather.7
  106.1 36.2 all-gather.9
  146.0 36.3 all-gather.11
  221.8 36.2 all-gather.13
  404.9 33.7 reduce-scatter.5
  451.3 34.3 reduce-scatter.7
  524.0 35.2 reduce-scatter.13
  561.6 28.1 reduce-scatter.11
  620.9 39.9 reduce-scatter.9

commit v5 on v4

--- a/solution.py
+++ b/solution.py
@@ -469,6 +469,24 @@
     )
     gain_one = first[:, 3 * quarter + head_count].astype(jnp.float32)
     gain_two = first[:, 3 * quarter + head_count + 1].astype(jnp.float32)
+    def replicas(values):
+        total = values
+        step = 2
+        while step < reps:
+            other = lax.ppermute(total, "rep", [(r, r ^ step) for r in range(reps)])
+            total = add_low(total, other)
+            step *= 2
+        return total
+
+    def own_of(values):
+        pair = replicas(values).reshape(2, shard_rows, values.shape[1])
+        sides = both(side == 0, pick(pair, side, 0), swap_side(pick(pair, 1 - side, 0)))
+        return both(core == 0, sides, swap_core(sides))
+
+    def both_cores(values):
+        mine = replicas(values)
+        return both(core == 0, mine, swap_core(mine))
+
     def turn_rows(values):
         cut = values.reshape(2, 2, quarter, quarter)
         mine = pick(cut, side, 0)
@@ -496,9 +514,7 @@
     scaled1 = scaled_all[:own_rows]
     inverse1 = inverse_all[:own_rows]
     inputs = inputs_all[:own_rows]
-    normed1 = after(
-        (scaled_all * gain_one).astype(jnp.bfloat16), second_line, cotangent_all
-    )
+    normed1 = after((scaled_all * gain_one).astype(jnp.bfloat16), second_line)
     row_count = normed1.shape[0]
 
     qkv_low = matmul(normed1, first[:, : 3 * quarter]).astype(jnp.bfloat16)
@@ -517,7 +533,7 @@
 
     decay_cols = jnp.transpose(decay_sum, (0, 2, 1))
     attended = attend(
-        after(qkv_low, gate_line),
+        after(qkv_low, gate_line, cotangent_all),
         decay_cols,
         decay_sum,
         facts_all,
@@ -546,18 +562,19 @@
     pair_normed2 = core_sum(matmul_nt(grad_gate, gate_w) + matmul_nt(grad_up, up_w))
     normed2_late = after(normed2, pair_normed2)
     part_gate_w = matmul_tn(normed2_late, grad_gate).astype(jnp.bfloat16)
-    part_up_w = matmul_tn(normed2_late, grad_up).astype(jnp.bfloat16)
-    grad_normed2 = after(side_sum(pair_normed2), part_gate_w, part_up_w)
+    grad_normed2 = after(side_sum(pair_normed2), part_gate_w)
     down_held = down_sum(grad_normed2)
     grad_down = scatter_line(down_held, count)
-    gate_sum = scatter_rest(after(part_gate_w, part_up_w), count, index)
-    up_sum = scatter_rest(part_up_w, count, index)
+    gate_sum = scatter_rest(part_gate_w, count, index)
     grad_resid = cotangent.astype(jnp.float32) + norm_back(
         grad_normed2 * gain_two, scaled2, inverse2
     )
     grad_attn_own = grad_resid.astype(jnp.bfloat16)
-    pair_out = core_sum(matmul(after(act_low, grad_attn_own, down_held), down_w))
-    gate_held = gate_sum()
+    normed2_last, act_late = lax.optimization_barrier((normed2_late, act_low, grad_attn_own))[:2]
+    part_up_w = matmul_tn(normed2_last, grad_up).astype(jnp.bfloat16)
+    up_sum = scatter_rest(part_up_w, count, index)
+    part_out = matmul(after(act_late, down_held), down_w)
+    gate_held = gate_sum(part_out, part_up_w)
     grad_gate_w = scatter_line(gate_held, count)
     grad_attn = after(team_rows(grad_attn_own, gate_held), grad_down)
     grad_gated = matmul_nt(grad_attn, output_w)
@@ -583,7 +600,7 @@
     second_held = second_sum(grad_qkv)
     grad_qkv = after(grad_qkv, grad_gate_w, second_held)
     sum_second = scatter_line(second_held, count)
-    layer_out = (residual + side_sum(after(pair_out, grad_qkv))).astype(jnp.bfloat16)
+    layer_out = (residual + team_sum(after(part_out, grad_qkv))).astype(jnp.bfloat16)
     grad_decay = jnp.transpose(grad_logit_rows, (0, 2, 1)) - grad_logit_cols
     grad_log_forget = jnp.einsum(
         "bij,bhi->bjh", chain_float, grad_decay, precision=lax.Precision.HIGHEST
@@ -608,48 +625,34 @@
     part_normed1 = matmul_nt(after(grad_first, part_first_w), first) + matmul_nt(
         grad_outgate, outgate_w
     )
-    first_held = first_sum()
+    down_own = both_cores(after(grad_down, part_first_w))
+    first_held = first_sum(grad_bias, layer_out, down_own)
     grad_normed1 = team_sum(after(part_normed1, first_held))
     tokens_grad = grad_resid + norm_back(grad_normed1 * gain_one, scaled1, inverse1)
     sum_first = scatter_line(first_held, count)
-    grad_down = after(grad_down, part_first_w)
-    grad_gate_w = after(grad_gate_w, part_first_w)
+    gate_own = own_of(after(grad_gate_w, grad_normed1))
     grad_up_w = after(grad_up_w, grad_normed1)
     sum_second = after(sum_second, grad_normed1)
 
-    def replicas(values):
-        total = values
-        step = 2
-        while step < reps:
-            other = lax.ppermute(total, "rep", [(r, r ^ step) for r in range(reps)])
-            total = add_low(total, other)
-            step *= 2
-        return total
-
-    def own_of(values):
-        pair = replicas(values).reshape(2, shard_rows, values.shape[1])
-        sides = both(side == 0, pick(pair, side, 0), swap_side(pick(pair, 1 - side, 0)))
-        cores = both(core == 0, sides, swap_core(sides))
-        return jnp.transpose(cores.astype(jnp.float32), (1, 0, 2, 3))
-
     def whole_cols(own):
         parts = own.shape[3] // quarter
-        quad = own.reshape(2, 2, shard_rows, parts, quarter)
+        quad = jnp.transpose(own.astype(jnp.float32), (1, 0, 2, 3))
+        quad = quad.reshape(2, 2, shard_rows, parts, quarter)
         quad = jnp.transpose(quad, (3, 2, 0, 1, 4)).reshape(parts, shard_rows, model_width)
         return [quad[p] for p in range(parts)]
 
-    def whole_units(values):
-        quad = own_of(values).reshape(2, 2, shard_rows, count // 2, unit)
+    def whole_units(own):
+        quad = jnp.transpose(own.astype(jnp.float32), (1, 0, 2, 3))
+        quad = quad.reshape(2, 2, shard_rows, count // 2, unit)
         return jnp.transpose(quad, (2, 3, 0, 1, 4)).reshape(shard_rows, team * quarter_ff)
 
-    down_mine = replicas(grad_down)
-    down_own = both(core == 0, down_mine, swap_core(down_mine)).astype(jnp.float32)
     first_own = own_of(sum_first)
     query_g, key_g, value_g = whole_cols(first_own[..., : 3 * quarter])
-    forget_g = jnp.sum(first_own[..., 3 * quarter : 3 * quarter + head_count], axis=(0, 1))
+    forget_own = first_own[..., 3 * quarter : 3 * quarter + head_count]
+    forget_g = jnp.sum(forget_own.astype(jnp.float32), axis=(0, 1))
     outgate_g, output_g = whole_cols(own_of(sum_second))
-    gate_g = whole_units(grad_gate_w)
-    up_g = whole_units(grad_up_w)
+    gate_g = whole_units(gate_own)
+    up_g = whole_units(own_of(grad_up_w))
 
     def gain_grad(gain, *pairs):
         total = sum(jnp.sum(w.astype(jnp.float32) * grad, axis=1) for w, grad in pairs)
@@ -678,7 +681,7 @@
         gain_two_g,
         gate_g,
         up_g,
-        down_own.reshape(shard_ff, model_width),
+        down_own.astype(jnp.float32).reshape(shard_ff, model_width),
     )
 
 

time: 731 us -> 743 us (1.016)
  waiting for transfers between devices: 259 us -> 286 us
  other arithmetic: 117 us -> 107 us
    ppermute x5, waiting for transfers between devices: 48 us -> 29.3 us  [scatter_rest(): lax.ppermute(pick(halves, 1 - at, 1), 'shard', swap_pairs(count, step))]
    all_gather x5, waiting for transfers between devices: 29.1 us -> 45.2 us  [gather_line(): lax.all_gather(block, 'shard', axis=0, tiled=True, axis_index_groups=line...]
    ppermute x5, waiting for transfers between devices: 23.7 us -> 37.9 us  [gather_rest(): other = lax.ppermute(held, 'shard', swap_pairs(count, step))]
    dot_general x7, matrix products: 42 us -> 50 us  [matmul(): return jnp.dot(left_side, right_side, preferred_element_type=jnp.float32)]
    unnamed x211 -> x217, local copies, waits for them, and re-layouts: 29.6 us -> 26 us
  transfers between devices with their start and end apart: 58 -> 58, of which waited for: 23 -> 28; matrix products, arithmetic and copies ran while one was open for 37% -> 37% of each run, Pallas kernels for 6% -> 6%
where the time goes in v5:
time: 743 us; the launch traced here: 734 us
  waiting for transfers between devices  286 us (38%)
  matrix products  137 us (18%)
  local copies, waits for them, and re-layouts  107 us (14%)
  other arithmetic  107 us (14%)
  Pallas kernels  43.1 us (6%)
  starting transfers between devices  38.1 us (5%)
  between operations  16.5 us (2%)
    ppermute x17, waiting for transfers between devices, swap_side(): return lax.ppermute(values, 'shard', side_pairs)  144 us
    dot_general x7, matrix products, matmul(): return jnp.dot(left_side, right_side, preferred_element_type=jnp.float32)  50 us
    all_gather x5, waiting for transfers between devices, gather_line(): lax.all_gather(block, 'shard', axis=0, tiled=True, axis_index_groups=line...  45.2 us
    dot_general x6, matrix products, matmul_nt(): lax.dot_general(left_side, right_side, (((1,), (1,)), ((), ())), preferre...  43.2 us
    dot_general x6, matrix products, matmul_tn(): lax.dot_general(left_side, right_side, (((0,), (0,)), ((), ())), preferre...  40.3 us
    ppermute x5, waiting for transfers between devices, gather_rest(): other = lax.ppermute(held, 'shard', swap_pairs(count, step))  37.9 us
    ppermute x5, waiting for transfers between devices, scatter_rest(): lax.ppermute(pick(halves, 1 - at, 1), 'shard', swap_pairs(count, step))  29.3 us
    unnamed x217, local copies, waits for them, and re-layouts  26 us
  transfers between devices with their start and end apart: 58, of which 28 were waited for; matrix products, arithmetic and copies ran while one was open for 37% of the time, Pallas kernels for 6%

profile of v5, /device:TPU:0, one launch (start us, length us, event | category | flops | bytes accessed | tf_op | source)
XLA Modules:
  0.0 734.3 jit_solution(10721273775974772893)
XLA Ops:
  30.9 11.2 %collective-permute-done.1 = bf16[96,2816]{1,0:T(8,128)(2,1)S(1)} collective-permute-done((bf16[96,2816]{1,0:T(8,128)(2,1)S(1)}, bf16[96,2816]{1,0:T(8,128)(2,1)S(1)}, u32[]{:S(2)}, u32[]{:S(2)}) %collective-permute-start.1) | collective-permute-done | bytes 540704 | tf_op jit(solution)/shard_map/ppermute | solution.py:393
  44.2 23.4 %all-gather.6.cloned.1.call-done = bf16[768,1280]{1,0:T(8,128)(2,1)} async-done(((bf16[192,1280]{1,0:T(8,128)(2,1)}), bf16[768,1280]{1,0:T(8,128)(2,1)}) %all-gather.6.cloned.1.call-update) | async-done | bytes 1966096 | tf_op jit(solution)/shard_map/all_gather | solution.py:296
  77.1 21.8 %all-gather.8.cloned.1.call-done = bf16[768,768]{1,0:T(8,128)(2,1)} async-done(((bf16[192,768]{1,0:T(8,128)(2,1)}), bf16[768,768]{1,0:T(8,128)(2,1)}) %all-gather.8.cloned.1.call-update) | async-done | bytes 1179664 | tf_op jit(solution)/shard_map/all_gather | solution.py:296
  100.7 13.0 %collective-permute-done.6 = bf16[4,192,1280]{2,1,0:T(8,128)(2,1)} collective-permute-done((bf16[4,192,1280]{2,1,0:T(8,128)(2,1)}, bf16[4,192,1280]{2,1,0:T(8,128)(2,1)}, u32[]{:S(2)}, u32[]{:S(2)}) %collective-permute-start.6) | collective-permute-done | bytes 1966112 | tf_op jit(solution)/shard_map/ppermute | solution.py:303
  123.4 6.4 broadcast_multiply_fusion
  129.9 9.6 %convolution_convert_fusion.1.qkv_ref = bf16[1536,1152]{1,0:T(8,128)(2,1)} fusion(bf16[1536,1536]{1,0:T(8,128)(2,1)} %get-tuple-element.80, bf16[1536,1280]{1,0:T(8,128)(2,1)S(1)} %bitcast.352), kind=kOutput, calls=%fused_computation.5 | convolution fusion | flops 5437587456 | bytes 11796480 | tf_op jit(solution)/shard_map/dot_general | solution.py:244
  164.8 6.6 fusion.8
  181.7 18.7 %attend.1 = f32[1536,384]{1,0:T(8,128)} custom-call(s32[4,8]{1,0:T(4,128)} %pad_add_fusion.1.facts_ref, bf16[1536,1152]{1,0:T(8,128)(2,1)} %convolution_convert_fusion.1.qkv_ref, f32[4,384,6]{2,1,0:T(8,128)} %bitcast.408, f32[4,6,384]{2,1,0:T(8,128)} %copy-done.78), custom_call_target="tpu_custom_call" | custom-call | flops 14495514624 | bytes 9437184 | tf_op jit(solution)/shard_map/attend/pallas_call | solution.py:129
  200.5 11.6 %collective-permute-done.9 = bf16[4,192,1024]{2,1,0:T(8,128)(2,1)} collective-permute-done((bf16[4,192,1024]{2,1,0:T(8,128)(2,1)S(1)}, bf16[4,192,1024]{2,1,0:T(8,128)(2,1)}, u32[]{:S(2)}, u32[]{:S(2)}) %collective-permute-start.9) | collective-permute-done | bytes 1572896 | tf_op jit(solution)/shard_map/ppermute | solution.py:303
  233.8 20.7 %collective-permute-done.14 = bf16[384,1536]{1,0:T(8,128)(2,1)} collective-permute-done((bf16[384,1536]{1,0:T(8,128)(2,1)S(1)}, bf16[384,1536]{1,0:T(8,128)(2,1)}, u32[]{:S(2)}, u32[]{:S(2)}) %collective-permute-start.14) | collective-permute-done | bytes 1179680 | tf_op jit(solution)/shard_map/ppermute | solution.py:393
  256.7 7.3 collective-permute-done.15
  271.4 21.5 %collective-permute-done.16 = bf16[384,1536]{1,0:T(8,128)(2,1)} collective-permute-done((bf16[384,1536]{1,0:T(8,128)(2,1)}, bf16[384,1536]{1,0:T(8,128)(2,1)}, u32[]{:S(2)}, u32[]{:S(2)}) %collective-permute-start.16) | collective-permute-done | bytes 1179680 | tf_op jit(solution)/shard_map/ppermute | solution.py:393
  296.7 6.0 collective-permute-done.18
  303.2 10.4 %fusion.71 = f32[1536,1024]{1,0:T(8,128)} fusion(bf16[1536,1536]{1,0:T(8,128)(2,1)} %constant_dynamic-update-slice_fusion.2, bf16[1024,1536]{1,0:T(8,128)(2,1)S(1)} %bitcast.381), kind=kOutput, calls=%fused_computation.299 | convolution fusion | flops 4831838208 | bytes 14155776 | tf_op jit(solution)/shard_map/dot_general | solution.py:254
  315.4 6.9 fusion.72
  322.3 11.5 %multiply_convert_fusion.1 = (bf16[1536,1024]{1,0:T(8,128)(2,1)}, bf16[1536,1024]{1,0:T(8,128)(2,1)S(1)}, bf16[1536,1024]{1,0:T(8,128)(2,1)S(1)}) fusion(f32[1536,1024]{1,0:T(8,128)} %fusion.72, f32[1536,1024]{1,0:T(8,128)} %fusion.71, bf16[1536,1536]{1,0:T(8,128)(2,1)S(1)} %pad_maximum_fusion, bf16[1536,1024]{1,0:T(8,128)(2,1)S(1)} %bitcast.389), kind=kOutput, calls=%fused_computation.6 | convolution fusion | flops 4855431168 | bytes 29884416 | tf_op jit(solution)/shard_map/dot_general | solution.py:244
  333.8 7.7 %fusion.73 = f32[1536,1536]{1,0:T(8,128)} fusion(bf16[1536,1024]{1,0:T(8,128)(2,1)S(1)} %get-tuple-element.155, bf16[1536,1024]{1,0:T(8,128)(2,1)S(1)} %bitcast.386), kind=kOutput, calls=%fused_computation.301 | convolution fusion | flops 4831838208 | bytes 15728640 | tf_op jit(solution)/shard_map/dot_general | solution.py:254
  341.5 7.9 %convolution_add_fusion.1 = f32[1536,1536]{1,0:T(8,128)S(1)} fusion(f32[1536,1536]{1,0:T(8,128)} %fusion.73, bf16[1536,1024]{1,0:T(8,128)(2,1)S(1)} %get-tuple-element.156, bf16[1536,1024]{1,0:T(8,128)(2,1)S(1)} %bitcast.390), kind=kOutput, calls=%fused_computation.3 | convolution fusion | flops 4834197504 | bytes 25165824 | tf_op jit(solution)/shard_map/dot_general | solution.py:254
  354.7 8.4 %convolution_convert_fusion.3 = bf16[1024,1536]{1,0:T(8,128)(2,1)S(1)} fusion(bf16[1536,1024]{1,0:T(8,128)(2,1)} %get-tuple-element.72, bf16[1536,1536]{1,0:T(8,128)(2,1)} %constant_dynamic-update-slice_fusion.2), kind=kOutput, calls=%fused_computation.27 | convolution fusion | flops 4833411072 | bytes 11010048 | tf_op jit(solution)/shard_map/dot_general | solution.py:248
  376.0 20.2 %collective-permute-done.20 = bf16[384,1536]{1,0:T(8,128)(2,1)S(1)} collective-permute-done((bf16[384,1536]{1,0:T(8,128)(2,1)S(1)}, bf16[384,1536]{1,0:T(8,128)(2,1)S(1)}, u32[]{:S(2)}, u32[]{:S(2)}) %collective-permute-start.20) | collective-permute-done | bytes 1179680 | tf_op jit(solution)/shard_map/ppermute | solution.py:393
  401.0 6.6 convolution_convert_fusion.2
  409.2 10.3 %fusion.74 = f32[1536,1536]{1,0:T(8,128)} fusion(bf16[1536,1024]{1,0:T(8,128)(2,1)} %get-tuple-element.72, bf16[1024,1536]{1,0:T(8,128)(2,1)} %bitcast.382), kind=kOutput, calls=%fused_computation.302 | convolution fusion | flops 4831838208 | bytes 15728640 | tf_op jit(solution)/shard_map/dot_general | solution.py:244
  419.4 14.5 %collective-permute-done.23 = bf16[4,192,1024]{2,1,0:T(8,128)(2,1)} collective-permute-done((bf16[4,192,1024]{2,1,0:T(8,128)(2,1)}, bf16[4,192,1024]{2,1,0:T(8,128)(2,1)}, u32[]{:S(2)}, u32[]{:S(2)}) %collective-permute-start.23) | collective-permute-done | bytes 1572896 | tf_op jit(solution)/shard_map/ppermute | solution.py:320
  450.0 6.0 convolution_convert_fusion.5
  469.7 10.4 %collective-permute-done.25 = bf16[4,192,1024]{2,1,0:T(8,128)(2,1)} collective-permute-done((bf16[4,192,1024]{2,1,0:T(8,128)(2,1)}, bf16[4,192,1024]{2,1,0:T(8,128)(2,1)}, u32[]{:S(2)}, u32[]{:S(2)}) %collective-permute-start.25) | collective-permute-done | bytes 1572896 | tf_op jit(solution)/shard_map/ppermute | solution.py:320
  491.1 6.1 collective-permute-done.27
  502.2 24.3 %attend_back.1 = (bf16[1536,1152]{1,0:T(8,128)(2,1)}, f32[4,384,6]{2,1,0:T(8,128)}, f32[4,6,384]{2,1,0:T(8,128)}) custom-call(s32[4,8]{1,0:T(4,128)} %pad_add_fusion.1.facts_ref, bf16[1536,1152]{1,0:T(8,128)(2,1)} %convolution_convert_fusion.1.qkv_ref, bf16[1536,384]{1,0:T(8,128)(2,1)} %get-tuple-element.78.grad_ref, f32[4,384,6]{2,1,0:T(8,128)} %bitcast.409, ...), custom_call_target="tpu_custom_call" | custom-call | flops 18119393280 | bytes 8257536 | tf_op jit(solution)/shard_map/attend_back/pallas_call | solution.py:208
  557.1 8.4 %convolution_convert_fusion = bf16[1536,1280]{1,0:T(8,128)(2,1)S(1)} fusion(bf16[1536,1536]{1,0:T(8,128)(2,1)} %get-tuple-element.80, bf16[1536,128]{1,0:T(8,128)(2,1)S(1)} %dynamic_update_slice.9, bf16[1536,1152]{1,0:T(8,128)(2,1)S(1)} %copy-done.32), kind=kOutput, calls=%fused_computation.4 | convolution fusion | flops 6049628160 | bytes 12582912 | tf_op jit(solution)/shard_map/dot_general | solution.py:248
  570.2 6.3 fusion.75
  586.3 20.9 %collective-permute-done.30 = bf16[384,1536]{1,0:T(8,128)(2,1)S(1)} collective-permute-done((bf16[384,1536]{1,0:T(8,128)(2,1)S(1)}, bf16[384,1536]{1,0:T(8,128)(2,1)S(1)}, u32[]{:S(2)}, u32[]{:S(2)}) %collective-permute-start.30) | collective-permute-done | bytes 1179680 | tf_op jit(solution)/shard_map/ppermute | solution.py:393
  634.7 26.1 %collective-permute-done.39 = bf16[384,1536]{1,0:T(8,128)(2,1)} collective-permute-done((bf16[384,1536]{1,0:T(8,128)(2,1)}, bf16[384,1536]{1,0:T(8,128)(2,1)}, u32[]{:S(2)}, u32[]{:S(2)}) %collective-permute-start.39) | collective-permute-done | bytes 1179680 | tf_op jit(solution)/shard_map/ppermute | solution.py:393
  684.2 6.9 reduce-scatter.10.cloned.1.call-done
  (513 shorter events, 320.2 us)
Async XLA Ops:
  7.2 60.4 %all-gather.6.cloned.1.call-start = ((), (), s32[]{:S(2)}) async-start(), calls=%async_computation.5 | async-start | bytes 2457600 | tf_op jit(solution)/shard_map/all_gather | solution.py:296
  22.5 76.4 %all-gather.8.cloned.1.call-start = ((), (), s32[]{:S(2)}) async-start(), calls=%async_computation.6 | async-start | bytes 1474560 | tf_op jit(solution)/shard_map/all_gather | solution.py:296
  42.4 28.3 %collective-permute-start.2 = (bf16[384,1536]{1,0:T(8,128)(2,1)S(1)}, bf16[384,1536]{1,0:T(8,128)(2,1)}, u32[]{:S(2)}, u32[]{:S(2)}) collective-permute-start(bf16[384,1536]{1,0:T(8,128)(2,1)S(1)} %copy-done.53), channel_id=1, source_target_pairs={{0,1},{1,0},{2,3},{3,2},{4,5},{5,4},{6,7},{7,6},{8,9},{9,8},{10,11... | collective-permute-start | bytes 3538952 | tf_op jit(solution)/shard_map/ppermute | solution.py:393
  44.1 25.0 %collective-permute-start.5 = (s32[2,8]{1,0:T(2,128)S(1)}, s32[2,8]{1,0:T(2,128)S(1)}, u32[]{:S(2)}, u32[]{:S(2)}) collective-permute-start(s32[2,8]{1,0:T(2,128)S(1)} %pad_add_fusion.2), channel_id=1, source_target_pairs={{0,16},{16,0},{1,17},{17,1},{2,18},{18,2},{3,19},{19,3},{4,20},{20... | collective-permute-start | bytes 200 | tf_op jit(solution)/shard_map/ppermute | solution.py:390
  67.6 46.0 %collective-permute-start.6 = (bf16[4,192,1280]{2,1,0:T(8,128)(2,1)}, bf16[4,192,1280]{2,1,0:T(8,128)(2,1)}, u32[]{:S(2)}, u32[]{:S(2)}) collective-permute-start(bf16[4,192,1280]{2,1,0:T(8,128)(2,1)} %bitcast.392), channel_id=1, source_target_pairs={{0,2},{1,3},{2,0},{3,1},{4,6},{5,7},{6,4},{7,5},{8,10},{9,11},{10,... | collective-permute-start | bytes 5898248 | tf_op jit(solution)/shard_map/ppermute | solution.py:303
  69.9 94.5 %all-gather.10.cloned.1.call-start = ((), (), s32[]{:S(2)}) async-start(), calls=%async_computation.7 | async-start | bytes 1966080 | tf_op jit(solution)/shard_map/all_gather | solution.py:296
  72.6 44.6 %collective-permute-start.3 = (bf16[768,1536]{1,0:T(8,128)(2,1)S(1)}, bf16[768,1536]{1,0:T(8,128)(2,1)}, u32[]{:S(2)}, u32[]{:S(2)}) collective-permute-start(bf16[768,1536]{1,0:T(8,128)(2,1)S(1)} %pad_maximum_fusion.7), channel_id=1, source_target_pairs={{0,16},{16,0},{1,17},{17,1},{2,18},{18,2},{3,19},{19,3},{4,20},{20... | collective-permute-start | bytes 7077896 | tf_op jit(solution)/shard_map/ppermute | solution.py:390
  98.9 113.2 %all-gather.12.cloned.1.call-start = ((), (), s32[]{:S(2)}) async-start(), calls=%async_computation.8 | async-start | bytes 1966080 | tf_op jit(solution)/shard_map/all_gather | solution.py:296
  99.1 42.8 %collective-permute-start.10 = (bf16[4,192,768]{2,1,0:T(8,128)(2,1)}, bf16[4,192,768]{2,1,0:T(8,128)(2,1)}, u32[]{:S(2)}, u32[]{:S(2)}) collective-permute-start(bf16[4,192,768]{2,1,0:T(8,128)(2,1)} %bitcast.400), channel_id=1, source_target_pairs={{0,2},{1,3},{2,0},{3,1},{4,6},{5,7},{6,4},{7,5},{8,10},{9,11},{10,... | collective-permute-start | bytes 3538952 | tf_op jit(solution)/shard_map/ppermute | solution.py:303
  122.0 26.6 %collective-permute-start.7 = (bf16[384,1536]{1,0:T(8,128)(2,1)S(1)}, bf16[384,1536]{1,0:T(8,128)(2,1)S(1)}, u32[]{:S(2)}, u32[]{:S(2)}) collective-permute-start(bf16[384,1536]{1,0:T(8,128)(2,1)S(1)} %copy-done.4), channel_id=1, source_target_pairs={{0,1},{1,0},{2,3},{3,2},{4,5},{5,4},{6,7},{7,6},{8,9},{9,8},{10,11... | collective-permute-start | bytes 3538952 | tf_op jit(solution)/shard_map/ppermute | solution.py:393
  150.3 27.7 %collective-permute-start.8 = (bf16[768,1536]{1,0:T(8,128)(2,1)}, bf16[768,1536]{1,0:T(8,128)(2,1)}, u32[]{:S(2)}, u32[]{:S(2)}) collective-permute-start(bf16[768,1536]{1,0:T(8,128)(2,1)} %pad_maximum_fusion.8), channel_id=1, source_target_pairs={{0,16},{16,0},{1,17},{17,1},{2,18},{18,2},{3,19},{19,3},{4,20},{20... | collective-permute-start | bytes 7077896 | tf_op jit(solution)/shard_map/ppermute | solution.py:390
  164.5 102.7 %all-gather.14.cloned.1.call-start = ((), (), s32[]{:S(2)}) async-start(), calls=%async_computation.9 | async-start | bytes 1966080 | tf_op jit(solution)/shard_map/all_gather | solution.py:296
  175.2 36.9 %collective-permute-start.9 = (bf16[4,192,1024]{2,1,0:T(8,128)(2,1)S(1)}, bf16[4,192,1024]{2,1,0:T(8,128)(2,1)}, u32[]{:S(2)}, u32[]{:S(2)}) collective-permute-start(bf16[4,192,1024]{2,1,0:T(8,128)(2,1)S(1)} %bitcast.395), channel_id=1, source_target_pairs={{0,2},{1,3},{2,0},{3,1},{4,6},{5,7},{6,4},{7,5},{8,10},{9,11},{10,... | collective-permute-start | bytes 4718600 | tf_op jit(solution)/shard_map/ppermute | solution.py:303
  226.2 28.2 %collective-permute-start.14 = (bf16[384,1536]{1,0:T(8,128)(2,1)S(1)}, bf16[384,1536]{1,0:T(8,128)(2,1)}, u32[]{:S(2)}, u32[]{:S(2)}) collective-permute-start(bf16[384,1536]{1,0:T(8,128)(2,1)S(1)} %slice.273), channel_id=1, source_target_pairs={{0,1},{1,0},{2,3},{3,2},{4,5},{5,4},{6,7},{7,6},{8,9},{9,8},{10,11... | collective-permute-start | bytes 3538952 | tf_op jit(solution)/shard_map/ppermute | solution.py:393
  227.8 36.3 %collective-permute-start.15 = (bf16[4,192,1024]{2,1,0:T(8,128)(2,1)S(1)}, bf16[4,192,1024]{2,1,0:T(8,128)(2,1)}, u32[]{:S(2)}, u32[]{:S(2)}) collective-permute-start(bf16[4,192,1024]{2,1,0:T(8,128)(2,1)S(1)} %bitcast.396), channel_id=1, source_target_pairs={{0,2},{1,3},{2,0},{3,1},{4,6},{5,7},{6,4},{7,5},{8,10},{9,11},{10,... | collective-permute-start | bytes 4718600 | tf_op jit(solution)/shard_map/ppermute | solution.py:303
  230.0 219.9 %reduce-scatter.6.cloned.1.call-start = ((), (), s32[]{:S(2)}) async-start(), calls=%async_computation.10 | async-start | bytes 1966080 | tf_op jit(solution)/shard_map/reduce_scatter | solution.py:330
  265.7 27.2 %collective-permute-start.16 = (bf16[384,1536]{1,0:T(8,128)(2,1)}, bf16[384,1536]{1,0:T(8,128)(2,1)}, u32[]{:S(2)}, u32[]{:S(2)}) collective-permute-start(bf16[384,1536]{1,0:T(8,128)(2,1)} %multiply_convert_fusion.6), channel_id=1, source_target_pairs={{0,1},{1,0},{2,3},{3,2},{4,5},{5,4},{6,7},{7,6},{8,9},{9,8},{10,11... | collective-permute-start | bytes 3538952 | tf_op jit(solution)/shard_map/ppermute | solution.py:393
  267.2 35.5 %collective-permute-start.18 = (bf16[4,128,1536]{2,1,0:T(8,128)(2,1)}, bf16[4,128,1536]{2,1,0:T(8,128)(2,1)S(1)}, u32[]{:S(2)}, u32[]{:S(2)}) collective-permute-start(bf16[4,128,1536]{2,1,0:T(8,128)(2,1)} %bitcast.398), channel_id=1, source_target_pairs={{0,2},{1,3},{2,0},{3,1},{4,6},{5,7},{6,4},{7,5},{8,10},{9,11},{10,... | collective-permute-start | bytes 4718600 | tf_op jit(solution)/shard_map/ppermute | solution.py:303
  363.3 44.3 %collective-permute-start.21 = (bf16[4,128,1536]{2,1,0:T(8,128)(2,1)S(1)}, bf16[4,128,1536]{2,1,0:T(8,128)(2,1)S(1)}, u32[]{:S(2)}, u32[]{:S(2)}) collective-permute-start(bf16[4,128,1536]{2,1,0:T(8,128)(2,1)S(1)} %dynamic-slice_bitcast_fusion.3), channel_id=1, source_target_pairs={{0,2},{1,3},{2,0},{3,1},{4,6},{5,7},{6,4},{7,5},{8,10},{9,11},{10,... | collective-permute-start | bytes 4718600 | tf_op jit(solution)/shard_map/ppermute | solution.py:320
  368.0 28.2 %collective-permute-start.20 = (bf16[384,1536]{1,0:T(8,128)(2,1)S(1)}, bf16[384,1536]{1,0:T(8,128)(2,1)S(1)}, u32[]{:S(2)}, u32[]{:S(2)}) collective-permute-start(bf16[384,1536]{1,0:T(8,128)(2,1)S(1)} %slice.272), channel_id=1, source_target_pairs={{0,1},{1,0},{2,3},{3,2},{4,5},{5,4},{6,7},{7,6},{8,9},{9,8},{10,11... | collective-permute-start | bytes 3538952 | tf_op jit(solution)/shard_map/ppermute | solution.py:393
  375.2 58.7 %collective-permute-start.23 = (bf16[4,192,1024]{2,1,0:T(8,128)(2,1)}, bf16[4,192,1024]{2,1,0:T(8,128)(2,1)}, u32[]{:S(2)}, u32[]{:S(2)}) collective-permute-start(bf16[4,192,1024]{2,1,0:T(8,128)(2,1)} %dynamic-slice_bitcast_fusion.2), channel_id=1, source_target_pairs={{0,2},{1,3},{2,0},{3,1},{4,6},{5,7},{6,4},{7,5},{8,10},{9,11},{10,... | collective-permute-start | bytes 4718600 | tf_op jit(solution)/shard_map/ppermute | solution.py:320
  400.3 36.9 %collective-permute-start.22 = (bf16[384,1536]{1,0:T(8,128)(2,1)}, bf16[384,1536]{1,0:T(8,128)(2,1)}, u32[]{:S(2)}, u32[]{:S(2)}) collective-permute-start(bf16[384,1536]{1,0:T(8,128)(2,1)} %fusion.65), channel_id=1, source_target_pairs={{0,1},{1,0},{2,3},{3,2},{4,5},{5,4},{6,7},{7,6},{8,9},{9,8},{10,11... | collective-permute-start | bytes 3538952 | tf_op jit(solution)/shard_map/ppermute | solution.py:393
  409.1 142.0 %reduce-scatter.8.cloned.1.call-start = ((), (), s32[]{:S(2)}) async-start(), calls=%async_computation.11 | async-start | bytes 1966080 | tf_op jit(solution)/shard_map/reduce_scatter | solution.py:330
  443.0 37.1 %collective-permute-start.25 = (bf16[4,192,1024]{2,1,0:T(8,128)(2,1)}, bf16[4,192,1024]{2,1,0:T(8,128)(2,1)}, u32[]{:S(2)}, u32[]{:S(2)}) collective-permute-start(bf16[4,192,1024]{2,1,0:T(8,128)(2,1)} %dynamic-slice_bitcast_fusion.1), channel_id=1, source_target_pairs={{0,2},{1,3},{2,0},{3,1},{4,6},{5,7},{6,4},{7,5},{8,10},{9,11},{10,... | collective-permute-start | bytes 4718600 | tf_op jit(solution)/shard_map/ppermute | solution.py:320
  444.5 220.9 %reduce-scatter.14.cloned.1.call-start = ((), (), s32[]{:S(2)}) async-start(), calls=%async_computation.14 | async-start | bytes 1966080 | tf_op jit(solution)/shard_map/reduce_scatter | solution.py:330
  500.7 47.5 %collective-permute-start.28 = (bf16[4,192,768]{2,1,0:T(8,128)(2,1)}, bf16[4,192,768]{2,1,0:T(8,128)(2,1)}, u32[]{:S(2)}, u32[]{:S(2)}) collective-permute-start(bf16[4,192,768]{2,1,0:T(8,128)(2,1)} %fusion.13), channel_id=1, source_target_pairs={{0,2},{1,3},{2,0},{3,1},{4,6},{5,7},{6,4},{7,5},{8,10},{9,11},{10,... | collective-permute-start | bytes 3538952 | tf_op jit(solution)/shard_map/ppermute | solution.py:320
  543.0 125.6 %reduce-scatter.12.cloned.1.call-start = ((), (), s32[]{:S(2)}) async-start(), calls=%async_computation.13 | async-start | bytes 1474560 | tf_op jit(solution)/shard_map/reduce_scatter | solution.py:330
  568.1 45.1 %collective-permute-start.32 = (bf16[4,192,1280]{2,1,0:T(8,128)(2,1)}, bf16[4,192,1280]{2,1,0:T(8,128)(2,1)}, u32[]{:S(2)}, u32[]{:S(2)}) collective-permute-start(bf16[4,192,1280]{2,1,0:T(8,128)(2,1)} %dynamic-slice_bitcast_fusion), channel_id=1, source_target_pairs={{0,2},{1,3},{2,0},{3,1},{4,6},{5,7},{6,4},{7,5},{8,10},{9,11},{10,... | collective-permute-start | bytes 5898248 | tf_op jit(solution)/shard_map/ppermute | solution.py:320
  579.2 28.0 %collective-permute-start.30 = (bf16[384,1536]{1,0:T(8,128)(2,1)S(1)}, bf16[384,1536]{1,0:T(8,128)(2,1)S(1)}, u32[]{:S(2)}, u32[]{:S(2)}) collective-permute-start(bf16[384,1536]{1,0:T(8,128)(2,1)S(1)} %slice.271), channel_id=1, source_target_pairs={{0,1},{1,0},{2,3},{3,2},{4,5},{5,4},{6,7},{7,6},{8,9},{9,8},{10,11... | collective-permute-start | bytes 3538952 | tf_op jit(solution)/shard_map/ppermute | solution.py:393
  620.6 70.5 %reduce-scatter.10.cloned.1.call-start = ((), (), s32[]{:S(2)}) async-start(), calls=%async_computation.12 | async-start | bytes 2457600 | tf_op jit(solution)/shard_map/reduce_scatter | solution.py:330
  632.5 28.3 %collective-permute-start.39 = (bf16[384,1536]{1,0:T(8,128)(2,1)}, bf16[384,1536]{1,0:T(8,128)(2,1)}, u32[]{:S(2)}, u32[]{:S(2)}) collective-permute-start(bf16[384,1536]{1,0:T(8,128)(2,1)} %slice.270), channel_id=1, source_target_pairs={{0,1},{1,0},{2,3},{3,2},{4,5},{5,4},{6,7},{7,6},{8,9},{9,8},{10,11... | collective-permute-start | bytes 3538952 | tf_op jit(solution)/shard_map/ppermute | solution.py:393
  684.1 21.7 %collective-permute-start.45 = (bf16[2,96,1024]{2,1,0:T(8,128)(2,1)}, bf16[2,96,1024]{2,1,0:T(8,128)(2,1)}, u32[]{:S(2)}, u32[]{:S(2)}) collective-permute-start(bf16[2,96,1024]{2,1,0:T(8,128)(2,1)} %pad_maximum_fusion.20), channel_id=1, source_target_pairs={{0,16},{16,0},{1,17},{17,1},{2,18},{18,2},{3,19},{19,3},{4,20},{20... | collective-permute-start | bytes 1179656 | tf_op jit(solution)/shard_map/ppermute | solution.py:390
  (130 other events, 1534.8 us)
Sparse Core Ops, SparseCore 0:
  22.6 44.9 all-gather.5
  70.1 28.7 all-gather.7
  101.0 36.2 all-gather.9
  164.6 36.5 all-gather.11
  230.2 35.3 all-gather.13
  409.2 33.9 reduce-scatter.5
  446.1 34.2 reduce-scatter.7
  543.1 33.9 reduce-scatter.13
  620.8 27.9 reduce-scatter.11
  650.9 40.1 reduce-scatter.9

commit v6 on v5

--- a/solution.py
+++ b/solution.py
@@ -140,7 +140,7 @@
         ),
         out_shape=jax.ShapeDtypeStruct((team * rows, width), jnp.float32),
         cost_estimate=pl.CostEstimate(
-            flops=64 * team * rows * rows * width,
+            flops=8 * team * rows * rows * width,
             bytes_accessed=8 * team * rows * width * 2,
             transcendentals=team * rows * PROMPTS * heads,
         ),
@@ -332,18 +332,22 @@
     )
 
 
-def sum_all(values, count, reps):
+def sum_near(values, count):
     total = values
     for step in middle_strides(count):
         total = total + lax.ppermute(total, "shard", swap_pairs(count, step))
-    near = total
+    return total
+
+
+def sum_far(near, count, reps):
+    total = near
     for step in (count // 2, count // 4, 1):
         total = total + lax.ppermute(total, "shard", swap_pairs(count, step))
     step = 1
     while step < reps:
         total = total + lax.ppermute(total, "rep", [(r, r ^ step) for r in range(reps)])
         step *= 2
-    return near, total[0]
+    return total[0]
 
 
 def local(
@@ -504,7 +508,6 @@
         return quad.reshape(model_width, quarter)
 
     tokens_all = team_rows(after(tokens, rest_block), first_line)
-    cotangent_all = team_rows(after(cotangent, tokens_all))
     facts_all = team_rows(jnp.concatenate([prompt_ids[0], seq_offsets[0]])[None, :])
     chain_ok = jnp.stack([chain_mask(facts_all[b, :NC], facts_all[b, NC:]) for b in range(team)])
     chain_float = chain_ok.astype(jnp.float32)
@@ -514,10 +517,11 @@
     scaled1 = scaled_all[:own_rows]
     inverse1 = inverse_all[:own_rows]
     inputs = inputs_all[:own_rows]
-    normed1 = after((scaled_all * gain_one).astype(jnp.bfloat16), second_line)
+    normed1 = after((scaled_all * gain_one).astype(jnp.bfloat16), gate_line)
     row_count = normed1.shape[0]
 
     qkv_low = matmul(normed1, first[:, : 3 * quarter]).astype(jnp.bfloat16)
+    cotangent_all = team_rows(after(cotangent, first_line), qkv_low)
     second = gather_rest(second_line, count, index, qkv_low)[0]
     outgate_w = second[:, :quarter]
     output_w = turn_rows(second[:, quarter:])
@@ -533,7 +537,7 @@
 
     decay_cols = jnp.transpose(decay_sum, (0, 2, 1))
     attended = attend(
-        after(qkv_low, gate_line, cotangent_all),
+        qkv_low,
         decay_cols,
         decay_sum,
         facts_all,
@@ -543,7 +547,7 @@
         own_rows,
     )
     gate_open = jax.nn.sigmoid(outgate_pre)
-    gated_low = (after(attended, up_line, gate_last) * gate_open).astype(jnp.bfloat16)
+    gated_low = (after(attended, up_line, gate_last, cotangent_all) * gate_open).astype(jnp.bfloat16)
 
     residual = inputs + after(team_sum(matmul(gated_low, output_w)), up_last)
     scaled2, inverse2 = normalize(residual)
@@ -598,7 +602,7 @@
         own_rows,
     )
     second_held = second_sum(grad_qkv)
-    grad_qkv = after(grad_qkv, grad_gate_w, second_held)
+    grad_qkv = after(grad_qkv, grad_gate_w, second_held, grad_up_w)
     sum_second = scatter_line(second_held, count)
     layer_out = (residual + team_sum(after(part_out, grad_qkv))).astype(jnp.bfloat16)
     grad_decay = jnp.transpose(grad_logit_rows, (0, 2, 1)) - grad_logit_cols
@@ -612,7 +616,7 @@
         rank * heads,
         axis=0,
     )
-    bias_near, grad_bias = sum_all(bias_sum[None, :], count, reps)
+    bias_near = sum_near(bias_sum[None, :], count)
     grad_forget_low = lax.dynamic_update_slice_in_dim(
         jnp.zeros((row_count, small.shape[1]), jnp.bfloat16),
         grad_forget_in.astype(jnp.bfloat16),
@@ -626,7 +630,8 @@
         grad_outgate, outgate_w
     )
     down_own = both_cores(after(grad_down, part_first_w))
-    first_held = first_sum(grad_bias, layer_out, down_own)
+    grad_bias = sum_far(after(bias_near, part_first_w), count, reps)
+    first_held = first_sum(grad_bias, layer_out, down_own, sum_second)
     grad_normed1 = team_sum(after(part_normed1, first_held))
     tokens_grad = grad_resid + norm_back(grad_normed1 * gain_one, scaled1, inverse1)
     sum_first = scatter_line(first_held, count)

time: 743 us -> 704 us (0.948)
  waiting for transfers between devices: 286 us -> 259 us
  local copies, waits for them, and re-layouts: 107 us -> 97.8 us
    ppermute x17, waiting for transfers between devices: 144 us -> 161 us  [swap_side(): return lax.ppermute(values, 'shard', side_pairs)]
    all_gather x5, waiting for transfers between devices: 45.2 us -> 31.6 us  [gather_line(): lax.all_gather(block, 'shard', axis=0, tiled=True, axis_index_groups=line...]
    ppermute x5, waiting for transfers between devices: 37.9 us -> 24.4 us  [gather_rest(): other = lax.ppermute(held, 'shard', swap_pairs(count, step))]
    unnamed x217 -> x209, local copies, waits for them, and re-layouts: 26 us -> 21.7 us
  transfers between devices with their start and end apart: 58 -> 58, of which waited for: 28 -> 25; matrix products, arithmetic and copies ran while one was open for 37% -> 36% of each run, Pallas kernels for 6% -> 6%
where the time goes in v6:
time: 704 us; the launch traced here: 696 us
  waiting for transfers between devices  259 us (37%)
  matrix products  136 us (19%)
  other arithmetic  109 us (15%)
  local copies, waits for them, and re-layouts  97.8 us (14%)
  Pallas kernels  42.9 us (6%)
  starting transfers between devices  34.6 us (5%)
  between operations  16.3 us (2%)
    ppermute x17, waiting for transfers between devices, swap_side(): return lax.ppermute(values, 'shard', side_pairs)  161 us
    dot_general x7, matrix products, matmul(): return jnp.dot(left_side, right_side, preferred_element_type=jnp.float32)  51.1 us
    dot_general x6, matrix products, matmul_tn(): lax.dot_general(left_side, right_side, (((0,), (0,)), ((), ())), preferre...  41 us
    dot_general x6, matrix products, matmul_nt(): lax.dot_general(left_side, right_side, (((1,), (1,)), ((), ())), preferre...  40.9 us
    all_gather x5, waiting for transfers between devices, gather_line(): lax.all_gather(block, 'shard', axis=0, tiled=True, axis_index_groups=line...  31.6 us
    ppermute x5, waiting for transfers between devices, scatter_rest(): lax.ppermute(pick(halves, 1 - at, 1), 'shard', swap_pairs(count, step))  25.6 us
    ppermute x5, waiting for transfers between devices, gather_rest(): other = lax.ppermute(held, 'shard', swap_pairs(count, step))  24.4 us
    pallas_call x1, Pallas kernels, attend_back(): pl.pallas_call(body, grid_spec=pltpu.PrefetchScalarGridSpec(num_scalar_pr...  24.2 us
  transfers between devices with their start and end apart: 58, of which 25 were waited for; matrix products, arithmetic and copies ran while one was open for 36% of the time, Pallas kernels for 6%

profile of v6, /device:TPU:0, one launch (start us, length us, event | category | flops | bytes accessed | tf_op | source)
XLA Modules:
  0.0 696.0 jit_solution(13163295721278214932)
XLA Ops:
  15.7 5.8 collective-permute-done
  30.9 11.2 %collective-permute-done.1 = bf16[96,2816]{1,0:T(8,128)(2,1)S(1)} collective-permute-done((bf16[96,2816]{1,0:T(8,128)(2,1)S(1)}, bf16[96,2816]{1,0:T(8,128)(2,1)S(1)}, u32[]{:S(2)}, u32[]{:S(2)}) %collective-permute-start.1) | collective-permute-done | bytes 540704 | tf_op jit(solution)/shard_map/ppermute | solution.py:397
  44.3 23.4 %all-gather.6.cloned.1.call-done = bf16[768,1280]{1,0:T(8,128)(2,1)} async-done(((bf16[192,1280]{1,0:T(8,128)(2,1)}), bf16[768,1280]{1,0:T(8,128)(2,1)}) %all-gather.6.cloned.1.call-update) | async-done | bytes 1966096 | tf_op jit(solution)/shard_map/all_gather | solution.py:296
  77.1 20.5 %collective-permute-done.8 = bf16[384,1536]{1,0:T(8,128)(2,1)S(1)} collective-permute-done((bf16[384,1536]{1,0:T(8,128)(2,1)}, bf16[384,1536]{1,0:T(8,128)(2,1)S(1)}, u32[]{:S(2)}, u32[]{:S(2)}) %collective-permute-start.8) | collective-permute-done | bytes 1179680 | tf_op jit(solution)/shard_map/ppermute | solution.py:397
  101.4 12.3 %collective-permute-done.6 = bf16[4,192,1280]{2,1,0:T(8,128)(2,1)} collective-permute-done((bf16[4,192,1280]{2,1,0:T(8,128)(2,1)}, bf16[4,192,1280]{2,1,0:T(8,128)(2,1)}, u32[]{:S(2)}, u32[]{:S(2)}) %collective-permute-start.6) | collective-permute-done | bytes 1966112 | tf_op jit(solution)/shard_map/ppermute | solution.py:303
  121.1 8.0 %broadcast_multiply_fusion = (f32[1536,1536]{1,0:T(8,128)}, bf16[1536,1536]{1,0:T(8,128)(2,1)}) fusion(f32[1536]{0:T(1024)S(1)} %add_rsqrt_fusion, bf16[768,1536]{1,0:T(8,128)(2,1)} %collective-permute-done.3, bf16[768,1536]{1,0:T(8,128)(2,1)S(1)} %pad_maximum_fusion.7, f32[1536]{0:T(1024)S(1)} %get-tuple-element.139), kind=kLoop, calls=%fused_computation.22 | loop fusion | flops 16515072 | bytes 18886656 | tf_op jit(solution)/shard_map/mul | solution.py:35
  129.1 8.2 %all-gather.10.cloned.1.call-done = bf16[768,1024]{1,0:T(8,128)(2,1)} async-done(((bf16[192,1024]{1,0:T(8,128)(2,1)}), bf16[768,1024]{1,0:T(8,128)(2,1)}) %all-gather.10.cloned.1.call-update) | async-done | bytes 1572880 | tf_op jit(solution)/shard_map/all_gather | solution.py:296
  137.3 10.4 %convolution_convert_fusion.1.qkv_ref = bf16[1536,1152]{1,0:T(8,128)(2,1)} fusion(bf16[1536,1536]{1,0:T(8,128)(2,1)} %get-tuple-element.81, bf16[1536,1280]{1,0:T(8,128)(2,1)} %bitcast.350), kind=kOutput, calls=%fused_computation.5 | convolution fusion | flops 5437587456 | bytes 11796480 | tf_op jit(solution)/shard_map/dot_general | solution.py:244
  160.5 18.7 %attend.1 = f32[1536,384]{1,0:T(8,128)} custom-call(s32[4,8]{1,0:T(4,128)} %pad_add_fusion.1.facts_ref, bf16[1536,1152]{1,0:T(8,128)(2,1)} %convolution_convert_fusion.1.qkv_ref, f32[4,384,6]{2,1,0:T(8,128)} %bitcast.379, f32[4,6,384]{2,1,0:T(8,128)} %copy-done.61), custom_call_target="tpu_custom_call" | custom-call | flops 1811939328 | bytes 9437184 | tf_op jit(solution)/shard_map/attend/pallas_call | solution.py:129
  187.0 6.9 fusion.8
  222.1 23.6 %collective-permute-done.14 = bf16[384,1536]{1,0:T(8,128)(2,1)} collective-permute-done((bf16[384,1536]{1,0:T(8,128)(2,1)}, bf16[384,1536]{1,0:T(8,128)(2,1)}, u32[]{:S(2)}, u32[]{:S(2)}) %collective-permute-start.14) | collective-permute-done | bytes 1179680 | tf_op jit(solution)/shard_map/ppermute | solution.py:397
  248.1 6.4 collective-permute-done.15
  260.9 22.6 %collective-permute-done.16 = bf16[384,1536]{1,0:T(8,128)(2,1)} collective-permute-done((bf16[384,1536]{1,0:T(8,128)(2,1)}, bf16[384,1536]{1,0:T(8,128)(2,1)}, u32[]{:S(2)}, u32[]{:S(2)}) %collective-permute-start.16) | collective-permute-done | bytes 1179680 | tf_op jit(solution)/shard_map/ppermute | solution.py:397
  293.6 7.2 %fusion.71 = f32[1536,1024]{1,0:T(8,128)} fusion(bf16[1536,1536]{1,0:T(8,128)(2,1)S(1)} %bitcast.405, bf16[1024,1536]{1,0:T(8,128)(2,1)S(1)} %bitcast.383), kind=kOutput, calls=%fused_computation.297 | convolution fusion | flops 4831838208 | bytes 14155776 | tf_op jit(solution)/shard_map/dot_general | solution.py:254
  302.6 6.9 fusion.72
  309.5 11.5 %multiply_convert_fusion.1 = (bf16[1536,1024]{1,0:T(8,128)(2,1)}, bf16[1536,1024]{1,0:T(8,128)(2,1)S(1)}, bf16[1536,1024]{1,0:T(8,128)(2,1)S(1)}) fusion(f32[1536,1024]{1,0:T(8,128)} %fusion.72, f32[1536,1024]{1,0:T(8,128)} %fusion.71, bf16[1536,1536]{1,0:T(8,128)(2,1)S(1)} %pad_maximum_fusion, bf16[1536,1024]{1,0:T(8,128)(2,1)S(1)} %bitcast.391), kind=kOutput, calls=%fused_computation.6 | convolution fusion | flops 4855431168 | bytes 29884416 | tf_op jit(solution)/shard_map/dot_general | solution.py:244
  321.0 7.6 %fusion.73 = f32[1536,1536]{1,0:T(8,128)} fusion(bf16[1536,1024]{1,0:T(8,128)(2,1)S(1)} %get-tuple-element.157, bf16[1536,1024]{1,0:T(8,128)(2,1)S(1)} %bitcast.388), kind=kOutput, calls=%fused_computation.299 | convolution fusion | flops 4831838208 | bytes 15728640 | tf_op jit(solution)/shard_map/dot_general | solution.py:254
  328.6 7.9 %convolution_add_fusion.1 = f32[1536,1536]{1,0:T(8,128)S(1)} fusion(f32[1536,1536]{1,0:T(8,128)} %fusion.73, bf16[1536,1024]{1,0:T(8,128)(2,1)S(1)} %get-tuple-element.158, bf16[1536,1024]{1,0:T(8,128)(2,1)S(1)} %bitcast.392), kind=kOutput, calls=%fused_computation.3 | convolution fusion | flops 4834197504 | bytes 25165824 | tf_op jit(solution)/shard_map/dot_general | solution.py:254
  341.8 8.7 %convolution_convert_fusion.3 = bf16[1024,1536]{1,0:T(8,128)(2,1)S(1)} fusion(bf16[1536,1024]{1,0:T(8,128)(2,1)} %get-tuple-element.73, bf16[1536,1536]{1,0:T(8,128)(2,1)} %constant_dynamic-update-slice_fusion), kind=kOutput, calls=%fused_computation.28 | convolution fusion | flops 4833411072 | bytes 11010048 | tf_op jit(solution)/shard_map/dot_general | solution.py:248
  363.4 18.8 %collective-permute-done.20 = bf16[384,1536]{1,0:T(8,128)(2,1)S(1)} collective-permute-done((bf16[384,1536]{1,0:T(8,128)(2,1)S(1)}, bf16[384,1536]{1,0:T(8,128)(2,1)S(1)}, u32[]{:S(2)}, u32[]{:S(2)}) %collective-permute-start.20) | collective-permute-done | bytes 1179680 | tf_op jit(solution)/shard_map/ppermute | solution.py:397
  388.0 6.6 convolution_convert_fusion.2
  396.2 10.1 %fusion.74 = f32[1536,1536]{1,0:T(8,128)} fusion(bf16[1536,1024]{1,0:T(8,128)(2,1)} %get-tuple-element.73, bf16[1024,1536]{1,0:T(8,128)(2,1)} %bitcast.384), kind=kOutput, calls=%fused_computation.300 | convolution fusion | flops 4831838208 | bytes 15728640 | tf_op jit(solution)/shard_map/dot_general | solution.py:244
  406.4 15.0 %collective-permute-done.23 = bf16[4,192,1024]{2,1,0:T(8,128)(2,1)} collective-permute-done((bf16[4,192,1024]{2,1,0:T(8,128)(2,1)}, bf16[4,192,1024]{2,1,0:T(8,128)(2,1)}, u32[]{:S(2)}, u32[]{:S(2)}) %collective-permute-start.23) | collective-permute-done | bytes 1572896 | tf_op jit(solution)/shard_map/ppermute | solution.py:320
  436.7 6.0 convolution_convert_fusion.5
  450.9 6.6 multiply_convert_fusion.4
  457.5 10.3 %collective-permute-done.25 = bf16[4,192,1024]{2,1,0:T(8,128)(2,1)} collective-permute-done((bf16[4,192,1024]{2,1,0:T(8,128)(2,1)}, bf16[4,192,1024]{2,1,0:T(8,128)(2,1)}, u32[]{:S(2)}, u32[]{:S(2)}) %collective-permute-start.25) | collective-permute-done | bytes 1572896 | tf_op jit(solution)/shard_map/ppermute | solution.py:320
  479.0 5.8 collective-permute-done.27
  489.1 24.2 %attend_back.1 = (bf16[1536,1152]{1,0:T(8,128)(2,1)}, f32[4,384,6]{2,1,0:T(8,128)}, f32[4,6,384]{2,1,0:T(8,128)}) custom-call(s32[4,8]{1,0:T(4,128)} %pad_add_fusion.1.facts_ref, bf16[1536,1152]{1,0:T(8,128)(2,1)} %convolution_convert_fusion.1.qkv_ref, bf16[1536,384]{1,0:T(8,128)(2,1)} %get-tuple-element.79.grad_ref, f32[4,384,6]{2,1,0:T(8,128)} %bitcast.380, ...), custom_call_target="tpu_custom_call" | custom-call | flops 18119393280 | bytes 8257536 | tf_op jit(solution)/shard_map/attend_back/pallas_call | solution.py:208
  528.2 8.8 %convolution_convert_fusion = bf16[1536,1280]{1,0:T(8,128)(2,1)S(1)} fusion(bf16[1536,1536]{1,0:T(8,128)(2,1)} %get-tuple-element.81, bf16[1536,128]{1,0:T(8,128)(2,1)S(1)} %dynamic_update_slice.9, bf16[1536,1152]{1,0:T(8,128)(2,1)S(1)} %copy-done.29), kind=kOutput, calls=%fused_computation.4 | convolution fusion | flops 6049628160 | bytes 12582912 | tf_op jit(solution)/shard_map/dot_general | solution.py:248
  543.2 6.3 fusion.75
  566.9 21.0 %collective-permute-done.30 = bf16[384,1536]{1,0:T(8,128)(2,1)S(1)} collective-permute-done((bf16[384,1536]{1,0:T(8,128)(2,1)S(1)}, bf16[384,1536]{1,0:T(8,128)(2,1)S(1)}, u32[]{:S(2)}, u32[]{:S(2)}) %collective-permute-start.30) | collective-permute-done | bytes 1179680 | tf_op jit(solution)/shard_map/ppermute | solution.py:397
  609.0 26.2 %collective-permute-done.39 = bf16[384,1536]{1,0:T(8,128)(2,1)} collective-permute-done((bf16[384,1536]{1,0:T(8,128)(2,1)}, bf16[384,1536]{1,0:T(8,128)(2,1)}, u32[]{:S(2)}, u32[]{:S(2)}) %collective-permute-start.39) | collective-permute-done | bytes 1179680 | tf_op jit(solution)/shard_map/ppermute | solution.py:397
  (505 shorter events, 285.9 us)
Async XLA Ops:
  7.2 60.4 %all-gather.6.cloned.1.call-start = ((), (), s32[]{:S(2)}) async-start(), calls=%async_computation.5 | async-start | bytes 2457600 | tf_op jit(solution)/shard_map/all_gather | solution.py:296
  22.5 78.0 %all-gather.8.cloned.1.call-start = ((), (), s32[]{:S(2)}) async-start(), calls=%async_computation.6 | async-start | bytes 1474560 | tf_op jit(solution)/shard_map/all_gather | solution.py:296
  42.4 29.9 %collective-permute-start.2 = (bf16[384,1536]{1,0:T(8,128)(2,1)S(1)}, bf16[384,1536]{1,0:T(8,128)(2,1)}, u32[]{:S(2)}, u32[]{:S(2)}) collective-permute-start(bf16[384,1536]{1,0:T(8,128)(2,1)S(1)} %copy-done.49), channel_id=1, source_target_pairs={{0,1},{1,0},{2,3},{3,2},{4,5},{5,4},{6,7},{7,6},{8,9},{9,8},{10,11... | collective-permute-start | bytes 3538952 | tf_op jit(solution)/shard_map/ppermute | solution.py:397
  67.6 46.0 %collective-permute-start.6 = (bf16[4,192,1280]{2,1,0:T(8,128)(2,1)}, bf16[4,192,1280]{2,1,0:T(8,128)(2,1)}, u32[]{:S(2)}, u32[]{:S(2)}) collective-permute-start(bf16[4,192,1280]{2,1,0:T(8,128)(2,1)} %bitcast.394), channel_id=1, source_target_pairs={{0,2},{1,3},{2,0},{3,1},{4,6},{5,7},{6,4},{7,5},{8,10},{9,11},{10,... | collective-permute-start | bytes 5898248 | tf_op jit(solution)/shard_map/ppermute | solution.py:303
  69.9 67.4 %all-gather.10.cloned.1.call-start = ((), (), s32[]{:S(2)}) async-start(), calls=%async_computation.7 | async-start | bytes 1966080 | tf_op jit(solution)/shard_map/all_gather | solution.py:296
  70.1 27.5 %collective-permute-start.8 = (bf16[384,1536]{1,0:T(8,128)(2,1)}, bf16[384,1536]{1,0:T(8,128)(2,1)S(1)}, u32[]{:S(2)}, u32[]{:S(2)}) collective-permute-start(bf16[384,1536]{1,0:T(8,128)(2,1)} %param.31), channel_id=1, source_target_pairs={{0,1},{1,0},{2,3},{3,2},{4,5},{5,4},{6,7},{7,6},{8,9},{9,8},{10,11... | collective-permute-start | bytes 3538952 | tf_op jit(solution)/shard_map/ppermute | solution.py:397
  74.1 42.9 %collective-permute-start.3 = (bf16[768,1536]{1,0:T(8,128)(2,1)S(1)}, bf16[768,1536]{1,0:T(8,128)(2,1)}, u32[]{:S(2)}, u32[]{:S(2)}) collective-permute-start(bf16[768,1536]{1,0:T(8,128)(2,1)S(1)} %pad_maximum_fusion.7), channel_id=1, source_target_pairs={{0,16},{16,0},{1,17},{17,1},{2,18},{18,2},{3,19},{19,3},{4,20},{20... | collective-permute-start | bytes 7077896 | tf_op jit(solution)/shard_map/ppermute | solution.py:394
  100.5 101.3 %all-gather.12.cloned.1.call-start = ((), (), s32[]{:S(2)}) async-start(), calls=%async_computation.8 | async-start | bytes 1966080 | tf_op jit(solution)/shard_map/all_gather | solution.py:296
  100.7 47.0 %collective-permute-start.10 = (bf16[4,192,768]{2,1,0:T(8,128)(2,1)}, bf16[4,192,768]{2,1,0:T(8,128)(2,1)}, u32[]{:S(2)}, u32[]{:S(2)}) collective-permute-start(bf16[4,192,768]{2,1,0:T(8,128)(2,1)} %bitcast.402), channel_id=1, source_target_pairs={{0,2},{1,3},{2,0},{3,1},{4,6},{5,7},{6,4},{7,5},{8,10},{9,11},{10,... | collective-permute-start | bytes 3538952 | tf_op jit(solution)/shard_map/ppermute | solution.py:303
  147.8 50.8 %collective-permute-start.9 = (bf16[768,1536]{1,0:T(8,128)(2,1)}, bf16[768,1536]{1,0:T(8,128)(2,1)}, u32[]{:S(2)}, u32[]{:S(2)}) collective-permute-start(bf16[768,1536]{1,0:T(8,128)(2,1)} %pad_maximum_fusion.8), channel_id=1, source_target_pairs={{0,16},{16,0},{1,17},{17,1},{2,18},{18,2},{3,19},{19,3},{4,20},{20... | collective-permute-start | bytes 7077896 | tf_op jit(solution)/shard_map/ppermute | solution.py:394
  151.8 30.7 %collective-permute-start.11 = (bf16[2,384,384]{2,1,0:T(8,128)(2,1)}, bf16[2,384,384]{2,1,0:T(8,128)(2,1)}, u32[]{:S(2)}, u32[]{:S(2)}) collective-permute-start(bf16[2,384,384]{2,1,0:T(8,128)(2,1)} %dynamic-slice_bitcast_fusion.4), channel_id=1, source_target_pairs={{0,1},{1,0},{2,3},{3,2},{4,5},{5,4},{6,7},{7,6},{8,9},{9,8},{10,11... | collective-permute-start | bytes 1769480 | tf_op jit(solution)/shard_map/ppermute | solution.py:397
  158.5 99.0 %all-gather.14.cloned.1.call-start = ((), (), s32[]{:S(2)}) async-start(), calls=%async_computation.9 | async-start | bytes 1966080 | tf_op jit(solution)/shard_map/all_gather | solution.py:296
  159.0 42.8 %collective-permute-start.7 = (bf16[4,192,1024]{2,1,0:T(8,128)(2,1)}, bf16[4,192,1024]{2,1,0:T(8,128)(2,1)}, u32[]{:S(2)}, u32[]{:S(2)}) collective-permute-start(bf16[4,192,1024]{2,1,0:T(8,128)(2,1)} %bitcast.396), channel_id=1, source_target_pairs={{0,2},{1,3},{2,0},{3,1},{4,6},{5,7},{6,4},{7,5},{8,10},{9,11},{10,... | collective-permute-start | bytes 4718600 | tf_op jit(solution)/shard_map/ppermute | solution.py:303
  217.2 28.6 %collective-permute-start.14 = (bf16[384,1536]{1,0:T(8,128)(2,1)}, bf16[384,1536]{1,0:T(8,128)(2,1)}, u32[]{:S(2)}, u32[]{:S(2)}) collective-permute-start(bf16[384,1536]{1,0:T(8,128)(2,1)} %slice.273), channel_id=1, source_target_pairs={{0,1},{1,0},{2,3},{3,2},{4,5},{5,4},{6,7},{7,6},{8,9},{9,8},{10,11... | collective-permute-start | bytes 3538952 | tf_op jit(solution)/shard_map/ppermute | solution.py:397
  217.7 36.7 %collective-permute-start.15 = (bf16[4,192,1024]{2,1,0:T(8,128)(2,1)}, bf16[4,192,1024]{2,1,0:T(8,128)(2,1)}, u32[]{:S(2)}, u32[]{:S(2)}) collective-permute-start(bf16[4,192,1024]{2,1,0:T(8,128)(2,1)} %bitcast.398), channel_id=1, source_target_pairs={{0,2},{1,3},{2,0},{3,1},{4,6},{5,7},{6,4},{7,5},{8,10},{9,11},{10,... | collective-permute-start | bytes 4718600 | tf_op jit(solution)/shard_map/ppermute | solution.py:303
  219.1 217.6 %reduce-scatter.6.cloned.1.call-start = ((), (), s32[]{:S(2)}) async-start(), calls=%async_computation.10 | async-start | bytes 1966080 | tf_op jit(solution)/shard_map/reduce_scatter | solution.py:330
  256.1 27.4 %collective-permute-start.16 = (bf16[384,1536]{1,0:T(8,128)(2,1)}, bf16[384,1536]{1,0:T(8,128)(2,1)}, u32[]{:S(2)}, u32[]{:S(2)}) collective-permute-start(bf16[384,1536]{1,0:T(8,128)(2,1)} %multiply_convert_fusion.6), channel_id=1, source_target_pairs={{0,1},{1,0},{2,3},{3,2},{4,5},{5,4},{6,7},{7,6},{8,9},{9,8},{10,11... | collective-permute-start | bytes 3538952 | tf_op jit(solution)/shard_map/ppermute | solution.py:397
  257.5 35.5 %collective-permute-start.18 = (bf16[4,128,1536]{2,1,0:T(8,128)(2,1)}, bf16[4,128,1536]{2,1,0:T(8,128)(2,1)S(1)}, u32[]{:S(2)}, u32[]{:S(2)}) collective-permute-start(bf16[4,128,1536]{2,1,0:T(8,128)(2,1)} %bitcast.400), channel_id=1, source_target_pairs={{0,2},{1,3},{2,0},{3,1},{4,6},{5,7},{6,4},{7,5},{8,10},{9,11},{10,... | collective-permute-start | bytes 4718600 | tf_op jit(solution)/shard_map/ppermute | solution.py:303
  350.7 37.3 %collective-permute-start.21 = (bf16[4,128,1536]{2,1,0:T(8,128)(2,1)S(1)}, bf16[4,128,1536]{2,1,0:T(8,128)(2,1)S(1)}, u32[]{:S(2)}, u32[]{:S(2)}) collective-permute-start(bf16[4,128,1536]{2,1,0:T(8,128)(2,1)S(1)} %dynamic-slice_bitcast_fusion.3), channel_id=1, source_target_pairs={{0,2},{1,3},{2,0},{3,1},{4,6},{5,7},{6,4},{7,5},{8,10},{9,11},{10,... | collective-permute-start | bytes 4718600 | tf_op jit(solution)/shard_map/ppermute | solution.py:320
  354.2 28.0 %collective-permute-start.20 = (bf16[384,1536]{1,0:T(8,128)(2,1)S(1)}, bf16[384,1536]{1,0:T(8,128)(2,1)S(1)}, u32[]{:S(2)}, u32[]{:S(2)}) collective-permute-start(bf16[384,1536]{1,0:T(8,128)(2,1)S(1)} %slice.272), channel_id=1, source_target_pairs={{0,1},{1,0},{2,3},{3,2},{4,5},{5,4},{6,7},{7,6},{8,9},{9,8},{10,11... | collective-permute-start | bytes 3538952 | tf_op jit(solution)/shard_map/ppermute | solution.py:397
  361.8 59.6 %collective-permute-start.23 = (bf16[4,192,1024]{2,1,0:T(8,128)(2,1)}, bf16[4,192,1024]{2,1,0:T(8,128)(2,1)}, u32[]{:S(2)}, u32[]{:S(2)}) collective-permute-start(bf16[4,192,1024]{2,1,0:T(8,128)(2,1)} %dynamic-slice_bitcast_fusion.2), channel_id=1, source_target_pairs={{0,2},{1,3},{2,0},{3,1},{4,6},{5,7},{6,4},{7,5},{8,10},{9,11},{10,... | collective-permute-start | bytes 4718600 | tf_op jit(solution)/shard_map/ppermute | solution.py:320
  387.1 37.4 %collective-permute-start.22 = (bf16[384,1536]{1,0:T(8,128)(2,1)}, bf16[384,1536]{1,0:T(8,128)(2,1)}, u32[]{:S(2)}, u32[]{:S(2)}) collective-permute-start(bf16[384,1536]{1,0:T(8,128)(2,1)} %fusion.65), channel_id=1, source_target_pairs={{0,1},{1,0},{2,3},{3,2},{4,5},{5,4},{6,7},{7,6},{8,9},{9,8},{10,11... | collective-permute-start | bytes 3538952 | tf_op jit(solution)/shard_map/ppermute | solution.py:397
  396.2 127.8 %reduce-scatter.8.cloned.1.call-start = ((), (), s32[]{:S(2)}) async-start(), calls=%async_computation.11 | async-start | bytes 1966080 | tf_op jit(solution)/shard_map/reduce_scatter | solution.py:330
  427.8 96.2 %reduce-scatter.10.cloned.1.call-start = ((), (), s32[]{:S(2)}) async-start(), calls=%async_computation.12 | async-start | bytes 1966080 | tf_op jit(solution)/shard_map/reduce_scatter | solution.py:330
  430.7 37.1 %collective-permute-start.25 = (bf16[4,192,1024]{2,1,0:T(8,128)(2,1)}, bf16[4,192,1024]{2,1,0:T(8,128)(2,1)}, u32[]{:S(2)}, u32[]{:S(2)}) collective-permute-start(bf16[4,192,1024]{2,1,0:T(8,128)(2,1)} %dynamic-slice_bitcast_fusion.1), channel_id=1, source_target_pairs={{0,2},{1,3},{2,0},{3,1},{4,6},{5,7},{6,4},{7,5},{8,10},{9,11},{10,... | collective-permute-start | bytes 4718600 | tf_op jit(solution)/shard_map/ppermute | solution.py:320
  473.6 115.9 %reduce-scatter.12.cloned.1.call-start = ((), (), s32[]{:S(2)}) async-start(), calls=%async_computation.13 | async-start | bytes 1474560 | tf_op jit(solution)/shard_map/reduce_scatter | solution.py:330
  488.3 32.6 %collective-permute-start.28 = (bf16[4,192,768]{2,1,0:T(8,128)(2,1)}, bf16[4,192,768]{2,1,0:T(8,128)(2,1)}, u32[]{:S(2)}, u32[]{:S(2)}) collective-permute-start(bf16[4,192,768]{2,1,0:T(8,128)(2,1)} %fusion.13), channel_id=1, source_target_pairs={{0,2},{1,3},{2,0},{3,1},{4,6},{5,7},{6,4},{7,5},{8,10},{9,11},{10,... | collective-permute-start | bytes 3538952 | tf_op jit(solution)/shard_map/ppermute | solution.py:320
  523.9 129.2 %reduce-scatter.14.cloned.1.call-start = ((), (), s32[]{:S(2)}) async-start(), calls=%async_computation.14 | async-start | bytes 2457600 | tf_op jit(solution)/shard_map/reduce_scatter | solution.py:330
  528.2 28.6 %collective-permute-start.29 = (bf16[768,1536]{1,0:T(8,128)(2,1)}, bf16[768,1536]{1,0:T(8,128)(2,1)}, u32[]{:S(2)}, u32[]{:S(2)}) collective-permute-start(bf16[768,1536]{1,0:T(8,128)(2,1)} %slice.267), channel_id=1, source_target_pairs={{0,16},{16,0},{1,17},{17,1},{2,18},{18,2},{3,19},{19,3},{4,20},{20... | collective-permute-start | bytes 7077896 | tf_op jit(solution)/shard_map/ppermute | solution.py:394
  540.4 49.2 %collective-permute-start.32 = (bf16[4,192,1280]{2,1,0:T(8,128)(2,1)}, bf16[4,192,1280]{2,1,0:T(8,128)(2,1)}, u32[]{:S(2)}, u32[]{:S(2)}) collective-permute-start(bf16[4,192,1280]{2,1,0:T(8,128)(2,1)} %dynamic-slice_bitcast_fusion), channel_id=1, source_target_pairs={{0,2},{1,3},{2,0},{3,1},{4,6},{5,7},{6,4},{7,5},{8,10},{9,11},{10,... | collective-permute-start | bytes 5898248 | tf_op jit(solution)/shard_map/ppermute | solution.py:320
  559.5 28.4 %collective-permute-start.30 = (bf16[384,1536]{1,0:T(8,128)(2,1)S(1)}, bf16[384,1536]{1,0:T(8,128)(2,1)S(1)}, u32[]{:S(2)}, u32[]{:S(2)}) collective-permute-start(bf16[384,1536]{1,0:T(8,128)(2,1)S(1)} %slice.271), channel_id=1, source_target_pairs={{0,1},{1,0},{2,3},{3,2},{4,5},{5,4},{6,7},{7,6},{8,9},{9,8},{10,11... | collective-permute-start | bytes 3538952 | tf_op jit(solution)/shard_map/ppermute | solution.py:397
  606.9 28.3 %collective-permute-start.39 = (bf16[384,1536]{1,0:T(8,128)(2,1)}, bf16[384,1536]{1,0:T(8,128)(2,1)}, u32[]{:S(2)}, u32[]{:S(2)}) collective-permute-start(bf16[384,1536]{1,0:T(8,128)(2,1)} %slice.270), channel_id=1, source_target_pairs={{0,1},{1,0},{2,3},{3,2},{4,5},{5,4},{6,7},{7,6},{8,9},{9,8},{10,11... | collective-permute-start | bytes 3538952 | tf_op jit(solution)/shard_map/ppermute | solution.py:397
  (127 other events, 1286.3 us)
Sparse Core Ops, SparseCore 0:
  22.6 44.9 all-gather.5
  70.1 28.7 all-gather.7
  101.0 36.2 all-gather.9
  158.6 34.9 all-gather.11
  219.2 35.8 all-gather.13
  396.3 34.3 reduce-scatter.5
  433.6 34.2 reduce-scatter.7
  473.7 33.4 reduce-scatter.9
  524.0 27.5 reduce-scatter.11
  607.8 39.8 reduce-scatter.13

commit v7 on v6

--- a/solution.py
+++ b/solution.py
@@ -585,26 +585,15 @@
     grad_output_cols = turn_cols(matmul_tn(gated_low, grad_attn).astype(jnp.bfloat16))
     grad_attended = (grad_gated * gate_open).astype(jnp.bfloat16)
     grad_outgate = (grad_gated * attended * gate_open * (1.0 - gate_open)).astype(jnp.bfloat16)
-    up_held = up_sum(grad_outgate)
-    grad_outgate_w = matmul_tn(after(normed1, up_held), grad_outgate).astype(jnp.bfloat16)
-    part_second_w = jnp.concatenate([grad_outgate_w, grad_output_cols], axis=1)
+    grad_qkv, grad_logit_rows, grad_logit_cols = attend_back(
+        qkv_low, grad_attended, decay_cols, decay_sum, facts_all, heads, head_dim, team, own_rows
+    )
+    up_held = up_sum(grad_qkv)
+    grad_up_w = scatter_line(up_held, count)
+    grad_outgate_w = matmul_tn(after(normed1, grad_qkv), grad_outgate).astype(jnp.bfloat16)
+    part_second_w = jnp.concatenate([grad_outgate_w, after(grad_output_cols, grad_qkv)], axis=1)
     second_sum = scatter_rest(part_second_w, count, index)
-    grad_up_w = scatter_line(up_held, count)
-    grad_qkv, grad_logit_rows, grad_logit_cols = attend_back(
-        qkv_low,
-        after(grad_attended, up_held, part_second_w),
-        decay_cols,
-        decay_sum,
-        facts_all,
-        heads,
-        head_dim,
-        team,
-        own_rows,
-    )
-    second_held = second_sum(grad_qkv)
-    grad_qkv = after(grad_qkv, grad_gate_w, second_held, grad_up_w)
-    sum_second = scatter_line(second_held, count)
-    layer_out = (residual + team_sum(after(part_out, grad_qkv))).astype(jnp.bfloat16)
+    grad_qkv = after(grad_qkv, grad_gate_w, part_second_w)
     grad_decay = jnp.transpose(grad_logit_rows, (0, 2, 1)) - grad_logit_cols
     grad_log_forget = jnp.einsum(
         "bij,bhi->bjh", chain_float, grad_decay, precision=lax.Precision.HIGHEST
@@ -625,12 +614,16 @@
     )
     grad_first = jnp.concatenate([grad_qkv, grad_forget_low], axis=1)
     part_first_w = matmul_tn(normed1, grad_first).astype(jnp.bfloat16)
-    first_sum = scatter_rest(after(part_first_w, bias_near), count, index)
-    part_normed1 = matmul_nt(after(grad_first, part_first_w), first) + matmul_nt(
+    second_held = second_sum(part_first_w)
+    sum_second = scatter_line(second_held, count)
+    part_first_w = after(part_first_w, bias_near, second_held)
+    first_sum = scatter_rest(part_first_w, count, index)
+    part_normed1 = matmul_nt(after(grad_first, part_first_w, grad_up_w), first) + matmul_nt(
         grad_outgate, outgate_w
     )
     down_own = both_cores(after(grad_down, part_first_w))
     grad_bias = sum_far(after(bias_near, part_first_w), count, reps)
+    layer_out = (residual + team_sum(after(part_out, grad_qkv))).astype(jnp.bfloat16)
     first_held = first_sum(grad_bias, layer_out, down_own, sum_second)
     grad_normed1 = team_sum(after(part_normed1, first_held))
     tokens_grad = grad_resid + norm_back(grad_normed1 * gain_one, scaled1, inverse1)

time: 704 us -> 721 us (1.024)
  local copies, waits for them, and re-layouts: 97.8 us -> 108 us
    ppermute x5, waiting for transfers between devices: 25.6 us -> 34.6 us  [scatter_rest(): lax.ppermute(pick(halves, 1 - at, 1), 'shard', swap_pairs(count, step))]
    ppermute x17, waiting for transfers between devices: 161 us -> 152 us  [swap_side(): return lax.ppermute(values, 'shard', side_pairs)]
    unnamed x209 -> x197, local copies, waits for them, and re-layouts: 21.7 us -> 20.4 us
    another operation x35 -> x33, other arithmetic: 23.1 us -> 22.5 us  [both(): jnp.stack([jnp.where(low_first, mine, other), jnp.where(low_first, other,...]
  transfers between devices with their start and end apart: 58 -> 58, of which waited for: 25 -> 27; matrix products, arithmetic and copies ran while one was open for 36% -> 38% of each run, Pallas kernels for 6% -> 6%
where the time goes in v7:
time: 721 us; the launch traced here: 713 us
  waiting for transfers between devices  259 us (36%)
  matrix products  138 us (19%)
  other arithmetic  114 us (16%)
  local copies, waits for them, and re-layouts  108 us (15%)
  Pallas kernels  42.8 us (6%)
  starting transfers between devices  35.3 us (5%)
  between operations  16.2 us (2%)
    ppermute x17, waiting for transfers between devices, swap_side(): return lax.ppermute(values, 'shard', side_pairs)  152 us
    dot_general x7, matrix products, matmul(): return jnp.dot(left_side, right_side, preferred_element_type=jnp.float32)  50.7 us
    dot_general x6, matrix products, matmul_tn(): lax.dot_general(left_side, right_side, (((0,), (0,)), ((), ())), preferre...  42 us
    dot_general x6, matrix products, matmul_nt(): lax.dot_general(left_side, right_side, (((1,), (1,)), ((), ())), preferre...  41.3 us
    ppermute x5, waiting for transfers between devices, scatter_rest(): lax.ppermute(pick(halves, 1 - at, 1), 'shard', swap_pairs(count, step))  34.6 us
    all_gather x5, waiting for transfers between devices, gather_line(): lax.all_gather(block, 'shard', axis=0, tiled=True, axis_index_groups=line...  31.6 us
    ppermute x5, waiting for transfers between devices, gather_rest(): other = lax.ppermute(held, 'shard', swap_pairs(count, step))  24.1 us
    pallas_call x1, Pallas kernels, attend_back(): pl.pallas_call(body, grid_spec=pltpu.PrefetchScalarGridSpec(num_scalar_pr...  24.1 us
  transfers between devices with their start and end apart: 58, of which 27 were waited for; matrix products, arithmetic and copies ran while one was open for 38% of the time, Pallas kernels for 6%

profile of v7, /device:TPU:0, one launch (start us, length us, event | category | flops | bytes accessed | tf_op | source)
XLA Modules:
  0.0 713.1 jit_solution(1223016300290971932)
XLA Ops:
  15.7 5.8 collective-permute-done
  30.9 11.2 %collective-permute-done.1 = bf16[96,2816]{1,0:T(8,128)(2,1)S(1)} collective-permute-done((bf16[96,2816]{1,0:T(8,128)(2,1)S(1)}, bf16[96,2816]{1,0:T(8,128)(2,1)S(1)}, u32[]{:S(2)}, u32[]{:S(2)}) %collective-permute-start.1) | collective-permute-done | bytes 540704 | tf_op jit(solution)/shard_map/ppermute | solution.py:397
  44.3 23.4 %all-gather.6.cloned.1.call-done = bf16[768,1280]{1,0:T(8,128)(2,1)} async-done(((bf16[192,1280]{1,0:T(8,128)(2,1)}), bf16[768,1280]{1,0:T(8,128)(2,1)}) %all-gather.6.cloned.1.call-update) | async-done | bytes 1966096 | tf_op jit(solution)/shard_map/all_gather | solution.py:296
  77.1 20.5 %collective-permute-done.8 = bf16[384,1536]{1,0:T(8,128)(2,1)S(1)} collective-permute-done((bf16[384,1536]{1,0:T(8,128)(2,1)}, bf16[384,1536]{1,0:T(8,128)(2,1)S(1)}, u32[]{:S(2)}, u32[]{:S(2)}) %collective-permute-start.8) | collective-permute-done | bytes 1179680 | tf_op jit(solution)/shard_map/ppermute | solution.py:397
  101.6 12.0 %collective-permute-done.6 = bf16[4,192,1280]{2,1,0:T(8,128)(2,1)} collective-permute-done((bf16[4,192,1280]{2,1,0:T(8,128)(2,1)}, bf16[4,192,1280]{2,1,0:T(8,128)(2,1)}, u32[]{:S(2)}, u32[]{:S(2)}) %collective-permute-start.6) | collective-permute-done | bytes 1966112 | tf_op jit(solution)/shard_map/ppermute | solution.py:303
  121.1 8.0 %broadcast_multiply_fusion = (f32[1536,1536]{1,0:T(8,128)}, bf16[1536,1536]{1,0:T(8,128)(2,1)}) fusion(f32[1536]{0:T(1024)S(1)} %add_rsqrt_fusion, bf16[768,1536]{1,0:T(8,128)(2,1)} %collective-permute-done.3, bf16[768,1536]{1,0:T(8,128)(2,1)S(1)} %pad_maximum_fusion.7, f32[1536]{0:T(1024)S(1)} %get-tuple-element.139), kind=kLoop, calls=%fused_computation.22 | loop fusion | flops 16515072 | bytes 18886656 | tf_op jit(solution)/shard_map/mul | solution.py:35
  129.1 8.2 %all-gather.10.cloned.1.call-done = bf16[768,1024]{1,0:T(8,128)(2,1)} async-done(((bf16[192,1024]{1,0:T(8,128)(2,1)}), bf16[768,1024]{1,0:T(8,128)(2,1)}) %all-gather.10.cloned.1.call-update) | async-done | bytes 1572880 | tf_op jit(solution)/shard_map/all_gather | solution.py:296
  137.4 10.4 %convolution_convert_fusion.1.qkv_ref = bf16[1536,1152]{1,0:T(8,128)(2,1)} fusion(bf16[1536,1536]{1,0:T(8,128)(2,1)} %get-tuple-element.79, bf16[1536,1280]{1,0:T(8,128)(2,1)} %bitcast.350), kind=kOutput, calls=%fused_computation.5 | convolution fusion | flops 5437587456 | bytes 11796480 | tf_op jit(solution)/shard_map/dot_general | solution.py:244
  160.0 18.7 %attend.1 = f32[1536,384]{1,0:T(8,128)} custom-call(s32[4,8]{1,0:T(4,128)} %pad_add_fusion.1.facts_ref, bf16[1536,1152]{1,0:T(8,128)(2,1)} %convolution_convert_fusion.1.qkv_ref, f32[4,384,6]{2,1,0:T(8,128)} %bitcast.376, f32[4,6,384]{2,1,0:T(8,128)} %copy-done.60), custom_call_target="tpu_custom_call" | custom-call | flops 1811939328 | bytes 9437184 | tf_op jit(solution)/shard_map/attend/pallas_call | solution.py:129
  183.8 6.6 fusion.8
  217.7 23.4 %collective-permute-done.14 = bf16[384,1536]{1,0:T(8,128)(2,1)} collective-permute-done((bf16[384,1536]{1,0:T(8,128)(2,1)}, bf16[384,1536]{1,0:T(8,128)(2,1)}, u32[]{:S(2)}, u32[]{:S(2)}) %collective-permute-start.14) | collective-permute-done | bytes 1179680 | tf_op jit(solution)/shard_map/ppermute | solution.py:397
  243.5 6.4 collective-permute-done.15
  256.3 22.4 %collective-permute-done.16 = bf16[384,1536]{1,0:T(8,128)(2,1)} collective-permute-done((bf16[384,1536]{1,0:T(8,128)(2,1)}, bf16[384,1536]{1,0:T(8,128)(2,1)}, u32[]{:S(2)}, u32[]{:S(2)}) %collective-permute-start.16) | collective-permute-done | bytes 1179680 | tf_op jit(solution)/shard_map/ppermute | solution.py:397
  282.5 5.7 collective-permute-done.18
  288.8 7.2 %fusion.67 = f32[1536,1024]{1,0:T(8,128)} fusion(bf16[1536,1536]{1,0:T(8,128)(2,1)S(1)} %bitcast.402, bf16[1024,1536]{1,0:T(8,128)(2,1)S(1)} %bitcast.380), kind=kOutput, calls=%fused_computation.292 | convolution fusion | flops 4831838208 | bytes 14155776 | tf_op jit(solution)/shard_map/dot_general | solution.py:254
  297.8 6.9 fusion.68
  304.7 11.5 %multiply_convert_fusion.1 = (bf16[1536,1024]{1,0:T(8,128)(2,1)}, bf16[1536,1024]{1,0:T(8,128)(2,1)S(1)}, bf16[1536,1024]{1,0:T(8,128)(2,1)S(1)}) fusion(f32[1536,1024]{1,0:T(8,128)} %fusion.68, f32[1536,1024]{1,0:T(8,128)} %fusion.67, bf16[1536,1536]{1,0:T(8,128)(2,1)S(1)} %pad_maximum_fusion, bf16[1536,1024]{1,0:T(8,128)(2,1)S(1)} %bitcast.388), kind=kOutput, calls=%fused_computation.6 | convolution fusion | flops 4855431168 | bytes 29884416 | tf_op jit(solution)/shard_map/dot_general | solution.py:244
  316.2 7.8 %fusion.69 = f32[1536,1536]{1,0:T(8,128)} fusion(bf16[1536,1024]{1,0:T(8,128)(2,1)S(1)} %get-tuple-element.157, bf16[1536,1024]{1,0:T(8,128)(2,1)S(1)} %bitcast.385), kind=kOutput, calls=%fused_computation.294 | convolution fusion | flops 4831838208 | bytes 15728640 | tf_op jit(solution)/shard_map/dot_general | solution.py:254
  324.0 7.9 %convolution_add_fusion.1 = f32[1536,1536]{1,0:T(8,128)S(1)} fusion(f32[1536,1536]{1,0:T(8,128)} %fusion.69, bf16[1536,1024]{1,0:T(8,128)(2,1)S(1)} %get-tuple-element.158, bf16[1536,1024]{1,0:T(8,128)(2,1)S(1)} %bitcast.389), kind=kOutput, calls=%fused_computation.3 | convolution fusion | flops 4834197504 | bytes 25165824 | tf_op jit(solution)/shard_map/dot_general | solution.py:254
  337.2 8.8 %convolution_convert_fusion.3 = bf16[1024,1536]{1,0:T(8,128)(2,1)S(1)} fusion(bf16[1536,1024]{1,0:T(8,128)(2,1)} %get-tuple-element.73, bf16[1536,1536]{1,0:T(8,128)(2,1)} %constant_dynamic-update-slice_fusion), kind=kOutput, calls=%fused_computation.28 | convolution fusion | flops 4833411072 | bytes 11010048 | tf_op jit(solution)/shard_map/dot_general | solution.py:248
  358.9 18.9 %collective-permute-done.20 = bf16[384,1536]{1,0:T(8,128)(2,1)S(1)} collective-permute-done((bf16[384,1536]{1,0:T(8,128)(2,1)S(1)}, bf16[384,1536]{1,0:T(8,128)(2,1)S(1)}, u32[]{:S(2)}, u32[]{:S(2)}) %collective-permute-start.20) | collective-permute-done | bytes 1179680 | tf_op jit(solution)/shard_map/ppermute | solution.py:397
  383.5 6.6 convolution_convert_fusion.2
  391.7 10.2 %fusion.70 = f32[1536,1536]{1,0:T(8,128)} fusion(bf16[1536,1024]{1,0:T(8,128)(2,1)} %get-tuple-element.73, bf16[1024,1536]{1,0:T(8,128)(2,1)} %bitcast.381), kind=kOutput, calls=%fused_computation.295 | convolution fusion | flops 4831838208 | bytes 15728640 | tf_op jit(solution)/shard_map/dot_general | solution.py:244
  401.9 14.9 %collective-permute-done.23 = bf16[4,192,1024]{2,1,0:T(8,128)(2,1)} collective-permute-done((bf16[4,192,1024]{2,1,0:T(8,128)(2,1)}, bf16[4,192,1024]{2,1,0:T(8,128)(2,1)}, u32[]{:S(2)}, u32[]{:S(2)}) %collective-permute-start.23) | collective-permute-done | bytes 1572896 | tf_op jit(solution)/shard_map/ppermute | solution.py:320
  432.9 6.0 convolution_convert_fusion.5
  449.1 6.6 multiply_convert_fusion.4
  455.7 24.1 %attend_back.1 = (bf16[1536,1152]{1,0:T(8,128)(2,1)}, f32[4,384,6]{2,1,0:T(8,128)}, f32[4,6,384]{2,1,0:T(8,128)}) custom-call(s32[4,8]{1,0:T(4,128)} %pad_add_fusion.1.facts_ref, bf16[1536,1152]{1,0:T(8,128)(2,1)} %convolution_convert_fusion.1.qkv_ref, bf16[1536,384]{1,0:T(8,128)(2,1)} %get-tuple-element.162.grad_ref, f32[4,384,6]{2,1,0:T(8,128)} %bitcast.377, ...), custom_call_target="tpu_custom_call" | custom-call | flops 18119393280 | bytes 8257536 | tf_op jit(solution)/shard_map/attend_back/pallas_call | solution.py:208
  525.8 9.7 %convolution_convert_fusion = bf16[1536,1280]{1,0:T(8,128)(2,1)} fusion(bf16[1536,1536]{1,0:T(8,128)(2,1)} %get-tuple-element.79, bf16[1536,128]{1,0:T(8,128)(2,1)S(1)} %copy-done.46, bf16[1536,1152]{1,0:T(8,128)(2,1)S(1)} %copy-done.28), kind=kOutput, calls=%fused_computation.4 | convolution fusion | flops 6049628160 | bytes 12582912 | tf_op jit(solution)/shard_map/dot_general | solution.py:248
  537.7 15.1 %collective-permute-done.30 = bf16[4,192,768]{2,1,0:T(8,128)(2,1)S(1)} collective-permute-done((bf16[4,192,768]{2,1,0:T(8,128)(2,1)S(1)}, bf16[4,192,768]{2,1,0:T(8,128)(2,1)S(1)}, u32[]{:S(2)}, u32[]{:S(2)}) %collective-permute-start.30) | collective-permute-done | bytes 1179680 | tf_op jit(solution)/shard_map/ppermute | solution.py:320
  573.1 6.3 fusion.71
  585.0 14.7 %collective-permute-done.28 = bf16[384,1536]{1,0:T(8,128)(2,1)S(1)} collective-permute-done((bf16[384,1536]{1,0:T(8,128)(2,1)S(1)}, bf16[384,1536]{1,0:T(8,128)(2,1)S(1)}, u32[]{:S(2)}, u32[]{:S(2)}) %collective-permute-start.28) | collective-permute-done | bytes 1179680 | tf_op jit(solution)/shard_map/ppermute | solution.py:397
  625.7 25.6 %collective-permute-done.39 = bf16[384,1536]{1,0:T(8,128)(2,1)} collective-permute-done((bf16[384,1536]{1,0:T(8,128)(2,1)}, bf16[384,1536]{1,0:T(8,128)(2,1)}, u32[]{:S(2)}, u32[]{:S(2)}) %collective-permute-start.39) | collective-permute-done | bytes 1179680 | tf_op jit(solution)/shard_map/ppermute | solution.py:397
  (495 shorter events, 305.3 us)
Async XLA Ops:
  7.2 60.4 %all-gather.6.cloned.1.call-start = ((), (), s32[]{:S(2)}) async-start(), calls=%async_computation.5 | async-start | bytes 2457600 | tf_op jit(solution)/shard_map/all_gather | solution.py:296
  22.5 78.0 %all-gather.8.cloned.1.call-start = ((), (), s32[]{:S(2)}) async-start(), calls=%async_computation.6 | async-start | bytes 1474560 | tf_op jit(solution)/shard_map/all_gather | solution.py:296
  42.4 29.9 %collective-permute-start.2 = (bf16[384,1536]{1,0:T(8,128)(2,1)S(1)}, bf16[384,1536]{1,0:T(8,128)(2,1)}, u32[]{:S(2)}, u32[]{:S(2)}) collective-permute-start(bf16[384,1536]{1,0:T(8,128)(2,1)S(1)} %copy-done.48), channel_id=1, source_target_pairs={{0,1},{1,0},{2,3},{3,2},{4,5},{5,4},{6,7},{7,6},{8,9},{9,8},{10,11... | collective-permute-start | bytes 3538952 | tf_op jit(solution)/shard_map/ppermute | solution.py:397
  67.6 46.0 %collective-permute-start.6 = (bf16[4,192,1280]{2,1,0:T(8,128)(2,1)}, bf16[4,192,1280]{2,1,0:T(8,128)(2,1)}, u32[]{:S(2)}, u32[]{:S(2)}) collective-permute-start(bf16[4,192,1280]{2,1,0:T(8,128)(2,1)} %bitcast.391), channel_id=1, source_target_pairs={{0,2},{1,3},{2,0},{3,1},{4,6},{5,7},{6,4},{7,5},{8,10},{9,11},{10,... | collective-permute-start | bytes 5898248 | tf_op jit(solution)/shard_map/ppermute | solution.py:303
  69.9 67.4 %all-gather.10.cloned.1.call-start = ((), (), s32[]{:S(2)}) async-start(), calls=%async_computation.7 | async-start | bytes 1966080 | tf_op jit(solution)/shard_map/all_gather | solution.py:296
  70.1 27.5 %collective-permute-start.8 = (bf16[384,1536]{1,0:T(8,128)(2,1)}, bf16[384,1536]{1,0:T(8,128)(2,1)S(1)}, u32[]{:S(2)}, u32[]{:S(2)}) collective-permute-start(bf16[384,1536]{1,0:T(8,128)(2,1)} %param.31), channel_id=1, source_target_pairs={{0,1},{1,0},{2,3},{3,2},{4,5},{5,4},{6,7},{7,6},{8,9},{9,8},{10,11... | collective-permute-start | bytes 3538952 | tf_op jit(solution)/shard_map/ppermute | solution.py:397
  74.1 42.9 %collective-permute-start.3 = (bf16[768,1536]{1,0:T(8,128)(2,1)S(1)}, bf16[768,1536]{1,0:T(8,128)(2,1)}, u32[]{:S(2)}, u32[]{:S(2)}) collective-permute-start(bf16[768,1536]{1,0:T(8,128)(2,1)S(1)} %pad_maximum_fusion.7), channel_id=1, source_target_pairs={{0,16},{16,0},{1,17},{17,1},{2,18},{18,2},{3,19},{19,3},{4,20},{20... | collective-permute-start | bytes 7077896 | tf_op jit(solution)/shard_map/ppermute | solution.py:394
  100.5 97.1 %all-gather.12.cloned.1.call-start = ((), (), s32[]{:S(2)}) async-start(), calls=%async_computation.8 | async-start | bytes 1966080 | tf_op jit(solution)/shard_map/all_gather | solution.py:296
  101.0 46.8 %collective-permute-start.10 = (bf16[4,192,768]{2,1,0:T(8,128)(2,1)}, bf16[4,192,768]{2,1,0:T(8,128)(2,1)}, u32[]{:S(2)}, u32[]{:S(2)}) collective-permute-start(bf16[4,192,768]{2,1,0:T(8,128)(2,1)} %bitcast.399), channel_id=1, source_target_pairs={{0,2},{1,3},{2,0},{3,1},{4,6},{5,7},{6,4},{7,5},{8,10},{9,11},{10,... | collective-permute-start | bytes 3538952 | tf_op jit(solution)/shard_map/ppermute | solution.py:303
  137.4 115.6 %all-gather.14.cloned.1.call-start = ((), (), s32[]{:S(2)}) async-start(), calls=%async_computation.9 | async-start | bytes 1966080 | tf_op jit(solution)/shard_map/all_gather | solution.py:296
  147.8 46.5 %collective-permute-start.9 = (bf16[768,1536]{1,0:T(8,128)(2,1)}, bf16[768,1536]{1,0:T(8,128)(2,1)}, u32[]{:S(2)}, u32[]{:S(2)}) collective-permute-start(bf16[768,1536]{1,0:T(8,128)(2,1)} %pad_maximum_fusion.8), channel_id=1, source_target_pairs={{0,16},{16,0},{1,17},{17,1},{2,18},{18,2},{3,19},{19,3},{4,20},{20... | collective-permute-start | bytes 7077896 | tf_op jit(solution)/shard_map/ppermute | solution.py:394
  151.9 30.1 %collective-permute-start.11 = (bf16[2,384,384]{2,1,0:T(8,128)(2,1)}, bf16[2,384,384]{2,1,0:T(8,128)(2,1)}, u32[]{:S(2)}, u32[]{:S(2)}) collective-permute-start(bf16[2,384,384]{2,1,0:T(8,128)(2,1)} %dynamic-slice_bitcast_fusion.5), channel_id=1, source_target_pairs={{0,1},{1,0},{2,3},{3,2},{4,5},{5,4},{6,7},{7,6},{8,9},{9,8},{10,11... | collective-permute-start | bytes 1769480 | tf_op jit(solution)/shard_map/ppermute | solution.py:397
  158.5 39.0 %collective-permute-start.7 = (bf16[4,192,1024]{2,1,0:T(8,128)(2,1)}, bf16[4,192,1024]{2,1,0:T(8,128)(2,1)}, u32[]{:S(2)}, u32[]{:S(2)}) collective-permute-start(bf16[4,192,1024]{2,1,0:T(8,128)(2,1)} %bitcast.393), channel_id=1, source_target_pairs={{0,2},{1,3},{2,0},{3,1},{4,6},{5,7},{6,4},{7,5},{8,10},{9,11},{10,... | collective-permute-start | bytes 4718600 | tf_op jit(solution)/shard_map/ppermute | solution.py:303
  212.8 28.4 %collective-permute-start.14 = (bf16[384,1536]{1,0:T(8,128)(2,1)}, bf16[384,1536]{1,0:T(8,128)(2,1)}, u32[]{:S(2)}, u32[]{:S(2)}) collective-permute-start(bf16[384,1536]{1,0:T(8,128)(2,1)} %slice.273), channel_id=1, source_target_pairs={{0,1},{1,0},{2,3},{3,2},{4,5},{5,4},{6,7},{7,6},{8,9},{9,8},{10,11... | collective-permute-start | bytes 3538952 | tf_op jit(solution)/shard_map/ppermute | solution.py:397
  213.4 36.5 %collective-permute-start.15 = (bf16[4,192,1024]{2,1,0:T(8,128)(2,1)}, bf16[4,192,1024]{2,1,0:T(8,128)(2,1)}, u32[]{:S(2)}, u32[]{:S(2)}) collective-permute-start(bf16[4,192,1024]{2,1,0:T(8,128)(2,1)} %bitcast.395), channel_id=1, source_target_pairs={{0,2},{1,3},{2,0},{3,1},{4,6},{5,7},{6,4},{7,5},{8,10},{9,11},{10,... | collective-permute-start | bytes 4718600 | tf_op jit(solution)/shard_map/ppermute | solution.py:303
  214.7 218.2 %reduce-scatter.6.cloned.1.call-start = ((), (), s32[]{:S(2)}) async-start(), calls=%async_computation.10 | async-start | bytes 1966080 | tf_op jit(solution)/shard_map/reduce_scatter | solution.py:330
  253.0 35.3 %collective-permute-start.18 = (bf16[4,128,1536]{2,1,0:T(8,128)(2,1)}, bf16[4,128,1536]{2,1,0:T(8,128)(2,1)S(1)}, u32[]{:S(2)}, u32[]{:S(2)}) collective-permute-start(bf16[4,128,1536]{2,1,0:T(8,128)(2,1)} %bitcast.397), channel_id=1, source_target_pairs={{0,2},{1,3},{2,0},{3,1},{4,6},{5,7},{6,4},{7,5},{8,10},{9,11},{10,... | collective-permute-start | bytes 4718600 | tf_op jit(solution)/shard_map/ppermute | solution.py:303
  346.2 37.3 %collective-permute-start.21 = (bf16[4,128,1536]{2,1,0:T(8,128)(2,1)S(1)}, bf16[4,128,1536]{2,1,0:T(8,128)(2,1)S(1)}, u32[]{:S(2)}, u32[]{:S(2)}) collective-permute-start(bf16[4,128,1536]{2,1,0:T(8,128)(2,1)S(1)} %dynamic-slice_bitcast_fusion.3), channel_id=1, source_target_pairs={{0,2},{1,3},{2,0},{3,1},{4,6},{5,7},{6,4},{7,5},{8,10},{9,11},{10,... | collective-permute-start | bytes 4718600 | tf_op jit(solution)/shard_map/ppermute | solution.py:320
  349.7 28.0 %collective-permute-start.20 = (bf16[384,1536]{1,0:T(8,128)(2,1)S(1)}, bf16[384,1536]{1,0:T(8,128)(2,1)S(1)}, u32[]{:S(2)}, u32[]{:S(2)}) collective-permute-start(bf16[384,1536]{1,0:T(8,128)(2,1)S(1)} %slice.272), channel_id=1, source_target_pairs={{0,1},{1,0},{2,3},{3,2},{4,5},{5,4},{6,7},{7,6},{8,9},{9,8},{10,11... | collective-permute-start | bytes 3538952 | tf_op jit(solution)/shard_map/ppermute | solution.py:397
  357.2 59.6 %collective-permute-start.23 = (bf16[4,192,1024]{2,1,0:T(8,128)(2,1)}, bf16[4,192,1024]{2,1,0:T(8,128)(2,1)}, u32[]{:S(2)}, u32[]{:S(2)}) collective-permute-start(bf16[4,192,1024]{2,1,0:T(8,128)(2,1)} %dynamic-slice_bitcast_fusion.2), channel_id=1, source_target_pairs={{0,2},{1,3},{2,0},{3,1},{4,6},{5,7},{6,4},{7,5},{8,10},{9,11},{10,... | collective-permute-start | bytes 4718600 | tf_op jit(solution)/shard_map/ppermute | solution.py:320
  382.6 37.4 %collective-permute-start.22 = (bf16[384,1536]{1,0:T(8,128)(2,1)}, bf16[384,1536]{1,0:T(8,128)(2,1)}, u32[]{:S(2)}, u32[]{:S(2)}) collective-permute-start(bf16[384,1536]{1,0:T(8,128)(2,1)} %fusion.61), channel_id=1, source_target_pairs={{0,1},{1,0},{2,3},{3,2},{4,5},{5,4},{6,7},{7,6},{8,9},{9,8},{10,11... | collective-permute-start | bytes 3538952 | tf_op jit(solution)/shard_map/ppermute | solution.py:397
  391.7 128.3 %reduce-scatter.8.cloned.1.call-start = ((), (), s32[]{:S(2)}) async-start(), calls=%async_computation.11 | async-start | bytes 1966080 | tf_op jit(solution)/shard_map/reduce_scatter | solution.py:330
  425.9 58.6 %collective-permute-start.31 = (bf16[4,192,1024]{2,1,0:T(8,128)(2,1)}, bf16[4,192,1024]{2,1,0:T(8,128)(2,1)}, u32[]{:S(2)}, u32[]{:S(2)}) collective-permute-start(bf16[4,192,1024]{2,1,0:T(8,128)(2,1)} %dynamic-slice_bitcast_fusion.1), channel_id=1, source_target_pairs={{0,2},{1,3},{2,0},{3,1},{4,6},{5,7},{6,4},{7,5},{8,10},{9,11},{10,... | collective-permute-start | bytes 4718600 | tf_op jit(solution)/shard_map/ppermute | solution.py:320
  426.5 141.0 %reduce-scatter.10.cloned.1.call-start = ((), (), s32[]{:S(2)}) async-start(), calls=%async_computation.12 | async-start | bytes 1966080 | tf_op jit(solution)/shard_map/reduce_scatter | solution.py:330
  448.9 39.5 %collective-permute-start.25 = (bf16[384,2,384]{2,0,1:T(8,128)(2,1)}, bf16[384,2,384]{2,0,1:T(8,128)(2,1)}, u32[]{:S(2)}, u32[]{:S(2)}) collective-permute-start(bf16[384,2,384]{2,0,1:T(8,128)(2,1)} %bitcast.336), channel_id=1, source_target_pairs={{0,16},{16,0},{1,17},{17,1},{2,18},{18,2},{3,19},{19,3},{4,20},{20... | collective-permute-start | bytes 1769480 | tf_op jit(solution)/shard_map/ppermute | solution.py:394
  488.3 117.3 %reduce-scatter.12.cloned.1.call-start = ((), (), s32[]{:S(2)}) async-start(), calls=%async_computation.13 | async-start | bytes 1474560 | tf_op jit(solution)/shard_map/reduce_scatter | solution.py:330
  524.2 43.3 %collective-permute-start.27 = (bf16[768,1536]{1,0:T(8,128)(2,1)}, bf16[768,1536]{1,0:T(8,128)(2,1)}, u32[]{:S(2)}, u32[]{:S(2)}) collective-permute-start(bf16[768,1536]{1,0:T(8,128)(2,1)} %slice.267), channel_id=1, source_target_pairs={{0,16},{16,0},{1,17},{17,1},{2,18},{18,2},{3,19},{19,3},{4,20},{20... | collective-permute-start | bytes 7077896 | tf_op jit(solution)/shard_map/ppermute | solution.py:394
  524.3 28.4 %collective-permute-start.30 = (bf16[4,192,768]{2,1,0:T(8,128)(2,1)S(1)}, bf16[4,192,768]{2,1,0:T(8,128)(2,1)S(1)}, u32[]{:S(2)}, u32[]{:S(2)}) collective-permute-start(bf16[4,192,768]{2,1,0:T(8,128)(2,1)S(1)} %dynamic-slice_bitcast_fusion.4), channel_id=1, source_target_pairs={{0,2},{1,3},{2,0},{3,1},{4,6},{5,7},{6,4},{7,5},{8,10},{9,11},{10,... | collective-permute-start | bytes 3538952 | tf_op jit(solution)/shard_map/ppermute | solution.py:320
  562.6 43.0 %collective-permute-start.32 = (bf16[4,192,1280]{2,1,0:T(8,128)(2,1)}, bf16[4,192,1280]{2,1,0:T(8,128)(2,1)}, u32[]{:S(2)}, u32[]{:S(2)}) collective-permute-start(bf16[4,192,1280]{2,1,0:T(8,128)(2,1)} %dynamic-slice_bitcast_fusion), channel_id=1, source_target_pairs={{0,2},{1,3},{2,0},{3,1},{4,6},{5,7},{6,4},{7,5},{8,10},{9,11},{10,... | collective-permute-start | bytes 5898248 | tf_op jit(solution)/shard_map/ppermute | solution.py:320
  565.7 103.5 %reduce-scatter.14.cloned.1.call-start = ((), (), s32[]{:S(2)}) async-start(), calls=%async_computation.14 | async-start | bytes 2457600 | tf_op jit(solution)/shard_map/reduce_scatter | solution.py:330
  571.7 28.1 %collective-permute-start.28 = (bf16[384,1536]{1,0:T(8,128)(2,1)S(1)}, bf16[384,1536]{1,0:T(8,128)(2,1)S(1)}, u32[]{:S(2)}, u32[]{:S(2)}) collective-permute-start(bf16[384,1536]{1,0:T(8,128)(2,1)S(1)} %slice.271), channel_id=1, source_target_pairs={{0,1},{1,0},{2,3},{3,2},{4,5},{5,4},{6,7},{7,6},{8,9},{9,8},{10,11... | collective-permute-start | bytes 3538952 | tf_op jit(solution)/shard_map/ppermute | solution.py:397
  623.0 28.3 %collective-permute-start.39 = (bf16[384,1536]{1,0:T(8,128)(2,1)}, bf16[384,1536]{1,0:T(8,128)(2,1)}, u32[]{:S(2)}, u32[]{:S(2)}) collective-permute-start(bf16[384,1536]{1,0:T(8,128)(2,1)} %slice.270), channel_id=1, source_target_pairs={{0,1},{1,0},{2,3},{3,2},{4,5},{5,4},{6,7},{7,6},{8,9},{9,8},{10,11... | collective-permute-start | bytes 3538952 | tf_op jit(solution)/shard_map/ppermute | solution.py:397
  (121 other events, 1203.4 us)
Sparse Core Ops, SparseCore 0:
  22.6 44.9 all-gather.5
  70.1 28.7 all-gather.7
  101.0 36.2 all-gather.9
  139.3 35.8 all-gather.11
  214.8 35.8 all-gather.13
  391.8 34.3 reduce-scatter.5
  429.1 34.2 reduce-scatter.7
  488.4 33.2 reduce-scatter.9
  565.8 28.0 reduce-scatter.11
  624.4 40.4 reduce-scatter.13

commit v8 on v7

--- a/solution.py
+++ b/solution.py
@@ -590,10 +590,7 @@
     )
     up_held = up_sum(grad_qkv)
     grad_up_w = scatter_line(up_held, count)
-    grad_outgate_w = matmul_tn(after(normed1, grad_qkv), grad_outgate).astype(jnp.bfloat16)
-    part_second_w = jnp.concatenate([grad_outgate_w, after(grad_output_cols, grad_qkv)], axis=1)
-    second_sum = scatter_rest(part_second_w, count, index)
-    grad_qkv = after(grad_qkv, grad_gate_w, part_second_w)
+    grad_qkv = after(grad_qkv, grad_gate_w)
     grad_decay = jnp.transpose(grad_logit_rows, (0, 2, 1)) - grad_logit_cols
     grad_log_forget = jnp.einsum(
         "bij,bhi->bjh", chain_float, grad_decay, precision=lax.Precision.HIGHEST
@@ -614,23 +611,24 @@
     )
     grad_first = jnp.concatenate([grad_qkv, grad_forget_low], axis=1)
     part_first_w = matmul_tn(normed1, grad_first).astype(jnp.bfloat16)
-    second_held = second_sum(part_first_w)
-    sum_second = scatter_line(second_held, count)
-    part_first_w = after(part_first_w, bias_near, second_held)
-    first_sum = scatter_rest(part_first_w, count, index)
-    part_normed1 = matmul_nt(after(grad_first, part_first_w, grad_up_w), first) + matmul_nt(
+    first_sum = scatter_rest(after(part_first_w, bias_near), count, index)
+    grad_outgate_w = matmul_tn(after(normed1, part_first_w), grad_outgate).astype(jnp.bfloat16)
+    part_second_w = jnp.concatenate([grad_outgate_w, grad_output_cols], axis=1)
+    second_sum = scatter_rest(part_second_w, count, index)
+    down_own = both_cores(after(grad_down, part_first_w))
+    grad_bias = sum_far(after(bias_near, part_second_w), count, reps)
+    layer_out = (residual + team_sum(after(part_out, grad_qkv))).astype(jnp.bfloat16)
+    first_held = first_sum(grad_bias, layer_out, down_own, part_second_w)
+    part_normed1 = matmul_nt(after(grad_first, first_held, grad_up_w), first) + matmul_nt(
         grad_outgate, outgate_w
     )
-    down_own = both_cores(after(grad_down, part_first_w))
-    grad_bias = sum_far(after(bias_near, part_first_w), count, reps)
-    layer_out = (residual + team_sum(after(part_out, grad_qkv))).astype(jnp.bfloat16)
-    first_held = first_sum(grad_bias, layer_out, down_own, sum_second)
-    grad_normed1 = team_sum(after(part_normed1, first_held))
+    second_held = second_sum(first_held)
+    sum_first = scatter_line(first_held, count)
+    grad_normed1 = after(team_sum(after(part_normed1, second_held)), sum_first)
     tokens_grad = grad_resid + norm_back(grad_normed1 * gain_one, scaled1, inverse1)
-    sum_first = scatter_line(first_held, count)
-    gate_own = own_of(after(grad_gate_w, grad_normed1))
+    sum_second = after(scatter_line(second_held, count), sum_first)
+    gate_own = own_of(after(grad_gate_w, part_normed1))
     grad_up_w = after(grad_up_w, grad_normed1)
-    sum_second = after(sum_second, grad_normed1)
 
     def whole_cols(own):
         parts = own.shape[3] // quarter

time: 721 us -> 723 us (level)
  other arithmetic: 114 us -> 124 us
  local copies, waits for them, and re-layouts: 108 us -> 100 us
    ppermute x17, waiting for transfers between devices: 152 us -> 130 us  [swap_side(): return lax.ppermute(values, 'shard', side_pairs)]
    ppermute x3, waiting for transfers between devices: 5.24 us -> 20.2 us  [sum_far(): total = total + lax.ppermute(total, 'shard', swap_pairs(count, step))]
    unnamed x197 -> x201, local copies, waits for them, and re-layouts: 20.4 us -> 17 us
    another operation x33 -> x35, other arithmetic: 22.5 us -> 25.3 us  [both(): jnp.stack([jnp.where(low_first, mine, other), jnp.where(low_first, other,...]
  transfers between devices with their start and end apart: 58 -> 58, of which waited for: 27 -> 25; matrix products, arithmetic and copies ran while one was open for 38% -> 40% of each run, Pallas kernels for 6% -> 6%
where the time goes in v8:
time: 723 us; the launch traced here: 715 us
  waiting for transfers between devices  254 us (35%)
  matrix products  139 us (19%)
  other arithmetic  124 us (17%)
  local copies, waits for them, and re-layouts  100 us (14%)
  Pallas kernels  42.7 us (6%)
  starting transfers between devices  38.8 us (5%)
  between operations  16.1 us (2%)
    ppermute x17, waiting for transfers between devices, swap_side(): return lax.ppermute(values, 'shard', side_pairs)  130 us
    dot_general x7, matrix products, matmul(): return jnp.dot(left_side, right_side, preferred_element_type=jnp.float32)  50.9 us
    dot_general x6, matrix products, matmul_tn(): lax.dot_general(left_side, right_side, (((0,), (0,)), ((), ())), preferre...  43.4 us
    ppermute x5, waiting for transfers between devices, scatter_rest(): lax.ppermute(pick(halves, 1 - at, 1), 'shard', swap_pairs(count, step))  41.6 us
    dot_general x6, matrix products, matmul_nt(): lax.dot_general(left_side, right_side, (((1,), (1,)), ((), ())), preferre...  41.5 us
    all_gather x5, waiting for transfers between devices, gather_line(): lax.all_gather(block, 'shard', axis=0, tiled=True, axis_index_groups=line...  31.6 us
    another operation x35, other arithmetic, both(): jnp.stack([jnp.where(low_first, mine, other), jnp.where(low_first, other,...  25.3 us
    ppermute x5, waiting for transfers between devices, gather_rest(): other = lax.ppermute(held, 'shard', swap_pairs(count, step))  24.1 us
  transfers between devices with their start and end apart: 58, of which 25 were waited for; matrix products, arithmetic and copies ran while one was open for 40% of the time, Pallas kernels for 6%

profile of v8, /device:TPU:0, one launch (start us, length us, event | category | flops | bytes accessed | tf_op | source)
XLA Modules:
  0.0 715.0 jit_solution(1865925365033219260)
XLA Ops:
  15.7 5.8 collective-permute-done
  30.9 11.2 %collective-permute-done.1 = bf16[96,2816]{1,0:T(8,128)(2,1)S(1)} collective-permute-done((bf16[96,2816]{1,0:T(8,128)(2,1)S(1)}, bf16[96,2816]{1,0:T(8,128)(2,1)S(1)}, u32[]{:S(2)}, u32[]{:S(2)}) %collective-permute-start.1) | collective-permute-done | bytes 540704 | tf_op jit(solution)/shard_map/ppermute | solution.py:397
  44.3 23.4 %all-gather.6.cloned.1.call-done = bf16[768,1280]{1,0:T(8,128)(2,1)} async-done(((bf16[192,1280]{1,0:T(8,128)(2,1)}), bf16[768,1280]{1,0:T(8,128)(2,1)}) %all-gather.6.cloned.1.call-update) | async-done | bytes 1966096 | tf_op jit(solution)/shard_map/all_gather | solution.py:296
  77.1 20.5 %collective-permute-done.8 = bf16[384,1536]{1,0:T(8,128)(2,1)S(1)} collective-permute-done((bf16[384,1536]{1,0:T(8,128)(2,1)}, bf16[384,1536]{1,0:T(8,128)(2,1)S(1)}, u32[]{:S(2)}, u32[]{:S(2)}) %collective-permute-start.8) | collective-permute-done | bytes 1179680 | tf_op jit(solution)/shard_map/ppermute | solution.py:397
  101.6 12.0 %collective-permute-done.6 = bf16[4,192,1280]{2,1,0:T(8,128)(2,1)} collective-permute-done((bf16[4,192,1280]{2,1,0:T(8,128)(2,1)}, bf16[4,192,1280]{2,1,0:T(8,128)(2,1)}, u32[]{:S(2)}, u32[]{:S(2)}) %collective-permute-start.6) | collective-permute-done | bytes 1966112 | tf_op jit(solution)/shard_map/ppermute | solution.py:303
  121.1 8.0 %broadcast_multiply_fusion = (f32[1536,1536]{1,0:T(8,128)}, bf16[1536,1536]{1,0:T(8,128)(2,1)}) fusion(f32[1536]{0:T(1024)S(1)} %add_rsqrt_fusion, bf16[768,1536]{1,0:T(8,128)(2,1)} %collective-permute-done.3, bf16[768,1536]{1,0:T(8,128)(2,1)S(1)} %pad_maximum_fusion.7, f32[1536]{0:T(1024)S(1)} %get-tuple-element.139), kind=kLoop, calls=%fused_computation.22 | loop fusion | flops 16515072 | bytes 18886656 | tf_op jit(solution)/shard_map/mul | solution.py:35
  129.1 8.2 %all-gather.10.cloned.1.call-done = bf16[768,1024]{1,0:T(8,128)(2,1)} async-done(((bf16[192,1024]{1,0:T(8,128)(2,1)}), bf16[768,1024]{1,0:T(8,128)(2,1)}) %all-gather.10.cloned.1.call-update) | async-done | bytes 1572880 | tf_op jit(solution)/shard_map/all_gather | solution.py:296
  137.3 10.4 %convolution_convert_fusion.1.qkv_ref = bf16[1536,1152]{1,0:T(8,128)(2,1)} fusion(bf16[1536,1536]{1,0:T(8,128)(2,1)} %get-tuple-element.84, bf16[1536,1280]{1,0:T(8,128)(2,1)} %bitcast.351), kind=kOutput, calls=%fused_computation.5 | convolution fusion | flops 5437587456 | bytes 11796480 | tf_op jit(solution)/shard_map/dot_general | solution.py:244
  160.2 18.7 %attend.1 = f32[1536,384]{1,0:T(8,128)} custom-call(s32[4,8]{1,0:T(4,128)} %pad_add_fusion.1.facts_ref, bf16[1536,1152]{1,0:T(8,128)(2,1)} %convolution_convert_fusion.1.qkv_ref, f32[4,384,6]{2,1,0:T(8,128)} %bitcast.378, f32[4,6,384]{2,1,0:T(8,128)} %copy-done.62), custom_call_target="tpu_custom_call" | custom-call | flops 1811939328 | bytes 9437184 | tf_op jit(solution)/shard_map/attend/pallas_call | solution.py:129
  186.7 7.0 fusion.8
  221.8 23.6 %collective-permute-done.14 = bf16[384,1536]{1,0:T(8,128)(2,1)} collective-permute-done((bf16[384,1536]{1,0:T(8,128)(2,1)}, bf16[384,1536]{1,0:T(8,128)(2,1)}, u32[]{:S(2)}, u32[]{:S(2)}) %collective-permute-start.14) | collective-permute-done | bytes 1179680 | tf_op jit(solution)/shard_map/ppermute | solution.py:397
  247.7 6.4 collective-permute-done.15
  260.6 22.6 %collective-permute-done.16 = bf16[384,1536]{1,0:T(8,128)(2,1)} collective-permute-done((bf16[384,1536]{1,0:T(8,128)(2,1)}, bf16[384,1536]{1,0:T(8,128)(2,1)}, u32[]{:S(2)}, u32[]{:S(2)}) %collective-permute-start.16) | collective-permute-done | bytes 1179680 | tf_op jit(solution)/shard_map/ppermute | solution.py:397
  293.3 7.4 %fusion.71 = f32[1536,1024]{1,0:T(8,128)} fusion(bf16[1536,1536]{1,0:T(8,128)(2,1)S(1)} %bitcast.404, bf16[1024,1536]{1,0:T(8,128)(2,1)S(1)} %bitcast.382), kind=kOutput, calls=%fused_computation.298 | convolution fusion | flops 4831838208 | bytes 14155776 | tf_op jit(solution)/shard_map/dot_general | solution.py:254
  302.5 6.9 fusion.72
  309.4 11.5 %multiply_convert_fusion.1 = (bf16[1536,1024]{1,0:T(8,128)(2,1)}, bf16[1536,1024]{1,0:T(8,128)(2,1)S(1)}, bf16[1536,1024]{1,0:T(8,128)(2,1)S(1)}) fusion(f32[1536,1024]{1,0:T(8,128)} %fusion.72, f32[1536,1024]{1,0:T(8,128)} %fusion.71, bf16[1536,1536]{1,0:T(8,128)(2,1)S(1)} %pad_maximum_fusion, bf16[1536,1024]{1,0:T(8,128)(2,1)S(1)} %bitcast.390), kind=kOutput, calls=%fused_computation.6 | convolution fusion | flops 4855431168 | bytes 29884416 | tf_op jit(solution)/shard_map/dot_general | solution.py:244
  320.9 7.6 %fusion.73 = f32[1536,1536]{1,0:T(8,128)} fusion(bf16[1536,1024]{1,0:T(8,128)(2,1)S(1)} %get-tuple-element.155, bf16[1536,1024]{1,0:T(8,128)(2,1)S(1)} %bitcast.387), kind=kOutput, calls=%fused_computation.300 | convolution fusion | flops 4831838208 | bytes 15728640 | tf_op jit(solution)/shard_map/dot_general | solution.py:254
  328.5 8.0 %convolution_add_fusion.1 = f32[1536,1536]{1,0:T(8,128)S(1)} fusion(f32[1536,1536]{1,0:T(8,128)} %fusion.73, bf16[1536,1024]{1,0:T(8,128)(2,1)S(1)} %get-tuple-element.156, bf16[1536,1024]{1,0:T(8,128)(2,1)S(1)} %bitcast.391), kind=kOutput, calls=%fused_computation.3 | convolution fusion | flops 4834197504 | bytes 25165824 | tf_op jit(solution)/shard_map/dot_general | solution.py:254
  341.7 8.5 %convolution_convert_fusion.3 = bf16[1024,1536]{1,0:T(8,128)(2,1)S(1)} fusion(bf16[1536,1024]{1,0:T(8,128)(2,1)} %get-tuple-element.73, bf16[1536,1536]{1,0:T(8,128)(2,1)} %constant_dynamic-update-slice_fusion), kind=kOutput, calls=%fused_computation.28 | convolution fusion | flops 4833411072 | bytes 11010048 | tf_op jit(solution)/shard_map/dot_general | solution.py:248
  363.1 18.9 %collective-permute-done.20 = bf16[384,1536]{1,0:T(8,128)(2,1)S(1)} collective-permute-done((bf16[384,1536]{1,0:T(8,128)(2,1)S(1)}, bf16[384,1536]{1,0:T(8,128)(2,1)S(1)}, u32[]{:S(2)}, u32[]{:S(2)}) %collective-permute-start.20) | collective-permute-done | bytes 1179680 | tf_op jit(solution)/shard_map/ppermute | solution.py:397
  387.7 6.6 convolution_convert_fusion.2
  395.9 10.0 %fusion.74 = f32[1536,1536]{1,0:T(8,128)} fusion(bf16[1536,1024]{1,0:T(8,128)(2,1)} %get-tuple-element.73, bf16[1024,1536]{1,0:T(8,128)(2,1)} %bitcast.383), kind=kOutput, calls=%fused_computation.301 | convolution fusion | flops 4831838208 | bytes 15728640 | tf_op jit(solution)/shard_map/dot_general | solution.py:244
  405.9 15.1 %collective-permute-done.23 = bf16[4,192,1024]{2,1,0:T(8,128)(2,1)} collective-permute-done((bf16[4,192,1024]{2,1,0:T(8,128)(2,1)}, bf16[4,192,1024]{2,1,0:T(8,128)(2,1)}, u32[]{:S(2)}, u32[]{:S(2)}) %collective-permute-start.23) | collective-permute-done | bytes 1572896 | tf_op jit(solution)/shard_map/ppermute | solution.py:320
  437.1 6.2 convolution_convert_fusion.5
  447.6 24.0 %attend_back.1 = (bf16[1536,1152]{1,0:T(8,128)(2,1)}, f32[4,384,6]{2,1,0:T(8,128)}, f32[4,6,384]{2,1,0:T(8,128)}) custom-call(s32[4,8]{1,0:T(4,128)} %pad_add_fusion.1.facts_ref, bf16[1536,1152]{1,0:T(8,128)(2,1)} %convolution_convert_fusion.1.qkv_ref, bf16[1536,384]{1,0:T(8,128)(2,1)} %get-tuple-element.160.grad_ref, f32[4,384,6]{2,1,0:T(8,128)} %bitcast.379, ...), custom_call_target="tpu_custom_call" | custom-call | flops 18119393280 | bytes 8257536 | tf_op jit(solution)/shard_map/attend_back/pallas_call | solution.py:208
  492.6 10.7 %convolution_convert_fusion = bf16[1536,1280]{1,0:T(8,128)(2,1)} fusion(bf16[1536,1536]{1,0:T(8,128)(2,1)} %get-tuple-element.84, bf16[1536,128]{1,0:T(8,128)(2,1)S(1)} %dynamic_update_slice.9, bf16[1536,1152]{1,0:T(8,128)(2,1)} %get-tuple-element.79), kind=kOutput, calls=%fused_computation.4 | convolution fusion | flops 6049628160 | bytes 12582912 | tf_op jit(solution)/shard_map/dot_general | solution.py:248
  516.6 6.0 convolution_convert_fusion.6
  549.1 15.2 %collective-permute-done.33 = f32[1,24]{1,0:T(1,128)S(1)} collective-permute-done((f32[1,24]{1,0:T(1,128)S(1)}, f32[1,24]{1,0:T(1,128)S(1)}, u32[]{:S(2)}, u32[]{:S(2)}) %collective-permute-start.33) | collective-permute-done | bytes 128 | tf_op jit(solution)/shard_map/ppermute | solution.py:345
  574.2 22.1 %collective-permute-done.37 = bf16[4,192,768]{2,1,0:T(8,128)(2,1)} collective-permute-done((bf16[4,192,768]{2,1,0:T(8,128)(2,1)}, bf16[4,192,768]{2,1,0:T(8,128)(2,1)}, u32[]{:S(2)}, u32[]{:S(2)}) %collective-permute-start.37) | collective-permute-done | bytes 1179680 | tf_op jit(solution)/shard_map/ppermute | solution.py:320
  599.3 8.9 %fusion.75 = f32[1536,1536]{1,0:T(8,128)S(1)} fusion(bf16[1536,1280]{1,0:T(8,128)(2,1)} %pad_maximum_fusion.3, bf16[1536,1280]{1,0:T(8,128)(2,1)S(1)} %bitcast.352), kind=kOutput, calls=%fused_computation.302 | convolution fusion | flops 6039797760 | bytes 17301504 | tf_op jit(solution)/shard_map/dot_general | solution.py:254
  619.4 6.5 collective-permute-done.44
  643.6 16.1 %collective-permute-done.39 = bf16[384,1536]{1,0:T(8,128)(2,1)} collective-permute-done((bf16[384,1536]{1,0:T(8,128)(2,1)}, bf16[384,1536]{1,0:T(8,128)(2,1)}, u32[]{:S(2)}, u32[]{:S(2)}) %collective-permute-start.39) | collective-permute-done | bytes 1179680 | tf_op jit(solution)/shard_map/ppermute | solution.py:397
  (497 shorter events, 304.7 us)
Async XLA Ops:
  7.2 60.4 %all-gather.6.cloned.1.call-start = ((), (), s32[]{:S(2)}) async-start(), calls=%async_computation.5 | async-start | bytes 2457600 | tf_op jit(solution)/shard_map/all_gather | solution.py:296
  22.5 78.0 %all-gather.8.cloned.1.call-start = ((), (), s32[]{:S(2)}) async-start(), calls=%async_computation.6 | async-start | bytes 1474560 | tf_op jit(solution)/shard_map/all_gather | solution.py:296
  42.4 29.9 %collective-permute-start.2 = (bf16[384,1536]{1,0:T(8,128)(2,1)S(1)}, bf16[384,1536]{1,0:T(8,128)(2,1)}, u32[]{:S(2)}, u32[]{:S(2)}) collective-permute-start(bf16[384,1536]{1,0:T(8,128)(2,1)S(1)} %copy-done.49), channel_id=1, source_target_pairs={{0,1},{1,0},{2,3},{3,2},{4,5},{5,4},{6,7},{7,6},{8,9},{9,8},{10,11... | collective-permute-start | bytes 3538952 | tf_op jit(solution)/shard_map/ppermute | solution.py:397
  67.6 46.0 %collective-permute-start.6 = (bf16[4,192,1280]{2,1,0:T(8,128)(2,1)}, bf16[4,192,1280]{2,1,0:T(8,128)(2,1)}, u32[]{:S(2)}, u32[]{:S(2)}) collective-permute-start(bf16[4,192,1280]{2,1,0:T(8,128)(2,1)} %bitcast.393), channel_id=1, source_target_pairs={{0,2},{1,3},{2,0},{3,1},{4,6},{5,7},{6,4},{7,5},{8,10},{9,11},{10,... | collective-permute-start | bytes 5898248 | tf_op jit(solution)/shard_map/ppermute | solution.py:303
  69.9 67.4 %all-gather.10.cloned.1.call-start = ((), (), s32[]{:S(2)}) async-start(), calls=%async_computation.7 | async-start | bytes 1966080 | tf_op jit(solution)/shard_map/all_gather | solution.py:296
  74.1 42.9 %collective-permute-start.3 = (bf16[768,1536]{1,0:T(8,128)(2,1)S(1)}, bf16[768,1536]{1,0:T(8,128)(2,1)}, u32[]{:S(2)}, u32[]{:S(2)}) collective-permute-start(bf16[768,1536]{1,0:T(8,128)(2,1)S(1)} %pad_maximum_fusion.7), channel_id=1, source_target_pairs={{0,16},{16,0},{1,17},{17,1},{2,18},{18,2},{3,19},{19,3},{4,20},{20... | collective-permute-start | bytes 7077896 | tf_op jit(solution)/shard_map/ppermute | solution.py:394
  100.5 101.1 %all-gather.12.cloned.1.call-start = ((), (), s32[]{:S(2)}) async-start(), calls=%async_computation.8 | async-start | bytes 1966080 | tf_op jit(solution)/shard_map/all_gather | solution.py:296
  101.0 46.8 %collective-permute-start.10 = (bf16[4,192,768]{2,1,0:T(8,128)(2,1)}, bf16[4,192,768]{2,1,0:T(8,128)(2,1)}, u32[]{:S(2)}, u32[]{:S(2)}) collective-permute-start(bf16[4,192,768]{2,1,0:T(8,128)(2,1)} %bitcast.401), channel_id=1, source_target_pairs={{0,2},{1,3},{2,0},{3,1},{4,6},{5,7},{6,4},{7,5},{8,10},{9,11},{10,... | collective-permute-start | bytes 3538952 | tf_op jit(solution)/shard_map/ppermute | solution.py:303
  147.8 50.5 %collective-permute-start.9 = (bf16[768,1536]{1,0:T(8,128)(2,1)}, bf16[768,1536]{1,0:T(8,128)(2,1)}, u32[]{:S(2)}, u32[]{:S(2)}) collective-permute-start(bf16[768,1536]{1,0:T(8,128)(2,1)} %pad_maximum_fusion.8), channel_id=1, source_target_pairs={{0,16},{16,0},{1,17},{17,1},{2,18},{18,2},{3,19},{19,3},{4,20},{20... | collective-permute-start | bytes 7077896 | tf_op jit(solution)/shard_map/ppermute | solution.py:394
  151.8 30.4 %collective-permute-start.11 = (bf16[2,384,384]{2,1,0:T(8,128)(2,1)}, bf16[2,384,384]{2,1,0:T(8,128)(2,1)}, u32[]{:S(2)}, u32[]{:S(2)}) collective-permute-start(bf16[2,384,384]{2,1,0:T(8,128)(2,1)} %dynamic-slice_bitcast_fusion.4), channel_id=1, source_target_pairs={{0,1},{1,0},{2,3},{3,2},{4,5},{5,4},{6,7},{7,6},{8,9},{9,8},{10,11... | collective-permute-start | bytes 1769480 | tf_op jit(solution)/shard_map/ppermute | solution.py:397
  158.4 98.8 %all-gather.14.cloned.1.call-start = ((), (), s32[]{:S(2)}) async-start(), calls=%async_computation.9 | async-start | bytes 1966080 | tf_op jit(solution)/shard_map/all_gather | solution.py:296
  158.7 42.9 %collective-permute-start.7 = (bf16[4,192,1024]{2,1,0:T(8,128)(2,1)}, bf16[4,192,1024]{2,1,0:T(8,128)(2,1)}, u32[]{:S(2)}, u32[]{:S(2)}) collective-permute-start(bf16[4,192,1024]{2,1,0:T(8,128)(2,1)} %bitcast.395), channel_id=1, source_target_pairs={{0,2},{1,3},{2,0},{3,1},{4,6},{5,7},{6,4},{7,5},{8,10},{9,11},{10,... | collective-permute-start | bytes 4718600 | tf_op jit(solution)/shard_map/ppermute | solution.py:303
  216.9 28.6 %collective-permute-start.14 = (bf16[384,1536]{1,0:T(8,128)(2,1)}, bf16[384,1536]{1,0:T(8,128)(2,1)}, u32[]{:S(2)}, u32[]{:S(2)}) collective-permute-start(bf16[384,1536]{1,0:T(8,128)(2,1)} %slice.273), channel_id=1, source_target_pairs={{0,1},{1,0},{2,3},{3,2},{4,5},{5,4},{6,7},{7,6},{8,9},{9,8},{10,11... | collective-permute-start | bytes 3538952 | tf_op jit(solution)/shard_map/ppermute | solution.py:397
  217.4 36.7 %collective-permute-start.15 = (bf16[4,192,1024]{2,1,0:T(8,128)(2,1)}, bf16[4,192,1024]{2,1,0:T(8,128)(2,1)}, u32[]{:S(2)}, u32[]{:S(2)}) collective-permute-start(bf16[4,192,1024]{2,1,0:T(8,128)(2,1)} %bitcast.397), channel_id=1, source_target_pairs={{0,2},{1,3},{2,0},{3,1},{4,6},{5,7},{6,4},{7,5},{8,10},{9,11},{10,... | collective-permute-start | bytes 4718600 | tf_op jit(solution)/shard_map/ppermute | solution.py:303
  218.8 218.3 %reduce-scatter.6.cloned.1.call-start = ((), (), s32[]{:S(2)}) async-start(), calls=%async_computation.10 | async-start | bytes 1966080 | tf_op jit(solution)/shard_map/reduce_scatter | solution.py:330
  257.2 35.5 %collective-permute-start.18 = (bf16[4,128,1536]{2,1,0:T(8,128)(2,1)}, bf16[4,128,1536]{2,1,0:T(8,128)(2,1)S(1)}, u32[]{:S(2)}, u32[]{:S(2)}) collective-permute-start(bf16[4,128,1536]{2,1,0:T(8,128)(2,1)} %bitcast.399), channel_id=1, source_target_pairs={{0,2},{1,3},{2,0},{3,1},{4,6},{5,7},{6,4},{7,5},{8,10},{9,11},{10,... | collective-permute-start | bytes 4718600 | tf_op jit(solution)/shard_map/ppermute | solution.py:303
  350.4 37.3 %collective-permute-start.21 = (bf16[4,128,1536]{2,1,0:T(8,128)(2,1)S(1)}, bf16[4,128,1536]{2,1,0:T(8,128)(2,1)S(1)}, u32[]{:S(2)}, u32[]{:S(2)}) collective-permute-start(bf16[4,128,1536]{2,1,0:T(8,128)(2,1)S(1)} %dynamic-slice_bitcast_fusion.3), channel_id=1, source_target_pairs={{0,2},{1,3},{2,0},{3,1},{4,6},{5,7},{6,4},{7,5},{8,10},{9,11},{10,... | collective-permute-start | bytes 4718600 | tf_op jit(solution)/shard_map/ppermute | solution.py:320
  353.9 28.0 %collective-permute-start.20 = (bf16[384,1536]{1,0:T(8,128)(2,1)S(1)}, bf16[384,1536]{1,0:T(8,128)(2,1)S(1)}, u32[]{:S(2)}, u32[]{:S(2)}) collective-permute-start(bf16[384,1536]{1,0:T(8,128)(2,1)S(1)} %slice.272), channel_id=1, source_target_pairs={{0,1},{1,0},{2,3},{3,2},{4,5},{5,4},{6,7},{7,6},{8,9},{9,8},{10,11... | collective-permute-start | bytes 3538952 | tf_op jit(solution)/shard_map/ppermute | solution.py:397
  361.4 59.6 %collective-permute-start.23 = (bf16[4,192,1024]{2,1,0:T(8,128)(2,1)}, bf16[4,192,1024]{2,1,0:T(8,128)(2,1)}, u32[]{:S(2)}, u32[]{:S(2)}) collective-permute-start(bf16[4,192,1024]{2,1,0:T(8,128)(2,1)} %dynamic-slice_bitcast_fusion.2), channel_id=1, source_target_pairs={{0,2},{1,3},{2,0},{3,1},{4,6},{5,7},{6,4},{7,5},{8,10},{9,11},{10,... | collective-permute-start | bytes 4718600 | tf_op jit(solution)/shard_map/ppermute | solution.py:320
  386.8 37.5 %collective-permute-start.22 = (bf16[384,1536]{1,0:T(8,128)(2,1)}, bf16[384,1536]{1,0:T(8,128)(2,1)}, u32[]{:S(2)}, u32[]{:S(2)}) collective-permute-start(bf16[384,1536]{1,0:T(8,128)(2,1)} %fusion.65), channel_id=1, source_target_pairs={{0,1},{1,0},{2,3},{3,2},{4,5},{5,4},{6,7},{7,6},{8,9},{9,8},{10,11... | collective-permute-start | bytes 3538952 | tf_op jit(solution)/shard_map/ppermute | solution.py:397
  395.9 75.7 %reduce-scatter.8.cloned.1.call-start = ((), (), s32[]{:S(2)}) async-start(), calls=%async_computation.11 | async-start | bytes 1966080 | tf_op jit(solution)/shard_map/reduce_scatter | solution.py:330
  430.1 74.8 %collective-permute-start.36 = (bf16[4,192,1024]{2,1,0:T(8,128)(2,1)}, bf16[4,192,1024]{2,1,0:T(8,128)(2,1)}, u32[]{:S(2)}, u32[]{:S(2)}) collective-permute-start(bf16[4,192,1024]{2,1,0:T(8,128)(2,1)} %dynamic-slice_bitcast_fusion.1), channel_id=1, source_target_pairs={{0,2},{1,3},{2,0},{3,1},{4,6},{5,7},{6,4},{7,5},{8,10},{9,11},{10,... | collective-permute-start | bytes 4718600 | tf_op jit(solution)/shard_map/ppermute | solution.py:320
  430.7 143.5 %reduce-scatter.10.cloned.1.call-start = ((), (), s32[]{:S(2)}) async-start(), calls=%async_computation.12 | async-start | bytes 1966080 | tf_op jit(solution)/shard_map/reduce_scatter | solution.py:330
  475.7 57.0 %collective-permute-start.25 = (bf16[768,1536]{1,0:T(8,128)(2,1)}, bf16[768,1536]{1,0:T(8,128)(2,1)}, u32[]{:S(2)}, u32[]{:S(2)}) collective-permute-start(bf16[768,1536]{1,0:T(8,128)(2,1)} %slice.267), channel_id=1, source_target_pairs={{0,16},{16,0},{1,17},{17,1},{2,18},{18,2},{3,19},{19,3},{4,20},{20... | collective-permute-start | bytes 7077896 | tf_op jit(solution)/shard_map/ppermute | solution.py:394
  480.4 42.2 %collective-permute-start.27 = (f32[1,24]{1,0:T(1,128)}, f32[1,24]{1,0:T(1,128)}, u32[]{:S(2)}, u32[]{:S(2)}) collective-permute-start(f32[1,24]{1,0:T(1,128)} %dynamic_update_slice.10), channel_id=1, source_target_pairs={{0,2},{1,3},{2,0},{3,1},{4,6},{5,7},{6,4},{7,5},{8,10},{9,11},{10,... | collective-permute-start | bytes 296 | tf_op jit(solution)/shard_map/ppermute | solution.py:338
  503.4 36.2 %collective-permute-start.35 = (bf16[128,1536]{1,0:T(8,128)(2,1)S(1)}, bf16[128,1536]{1,0:T(8,128)(2,1)}, u32[]{:S(2)}, u32[]{:S(2)}) collective-permute-start(bf16[128,1536]{1,0:T(8,128)(2,1)S(1)} %copy-done.59), channel_id=1, source_target_pairs={{0,16},{16,0},{1,17},{17,1},{2,18},{18,2},{3,19},{19,3},{4,20},{20... | collective-permute-start | bytes 1179656 | tf_op jit(solution)/shard_map/ppermute | solution.py:394
  508.2 155.2 %reduce-scatter.12.cloned.1.call-start = ((), (), s32[]{:S(2)}) async-start(), calls=%async_computation.13 | async-start | bytes 2457600 | tf_op jit(solution)/shard_map/reduce_scatter | solution.py:330
  526.3 45.8 %collective-permute-start.28 = (bf16[4,192,1280]{2,1,0:T(8,128)(2,1)S(1)}, bf16[4,192,1280]{2,1,0:T(8,128)(2,1)S(1)}, u32[]{:S(2)}, u32[]{:S(2)}) collective-permute-start(bf16[4,192,1280]{2,1,0:T(8,128)(2,1)S(1)} %dynamic-slice_bitcast_fusion), channel_id=1, source_target_pairs={{0,2},{1,3},{2,0},{3,1},{4,6},{5,7},{6,4},{7,5},{8,10},{9,11},{10,... | collective-permute-start | bytes 5898248 | tf_op jit(solution)/shard_map/ppermute | solution.py:320
  537.1 29.3 %collective-permute-start.26 = (bf16[384,1536]{1,0:T(8,128)(2,1)S(1)}, bf16[384,1536]{1,0:T(8,128)(2,1)S(1)}, u32[]{:S(2)}, u32[]{:S(2)}) collective-permute-start(bf16[384,1536]{1,0:T(8,128)(2,1)S(1)} %slice.271), channel_id=1, source_target_pairs={{0,1},{1,0},{2,3},{3,2},{4,5},{5,4},{6,7},{7,6},{8,9},{9,8},{10,11... | collective-permute-start | bytes 3538952 | tf_op jit(solution)/shard_map/ppermute | solution.py:397
  564.3 32.0 %collective-permute-start.37 = (bf16[4,192,768]{2,1,0:T(8,128)(2,1)}, bf16[4,192,768]{2,1,0:T(8,128)(2,1)}, u32[]{:S(2)}, u32[]{:S(2)}) collective-permute-start(bf16[4,192,768]{2,1,0:T(8,128)(2,1)} %fusion.13), channel_id=1, source_target_pairs={{0,2},{1,3},{2,0},{3,1},{4,6},{5,7},{6,4},{7,5},{8,10},{9,11},{10,... | collective-permute-start | bytes 3538952 | tf_op jit(solution)/shard_map/ppermute | solution.py:320
  573.9 95.0 %reduce-scatter.14.cloned.1.call-start = ((), (), s32[]{:S(2)}) async-start(), calls=%async_computation.14 | async-start | bytes 1474560 | tf_op jit(solution)/shard_map/reduce_scatter | solution.py:330
  631.9 27.8 %collective-permute-start.39 = (bf16[384,1536]{1,0:T(8,128)(2,1)}, bf16[384,1536]{1,0:T(8,128)(2,1)}, u32[]{:S(2)}, u32[]{:S(2)}) collective-permute-start(bf16[384,1536]{1,0:T(8,128)(2,1)} %slice.270), channel_id=1, source_target_pairs={{0,1},{1,0},{2,3},{3,2},{4,5},{5,4},{6,7},{7,6},{8,9},{9,8},{10,11... | collective-permute-start | bytes 3538952 | tf_op jit(solution)/shard_map/ppermute | solution.py:397
  (123 other events, 1109.7 us)
Sparse Core Ops, SparseCore 0:
  22.6 44.9 all-gather.5
  70.1 28.7 all-gather.7
  101.0 36.2 all-gather.9
  158.6 34.9 all-gather.11
  218.9 35.8 all-gather.13
  396.0 34.3 reduce-scatter.5
  433.3 34.2 reduce-scatter.7
  508.3 33.7 reduce-scatter.9
  574.0 40.3 reduce-scatter.11
  619.5 27.7 reduce-scatter.13

commit v9 on v6

--- a/solution.py
+++ b/solution.py
@@ -632,10 +632,10 @@
     down_own = both_cores(after(grad_down, part_first_w))
     grad_bias = sum_far(after(bias_near, part_first_w), count, reps)
     first_held = first_sum(grad_bias, layer_out, down_own, sum_second)
-    grad_normed1 = team_sum(after(part_normed1, first_held))
+    sum_first = scatter_line(first_held, count)
+    grad_normed1 = after(team_sum(after(part_normed1, first_held)), sum_first)
     tokens_grad = grad_resid + norm_back(grad_normed1 * gain_one, scaled1, inverse1)
-    sum_first = scatter_line(first_held, count)
-    gate_own = own_of(after(grad_gate_w, grad_normed1))
+    gate_own = own_of(after(grad_gate_w, first_held))
     grad_up_w = after(grad_up_w, grad_normed1)
     sum_second = after(sum_second, grad_normed1)
 

time: 704 us -> 702 us (level)
    unnamed x209 -> x205, local copies, waits for them, and re-layouts: 21.7 us -> 19.6 us
  transfers between devices with their start and end apart: 58 -> 58, of which waited for: 25 -> 26; matrix products, arithmetic and copies ran while one was open for 36% -> 37% of each run, Pallas kernels for 6% -> 6%
where the time goes in v9:
time: 702 us; the launch traced here: 694 us
  waiting for transfers between devices  255 us (36%)
  matrix products  136 us (19%)
  other arithmetic  112 us (16%)
  local copies, waits for them, and re-layouts  97.5 us (14%)
  Pallas kernels  42.9 us (6%)
  starting transfers between devices  34.8 us (5%)
  between operations  16.3 us (2%)
    ppermute x17, waiting for transfers between devices, swap_side(): return lax.ppermute(values, 'shard', side_pairs)  160 us
    dot_general x7, matrix products, matmul(): return jnp.dot(left_side, right_side, preferred_element_type=jnp.float32)  51.1 us
    dot_general x6, matrix products, matmul_tn(): lax.dot_general(left_side, right_side, (((0,), (0,)), ((), ())), preferre...  41 us
    dot_general x6, matrix products, matmul_nt(): lax.dot_general(left_side, right_side, (((1,), (1,)), ((), ())), preferre...  40.8 us
    all_gather x5, waiting for transfers between devices, gather_line(): lax.all_gather(block, 'shard', axis=0, tiled=True, axis_index_groups=line...  31.6 us
    ppermute x5, waiting for transfers between devices, scatter_rest(): lax.ppermute(pick(halves, 1 - at, 1), 'shard', swap_pairs(count, step))  25.7 us
    ppermute x5, waiting for transfers between devices, gather_rest(): other = lax.ppermute(held, 'shard', swap_pairs(count, step))  24.4 us
    pallas_call x1, Pallas kernels, attend_back(): pl.pallas_call(body, grid_spec=pltpu.PrefetchScalarGridSpec(num_scalar_pr...  24.2 us
  transfers between devices with their start and end apart: 58, of which 26 were waited for; matrix products, arithmetic and copies ran while one was open for 37% of the time, Pallas kernels for 6%

profile of v9, /device:TPU:0, one launch (start us, length us, event | category | flops | bytes accessed | tf_op | source)
XLA Modules:
  0.0 694.4 jit_solution(2966510561728267305)
XLA Ops:
  15.7 5.8 collective-permute-done
  30.9 11.2 %collective-permute-done.1 = bf16[96,2816]{1,0:T(8,128)(2,1)S(1)} collective-permute-done((bf16[96,2816]{1,0:T(8,128)(2,1)S(1)}, bf16[96,2816]{1,0:T(8,128)(2,1)S(1)}, u32[]{:S(2)}, u32[]{:S(2)}) %collective-permute-start.1) | collective-permute-done | bytes 540704 | tf_op jit(solution)/shard_map/ppermute | solution.py:397
  44.3 23.4 %all-gather.6.cloned.1.call-done = bf16[768,1280]{1,0:T(8,128)(2,1)} async-done(((bf16[192,1280]{1,0:T(8,128)(2,1)}), bf16[768,1280]{1,0:T(8,128)(2,1)}) %all-gather.6.cloned.1.call-update) | async-done | bytes 1966096 | tf_op jit(solution)/shard_map/all_gather | solution.py:296
  77.0 20.5 %collective-permute-done.8 = bf16[384,1536]{1,0:T(8,128)(2,1)S(1)} collective-permute-done((bf16[384,1536]{1,0:T(8,128)(2,1)}, bf16[384,1536]{1,0:T(8,128)(2,1)S(1)}, u32[]{:S(2)}, u32[]{:S(2)}) %collective-permute-start.8) | collective-permute-done | bytes 1179680 | tf_op jit(solution)/shard_map/ppermute | solution.py:397
  101.4 12.3 %collective-permute-done.6 = bf16[4,192,1280]{2,1,0:T(8,128)(2,1)} collective-permute-done((bf16[4,192,1280]{2,1,0:T(8,128)(2,1)}, bf16[4,192,1280]{2,1,0:T(8,128)(2,1)}, u32[]{:S(2)}, u32[]{:S(2)}) %collective-permute-start.6) | collective-permute-done | bytes 1966112 | tf_op jit(solution)/shard_map/ppermute | solution.py:303
  121.1 8.0 %broadcast_multiply_fusion = (f32[1536,1536]{1,0:T(8,128)}, bf16[1536,1536]{1,0:T(8,128)(2,1)}) fusion(f32[1536]{0:T(1024)S(1)} %add_rsqrt_fusion, bf16[768,1536]{1,0:T(8,128)(2,1)} %collective-permute-done.3, bf16[768,1536]{1,0:T(8,128)(2,1)S(1)} %pad_maximum_fusion.7, f32[1536]{0:T(1024)S(1)} %get-tuple-element.141), kind=kLoop, calls=%fused_computation.22 | loop fusion | flops 16515072 | bytes 18886656 | tf_op jit(solution)/shard_map/mul | solution.py:35
  129.1 8.2 %all-gather.10.cloned.1.call-done = bf16[768,1024]{1,0:T(8,128)(2,1)} async-done(((bf16[192,1024]{1,0:T(8,128)(2,1)}), bf16[768,1024]{1,0:T(8,128)(2,1)}) %all-gather.10.cloned.1.call-update) | async-done | bytes 1572880 | tf_op jit(solution)/shard_map/all_gather | solution.py:296
  137.3 10.4 %convolution_convert_fusion.1.qkv_ref = bf16[1536,1152]{1,0:T(8,128)(2,1)} fusion(bf16[1536,1536]{1,0:T(8,128)(2,1)} %get-tuple-element.82, bf16[1536,1280]{1,0:T(8,128)(2,1)} %bitcast.350), kind=kOutput, calls=%fused_computation.5 | convolution fusion | flops 5437587456 | bytes 11796480 | tf_op jit(solution)/shard_map/dot_general | solution.py:244
  160.5 18.7 %attend.1 = f32[1536,384]{1,0:T(8,128)} custom-call(s32[4,8]{1,0:T(4,128)} %pad_add_fusion.1.facts_ref, bf16[1536,1152]{1,0:T(8,128)(2,1)} %convolution_convert_fusion.1.qkv_ref, f32[4,384,6]{2,1,0:T(8,128)} %bitcast.379, f32[4,6,384]{2,1,0:T(8,128)} %copy-done.63), custom_call_target="tpu_custom_call" | custom-call | flops 1811939328 | bytes 9437184 | tf_op jit(solution)/shard_map/attend/pallas_call | solution.py:129
  186.9 7.0 %fusion.8 = f32[1536,384]{1,0:T(8,128)} fusion(bf16[1536,1536]{1,0:T(8,128)(2,1)} %get-tuple-element.82, bf16[1536,768]{1,0:T(8,128)(2,1)} %bitcast.344), kind=kOutput, calls=%fused_computation.43 | convolution fusion | flops 1813708800 | bytes 8257536 | tf_op jit(solution)/shard_map/dot_general | solution.py:244
  222.1 23.6 %collective-permute-done.14 = bf16[384,1536]{1,0:T(8,128)(2,1)} collective-permute-done((bf16[384,1536]{1,0:T(8,128)(2,1)}, bf16[384,1536]{1,0:T(8,128)(2,1)}, u32[]{:S(2)}, u32[]{:S(2)}) %collective-permute-start.14) | collective-permute-done | bytes 1179680 | tf_op jit(solution)/shard_map/ppermute | solution.py:397
  248.0 6.4 collective-permute-done.15
  260.8 22.6 %collective-permute-done.16 = bf16[384,1536]{1,0:T(8,128)(2,1)} collective-permute-done((bf16[384,1536]{1,0:T(8,128)(2,1)}, bf16[384,1536]{1,0:T(8,128)(2,1)}, u32[]{:S(2)}, u32[]{:S(2)}) %collective-permute-start.16) | collective-permute-done | bytes 1179680 | tf_op jit(solution)/shard_map/ppermute | solution.py:397
  293.5 7.2 %fusion.71 = f32[1536,1024]{1,0:T(8,128)} fusion(bf16[1536,1536]{1,0:T(8,128)(2,1)S(1)} %bitcast.405, bf16[1024,1536]{1,0:T(8,128)(2,1)S(1)} %bitcast.383), kind=kOutput, calls=%fused_computation.297 | convolution fusion | flops 4831838208 | bytes 14155776 | tf_op jit(solution)/shard_map/dot_general | solution.py:254
  302.5 6.9 fusion.72
  309.4 11.5 %multiply_convert_fusion.1 = (bf16[1536,1024]{1,0:T(8,128)(2,1)}, bf16[1536,1024]{1,0:T(8,128)(2,1)S(1)}, bf16[1536,1024]{1,0:T(8,128)(2,1)S(1)}) fusion(f32[1536,1024]{1,0:T(8,128)} %fusion.72, f32[1536,1024]{1,0:T(8,128)} %fusion.71, bf16[1536,1536]{1,0:T(8,128)(2,1)S(1)} %pad_maximum_fusion, bf16[1536,1024]{1,0:T(8,128)(2,1)S(1)} %bitcast.391), kind=kOutput, calls=%fused_computation.6 | convolution fusion | flops 4855431168 | bytes 29884416 | tf_op jit(solution)/shard_map/dot_general | solution.py:244
  320.9 7.6 %fusion.73 = f32[1536,1536]{1,0:T(8,128)} fusion(bf16[1536,1024]{1,0:T(8,128)(2,1)S(1)} %get-tuple-element.157, bf16[1536,1024]{1,0:T(8,128)(2,1)S(1)} %bitcast.388), kind=kOutput, calls=%fused_computation.299 | convolution fusion | flops 4831838208 | bytes 15728640 | tf_op jit(solution)/shard_map/dot_general | solution.py:254
  328.5 7.9 %convolution_add_fusion.1 = f32[1536,1536]{1,0:T(8,128)S(1)} fusion(f32[1536,1536]{1,0:T(8,128)} %fusion.73, bf16[1536,1024]{1,0:T(8,128)(2,1)S(1)} %get-tuple-element.158, bf16[1536,1024]{1,0:T(8,128)(2,1)S(1)} %bitcast.392), kind=kOutput, calls=%fused_computation.3 | convolution fusion | flops 4834197504 | bytes 25165824 | tf_op jit(solution)/shard_map/dot_general | solution.py:254
  341.7 8.7 %convolution_convert_fusion.3 = bf16[1024,1536]{1,0:T(8,128)(2,1)S(1)} fusion(bf16[1536,1024]{1,0:T(8,128)(2,1)} %get-tuple-element.74, bf16[1536,1536]{1,0:T(8,128)(2,1)} %constant_dynamic-update-slice_fusion), kind=kOutput, calls=%fused_computation.28 | convolution fusion | flops 4833411072 | bytes 11010048 | tf_op jit(solution)/shard_map/dot_general | solution.py:248
  363.4 18.8 %collective-permute-done.20 = bf16[384,1536]{1,0:T(8,128)(2,1)S(1)} collective-permute-done((bf16[384,1536]{1,0:T(8,128)(2,1)S(1)}, bf16[384,1536]{1,0:T(8,128)(2,1)S(1)}, u32[]{:S(2)}, u32[]{:S(2)}) %collective-permute-start.20) | collective-permute-done | bytes 1179680 | tf_op jit(solution)/shard_map/ppermute | solution.py:397
  387.9 6.6 convolution_convert_fusion.2
  396.1 10.2 %fusion.74 = f32[1536,1536]{1,0:T(8,128)} fusion(bf16[1536,1024]{1,0:T(8,128)(2,1)} %get-tuple-element.74, bf16[1024,1536]{1,0:T(8,128)(2,1)} %bitcast.384), kind=kOutput, calls=%fused_computation.300 | convolution fusion | flops 4831838208 | bytes 15728640 | tf_op jit(solution)/shard_map/dot_general | solution.py:244
  406.3 15.0 %collective-permute-done.23 = bf16[4,192,1024]{2,1,0:T(8,128)(2,1)} collective-permute-done((bf16[4,192,1024]{2,1,0:T(8,128)(2,1)}, bf16[4,192,1024]{2,1,0:T(8,128)(2,1)}, u32[]{:S(2)}, u32[]{:S(2)}) %collective-permute-start.23) | collective-permute-done | bytes 1572896 | tf_op jit(solution)/shard_map/ppermute | solution.py:320
  436.6 6.0 convolution_convert_fusion.5
  450.8 6.6 multiply_convert_fusion.4
  457.4 10.4 %collective-permute-done.25 = bf16[4,192,1024]{2,1,0:T(8,128)(2,1)} collective-permute-done((bf16[4,192,1024]{2,1,0:T(8,128)(2,1)}, bf16[4,192,1024]{2,1,0:T(8,128)(2,1)}, u32[]{:S(2)}, u32[]{:S(2)}) %collective-permute-start.25) | collective-permute-done | bytes 1572896 | tf_op jit(solution)/shard_map/ppermute | solution.py:320
  489.0 24.2 %attend_back.1 = (bf16[1536,1152]{1,0:T(8,128)(2,1)}, f32[4,384,6]{2,1,0:T(8,128)}, f32[4,6,384]{2,1,0:T(8,128)}) custom-call(s32[4,8]{1,0:T(4,128)} %pad_add_fusion.1.facts_ref, bf16[1536,1152]{1,0:T(8,128)(2,1)} %convolution_convert_fusion.1.qkv_ref, bf16[1536,384]{1,0:T(8,128)(2,1)} %get-tuple-element.80.grad_ref, f32[4,384,6]{2,1,0:T(8,128)} %bitcast.380, ...), custom_call_target="tpu_custom_call" | custom-call | flops 18119393280 | bytes 8257536 | tf_op jit(solution)/shard_map/attend_back/pallas_call | solution.py:208
  528.1 8.9 %convolution_convert_fusion = bf16[1536,1280]{1,0:T(8,128)(2,1)S(1)} fusion(bf16[1536,1536]{1,0:T(8,128)(2,1)} %get-tuple-element.82, bf16[1536,128]{1,0:T(8,128)(2,1)S(1)} %dynamic_update_slice.9, bf16[1536,1152]{1,0:T(8,128)(2,1)S(1)} %copy-done.29), kind=kOutput, calls=%fused_computation.4 | convolution fusion | flops 6049628160 | bytes 12582912 | tf_op jit(solution)/shard_map/dot_general | solution.py:248
  543.2 6.3 fusion.75
  567.0 20.9 %collective-permute-done.30 = bf16[384,1536]{1,0:T(8,128)(2,1)S(1)} collective-permute-done((bf16[384,1536]{1,0:T(8,128)(2,1)S(1)}, bf16[384,1536]{1,0:T(8,128)(2,1)S(1)}, u32[]{:S(2)}, u32[]{:S(2)}) %collective-permute-start.30) | collective-permute-done | bytes 1179680 | tf_op jit(solution)/shard_map/ppermute | solution.py:397
  598.4 6.7 collective-permute-done.44
  620.5 17.4 %collective-permute-done.39 = bf16[384,1536]{1,0:T(8,128)(2,1)} collective-permute-done((bf16[384,1536]{1,0:T(8,128)(2,1)}, bf16[384,1536]{1,0:T(8,128)(2,1)}, u32[]{:S(2)}, u32[]{:S(2)}) %collective-permute-start.39) | collective-permute-done | bytes 1179680 | tf_op jit(solution)/shard_map/ppermute | solution.py:397
  (502 shorter events, 292.3 us)
Async XLA Ops:
  7.2 60.4 %all-gather.6.cloned.1.call-start = ((), (), s32[]{:S(2)}) async-start(), calls=%async_computation.5 | async-start | bytes 2457600 | tf_op jit(solution)/shard_map/all_gather | solution.py:296
  22.5 78.0 %all-gather.8.cloned.1.call-start = ((), (), s32[]{:S(2)}) async-start(), calls=%async_computation.6 | async-start | bytes 1474560 | tf_op jit(solution)/shard_map/all_gather | solution.py:296
  42.4 29.8 %collective-permute-start.2 = (bf16[384,1536]{1,0:T(8,128)(2,1)S(1)}, bf16[384,1536]{1,0:T(8,128)(2,1)}, u32[]{:S(2)}, u32[]{:S(2)}) collective-permute-start(bf16[384,1536]{1,0:T(8,128)(2,1)S(1)} %copy-done.51), channel_id=1, source_target_pairs={{0,1},{1,0},{2,3},{3,2},{4,5},{5,4},{6,7},{7,6},{8,9},{9,8},{10,11... | collective-permute-start | bytes 3538952 | tf_op jit(solution)/shard_map/ppermute | solution.py:397
  67.6 46.0 %collective-permute-start.6 = (bf16[4,192,1280]{2,1,0:T(8,128)(2,1)}, bf16[4,192,1280]{2,1,0:T(8,128)(2,1)}, u32[]{:S(2)}, u32[]{:S(2)}) collective-permute-start(bf16[4,192,1280]{2,1,0:T(8,128)(2,1)} %bitcast.394), channel_id=1, source_target_pairs={{0,2},{1,3},{2,0},{3,1},{4,6},{5,7},{6,4},{7,5},{8,10},{9,11},{10,... | collective-permute-start | bytes 5898248 | tf_op jit(solution)/shard_map/ppermute | solution.py:303
  69.9 67.4 %all-gather.10.cloned.1.call-start = ((), (), s32[]{:S(2)}) async-start(), calls=%async_computation.7 | async-start | bytes 1966080 | tf_op jit(solution)/shard_map/all_gather | solution.py:296
  70.1 27.5 %collective-permute-start.8 = (bf16[384,1536]{1,0:T(8,128)(2,1)}, bf16[384,1536]{1,0:T(8,128)(2,1)S(1)}, u32[]{:S(2)}, u32[]{:S(2)}) collective-permute-start(bf16[384,1536]{1,0:T(8,128)(2,1)} %param.31), channel_id=1, source_target_pairs={{0,1},{1,0},{2,3},{3,2},{4,5},{5,4},{6,7},{7,6},{8,9},{9,8},{10,11... | collective-permute-start | bytes 3538952 | tf_op jit(solution)/shard_map/ppermute | solution.py:397
  74.1 42.9 %collective-permute-start.3 = (bf16[768,1536]{1,0:T(8,128)(2,1)S(1)}, bf16[768,1536]{1,0:T(8,128)(2,1)}, u32[]{:S(2)}, u32[]{:S(2)}) collective-permute-start(bf16[768,1536]{1,0:T(8,128)(2,1)S(1)} %pad_maximum_fusion.7), channel_id=1, source_target_pairs={{0,16},{16,0},{1,17},{17,1},{2,18},{18,2},{3,19},{19,3},{4,20},{20... | collective-permute-start | bytes 7077896 | tf_op jit(solution)/shard_map/ppermute | solution.py:394
  100.5 101.3 %all-gather.12.cloned.1.call-start = ((), (), s32[]{:S(2)}) async-start(), calls=%async_computation.8 | async-start | bytes 1966080 | tf_op jit(solution)/shard_map/all_gather | solution.py:296
  100.7 47.1 %collective-permute-start.10 = (bf16[4,192,768]{2,1,0:T(8,128)(2,1)}, bf16[4,192,768]{2,1,0:T(8,128)(2,1)}, u32[]{:S(2)}, u32[]{:S(2)}) collective-permute-start(bf16[4,192,768]{2,1,0:T(8,128)(2,1)} %bitcast.402), channel_id=1, source_target_pairs={{0,2},{1,3},{2,0},{3,1},{4,6},{5,7},{6,4},{7,5},{8,10},{9,11},{10,... | collective-permute-start | bytes 3538952 | tf_op jit(solution)/shard_map/ppermute | solution.py:303
  147.8 50.7 %collective-permute-start.9 = (bf16[768,1536]{1,0:T(8,128)(2,1)}, bf16[768,1536]{1,0:T(8,128)(2,1)}, u32[]{:S(2)}, u32[]{:S(2)}) collective-permute-start(bf16[768,1536]{1,0:T(8,128)(2,1)} %pad_maximum_fusion.8), channel_id=1, source_target_pairs={{0,16},{16,0},{1,17},{17,1},{2,18},{18,2},{3,19},{19,3},{4,20},{20... | collective-permute-start | bytes 7077896 | tf_op jit(solution)/shard_map/ppermute | solution.py:394
  151.8 30.7 %collective-permute-start.11 = (bf16[2,384,384]{2,1,0:T(8,128)(2,1)}, bf16[2,384,384]{2,1,0:T(8,128)(2,1)}, u32[]{:S(2)}, u32[]{:S(2)}) collective-permute-start(bf16[2,384,384]{2,1,0:T(8,128)(2,1)} %dynamic-slice_bitcast_fusion.4), channel_id=1, source_target_pairs={{0,1},{1,0},{2,3},{3,2},{4,5},{5,4},{6,7},{7,6},{8,9},{9,8},{10,11... | collective-permute-start | bytes 1769480 | tf_op jit(solution)/shard_map/ppermute | solution.py:397
  158.5 99.0 %all-gather.14.cloned.1.call-start = ((), (), s32[]{:S(2)}) async-start(), calls=%async_computation.9 | async-start | bytes 1966080 | tf_op jit(solution)/shard_map/all_gather | solution.py:296
  158.9 42.9 %collective-permute-start.7 = (bf16[4,192,1024]{2,1,0:T(8,128)(2,1)}, bf16[4,192,1024]{2,1,0:T(8,128)(2,1)}, u32[]{:S(2)}, u32[]{:S(2)}) collective-permute-start(bf16[4,192,1024]{2,1,0:T(8,128)(2,1)} %bitcast.396), channel_id=1, source_target_pairs={{0,2},{1,3},{2,0},{3,1},{4,6},{5,7},{6,4},{7,5},{8,10},{9,11},{10,... | collective-permute-start | bytes 4718600 | tf_op jit(solution)/shard_map/ppermute | solution.py:303
  217.1 28.6 %collective-permute-start.14 = (bf16[384,1536]{1,0:T(8,128)(2,1)}, bf16[384,1536]{1,0:T(8,128)(2,1)}, u32[]{:S(2)}, u32[]{:S(2)}) collective-permute-start(bf16[384,1536]{1,0:T(8,128)(2,1)} %slice.273), channel_id=1, source_target_pairs={{0,1},{1,0},{2,3},{3,2},{4,5},{5,4},{6,7},{7,6},{8,9},{9,8},{10,11... | collective-permute-start | bytes 3538952 | tf_op jit(solution)/shard_map/ppermute | solution.py:397
  217.7 36.7 %collective-permute-start.15 = (bf16[4,192,1024]{2,1,0:T(8,128)(2,1)}, bf16[4,192,1024]{2,1,0:T(8,128)(2,1)}, u32[]{:S(2)}, u32[]{:S(2)}) collective-permute-start(bf16[4,192,1024]{2,1,0:T(8,128)(2,1)} %bitcast.398), channel_id=1, source_target_pairs={{0,2},{1,3},{2,0},{3,1},{4,6},{5,7},{6,4},{7,5},{8,10},{9,11},{10,... | collective-permute-start | bytes 4718600 | tf_op jit(solution)/shard_map/ppermute | solution.py:303
  219.1 217.6 %reduce-scatter.6.cloned.1.call-start = ((), (), s32[]{:S(2)}) async-start(), calls=%async_computation.10 | async-start | bytes 1966080 | tf_op jit(solution)/shard_map/reduce_scatter | solution.py:330
  256.0 27.4 %collective-permute-start.16 = (bf16[384,1536]{1,0:T(8,128)(2,1)}, bf16[384,1536]{1,0:T(8,128)(2,1)}, u32[]{:S(2)}, u32[]{:S(2)}) collective-permute-start(bf16[384,1536]{1,0:T(8,128)(2,1)} %multiply_convert_fusion.6), channel_id=1, source_target_pairs={{0,1},{1,0},{2,3},{3,2},{4,5},{5,4},{6,7},{7,6},{8,9},{9,8},{10,11... | collective-permute-start | bytes 3538952 | tf_op jit(solution)/shard_map/ppermute | solution.py:397
  257.5 35.5 %collective-permute-start.18 = (bf16[4,128,1536]{2,1,0:T(8,128)(2,1)}, bf16[4,128,1536]{2,1,0:T(8,128)(2,1)S(1)}, u32[]{:S(2)}, u32[]{:S(2)}) collective-permute-start(bf16[4,128,1536]{2,1,0:T(8,128)(2,1)} %bitcast.400), channel_id=1, source_target_pairs={{0,2},{1,3},{2,0},{3,1},{4,6},{5,7},{6,4},{7,5},{8,10},{9,11},{10,... | collective-permute-start | bytes 4718600 | tf_op jit(solution)/shard_map/ppermute | solution.py:303
  350.6 37.3 %collective-permute-start.21 = (bf16[4,128,1536]{2,1,0:T(8,128)(2,1)S(1)}, bf16[4,128,1536]{2,1,0:T(8,128)(2,1)S(1)}, u32[]{:S(2)}, u32[]{:S(2)}) collective-permute-start(bf16[4,128,1536]{2,1,0:T(8,128)(2,1)S(1)} %dynamic-slice_bitcast_fusion.3), channel_id=1, source_target_pairs={{0,2},{1,3},{2,0},{3,1},{4,6},{5,7},{6,4},{7,5},{8,10},{9,11},{10,... | collective-permute-start | bytes 4718600 | tf_op jit(solution)/shard_map/ppermute | solution.py:320
  354.2 28.0 %collective-permute-start.20 = (bf16[384,1536]{1,0:T(8,128)(2,1)S(1)}, bf16[384,1536]{1,0:T(8,128)(2,1)S(1)}, u32[]{:S(2)}, u32[]{:S(2)}) collective-permute-start(bf16[384,1536]{1,0:T(8,128)(2,1)S(1)} %slice.272), channel_id=1, source_target_pairs={{0,1},{1,0},{2,3},{3,2},{4,5},{5,4},{6,7},{7,6},{8,9},{9,8},{10,11... | collective-permute-start | bytes 3538952 | tf_op jit(solution)/shard_map/ppermute | solution.py:397
  361.7 59.6 %collective-permute-start.23 = (bf16[4,192,1024]{2,1,0:T(8,128)(2,1)}, bf16[4,192,1024]{2,1,0:T(8,128)(2,1)}, u32[]{:S(2)}, u32[]{:S(2)}) collective-permute-start(bf16[4,192,1024]{2,1,0:T(8,128)(2,1)} %dynamic-slice_bitcast_fusion.2), channel_id=1, source_target_pairs={{0,2},{1,3},{2,0},{3,1},{4,6},{5,7},{6,4},{7,5},{8,10},{9,11},{10,... | collective-permute-start | bytes 4718600 | tf_op jit(solution)/shard_map/ppermute | solution.py:320
  387.0 37.5 %collective-permute-start.22 = (bf16[384,1536]{1,0:T(8,128)(2,1)}, bf16[384,1536]{1,0:T(8,128)(2,1)}, u32[]{:S(2)}, u32[]{:S(2)}) collective-permute-start(bf16[384,1536]{1,0:T(8,128)(2,1)} %fusion.65), channel_id=1, source_target_pairs={{0,1},{1,0},{2,3},{3,2},{4,5},{5,4},{6,7},{7,6},{8,9},{9,8},{10,11... | collective-permute-start | bytes 3538952 | tf_op jit(solution)/shard_map/ppermute | solution.py:397
  396.1 127.8 %reduce-scatter.8.cloned.1.call-start = ((), (), s32[]{:S(2)}) async-start(), calls=%async_computation.11 | async-start | bytes 1966080 | tf_op jit(solution)/shard_map/reduce_scatter | solution.py:330
  427.7 96.2 %reduce-scatter.10.cloned.1.call-start = ((), (), s32[]{:S(2)}) async-start(), calls=%async_computation.12 | async-start | bytes 1966080 | tf_op jit(solution)/shard_map/reduce_scatter | solution.py:330
  430.7 37.1 %collective-permute-start.25 = (bf16[4,192,1024]{2,1,0:T(8,128)(2,1)}, bf16[4,192,1024]{2,1,0:T(8,128)(2,1)}, u32[]{:S(2)}, u32[]{:S(2)}) collective-permute-start(bf16[4,192,1024]{2,1,0:T(8,128)(2,1)} %dynamic-slice_bitcast_fusion.1), channel_id=1, source_target_pairs={{0,2},{1,3},{2,0},{3,1},{4,6},{5,7},{6,4},{7,5},{8,10},{9,11},{10,... | collective-permute-start | bytes 4718600 | tf_op jit(solution)/shard_map/ppermute | solution.py:320
  473.5 116.0 %reduce-scatter.12.cloned.1.call-start = ((), (), s32[]{:S(2)}) async-start(), calls=%async_computation.13 | async-start | bytes 1474560 | tf_op jit(solution)/shard_map/reduce_scatter | solution.py:330
  488.3 32.6 %collective-permute-start.28 = (bf16[4,192,768]{2,1,0:T(8,128)(2,1)}, bf16[4,192,768]{2,1,0:T(8,128)(2,1)}, u32[]{:S(2)}, u32[]{:S(2)}) collective-permute-start(bf16[4,192,768]{2,1,0:T(8,128)(2,1)} %fusion.13), channel_id=1, source_target_pairs={{0,2},{1,3},{2,0},{3,1},{4,6},{5,7},{6,4},{7,5},{8,10},{9,11},{10,... | collective-permute-start | bytes 3538952 | tf_op jit(solution)/shard_map/ppermute | solution.py:320
  523.8 117.8 %reduce-scatter.14.cloned.1.call-start = ((), (), s32[]{:S(2)}) async-start(), calls=%async_computation.14 | async-start | bytes 2457600 | tf_op jit(solution)/shard_map/reduce_scatter | solution.py:330
  528.1 28.7 %collective-permute-start.29 = (bf16[768,1536]{1,0:T(8,128)(2,1)}, bf16[768,1536]{1,0:T(8,128)(2,1)}, u32[]{:S(2)}, u32[]{:S(2)}) collective-permute-start(bf16[768,1536]{1,0:T(8,128)(2,1)} %slice.267), channel_id=1, source_target_pairs={{0,16},{16,0},{1,17},{17,1},{2,18},{18,2},{3,19},{19,3},{4,20},{20... | collective-permute-start | bytes 7077896 | tf_op jit(solution)/shard_map/ppermute | solution.py:394
  540.4 49.1 %collective-permute-start.32 = (bf16[4,192,1280]{2,1,0:T(8,128)(2,1)}, bf16[4,192,1280]{2,1,0:T(8,128)(2,1)}, u32[]{:S(2)}, u32[]{:S(2)}) collective-permute-start(bf16[4,192,1280]{2,1,0:T(8,128)(2,1)} %dynamic-slice_bitcast_fusion), channel_id=1, source_target_pairs={{0,2},{1,3},{2,0},{3,1},{4,6},{5,7},{6,4},{7,5},{8,10},{9,11},{10,... | collective-permute-start | bytes 5898248 | tf_op jit(solution)/shard_map/ppermute | solution.py:320
  559.5 28.4 %collective-permute-start.30 = (bf16[384,1536]{1,0:T(8,128)(2,1)S(1)}, bf16[384,1536]{1,0:T(8,128)(2,1)S(1)}, u32[]{:S(2)}, u32[]{:S(2)}) collective-permute-start(bf16[384,1536]{1,0:T(8,128)(2,1)S(1)} %slice.271), channel_id=1, source_target_pairs={{0,1},{1,0},{2,3},{3,2},{4,5},{5,4},{6,7},{7,6},{8,9},{9,8},{10,11... | collective-permute-start | bytes 3538952 | tf_op jit(solution)/shard_map/ppermute | solution.py:397
  610.1 27.8 %collective-permute-start.39 = (bf16[384,1536]{1,0:T(8,128)(2,1)}, bf16[384,1536]{1,0:T(8,128)(2,1)}, u32[]{:S(2)}, u32[]{:S(2)}) collective-permute-start(bf16[384,1536]{1,0:T(8,128)(2,1)} %slice.270), channel_id=1, source_target_pairs={{0,1},{1,0},{2,3},{3,2},{4,5},{5,4},{6,7},{7,6},{8,9},{9,8},{10,11... | collective-permute-start | bytes 3538952 | tf_op jit(solution)/shard_map/ppermute | solution.py:397
  (125 other events, 1146.2 us)
Sparse Core Ops, SparseCore 0:
  22.6 44.9 all-gather.5
  70.1 28.7 all-gather.7
  101.0 36.2 all-gather.9
  158.6 34.9 all-gather.11
  219.2 35.8 all-gather.13
  396.2 34.3 reduce-scatter.5
  433.5 34.2 reduce-scatter.7
  473.6 33.4 reduce-scatter.9
  524.0 27.5 reduce-scatter.11
  597.7 40.0 reduce-scatter.13

commit v10 on v9

--- a/solution.py
+++ b/solution.py
@@ -636,7 +636,7 @@
     grad_normed1 = after(team_sum(after(part_normed1, first_held)), sum_first)
     tokens_grad = grad_resid + norm_back(grad_normed1 * gain_one, scaled1, inverse1)
     gate_own = own_of(after(grad_gate_w, first_held))
-    grad_up_w = after(grad_up_w, grad_normed1)
+    grad_up_w = after(grad_up_w, first_held)
     sum_second = after(sum_second, grad_normed1)
 
     def whole_cols(own):

time: 702 us -> 697 us (level)
  waiting for transfers between devices: 255 us -> 245 us
    ppermute x17, waiting for transfers between devices: 160 us -> 151 us  [swap_side(): return lax.ppermute(values, 'shard', side_pairs)]
    unnamed x205 -> x201, local copies, waits for them, and re-layouts: 19.6 us -> 20.2 us
  transfers between devices with their start and end apart: 58 -> 58, of which waited for: 26 -> 26; matrix products, arithmetic and copies ran while one was open for 37% -> 38% of each run, Pallas kernels for 6% -> 6%
where the time goes in v10:
time: 697 us; the launch traced here: 689 us
  waiting for transfers between devices  245 us (35%)
  matrix products  136 us (20%)
  other arithmetic  112 us (16%)
  local copies, waits for them, and re-layouts  101 us (14%)
  Pallas kernels  42.9 us (6%)
  starting transfers between devices  35.5 us (5%)
  between operations  16.3 us (2%)
    ppermute x17, waiting for transfers between devices, swap_side(): return lax.ppermute(values, 'shard', side_pairs)  151 us
    dot_general x7, matrix products, matmul(): return jnp.dot(left_side, right_side, preferred_element_type=jnp.float32)  51.1 us
    dot_general x6, matrix products, matmul_tn(): lax.dot_general(left_side, right_side, (((0,), (0,)), ((), ())), preferre...  41 us
    dot_general x6, matrix products, matmul_nt(): lax.dot_general(left_side, right_side, (((1,), (1,)), ((), ())), preferre...  40.9 us
    all_gather x5, waiting for transfers between devices, gather_line(): lax.all_gather(block, 'shard', axis=0, tiled=True, axis_index_groups=line...  31.6 us
    ppermute x5, waiting for transfers between devices, scatter_rest(): lax.ppermute(pick(halves, 1 - at, 1), 'shard', swap_pairs(count, step))  25.6 us
    ppermute x5, waiting for transfers between devices, gather_rest(): other = lax.ppermute(held, 'shard', swap_pairs(count, step))  24.4 us
    pallas_call x1, Pallas kernels, attend_back(): pl.pallas_call(body, grid_spec=pltpu.PrefetchScalarGridSpec(num_scalar_pr...  24.2 us
  transfers between devices with their start and end apart: 58, of which 26 were waited for; matrix products, arithmetic and copies ran while one was open for 38% of the time, Pallas kernels for 6%

profile of v10, /device:TPU:0, one launch (start us, length us, event | category | flops | bytes accessed | tf_op | source)
XLA Modules:
  0.0 688.7 jit_solution(3899383601420583739)
XLA Ops:
  15.7 5.8 collective-permute-done
  30.9 11.2 %collective-permute-done.1 = bf16[96,2816]{1,0:T(8,128)(2,1)S(1)} collective-permute-done((bf16[96,2816]{1,0:T(8,128)(2,1)S(1)}, bf16[96,2816]{1,0:T(8,128)(2,1)S(1)}, u32[]{:S(2)}, u32[]{:S(2)}) %collective-permute-start.1) | collective-permute-done | bytes 540704 | tf_op jit(solution)/shard_map/ppermute | solution.py:397
  44.3 23.4 %all-gather.6.cloned.1.call-done = bf16[768,1280]{1,0:T(8,128)(2,1)} async-done(((bf16[192,1280]{1,0:T(8,128)(2,1)}), bf16[768,1280]{1,0:T(8,128)(2,1)}) %all-gather.6.cloned.1.call-update) | async-done | bytes 1966096 | tf_op jit(solution)/shard_map/all_gather | solution.py:296
  77.1 20.5 %collective-permute-done.8 = bf16[384,1536]{1,0:T(8,128)(2,1)S(1)} collective-permute-done((bf16[384,1536]{1,0:T(8,128)(2,1)}, bf16[384,1536]{1,0:T(8,128)(2,1)S(1)}, u32[]{:S(2)}, u32[]{:S(2)}) %collective-permute-start.8) | collective-permute-done | bytes 1179680 | tf_op jit(solution)/shard_map/ppermute | solution.py:397
  101.3 12.3 %collective-permute-done.6 = bf16[4,192,1280]{2,1,0:T(8,128)(2,1)} collective-permute-done((bf16[4,192,1280]{2,1,0:T(8,128)(2,1)}, bf16[4,192,1280]{2,1,0:T(8,128)(2,1)}, u32[]{:S(2)}, u32[]{:S(2)}) %collective-permute-start.6) | collective-permute-done | bytes 1966112 | tf_op jit(solution)/shard_map/ppermute | solution.py:303
  121.1 8.0 %broadcast_multiply_fusion = (f32[1536,1536]{1,0:T(8,128)}, bf16[1536,1536]{1,0:T(8,128)(2,1)}) fusion(f32[1536]{0:T(1024)S(1)} %add_rsqrt_fusion, bf16[768,1536]{1,0:T(8,128)(2,1)} %collective-permute-done.3, bf16[768,1536]{1,0:T(8,128)(2,1)S(1)} %pad_maximum_fusion.7, f32[1536]{0:T(1024)S(1)} %get-tuple-element.141), kind=kLoop, calls=%fused_computation.22 | loop fusion | flops 16515072 | bytes 18886656 | tf_op jit(solution)/shard_map/mul | solution.py:35
  129.1 8.3 %all-gather.10.cloned.1.call-done = bf16[768,1024]{1,0:T(8,128)(2,1)} async-done(((bf16[192,1024]{1,0:T(8,128)(2,1)}), bf16[768,1024]{1,0:T(8,128)(2,1)}) %all-gather.10.cloned.1.call-update) | async-done | bytes 1572880 | tf_op jit(solution)/shard_map/all_gather | solution.py:296
  137.3 10.4 %convolution_convert_fusion.1.qkv_ref = bf16[1536,1152]{1,0:T(8,128)(2,1)} fusion(bf16[1536,1536]{1,0:T(8,128)(2,1)} %get-tuple-element.82, bf16[1536,1280]{1,0:T(8,128)(2,1)} %bitcast.350), kind=kOutput, calls=%fused_computation.5 | convolution fusion | flops 5437587456 | bytes 11796480 | tf_op jit(solution)/shard_map/dot_general | solution.py:244
  160.4 18.7 %attend.1 = f32[1536,384]{1,0:T(8,128)} custom-call(s32[4,8]{1,0:T(4,128)} %pad_add_fusion.1.facts_ref, bf16[1536,1152]{1,0:T(8,128)(2,1)} %convolution_convert_fusion.1.qkv_ref, f32[4,384,6]{2,1,0:T(8,128)} %bitcast.379, f32[4,6,384]{2,1,0:T(8,128)} %copy-done.61), custom_call_target="tpu_custom_call" | custom-call | flops 1811939328 | bytes 9437184 | tf_op jit(solution)/shard_map/attend/pallas_call | solution.py:129
  186.9 7.0 %fusion.8 = f32[1536,384]{1,0:T(8,128)} fusion(bf16[1536,1536]{1,0:T(8,128)(2,1)} %get-tuple-element.82, bf16[1536,768]{1,0:T(8,128)(2,1)} %bitcast.344), kind=kOutput, calls=%fused_computation.43 | convolution fusion | flops 1813708800 | bytes 8257536 | tf_op jit(solution)/shard_map/dot_general | solution.py:244
  222.1 23.6 %collective-permute-done.14 = bf16[384,1536]{1,0:T(8,128)(2,1)} collective-permute-done((bf16[384,1536]{1,0:T(8,128)(2,1)}, bf16[384,1536]{1,0:T(8,128)(2,1)}, u32[]{:S(2)}, u32[]{:S(2)}) %collective-permute-start.14) | collective-permute-done | bytes 1179680 | tf_op jit(solution)/shard_map/ppermute | solution.py:397
  248.0 6.4 collective-permute-done.15
  260.8 22.6 %collective-permute-done.16 = bf16[384,1536]{1,0:T(8,128)(2,1)} collective-permute-done((bf16[384,1536]{1,0:T(8,128)(2,1)}, bf16[384,1536]{1,0:T(8,128)(2,1)}, u32[]{:S(2)}, u32[]{:S(2)}) %collective-permute-start.16) | collective-permute-done | bytes 1179680 | tf_op jit(solution)/shard_map/ppermute | solution.py:397
  293.5 7.2 %fusion.71 = f32[1536,1024]{1,0:T(8,128)} fusion(bf16[1536,1536]{1,0:T(8,128)(2,1)S(1)} %bitcast.405, bf16[1024,1536]{1,0:T(8,128)(2,1)S(1)} %bitcast.383), kind=kOutput, calls=%fused_computation.297 | convolution fusion | flops 4831838208 | bytes 14155776 | tf_op jit(solution)/shard_map/dot_general | solution.py:254
  302.5 6.9 fusion.72
  309.4 11.5 %multiply_convert_fusion.1 = (bf16[1536,1024]{1,0:T(8,128)(2,1)}, bf16[1536,1024]{1,0:T(8,128)(2,1)S(1)}, bf16[1536,1024]{1,0:T(8,128)(2,1)S(1)}) fusion(f32[1536,1024]{1,0:T(8,128)} %fusion.72, f32[1536,1024]{1,0:T(8,128)} %fusion.71, bf16[1536,1536]{1,0:T(8,128)(2,1)S(1)} %pad_maximum_fusion, bf16[1536,1024]{1,0:T(8,128)(2,1)S(1)} %bitcast.391), kind=kOutput, calls=%fused_computation.6 | convolution fusion | flops 4855431168 | bytes 29884416 | tf_op jit(solution)/shard_map/dot_general | solution.py:244
  320.9 7.6 %fusion.73 = f32[1536,1536]{1,0:T(8,128)} fusion(bf16[1536,1024]{1,0:T(8,128)(2,1)S(1)} %get-tuple-element.157, bf16[1536,1024]{1,0:T(8,128)(2,1)S(1)} %bitcast.388), kind=kOutput, calls=%fused_computation.299 | convolution fusion | flops 4831838208 | bytes 15728640 | tf_op jit(solution)/shard_map/dot_general | solution.py:254
  328.5 7.9 %convolution_add_fusion.1 = f32[1536,1536]{1,0:T(8,128)S(1)} fusion(f32[1536,1536]{1,0:T(8,128)} %fusion.73, bf16[1536,1024]{1,0:T(8,128)(2,1)S(1)} %get-tuple-element.158, bf16[1536,1024]{1,0:T(8,128)(2,1)S(1)} %bitcast.392), kind=kOutput, calls=%fused_computation.3 | convolution fusion | flops 4834197504 | bytes 25165824 | tf_op jit(solution)/shard_map/dot_general | solution.py:254
  341.8 8.7 %convolution_convert_fusion.3 = bf16[1024,1536]{1,0:T(8,128)(2,1)S(1)} fusion(bf16[1536,1024]{1,0:T(8,128)(2,1)} %get-tuple-element.74, bf16[1536,1536]{1,0:T(8,128)(2,1)} %constant_dynamic-update-slice_fusion), kind=kOutput, calls=%fused_computation.28 | convolution fusion | flops 4833411072 | bytes 11010048 | tf_op jit(solution)/shard_map/dot_general | solution.py:248
  363.4 18.8 %collective-permute-done.20 = bf16[384,1536]{1,0:T(8,128)(2,1)S(1)} collective-permute-done((bf16[384,1536]{1,0:T(8,128)(2,1)S(1)}, bf16[384,1536]{1,0:T(8,128)(2,1)S(1)}, u32[]{:S(2)}, u32[]{:S(2)}) %collective-permute-start.20) | collective-permute-done | bytes 1179680 | tf_op jit(solution)/shard_map/ppermute | solution.py:397
  388.0 6.6 convolution_convert_fusion.2
  396.2 10.2 %fusion.74 = f32[1536,1536]{1,0:T(8,128)} fusion(bf16[1536,1024]{1,0:T(8,128)(2,1)} %get-tuple-element.74, bf16[1024,1536]{1,0:T(8,128)(2,1)} %bitcast.384), kind=kOutput, calls=%fused_computation.300 | convolution fusion | flops 4831838208 | bytes 15728640 | tf_op jit(solution)/shard_map/dot_general | solution.py:244
  406.4 14.9 %collective-permute-done.23 = bf16[4,192,1024]{2,1,0:T(8,128)(2,1)} collective-permute-done((bf16[4,192,1024]{2,1,0:T(8,128)(2,1)}, bf16[4,192,1024]{2,1,0:T(8,128)(2,1)}, u32[]{:S(2)}, u32[]{:S(2)}) %collective-permute-start.23) | collective-permute-done | bytes 1572896 | tf_op jit(solution)/shard_map/ppermute | solution.py:320
  436.7 6.0 convolution_convert_fusion.5
  450.9 6.6 multiply_convert_fusion.4
  457.4 10.4 %collective-permute-done.25 = bf16[4,192,1024]{2,1,0:T(8,128)(2,1)} collective-permute-done((bf16[4,192,1024]{2,1,0:T(8,128)(2,1)}, bf16[4,192,1024]{2,1,0:T(8,128)(2,1)}, u32[]{:S(2)}, u32[]{:S(2)}) %collective-permute-start.25) | collective-permute-done | bytes 1572896 | tf_op jit(solution)/shard_map/ppermute | solution.py:320
  479.0 5.8 collective-permute-done.27
  489.0 24.2 %attend_back.1 = (bf16[1536,1152]{1,0:T(8,128)(2,1)}, f32[4,384,6]{2,1,0:T(8,128)}, f32[4,6,384]{2,1,0:T(8,128)}) custom-call(s32[4,8]{1,0:T(4,128)} %pad_add_fusion.1.facts_ref, bf16[1536,1152]{1,0:T(8,128)(2,1)} %convolution_convert_fusion.1.qkv_ref, bf16[1536,384]{1,0:T(8,128)(2,1)} %get-tuple-element.80.grad_ref, f32[4,384,6]{2,1,0:T(8,128)} %bitcast.380, ...), custom_call_target="tpu_custom_call" | custom-call | flops 18119393280 | bytes 8257536 | tf_op jit(solution)/shard_map/attend_back/pallas_call | solution.py:208
  528.1 8.8 %convolution_convert_fusion = bf16[1536,1280]{1,0:T(8,128)(2,1)S(1)} fusion(bf16[1536,1536]{1,0:T(8,128)(2,1)} %get-tuple-element.82, bf16[1536,128]{1,0:T(8,128)(2,1)S(1)} %dynamic_update_slice.9, bf16[1536,1152]{1,0:T(8,128)(2,1)S(1)} %copy-done.29), kind=kOutput, calls=%fused_computation.4 | convolution fusion | flops 6049628160 | bytes 12582912 | tf_op jit(solution)/shard_map/dot_general | solution.py:248
  543.2 6.3 fusion.75
  566.9 20.9 %collective-permute-done.30 = bf16[384,1536]{1,0:T(8,128)(2,1)S(1)} collective-permute-done((bf16[384,1536]{1,0:T(8,128)(2,1)S(1)}, bf16[384,1536]{1,0:T(8,128)(2,1)S(1)}, u32[]{:S(2)}, u32[]{:S(2)}) %collective-permute-start.30) | collective-permute-done | bytes 1179680 | tf_op jit(solution)/shard_map/ppermute | solution.py:397
  632.8 11.1 %collective-permute-done.39 = bf16[384,1536]{1,0:T(8,128)(2,1)} collective-permute-done((bf16[384,1536]{1,0:T(8,128)(2,1)}, bf16[384,1536]{1,0:T(8,128)(2,1)}, u32[]{:S(2)}, u32[]{:S(2)}) %collective-permute-start.39) | collective-permute-done | bytes 1179680 | tf_op jit(solution)/shard_map/ppermute | solution.py:397
  (498 shorter events, 293.8 us)
Async XLA Ops:
  7.2 60.4 %all-gather.6.cloned.1.call-start = ((), (), s32[]{:S(2)}) async-start(), calls=%async_computation.5 | async-start | bytes 2457600 | tf_op jit(solution)/shard_map/all_gather | solution.py:296
  22.5 78.0 %all-gather.8.cloned.1.call-start = ((), (), s32[]{:S(2)}) async-start(), calls=%async_computation.6 | async-start | bytes 1474560 | tf_op jit(solution)/shard_map/all_gather | solution.py:296
  42.4 29.9 %collective-permute-start.2 = (bf16[384,1536]{1,0:T(8,128)(2,1)S(1)}, bf16[384,1536]{1,0:T(8,128)(2,1)}, u32[]{:S(2)}, u32[]{:S(2)}) collective-permute-start(bf16[384,1536]{1,0:T(8,128)(2,1)S(1)} %copy-done.49), channel_id=1, source_target_pairs={{0,1},{1,0},{2,3},{3,2},{4,5},{5,4},{6,7},{7,6},{8,9},{9,8},{10,11... | collective-permute-start | bytes 3538952 | tf_op jit(solution)/shard_map/ppermute | solution.py:397
  67.6 46.0 %collective-permute-start.6 = (bf16[4,192,1280]{2,1,0:T(8,128)(2,1)}, bf16[4,192,1280]{2,1,0:T(8,128)(2,1)}, u32[]{:S(2)}, u32[]{:S(2)}) collective-permute-start(bf16[4,192,1280]{2,1,0:T(8,128)(2,1)} %bitcast.394), channel_id=1, source_target_pairs={{0,2},{1,3},{2,0},{3,1},{4,6},{5,7},{6,4},{7,5},{8,10},{9,11},{10,... | collective-permute-start | bytes 5898248 | tf_op jit(solution)/shard_map/ppermute | solution.py:303
  69.9 67.4 %all-gather.10.cloned.1.call-start = ((), (), s32[]{:S(2)}) async-start(), calls=%async_computation.7 | async-start | bytes 1966080 | tf_op jit(solution)/shard_map/all_gather | solution.py:296
  70.1 27.5 %collective-permute-start.8 = (bf16[384,1536]{1,0:T(8,128)(2,1)}, bf16[384,1536]{1,0:T(8,128)(2,1)S(1)}, u32[]{:S(2)}, u32[]{:S(2)}) collective-permute-start(bf16[384,1536]{1,0:T(8,128)(2,1)} %param.31), channel_id=1, source_target_pairs={{0,1},{1,0},{2,3},{3,2},{4,5},{5,4},{6,7},{7,6},{8,9},{9,8},{10,11... | collective-permute-start | bytes 3538952 | tf_op jit(solution)/shard_map/ppermute | solution.py:397
  74.1 42.9 %collective-permute-start.3 = (bf16[768,1536]{1,0:T(8,128)(2,1)S(1)}, bf16[768,1536]{1,0:T(8,128)(2,1)}, u32[]{:S(2)}, u32[]{:S(2)}) collective-permute-start(bf16[768,1536]{1,0:T(8,128)(2,1)S(1)} %pad_maximum_fusion.7), channel_id=1, source_target_pairs={{0,16},{16,0},{1,17},{17,1},{2,18},{18,2},{3,19},{19,3},{4,20},{20... | collective-permute-start | bytes 7077896 | tf_op jit(solution)/shard_map/ppermute | solution.py:394
  100.5 101.3 %all-gather.12.cloned.1.call-start = ((), (), s32[]{:S(2)}) async-start(), calls=%async_computation.8 | async-start | bytes 1966080 | tf_op jit(solution)/shard_map/all_gather | solution.py:296
  100.7 47.1 %collective-permute-start.10 = (bf16[4,192,768]{2,1,0:T(8,128)(2,1)}, bf16[4,192,768]{2,1,0:T(8,128)(2,1)}, u32[]{:S(2)}, u32[]{:S(2)}) collective-permute-start(bf16[4,192,768]{2,1,0:T(8,128)(2,1)} %bitcast.402), channel_id=1, source_target_pairs={{0,2},{1,3},{2,0},{3,1},{4,6},{5,7},{6,4},{7,5},{8,10},{9,11},{10,... | collective-permute-start | bytes 3538952 | tf_op jit(solution)/shard_map/ppermute | solution.py:303
  147.8 50.8 %collective-permute-start.9 = (bf16[768,1536]{1,0:T(8,128)(2,1)}, bf16[768,1536]{1,0:T(8,128)(2,1)}, u32[]{:S(2)}, u32[]{:S(2)}) collective-permute-start(bf16[768,1536]{1,0:T(8,128)(2,1)} %pad_maximum_fusion.8), channel_id=1, source_target_pairs={{0,16},{16,0},{1,17},{17,1},{2,18},{18,2},{3,19},{19,3},{4,20},{20... | collective-permute-start | bytes 7077896 | tf_op jit(solution)/shard_map/ppermute | solution.py:394
  151.8 30.7 %collective-permute-start.11 = (bf16[2,384,384]{2,1,0:T(8,128)(2,1)}, bf16[2,384,384]{2,1,0:T(8,128)(2,1)}, u32[]{:S(2)}, u32[]{:S(2)}) collective-permute-start(bf16[2,384,384]{2,1,0:T(8,128)(2,1)} %dynamic-slice_bitcast_fusion.4), channel_id=1, source_target_pairs={{0,1},{1,0},{2,3},{3,2},{4,5},{5,4},{6,7},{7,6},{8,9},{9,8},{10,11... | collective-permute-start | bytes 1769480 | tf_op jit(solution)/shard_map/ppermute | solution.py:397
  158.4 99.1 %all-gather.14.cloned.1.call-start = ((), (), s32[]{:S(2)}) async-start(), calls=%async_computation.9 | async-start | bytes 1966080 | tf_op jit(solution)/shard_map/all_gather | solution.py:296
  158.9 42.9 %collective-permute-start.7 = (bf16[4,192,1024]{2,1,0:T(8,128)(2,1)}, bf16[4,192,1024]{2,1,0:T(8,128)(2,1)}, u32[]{:S(2)}, u32[]{:S(2)}) collective-permute-start(bf16[4,192,1024]{2,1,0:T(8,128)(2,1)} %bitcast.396), channel_id=1, source_target_pairs={{0,2},{1,3},{2,0},{3,1},{4,6},{5,7},{6,4},{7,5},{8,10},{9,11},{10,... | collective-permute-start | bytes 4718600 | tf_op jit(solution)/shard_map/ppermute | solution.py:303
  217.2 28.6 %collective-permute-start.14 = (bf16[384,1536]{1,0:T(8,128)(2,1)}, bf16[384,1536]{1,0:T(8,128)(2,1)}, u32[]{:S(2)}, u32[]{:S(2)}) collective-permute-start(bf16[384,1536]{1,0:T(8,128)(2,1)} %slice.273), channel_id=1, source_target_pairs={{0,1},{1,0},{2,3},{3,2},{4,5},{5,4},{6,7},{7,6},{8,9},{9,8},{10,11... | collective-permute-start | bytes 3538952 | tf_op jit(solution)/shard_map/ppermute | solution.py:397
  217.7 36.7 %collective-permute-start.15 = (bf16[4,192,1024]{2,1,0:T(8,128)(2,1)}, bf16[4,192,1024]{2,1,0:T(8,128)(2,1)}, u32[]{:S(2)}, u32[]{:S(2)}) collective-permute-start(bf16[4,192,1024]{2,1,0:T(8,128)(2,1)} %bitcast.398), channel_id=1, source_target_pairs={{0,2},{1,3},{2,0},{3,1},{4,6},{5,7},{6,4},{7,5},{8,10},{9,11},{10,... | collective-permute-start | bytes 4718600 | tf_op jit(solution)/shard_map/ppermute | solution.py:303
  219.1 217.6 %reduce-scatter.6.cloned.1.call-start = ((), (), s32[]{:S(2)}) async-start(), calls=%async_computation.10 | async-start | bytes 1966080 | tf_op jit(solution)/shard_map/reduce_scatter | solution.py:330
  256.0 27.4 %collective-permute-start.16 = (bf16[384,1536]{1,0:T(8,128)(2,1)}, bf16[384,1536]{1,0:T(8,128)(2,1)}, u32[]{:S(2)}, u32[]{:S(2)}) collective-permute-start(bf16[384,1536]{1,0:T(8,128)(2,1)} %multiply_convert_fusion.6), channel_id=1, source_target_pairs={{0,1},{1,0},{2,3},{3,2},{4,5},{5,4},{6,7},{7,6},{8,9},{9,8},{10,11... | collective-permute-start | bytes 3538952 | tf_op jit(solution)/shard_map/ppermute | solution.py:397
  257.5 35.5 %collective-permute-start.18 = (bf16[4,128,1536]{2,1,0:T(8,128)(2,1)}, bf16[4,128,1536]{2,1,0:T(8,128)(2,1)S(1)}, u32[]{:S(2)}, u32[]{:S(2)}) collective-permute-start(bf16[4,128,1536]{2,1,0:T(8,128)(2,1)} %bitcast.400), channel_id=1, source_target_pairs={{0,2},{1,3},{2,0},{3,1},{4,6},{5,7},{6,4},{7,5},{8,10},{9,11},{10,... | collective-permute-start | bytes 4718600 | tf_op jit(solution)/shard_map/ppermute | solution.py:303
  350.6 37.3 %collective-permute-start.21 = (bf16[4,128,1536]{2,1,0:T(8,128)(2,1)S(1)}, bf16[4,128,1536]{2,1,0:T(8,128)(2,1)S(1)}, u32[]{:S(2)}, u32[]{:S(2)}) collective-permute-start(bf16[4,128,1536]{2,1,0:T(8,128)(2,1)S(1)} %dynamic-slice_bitcast_fusion.3), channel_id=1, source_target_pairs={{0,2},{1,3},{2,0},{3,1},{4,6},{5,7},{6,4},{7,5},{8,10},{9,11},{10,... | collective-permute-start | bytes 4718600 | tf_op jit(solution)/shard_map/ppermute | solution.py:320
  354.2 28.0 %collective-permute-start.20 = (bf16[384,1536]{1,0:T(8,128)(2,1)S(1)}, bf16[384,1536]{1,0:T(8,128)(2,1)S(1)}, u32[]{:S(2)}, u32[]{:S(2)}) collective-permute-start(bf16[384,1536]{1,0:T(8,128)(2,1)S(1)} %slice.272), channel_id=1, source_target_pairs={{0,1},{1,0},{2,3},{3,2},{4,5},{5,4},{6,7},{7,6},{8,9},{9,8},{10,11... | collective-permute-start | bytes 3538952 | tf_op jit(solution)/shard_map/ppermute | solution.py:397
  361.7 59.6 %collective-permute-start.23 = (bf16[4,192,1024]{2,1,0:T(8,128)(2,1)}, bf16[4,192,1024]{2,1,0:T(8,128)(2,1)}, u32[]{:S(2)}, u32[]{:S(2)}) collective-permute-start(bf16[4,192,1024]{2,1,0:T(8,128)(2,1)} %dynamic-slice_bitcast_fusion.2), channel_id=1, source_target_pairs={{0,2},{1,3},{2,0},{3,1},{4,6},{5,7},{6,4},{7,5},{8,10},{9,11},{10,... | collective-permute-start | bytes 4718600 | tf_op jit(solution)/shard_map/ppermute | solution.py:320
  387.1 37.5 %collective-permute-start.22 = (bf16[384,1536]{1,0:T(8,128)(2,1)}, bf16[384,1536]{1,0:T(8,128)(2,1)}, u32[]{:S(2)}, u32[]{:S(2)}) collective-permute-start(bf16[384,1536]{1,0:T(8,128)(2,1)} %fusion.65), channel_id=1, source_target_pairs={{0,1},{1,0},{2,3},{3,2},{4,5},{5,4},{6,7},{7,6},{8,9},{9,8},{10,11... | collective-permute-start | bytes 3538952 | tf_op jit(solution)/shard_map/ppermute | solution.py:397
  396.1 127.8 %reduce-scatter.8.cloned.1.call-start = ((), (), s32[]{:S(2)}) async-start(), calls=%async_computation.11 | async-start | bytes 1966080 | tf_op jit(solution)/shard_map/reduce_scatter | solution.py:330
  427.8 96.1 %reduce-scatter.10.cloned.1.call-start = ((), (), s32[]{:S(2)}) async-start(), calls=%async_computation.12 | async-start | bytes 1966080 | tf_op jit(solution)/shard_map/reduce_scatter | solution.py:330
  430.7 37.1 %collective-permute-start.25 = (bf16[4,192,1024]{2,1,0:T(8,128)(2,1)}, bf16[4,192,1024]{2,1,0:T(8,128)(2,1)}, u32[]{:S(2)}, u32[]{:S(2)}) collective-permute-start(bf16[4,192,1024]{2,1,0:T(8,128)(2,1)} %dynamic-slice_bitcast_fusion.1), channel_id=1, source_target_pairs={{0,2},{1,3},{2,0},{3,1},{4,6},{5,7},{6,4},{7,5},{8,10},{9,11},{10,... | collective-permute-start | bytes 4718600 | tf_op jit(solution)/shard_map/ppermute | solution.py:320
  473.5 115.9 %reduce-scatter.12.cloned.1.call-start = ((), (), s32[]{:S(2)}) async-start(), calls=%async_computation.13 | async-start | bytes 1474560 | tf_op jit(solution)/shard_map/reduce_scatter | solution.py:330
  488.3 32.6 %collective-permute-start.28 = (bf16[4,192,768]{2,1,0:T(8,128)(2,1)}, bf16[4,192,768]{2,1,0:T(8,128)(2,1)}, u32[]{:S(2)}, u32[]{:S(2)}) collective-permute-start(bf16[4,192,768]{2,1,0:T(8,128)(2,1)} %fusion.13), channel_id=1, source_target_pairs={{0,2},{1,3},{2,0},{3,1},{4,6},{5,7},{6,4},{7,5},{8,10},{9,11},{10,... | collective-permute-start | bytes 3538952 | tf_op jit(solution)/shard_map/ppermute | solution.py:320
  523.8 123.8 %reduce-scatter.14.cloned.1.call-start = ((), (), s32[]{:S(2)}) async-start(), calls=%async_computation.14 | async-start | bytes 2457600 | tf_op jit(solution)/shard_map/reduce_scatter | solution.py:330
  528.1 28.6 %collective-permute-start.29 = (bf16[768,1536]{1,0:T(8,128)(2,1)}, bf16[768,1536]{1,0:T(8,128)(2,1)}, u32[]{:S(2)}, u32[]{:S(2)}) collective-permute-start(bf16[768,1536]{1,0:T(8,128)(2,1)} %slice.267), channel_id=1, source_target_pairs={{0,16},{16,0},{1,17},{17,1},{2,18},{18,2},{3,19},{19,3},{4,20},{20... | collective-permute-start | bytes 7077896 | tf_op jit(solution)/shard_map/ppermute | solution.py:394
  540.3 49.1 %collective-permute-start.32 = (bf16[4,192,1280]{2,1,0:T(8,128)(2,1)}, bf16[4,192,1280]{2,1,0:T(8,128)(2,1)}, u32[]{:S(2)}, u32[]{:S(2)}) collective-permute-start(bf16[4,192,1280]{2,1,0:T(8,128)(2,1)} %dynamic-slice_bitcast_fusion), channel_id=1, source_target_pairs={{0,2},{1,3},{2,0},{3,1},{4,6},{5,7},{6,4},{7,5},{8,10},{9,11},{10,... | collective-permute-start | bytes 5898248 | tf_op jit(solution)/shard_map/ppermute | solution.py:320
  559.4 28.4 %collective-permute-start.30 = (bf16[384,1536]{1,0:T(8,128)(2,1)S(1)}, bf16[384,1536]{1,0:T(8,128)(2,1)S(1)}, u32[]{:S(2)}, u32[]{:S(2)}) collective-permute-start(bf16[384,1536]{1,0:T(8,128)(2,1)S(1)} %slice.271), channel_id=1, source_target_pairs={{0,1},{1,0},{2,3},{3,2},{4,5},{5,4},{6,7},{7,6},{8,9},{9,8},{10,11... | collective-permute-start | bytes 3538952 | tf_op jit(solution)/shard_map/ppermute | solution.py:397
  615.2 28.7 %collective-permute-start.39 = (bf16[384,1536]{1,0:T(8,128)(2,1)}, bf16[384,1536]{1,0:T(8,128)(2,1)}, u32[]{:S(2)}, u32[]{:S(2)}) collective-permute-start(bf16[384,1536]{1,0:T(8,128)(2,1)} %slice.270), channel_id=1, source_target_pairs={{0,1},{1,0},{2,3},{3,2},{4,5},{5,4},{6,7},{7,6},{8,9},{9,8},{10,11... | collective-permute-start | bytes 3538952 | tf_op jit(solution)/shard_map/ppermute | solution.py:397
  (123 other events, 1127.4 us)
Sparse Core Ops, SparseCore 0:
  22.6 44.9 all-gather.5
  70.1 28.7 all-gather.7
  101.0 36.2 all-gather.9
  158.6 34.9 all-gather.11
  219.2 35.8 all-gather.13
  396.2 34.3 reduce-scatter.5
  433.5 34.2 reduce-scatter.7
  473.7 33.4 reduce-scatter.9
  524.0 27.5 reduce-scatter.11
  599.0 39.8 reduce-scatter.13
